TPU v7x, 32 devices: a whole 2x2x4 slice. The times are simulated.
32 devices in a mesh: dp: 16 (over z, y, core), fsdp: 2 (over x).
Axes of the slice: x: 2, y: 2, z: 4, core: 2. Of those that a mesh axis runs over, the one named last changes fastest.
Arguments:
- latents: bfloat16 [32768, 768], P(('dp', 'fsdp')), may hold values from -6 to 6
- size_tags: int32 [32], P(('dp', 'fsdp')), may hold values from 0 to 1
- timesteps: int32 [32, 4], P(('dp', 'fsdp')), may hold values from 0 to 999
- classes: int32 [32, 4], P(('dp', 'fsdp')), may hold values from 0 to 999
- step_table: bfloat16 [1000, 768], P('fsdp', 'dp'), may hold values from -5 to 5
- class_table: bfloat16 [1000, 768], P('fsdp', 'dp'), may hold values from -5 to 5
- modulation_weight: bfloat16 [768, 4608], P('fsdp', 'dp'), may hold values from -0.21875 to 0.21875
- attn_kernel: bfloat16 [9, 768], P(None, 'dp'), may hold values from -2 to 2
- qkv_weight: bfloat16 [768, 2304], P('fsdp', 'dp'), may hold values from -0.21875 to 0.21875
- proj_weight: bfloat16 [768, 768], P('fsdp', 'dp'), may hold values from -1.75 to 1.75
- expand_weight: bfloat16 [768, 3072], P('fsdp', 'dp'), may hold values from -0.21875 to 0.21875
- ffn_kernel: bfloat16 [9, 3072], P(None, 'dp'), may hold values from -2 to 2
- shrink_weight: bfloat16 [3072, 768], P('fsdp', 'dp'), may hold values from -0.109375 to 0.109375
- cotangent: bfloat16 [32768, 768], P(('dp', 'fsdp')), may hold values from -6 to 6
Outputs:
- block_output: bfloat16 [32768, 768], P(('dp', 'fsdp'))
- input_grad: float32 [32768, 768], P(('dp', 'fsdp'))
- step_table_grad: float32 [1000, 768], P('fsdp', 'dp')
- class_table_grad: float32 [1000, 768], P('fsdp', 'dp')
- modulation_grad: float32 [768, 4608], P('fsdp', 'dp')
- attn_kernel_grad: float32 [9, 768], P(None, 'dp')
- qkv_grad: float32 [768, 2304], P('fsdp', 'dp')
- proj_grad: float32 [768, 768], P('fsdp', 'dp')
- expand_grad: float32 [768, 3072], P('fsdp', 'dp')
- ffn_kernel_grad: float32 [9, 3072], P(None, 'dp')
- shrink_grad: float32 [3072, 768], P('fsdp', 'dp')
Inputs may be any that keep to these rules, and one draw needn't show every extreme that they name: `size_tags`: a slot with tag 0 holds one item of 1024 tokens, with tag 1 four items of 16 x 16 tokens. `timesteps`: in a slot with tag 0 only entry 0 is used. `classes`: in a slot with tag 0 only entry 0 is used.
All inputs are finite; a program needn't handle non-finite values.
Results may differ from a plain program's by a relative error of at most 0.019.
The roundings to bfloat16 on the way count: a program that leaves them out, or rounds other values in their place, can miss the bound.
Values may be sent and summed in bfloat16 or wider, within the bound.
No kernel may reach another device: no remote copies, remote signals or barrier semaphores. Data moves between devices by JAX's collectives and lax.ppermute only.
A program may use at most 384 MiB of HBM per device.

v0:
```python
import jax
import jax.numpy as jnp
from jax import lax
from jax.sharding import PartitionSpec as P

D = 768
H = 12
HD = 64
STEPS = 1000
CLASSES = 1000
SIDE = 32
GROUP = 256


def token_items(size_tag):
    row_index = jnp.arange(SIDE, dtype=jnp.int32)
    quadrant = row_index // (SIDE // 2)
    layout = quadrant[:, None] * 2 + quadrant[None, :]
    return (layout * size_tag).reshape(SIDE * SIDE)


def edge_masks(size_tag):
    row_index = jnp.arange(SIDE, dtype=jnp.int32)
    half_side = SIDE // 2
    collected = []
    for offset in (-1, 0, 1):
        neighbour = row_index + offset
        inside = (neighbour >= 0) & (neighbour < SIDE)
        same_item = jnp.maximum(neighbour, 0) // half_side == row_index // half_side
        collected.append((inside & (same_item | (size_tag == 0))).astype(jnp.float32))
    return collected


def depthwise(field, kernel, validity):
    channels = field.shape[-1]
    layout = field.reshape(SIDE, SIDE, channels)
    padded = jnp.pad(layout, ((1, 1), (1, 1), (0, 0)))
    summed = jnp.zeros_like(layout)
    for row_step in range(3):
        for col_step in range(3):
            window = padded[row_step : row_step + SIDE, col_step : col_step + SIDE]
            allowed = validity[row_step][:, None] * validity[col_step][None, :]
            summed = summed + window * allowed[:, :, None] * kernel[row_step * 3 + col_step]
    return summed.reshape(SIDE * SIDE, channels)


def to_groups(field):
    channels = field.shape[-1]
    layout = field.reshape(SIDE // 2, 2, SIDE // 2, 2, channels)
    return layout.transpose(1, 3, 0, 2, 4).reshape(4, GROUP, channels)


def from_groups(field):
    channels = field.shape[-1]
    layout = field.reshape(2, 2, SIDE // 2, SIDE // 2, channels)
    return layout.transpose(2, 0, 3, 1, 4).reshape(SIDE * SIDE, channels)


def same_item_mask(size_tag):
    position = jnp.arange(SIDE // 2, dtype=jnp.int32) // (SIDE // 4)
    labels = ((position[:, None] * 2 + position[None, :]) * size_tag).reshape(GROUP)
    return labels[:, None] == labels[None, :]


def normalize(values):
    centre = values - jnp.mean(values, axis=-1, keepdims=True)
    variance = jnp.mean(centre * centre, axis=-1, keepdims=True)
    return centre * lax.rsqrt(variance + 1e-06)


def modulate(values, offset_rows, scale_rows):
    return normalize(values) * (1.0 + scale_rows) + offset_rows


def per_token(mod_rows, labels):
    pieces = []
    for component in range(6):
        column = mod_rows[:, component * D : (component + 1) * D]
        chosen = column[0][None, :] * jnp.ones((labels.shape[0], 1), jnp.float32)
        for other_item in range(1, 4):
            chosen = jnp.where((labels == other_item)[:, None], column[other_item][None, :], chosen)
        pieces.append(chosen)
    return tuple(pieces)


def smooth_gate(values):
    return jax.nn.gelu(values, approximate=True)


def cross(left, right):
    return lax.dot_general(
        left, right, (((0,), (0,)), ((), ())), preferred_element_type=jnp.float32
    )


def against(left, right):
    return lax.dot_general(
        left, right, (((1,), (1,)), ((), ())), preferred_element_type=jnp.float32
    )


def attention_scores(queries, key_rows, allowed):
    scores = jnp.einsum(
        "gqhd,gkhd->ghqk", queries, key_rows, preferred_element_type=jnp.float32
    ) * HD ** (-0.5)
    return jnp.where(allowed[None, None], scores, -1e30)


def fetch_forward(
    step_table,
    class_table,
    modulation_weight,
    qkv_weight,
    proj_weight,
    expand_weight,
    shrink_weight,
    attn_kernel,
    ffn_kernel,
):
    gathered = (
        lax.all_gather(step_table, "fsdp", axis=0, tiled=True),
        lax.all_gather(class_table, "fsdp", axis=0, tiled=True),
        lax.all_gather(modulation_weight, "fsdp", axis=0, tiled=True),
        lax.all_gather(qkv_weight, "fsdp", axis=0, tiled=True),
        lax.all_gather(proj_weight, "fsdp", axis=0, tiled=True),
        lax.all_gather(expand_weight, "fsdp", axis=0, tiled=True),
        lax.all_gather(shrink_weight, "fsdp", axis=0, tiled=True),
    )
    return (
        lax.all_gather(gathered[0], "dp", axis=1, tiled=True),
        lax.all_gather(gathered[1], "dp", axis=1, tiled=True),
        lax.all_gather(gathered[2], "dp", axis=1, tiled=True),
        lax.all_gather(gathered[3], "dp", axis=1, tiled=True),
        lax.all_gather(gathered[4], "dp", axis=1, tiled=True),
        lax.all_gather(gathered[5], "dp", axis=1, tiled=True),
        lax.all_gather(gathered[6], "dp", axis=1, tiled=True),
        lax.all_gather(attn_kernel, "dp", axis=1, tiled=True),
        lax.all_gather(ffn_kernel, "dp", axis=1, tiled=True),
    )


def fetch_again(modulation_weight, qkv_weight, proj_weight, expand_weight, shrink_weight):
    gathered = (
        lax.all_gather(modulation_weight, "fsdp", axis=0, tiled=True),
        lax.all_gather(qkv_weight, "fsdp", axis=0, tiled=True),
        lax.all_gather(proj_weight, "fsdp", axis=0, tiled=True),
        lax.all_gather(expand_weight, "fsdp", axis=0, tiled=True),
        lax.all_gather(shrink_weight, "fsdp", axis=0, tiled=True),
    )
    return (
        lax.all_gather(gathered[0], "dp", axis=1, tiled=True),
        lax.all_gather(gathered[1], "dp", axis=1, tiled=True),
        lax.all_gather(gathered[2], "dp", axis=1, tiled=True),
        lax.all_gather(gathered[3], "dp", axis=1, tiled=True),
        lax.all_gather(gathered[4], "dp", axis=1, tiled=True),
    )


def body(
    latents,
    size_tags,
    timesteps,
    classes,
    step_table,
    class_table,
    modulation_weight,
    attn_kernel,
    qkv_weight,
    proj_weight,
    expand_weight,
    ffn_kernel,
    shrink_weight,
    cotangent,
):
    (
        step_full,
        class_full,
        mod_full,
        qkv_full,
        proj_full,
        expand_full,
        shrink_full,
        attn_full,
        ffn_full,
    ) = fetch_forward(
        step_table,
        class_table,
        modulation_weight,
        qkv_weight,
        proj_weight,
        expand_weight,
        shrink_weight,
        attn_kernel,
        ffn_kernel,
    )
    size_tag = size_tags[0]
    steps_hot = (timesteps[0][:, None] == jnp.arange(STEPS, dtype=jnp.int32)[None, :]).astype(
        jnp.float32
    )
    class_hot = (classes[0][:, None] == jnp.arange(CLASSES, dtype=jnp.int32)[None, :]).astype(
        jnp.float32
    )
    cond = jnp.dot(
        steps_hot.astype(jnp.bfloat16), step_full, preferred_element_type=jnp.float32
    ) + jnp.dot(class_hot.astype(jnp.bfloat16), class_full, preferred_element_type=jnp.float32)
    activated, silu_back = jax.vjp(jax.nn.silu, cond)
    act_low = activated.astype(jnp.bfloat16)
    mod_rows = jnp.dot(act_low, mod_full, preferred_element_type=jnp.float32)
    labels = token_items(size_tag)

    def spread_rows(rows):
        return per_token(rows, labels)

    (shift_one, scale_one, gate_one, shift_two, scale_two, gate_two), spread_back = jax.vjp(
        spread_rows, mod_rows
    )
    validity = edge_masks(size_tag)
    allowed = same_item_mask(size_tag)

    def conv_pass(field, kernel):
        return depthwise(field, kernel, validity)

    inputs = latents.astype(jnp.float32)
    first, first_back = jax.vjp(modulate, inputs, shift_one, scale_one)
    conv_out, conv_one_back = jax.vjp(conv_pass, first, attn_full.astype(jnp.float32))
    conv_low = conv_out.astype(jnp.bfloat16)
    qkv_low = jnp.dot(conv_low, qkv_full, preferred_element_type=jnp.float32).astype(jnp.bfloat16)
    grouped = to_groups(qkv_low).reshape(4, GROUP, 3, H, HD)
    queries = grouped[:, :, 0]
    key_rows = grouped[:, :, 1]
    value_rows = grouped[:, :, 2]
    scores = attention_scores(queries, key_rows, allowed)
    highest = jnp.max(scores, axis=-1, keepdims=True)
    raised = jnp.exp(scores - highest)
    totals = jnp.sum(raised, axis=-1, keepdims=True)
    probs_low = (raised / totals).astype(jnp.bfloat16)
    log_total = highest + jnp.log(totals)
    mixed = jnp.einsum("ghqk,gkhd->gqhd", probs_low, value_rows, preferred_element_type=jnp.float32)
    merged_low = from_groups(mixed.reshape(4, GROUP, D)).astype(jnp.bfloat16)
    attn = jnp.dot(merged_low, proj_full, preferred_element_type=jnp.float32)
    resid = inputs + gate_one * attn
    second, second_back = jax.vjp(modulate, resid, shift_two, scale_two)
    second_low = second.astype(jnp.bfloat16)
    expanded = jnp.dot(second_low, expand_full, preferred_element_type=jnp.float32)
    conved, conv_two_back = jax.vjp(conv_pass, expanded, ffn_full.astype(jnp.float32))
    hidden, gate_back = jax.vjp(smooth_gate, conved)
    hidden_low = hidden.astype(jnp.bfloat16)
    shrunk = jnp.dot(hidden_low, shrink_full, preferred_element_type=jnp.float32)
    block_output = (resid + gate_two * shrunk).astype(jnp.bfloat16)
    mod_back, qkv_back, proj_back, expand_back, shrink_back = fetch_again(
        modulation_weight, qkv_weight, proj_weight, expand_weight, shrink_weight
    )
    d_out = cotangent.astype(jnp.float32)
    d_gate_two = d_out * shrunk
    d_shrunk = (gate_two * d_out).astype(jnp.bfloat16)
    shrink_term = cross(hidden_low, d_shrunk)
    (d_conved,) = gate_back(against(d_shrunk, shrink_back))
    d_expanded, ffn_term = conv_two_back(d_conved)
    d_expanded_low = d_expanded.astype(jnp.bfloat16)
    expand_term = cross(second_low, d_expanded_low)
    d_resid_norm, d_shift_two, d_scale_two = second_back(against(d_expanded_low, expand_back))
    d_resid = d_out + d_resid_norm
    d_gate_one = d_resid * attn
    d_attn = (gate_one * d_resid).astype(jnp.bfloat16)
    proj_term = cross(merged_low, d_attn)
    d_merged = against(d_attn, proj_back).astype(jnp.bfloat16)
    d_mixed = to_groups(d_merged).reshape(4, GROUP, H, HD)
    probs_again = jnp.exp(attention_scores(queries, key_rows, allowed) - log_total)
    probs_again_low = probs_again.astype(jnp.bfloat16)
    d_values = jnp.einsum(
        "ghqk,gqhd->gkhd", probs_again_low, d_mixed, preferred_element_type=jnp.float32
    )
    d_probs = jnp.einsum("gqhd,gkhd->ghqk", d_mixed, value_rows, preferred_element_type=jnp.float32)
    inner = jnp.sum(probs_again * d_probs, axis=-1, keepdims=True)
    d_scores = (probs_again * (d_probs - inner)).astype(jnp.bfloat16)
    d_queries = jnp.einsum(
        "ghqk,gkhd->gqhd", d_scores, key_rows, preferred_element_type=jnp.float32
    ) * HD ** (-0.5)
    d_keys = jnp.einsum(
        "ghqk,gqhd->gkhd", d_scores, queries, preferred_element_type=jnp.float32
    ) * HD ** (-0.5)
    stacked = jnp.stack([d_queries, d_keys, d_values], axis=2).reshape(4, GROUP, 3 * D)
    d_qkv = from_groups(stacked).astype(jnp.bfloat16)
    qkv_term = cross(conv_low, d_qkv)
    d_first, attn_term = conv_one_back(against(d_qkv, qkv_back))
    d_input_norm, d_shift_one, d_scale_one = first_back(d_first)
    input_grad = d_resid + d_input_norm
    (d_mod,) = spread_back(
        (d_shift_one, d_scale_one, d_gate_one, d_shift_two, d_scale_two, d_gate_two)
    )
    d_mod_low = d_mod.astype(jnp.bfloat16)
    (d_cond,) = silu_back(against(d_mod_low, mod_back))
    mod_term = cross(act_low, d_mod_low)
    step_term = lax.dot_general(
        steps_hot, d_cond, (((0,), (0,)), ((), ())), precision=lax.Precision.HIGHEST
    )
    class_term = lax.dot_general(
        class_hot, d_cond, (((0,), (0,)), ((), ())), precision=lax.Precision.HIGHEST
    )
    (
        step_cols,
        class_cols,
        mod_cols_sum,
        qkv_cols,
        proj_cols,
        expand_cols,
        shrink_cols,
        attn_kernel_part,
        ffn_kernel_part,
    ) = (
        lax.psum_scatter(
            step_term.astype(jnp.bfloat16), "dp", scatter_dimension=1, tiled=True
        ).astype(jnp.float32),
        lax.psum_scatter(
            class_term.astype(jnp.bfloat16), "dp", scatter_dimension=1, tiled=True
        ).astype(jnp.float32),
        lax.psum_scatter(
            mod_term.astype(jnp.bfloat16), "dp", scatter_dimension=1, tiled=True
        ).astype(jnp.float32),
        lax.psum_scatter(
            qkv_term.astype(jnp.bfloat16), "dp", scatter_dimension=1, tiled=True
        ).astype(jnp.float32),
        lax.psum_scatter(
            proj_term.astype(jnp.bfloat16), "dp", scatter_dimension=1, tiled=True
        ).astype(jnp.float32),
        lax.psum_scatter(
            expand_term.astype(jnp.bfloat16), "dp", scatter_dimension=1, tiled=True
        ).astype(jnp.float32),
        lax.psum_scatter(
            shrink_term.astype(jnp.bfloat16), "dp", scatter_dimension=1, tiled=True
        ).astype(jnp.float32),
        lax.psum_scatter(
            attn_term.astype(jnp.bfloat16), "dp", scatter_dimension=1, tiled=True
        ).astype(jnp.float32),
        lax.psum_scatter(
            ffn_term.astype(jnp.bfloat16), "dp", scatter_dimension=1, tiled=True
        ).astype(jnp.float32),
    )
    step_grad, class_grad, mod_grad, qkv_grad, proj_grad, expand_grad, shrink_grad = (
        lax.psum_scatter(
            step_cols.astype(jnp.bfloat16), "fsdp", scatter_dimension=0, tiled=True
        ).astype(jnp.float32),
        lax.psum_scatter(
            class_cols.astype(jnp.bfloat16), "fsdp", scatter_dimension=0, tiled=True
        ).astype(jnp.float32),
        lax.psum_scatter(
            mod_cols_sum.astype(jnp.bfloat16), "fsdp", scatter_dimension=0, tiled=True
        ).astype(jnp.float32),
        lax.psum_scatter(
            qkv_cols.astype(jnp.bfloat16), "fsdp", scatter_dimension=0, tiled=True
        ).astype(jnp.float32),
        lax.psum_scatter(
            proj_cols.astype(jnp.bfloat16), "fsdp", scatter_dimension=0, tiled=True
        ).astype(jnp.float32),
        lax.psum_scatter(
            expand_cols.astype(jnp.bfloat16), "fsdp", scatter_dimension=0, tiled=True
        ).astype(jnp.float32),
        lax.psum_scatter(
            shrink_cols.astype(jnp.bfloat16), "fsdp", scatter_dimension=0, tiled=True
        ).astype(jnp.float32),
    )
    attn_kernel_grad, ffn_kernel_grad = lax.psum((attn_kernel_part, ffn_kernel_part), "fsdp")
    return (
        block_output,
        input_grad,
        step_grad,
        class_grad,
        mod_grad,
        attn_kernel_grad,
        qkv_grad,
        proj_grad,
        expand_grad,
        ffn_kernel_grad,
        shrink_grad,
    )


def solution(mesh):
    in_specs = (
        P(("dp", "fsdp"), None),
        P(("dp", "fsdp")),
        P(("dp", "fsdp"), None),
        P(("dp", "fsdp"), None),
        P("fsdp", "dp"),
        P("fsdp", "dp"),
        P("fsdp", "dp"),
        P(None, "dp"),
        P("fsdp", "dp"),
        P("fsdp", "dp"),
        P("fsdp", "dp"),
        P(None, "dp"),
        P("fsdp", "dp"),
        P(("dp", "fsdp"), None),
    )
    out_specs = (
        P(("dp", "fsdp"), None),
        P(("dp", "fsdp"), None),
        P("fsdp", "dp"),
        P("fsdp", "dp"),
        P("fsdp", "dp"),
        P(None, "dp"),
        P("fsdp", "dp"),
        P("fsdp", "dp"),
        P("fsdp", "dp"),
        P(None, "dp"),
        P("fsdp", "dp"),
    )
    return jax.shard_map(body, mesh=mesh, in_specs=in_specs, out_specs=out_specs, check_vma=False)
```

profile of v0, /device:TPU:0, one launch (start us, length us, event | category | flops | bytes accessed | tf_op | source)
XLA Modules:
  0.0 1364.4 jit_solution(2046139072494940579)
XLA Ops:
  7.3 6.1 all-gather
  14.3 5.0 all-gather.1
  20.2 8.5 all_gather.62
  28.8 5.7 all_gather.65
  34.6 6.5 all_gather.67
  41.2 6.5 all_gather.69
  47.8 5.9 all_gather.72
  56.5 21.9 %all-gather.2 = bf16[16,48,9]{1,2,0:T(8,128)(2,1)S(1)} all-gather(bf16[1,48,9]{1,2,0:T(8,128)(2,1)S(1)} %bitcast.230), channel_id=1, replica_groups=mesh['dp'=16,'fsdp'=2] {'dp'}, dimensions={0}, use_global_device_ids=true | all-gather | bytes 14688 | tf_op jit(solution)/shard_map/all_gather | solution.py:137
  78.7 17.9 %all-gather.3 = bf16[16,192,9]{1,2,0:T(8,128)(2,1)S(1)} all-gather(bf16[1,192,9]{1,2,0:T(8,128)(2,1)S(1)} %bitcast.229), channel_id=1, replica_groups=mesh['dp'=16,'fsdp'=2] {'dp'}, dimensions={0}, use_global_device_ids=true | all-gather | bytes 58752 | tf_op jit(solution)/shard_map/all_gather | solution.py:138
  101.4 63.7 %all-gather.16.cloned.1.call-done = bf16[768,4608]{0,1:T(8,128)(2,1)} async-done(((bf16[768,288]{0,1:T(8,128)(2,1)}), bf16[768,4608]{0,1:T(8,128)(2,1)}) %all-gather.16.cloned.1.call-update) | async-done | bytes 7077904 | tf_op jit(solution)/shard_map/all_gather | solution.py:132
  171.5 5.1 fusion.33
  178.2 5.7 add_convert_fusion.2
  184.0 29.0 %all-gather.18.cloned.1.call-done = bf16[768,2304]{0,1:T(8,128)(2,1)} async-done(((bf16[768,144]{0,1:T(8,128)(2,1)}), bf16[768,2304]{0,1:T(8,128)(2,1)}) %all-gather.18.cloned.1.call-update) | async-done | bytes 3538960 | tf_op jit(solution)/shard_map/all_gather | solution.py:133
  213.0 7.5 convolution_convert_fusion.1
  220.5 10.2 reshape.849
  230.7 5.1 copy.136
  235.8 14.9 %reshape_reshape.8 = bf16[4,256,3,12,64]{4,3,2,1,0:T(8,128)(2,1)} reshape(bf16[2,2,16,16,2304]{4,3,2,1,0:T(8,128)(2,1)} %bitcast.186) | data formatting | bytes 9437184 | tf_op jit(solution)/shard_map/reshape;reshape | solution.py:228
  250.7 9.1 fusion.88
  259.7 5.3 copy.129
  269.4 6.0 copy.131
  292.4 6.1 convert_element_type.225
  303.3 5.3 fusion.87
  311.6 9.6 fusion.84
  321.3 22.1 %multiply_add_fusion = f32[32,32,3072]{2,1,0:T(8,128)} fusion(f32[32,32,3072]{2,1,0:T(8,128)S(1)} %bitcast.180, f32[3072]{0:T(1024)S(1)} %bitcast.200, f32[32,32]{1,0:T(8,128)S(1)} %get-tuple-element.159, f32[3072]{0:T(1024)S(1)} %bitcast.202, f32[32,32]{1,0:T(8,128)S(1)} %get-tuple-element.154, f32[3072]{0:T(1024)S(1)} %bitcast.204, ...), kind=kLoop, calls=%fused_computation.57 | loop fusion | flops 81788928 | bytes 25313280 | tf_op jit(solution)/shard_map/jvp()/add | solution.py:43
  343.4 10.0 fusion.17
  353.5 7.8 all-gather.24.cloned.1.call-done
  361.3 63.5 %multiply_reduce_fusion.8 = (f32[3072]{0:T(1024)}, f32[3072]{0:T(1024)}, f32[3072]{0:T(1024)}, f32[3072]{0:T(1024)}, f32[3072]{0:T(1024)}, /*index=5*/f32[3072]{...) fusion(f32[32,32,3072]{2,1,0:T(8,128)} %bitcast.181, f32[32,32]{1,0:T(8,128)S(1)} %get-tuple-element.159, ...), kind=kOutput, calls=%fused_computation.44 | convolution fusion | flops 4971798528 | bytes 44186624 | tf_op jit(solution)/shard_map/dot_general | solution.py:97
  424.8 42.0 %multiply_multiply_fusion.10 = (f32[32,32,3072]{2,1,0:T(8,128)}, f32[32,32,3072]{2,1,0:T(8,128)}, f32[32,32,3072]{2,1,0:T(8,128)}, f32[32,32,3072]{2,1,0:T(8,128...) fusion(f32[32,32,3072]{2,1,0:T(8,128)} %bitcast.179, ...), kind=kLoop, calls=%fused_computation.56 | loop fusion | flops 56623104 | bytes 125976576 | tf_op jit(solution)/shard_map/transpose(jvp())/mul | solution.py:43
  466.8 23.6 %pad_add_fusion = f32[34,34,3072]{2,1,0:T(8,128)} fusion(f32[32,32,3072]{2,1,0:T(8,128)} %get-tuple-element.116, f32[32,32,3072]{2,1,0:T(8,128)} %get-tuple-element.117, f32[32,32,3072]{2,1,0:T(8,128)} %get-tuple-element.118, f32[32,32,3072]{2,1,0:T(8,128)} %get-tuple-element.110), kind=kLoop, calls=%fused_computation.10 | loop fusion | flops 10653696 | bytes 64536576 | tf_op jit(solution)/shard_map/transpose(jvp())/add_any | solution.py:41
  490.4 31.4 %fusion.14 = bf16[32,32,3072]{2,1,0:T(8,128)(2,1)} fusion(f32[32,32,3072]{2,1,0:T(8,128)} %get-tuple-element.111, f32[32,32,3072]{2,1,0:T(8,128)} %get-tuple-element.112, f32[32,32,3072]{2,1,0:T(8,128)} %get-tuple-element.113, f32[32,32,3072]{2,1,0:T(8,128)} %get-tuple-element.114, f32[32,32,3072]{2,1,0:T(8,128)} %get-tuple-element.115, ...), kind=kLoop, calls=%fused_computation.26 | loop fusion | flops 18874368 | bytes 81788928 | tf_op jit(solution)/shard_map/convert
  521.8 11.2 select_reduce_fusion.13
  533.2 12.0 fusion.86
  559.8 5.9 reshape_reshape.9
  570.1 8.7 fusion.46
  578.8 9.4 multiply_reduce_fusion.9
  588.2 7.3 multiply_convert_fusion
  603.9 15.1 %copy.106 = bf16[4,256,3,12,64]{4,3,2,1,0:T(8,128)(2,1)} copy(bf16[4,256,3,12,64]{1,4,3,0,2:T(8,128)(2,1)} %maximum_convert_fusion) | data formatting | bytes 9437184 | tf_op jit(solution)/shard_map/convert_element_type | solution.py:283
  619.0 15.7 %convert_element_type.240 = bf16[2,2,16,16,2304]{4,3,2,1,0:T(8,128)(2,1)} reshape(bf16[4,256,3,12,64]{4,3,2,1,0:T(8,128)(2,1)} %copy.106) | data formatting | bytes 9437184 | tf_op jit(solution)/shard_map/convert_element_type | solution.py:283
  634.7 9.4 copy.107
  644.2 10.6 convert_element_type.242
  654.8 14.1 %multiply_multiply_fusion.19 = (f32[32,32,768]{2,1,0:T(8,128)}, f32[32,32,768]{2,1,0:T(8,128)S(1)}, f32[32,32,768]{2,1,0:T(8,128)S(1)}, f32[32,32,768]{2,1,0:T(8...) fusion(f32[768]{0:T(1024)S(1)} %copy-done.69, ...), kind=kOutput, calls=%fused_computation.160 | convolution fusion | flops 3638034432 | bytes 39779328 | tf_op jit(solution)/shard_map/dot_general | solution.py:97
  674.0 7.2 select_reduce_fusion.1
  681.3 10.2 select_reduce_fusion.5
  698.5 11.1 convert_element_type.252
  709.6 8.6 convolution_convert_fusion.4
  719.0 12.4 convolution_convert_fusion.3
  731.6 10.4 convolution_convert_fusion.2
  748.0 18.9 %multiply_reduce_fusion.18 = (f32[768]{0:T(1024)S(1)}, f32[768]{0:T(1024)S(1)}, f32[768]{0:T(1024)S(1)}, f32[768]{0:T(1024)S(1)}, f32[768]{0:T(1024)S(1)}, /*ind...) fusion(f32[32,32,768]{2,1,0:T(8,128)} %get-tuple-element.167, f32[32,32,768]{2,1,0:T(8,128)} %bitcast.183, ...), kind=kLoop, calls=%fused_computation.126 | loop fusion | flops 30663936 | bytes 7964672 | tf_op jit(solution)/shard_map/transpose(jvp())/reduce_sum | solution.py:43
  767.9 10.0 multiply_reduce_fusion.4
  781.4 35.6 %reduce-scatter.29.cloned.1.call-done = bf16[1000,48]{0,1:T(8,128)(2,1)} async-done(((bf16[1000,768]{0,1:T(8,128)(2,1)}), bf16[1000,48]{0,1:T(8,128)(2,1)}) %reduce-scatter.29.cloned.1.call-update) | async-done | bytes 96016 | tf_op jit(solution)/shard_map/reduce_scatter | solution.py:311
  817.1 70.8 %reduce-scatter.35.cloned.1.call-done = bf16[768,144]{0,1:T(8,128)(2,1)} async-done(((bf16[768,2304]{0,1:T(8,128)(2,1)}), bf16[768,144]{0,1:T(8,128)(2,1)}) %reduce-scatter.35.cloned.1.call-update) | async-done | bytes 221200 | tf_op jit(solution)/shard_map/reduce_scatter | solution.py:320
  889.9 76.2 %reduce-scatter.39.cloned.1.call-done = bf16[768,192]{0,1:T(8,128)(2,1)} async-done(((bf16[768,3072]{0,1:T(8,128)(2,1)}), bf16[768,192]{0,1:T(8,128)(2,1)}) %reduce-scatter.39.cloned.1.call-update) | async-done | bytes 294928 | tf_op jit(solution)/shard_map/reduce_scatter | solution.py:326
  969.3 75.7 %reduce-scatter.41.cloned.1.call-done = bf16[3072,48]{0,1:T(8,128)(2,1)} async-done(((bf16[3072,768]{0,1:T(8,128)(2,1)}), bf16[3072,48]{0,1:T(8,128)(2,1)}) %reduce-scatter.41.cloned.1.call-update) | async-done | bytes 294928 | tf_op jit(solution)/shard_map/reduce_scatter | solution.py:329
  1045.3 5.2 fusion.85
  1050.5 87.5 %reduce-scatter.33.cloned.1.call-done = bf16[768,288]{0,1:T(8,128)(2,1)} async-done(((bf16[768,4608]{0,1:T(8,128)(2,1)}), bf16[768,288]{0,1:T(8,128)(2,1)}) %reduce-scatter.33.cloned.1.call-update) | async-done | bytes 442384 | tf_op jit(solution)/shard_map/reduce_scatter | solution.py:317
  1140.1 5.1 add_add_fusion.2
  1145.2 50.2 %reduce-scatter.47.cloned.1.call-done = bf16[48,9]{1,0:T(8,128)(2,1)} async-done(((bf16[768,9]{1,0:T(8,128)(2,1)}), bf16[48,9]{1,0:T(8,128)(2,1)}) %reduce-scatter.47.cloned.1.call-update) | async-done | bytes 880
  1196.2 58.7 %reduce-scatter.55.cloned.1.call-done = bf16[192,9]{1,0:T(8,128)(2,1)} async-done(((bf16[3072,9]{1,0:T(8,128)(2,1)}), bf16[192,9]{1,0:T(8,128)(2,1)}) %reduce-scatter.55.cloned.1.call-update) | async-done | bytes 3472
  1255.8 8.9 all-reduce.70
  1269.1 23.1 %all-reduce.74.cloned.1.call-done = (bf16[1000,48]{0,1:T(8,128)(2,1)}, bf16[1000,48]{0,1:T(8,128)(2,1)}) async-done(((bf16[1000,48]{0,1:T(8,128)(2,1)}, bf16[1000,48]{0,1:T(8,128)(2,1)}), (bf16[1000,48]{0,1:T(8,128)(2,1)}, bf16[1000,48]{0,1:T(8,128)(2,1)})) %all-reduce.74.cloned.1.call-update) | async-done | bytes 192016
  1295.3 12.9 reduce-scatter.49.cloned.1.call-done
  1309.9 13.6 reduce-scatter.53.cloned.1.call-done
  1325.3 12.5 reduce-scatter.43.cloned.1.call-done
  1339.5 15.9 %reduce-scatter.45.cloned.1.call-done = bf16[384,288]{1,0:T(8,128)(2,1)} async-done(((bf16[768,288]{1,0:T(8,128)(2,1)}), bf16[384,288]{1,0:T(8,128)(2,1)}) %reduce-scatter.45.cloned.1.call-update) | async-done | bytes 221200
  (449 shorter events, 119.2 us)
Async XLA Ops:
  7.2 34.0 %copy-start.24 = (bf16[384,192]{0,1:T(8,128)(2,1)S(1)}, bf16[384,192]{0,1:T(8,128)(2,1)}, u32[]{:S(2)}) copy-start(bf16[384,192]{0,1:T(8,128)(2,1)} %param.24) | copy-start | bytes 442372
  7.2 40.6 %copy-start.25 = (bf16[1536,48]{0,1:T(8,128)(2,1)S(1)}, bf16[1536,48]{0,1:T(8,128)(2,1)}, u32[]{:S(2)}) copy-start(bf16[1536,48]{0,1:T(8,128)(2,1)} %param.26) | copy-start | bytes 442372
  7.2 47.3 %copy-start.2 = (bf16[1024,768]{1,0:T(8,128)(2,1)S(1)}, bf16[1024,768]{1,0:T(8,128)(2,1)}, u32[]{:S(2)}) copy-start(bf16[1024,768]{1,0:T(8,128)(2,1)} %param.14) | copy-start | bytes 4718596
  7.2 90.3 %all-gather.12.cloned.1.call-start = ((), (), s32[]{:S(2)}) async-start(), calls=%async_computation.14 | async-start | bytes 1671168 | tf_op jit(solution)/shard_map/all_gather | solution.py:130
  14.2 85.3 %all-gather.14.cloned.1.call-start = ((), (), s32[]{:S(2)}) async-start(), calls=%async_computation.15 | async-start | bytes 1671168 | tf_op jit(solution)/shard_map/all_gather | solution.py:131
  20.1 145.0 %all-gather.16.cloned.1.call-start = ((), (), s32[]{:S(2)}) async-start(), calls=%async_computation.16 | async-start | bytes 7520256 | tf_op jit(solution)/shard_map/all_gather | solution.py:132
  28.7 27.8 %copy-start.106 = (bf16[9,48]{1,0:T(8,128)(2,1)S(1)}, bf16[9,48]{1,0:T(8,128)(2,1)}, u32[]{:S(2)}) copy-start(bf16[9,48]{1,0:T(8,128)(2,1)} %param.21) | copy-start | bytes 2596
  28.7 50.0 %copy-start.105 = (bf16[9,192]{1,0:T(8,128)(2,1)S(1)}, bf16[9,192]{1,0:T(8,128)(2,1)}, u32[]{:S(2)}) copy-start(bf16[9,192]{1,0:T(8,128)(2,1)} %param.25) | copy-start | bytes 10372
  28.7 184.3 %all-gather.18.cloned.1.call-start = ((), (), s32[]{:S(2)}) async-start(), calls=%async_computation.17 | async-start | bytes 3760128 | tf_op jit(solution)/shard_map/all_gather | solution.py:133
  34.5 268.7 %all-gather.20.cloned.1.call-start = ((), (), s32[]{:S(2)}) async-start(), calls=%async_computation.18 | async-start | bytes 1253376 | tf_op jit(solution)/shard_map/all_gather | solution.py:134
  41.1 56.5 %copy-start.127 = (s32[1,4]{1,0:T(1,128)S(1)}, s32[1,4]{1,0:T(1,128)}, u32[]{:S(2)}) copy-start(s32[1,4]{1,0:T(1,128)} %param.16) | copy-start | bytes 52
  41.1 270.4 %all-gather.22.cloned.1.call-start = ((), (), s32[]{:S(2)}) async-start(), calls=%async_computation.19 | async-start | bytes 5013504 | tf_op jit(solution)/shard_map/all_gather | solution.py:135
  47.7 313.6 %all-gather.24.cloned.1.call-start = ((), (), s32[]{:S(2)}) async-start(), calls=%async_computation.20 | async-start | bytes 5013504 | tf_op jit(solution)/shard_map/all_gather | solution.py:136
  53.7 725.9 %reduce-scatter.37.cloned.1.call-start = ((), (), s32[]{:S(2)}) async-start(), calls=%async_computation.25 | async-start | bytes 1253376 | tf_op jit(solution)/shard_map/reduce_scatter | solution.py:323
  54.4 45.1 %copy-start.103 = (f32[32]{0:T(128)}, f32[32]{0:T(128)S(1)}, u32[]{:S(2)}) copy-start(f32[32]{0:T(128)S(1)} %get-tuple-element.174) | copy-start | bytes 388
  54.5 45.0 %copy-start.125 = (s32[1,4]{1,0:T(1,128)S(1)}, s32[1,4]{1,0:T(1,128)}, u32[]{:S(2)}) copy-start(s32[1,4]{1,0:T(1,128)} %param.17) | copy-start | bytes 52
  54.8 116.7 %copy-start.26 = (f32[1024]{0:T(1024)}, f32[1024]{0:T(1024)S(1)}, u32[]{:S(2)}) copy-start(f32[1024]{0:T(1024)S(1)} %broadcast_multiply_fusion.10) | copy-start | bytes 12292
  55.4 116.1 %copy-start.32 = (f32[1024]{0:T(1024)}, f32[1024]{0:T(1024)S(1)}, u32[]{:S(2)}) copy-start(f32[1024]{0:T(1024)S(1)} %fusion.71) | copy-start | bytes 12292
  55.7 41.9 %copy-start.88 = (pred[32,32]{1,0:T(8,128)(4,1)}, pred[32,32]{1,0:T(8,128)(4,1)S(1)}, u32[]{:S(2)}) copy-start(pred[32,32]{1,0:T(8,128)(4,1)S(1)} %get-tuple-element.152) | copy-start | bytes 3076
  55.7 109.5 %copy-start.84 = (pred[32,32]{1,0:T(8,128)(4,1)}, pred[32,32]{1,0:T(8,128)(4,1)S(1)}, u32[]{:S(2)}) copy-start(pred[32,32]{1,0:T(8,128)(4,1)S(1)} %get-tuple-element.150) | copy-start | bytes 3076
  56.3 115.2 %copy-start.42 = (pred[1024]{0:T(1024)(128)(4,1)}, pred[1024]{0:T(1024)(128)(4,1)S(1)}, u32[]{:S(2)}) copy-start(pred[1024]{0:T(1024)(128)(4,1)S(1)} %eq.146) | copy-start | bytes 3076
  56.4 115.2 %copy-start.45 = (pred[1024]{0:T(1024)(128)(4,1)}, pred[1024]{0:T(1024)(128)(4,1)S(1)}, u32[]{:S(2)}) copy-start(pred[1024]{0:T(1024)(128)(4,1)S(1)} %eq.144) | copy-start | bytes 3076
  56.5 225.6 %copy-start.17 = (pred[256,256]{0,1:T(8,128)(4,1)}, pred[256,256]{0,1:T(8,128)(4,1)S(1)}, u32[]{:S(2)}) copy-start(pred[256,256]{0,1:T(8,128)(4,1)S(1)} %broadcast_compare_fusion) | copy-start | bytes 196612
  78.6 98.0 %copy-start.66 = (f32[768]{0:T(1024)}, f32[768]{0:T(1024)S(1)}, u32[]{:S(2)}) copy-start(f32[768]{0:T(1024)S(1)} %get-tuple-element.77) | copy-start | bytes 9220
  78.6 98.0 %copy-start.68 = (f32[768]{0:T(1024)}, f32[768]{0:T(1024)S(1)}, u32[]{:S(2)}) copy-start(f32[768]{0:T(1024)S(1)} %get-tuple-element.78) | copy-start | bytes 9220
  78.6 98.0 %copy-start.70 = (f32[768]{0:T(1024)}, f32[768]{0:T(1024)S(1)}, u32[]{:S(2)}) copy-start(f32[768]{0:T(1024)S(1)} %get-tuple-element.79) | copy-start | bytes 9220
  78.7 98.0 %copy-start.72 = (f32[768]{0:T(1024)}, f32[768]{0:T(1024)S(1)}, u32[]{:S(2)}) copy-start(f32[768]{0:T(1024)S(1)} %get-tuple-element.80) | copy-start | bytes 9220
  78.7 98.0 %copy-start.74 = (f32[768]{0:T(1024)}, f32[768]{0:T(1024)S(1)}, u32[]{:S(2)}) copy-start(f32[768]{0:T(1024)S(1)} %get-tuple-element.81) | copy-start | bytes 9220
  78.7 98.0 %copy-start.76 = (f32[768]{0:T(1024)}, f32[768]{0:T(1024)S(1)}, u32[]{:S(2)}) copy-start(f32[768]{0:T(1024)S(1)} %get-tuple-element.82) | copy-start | bytes 9220
  78.7 98.0 %copy-start.78 = (f32[768]{0:T(1024)}, f32[768]{0:T(1024)S(1)}, u32[]{:S(2)}) copy-start(f32[768]{0:T(1024)S(1)} %get-tuple-element.83) | copy-start | bytes 9220
  78.7 98.0 %copy-start.80 = (f32[768]{0:T(1024)}, f32[768]{0:T(1024)S(1)}, u32[]{:S(2)}) copy-start(f32[768]{0:T(1024)S(1)} %get-tuple-element.84) | copy-start | bytes 9220
  78.7 98.0 %copy-start.82 = (f32[768]{0:T(1024)}, f32[768]{0:T(1024)S(1)}, u32[]{:S(2)}) copy-start(f32[768]{0:T(1024)S(1)} %get-tuple-element.85) | copy-start | bytes 9220
  101.4 68.7 %copy-start.22 = (f32[4,768]{1,0:T(4,128)}, f32[4,768]{1,0:T(4,128)S(1)}, u32[]{:S(2)}) copy-start(f32[4,768]{1,0:T(4,128)S(1)} %convolution_add_fusion) | copy-start | bytes 36868
  170.8 13.2 copy-start.34
  171.5 12.5 copy-start.60
  184.0 36.5 %copy-start.20 = (bf16[32,32,768]{2,1,0:T(8,128)(2,1)}, bf16[32,32,768]{2,1,0:T(8,128)(2,1)S(1)}, u32[]{:S(2)}) copy-start(bf16[32,32,768]{2,1,0:T(8,128)(2,1)S(1)} %add_convert_fusion.2) | copy-start | bytes 4718596
  308.8 224.3 %copy-start.97 = (f32[1024]{0:T(1024)}, f32[1024]{0:T(1024)S(1)}, u32[]{:S(2)}) copy-start(f32[1024]{0:T(1024)S(1)} %broadcast_multiply_fusion.9) | copy-start | bytes 12292
  310.9 222.2 %copy-start.123 = (f32[1024]{0:T(1024)}, f32[1024]{0:T(1024)S(1)}, u32[]{:S(2)}) copy-start(f32[1024]{0:T(1024)S(1)} %fusion.72) | copy-start | bytes 12292
  321.2 22.2 %copy-start.1 = (f32[1024,3072]{1,0:T(8,128)}, f32[1024,3072]{1,0:T(8,128)S(1)}, u32[]{:S(2)}) copy-start(f32[1024,3072]{1,0:T(8,128)S(1)} %fusion.84) | copy-start | bytes 37748740
  343.4 17.9 %copy-start.6 = (bf16[1024,768]{1,0:T(8,128)(2,1)S(1)}, bf16[1024,768]{1,0:T(8,128)(2,1)}, u32[]{:S(2)}) copy-start(bf16[1024,768]{1,0:T(8,128)(2,1)} %param.27) | copy-start | bytes 4718596
  343.4 17.9 %copy-start.99 = (f32[768]{0:T(1024)S(1)}, f32[768]{0:T(1024)}, u32[]{:S(2)}) copy-start(f32[768]{0:T(1024)} %get-tuple-element.53) | copy-start | bytes 9220
  343.4 17.9 %copy-start.100 = (f32[768]{0:T(1024)S(1)}, f32[768]{0:T(1024)}, u32[]{:S(2)}) copy-start(f32[768]{0:T(1024)} %get-tuple-element.62) | copy-start | bytes 9220
  343.4 17.9 %copy-start.101 = (f32[768]{0:T(1024)S(1)}, f32[768]{0:T(1024)}, u32[]{:S(2)}) copy-start(f32[768]{0:T(1024)} %get-tuple-element.63) | copy-start | bytes 9220
  343.4 17.9 %copy-start.102 = (f32[768]{0:T(1024)S(1)}, f32[768]{0:T(1024)}, u32[]{:S(2)}) copy-start(f32[768]{0:T(1024)} %get-tuple-element.64) | copy-start | bytes 9220
  570.1 18.1 %slice-start = ((s8[12582912]{0:T(1024)(128)(4,1)}), s8[4194304]{0:T(1024)(128)(4,1)S(1)}, s32[]{:S(2)}) async-start(s8[12582912]{0:T(1024)(128)(4,1)} %bitcast.177), calls=%async_computation.36 | async-start | bytes 8388608
  570.1 18.1 %slice-start.1 = ((s8[12582912]{0:T(1024)(128)(4,1)}), s8[4194304]{0:T(1024)(128)(4,1)S(1)}, s32[]{:S(2)}) async-start(s8[12582912]{0:T(1024)(128)(4,1)} %bitcast.177), calls=%async_computation.37 | async-start | bytes 8388608
  599.9 181.5 %reduce-scatter.31.cloned.1.call-start = ((), (), s32[]{:S(2)}) async-start(), calls=%async_computation.22 | async-start | bytes 1671168 | tf_op jit(solution)/shard_map/reduce_scatter | solution.py:314
  669.0 22.9 %slice-start.3 = ((s8[7077888]{0:T(1024)(128)(4,1)}), s8[2883584]{0:T(1024)(128)(4,1)S(1)}, s32[]{:S(2)}) async-start(s8[7077888]{0:T(1024)(128)(4,1)} %bitcast.184), calls=%async_computation.39 | async-start | bytes 5767168
  673.9 18.0 %slice-start.4 = ((s8[7077888]{0:T(1024)(128)(4,1)}), s8[4194304]{0:T(1024)(128)(4,1)S(1)}, s32[]{:S(2)}) async-start(s8[7077888]{0:T(1024)(128)(4,1)} %bitcast.184), calls=%async_computation.40 | async-start | bytes 8388608
  695.8 121.2 %reduce-scatter.29.cloned.1.call-start = ((), (), s32[]{:S(2)}) async-start(), calls=%async_computation.21 | async-start | bytes 1671168 | tf_op jit(solution)/shard_map/reduce_scatter | solution.py:311
  698.5 189.4 %reduce-scatter.35.cloned.1.call-start = ((), (), s32[]{:S(2)}) async-start(), calls=%async_computation.24 | async-start | bytes 3760128 | tf_op jit(solution)/shard_map/reduce_scatter | solution.py:320
  718.3 247.7 %reduce-scatter.39.cloned.1.call-start = ((), (), s32[]{:S(2)}) async-start(), calls=%async_computation.26 | async-start | bytes 5013504 | tf_op jit(solution)/shard_map/reduce_scatter | solution.py:326
  731.4 313.6 %reduce-scatter.41.cloned.1.call-start = ((), (), s32[]{:S(2)}) async-start(), calls=%async_computation.27 | async-start | bytes 5013504 | tf_op jit(solution)/shard_map/reduce_scatter | solution.py:329
  742.1 395.9 %reduce-scatter.33.cloned.1.call-start = ((), (), s32[]{:S(2)}) async-start(), calls=%async_computation.23 | async-start | bytes 7520256 | tf_op jit(solution)/shard_map/reduce_scatter | solution.py:317
  747.1 448.3 %reduce-scatter.47.cloned.1.call-start = ((), (), s32[]{:S(2)}) async-start(), calls=%async_computation.30 | async-start | bytes 208896
  777.9 190.1 %copy-start.129 = (u32[32]{0:T(128)S(1)}, u32[32]{0:T(128)}, u32[]{:S(2)}) copy-start(u32[32]{0:T(128)} %constant.323) | copy-start | bytes 388
  777.9 267.4 %copy-start.65 = (f32[1024]{0:T(1024)S(1)}, f32[1024]{0:T(1024)}, u32[]{:S(2)}) copy-start(f32[1024]{0:T(1024)} %copy-done.64) | copy-start | bytes 12292
  778.0 476.9 %reduce-scatter.55.cloned.1.call-start = ((), (), s32[]{:S(2)}) async-start(), calls=%async_computation.34 | async-start | bytes 835584
  779.5 488.0 %reduce-scatter.51.cloned.1.call-start = ((), (), s32[]{:S(2)}) async-start(), calls=%async_computation.32 | async-start | bytes 294912
  781.3 510.9 %all-reduce.74.cloned.1.call-start = ((), (), s32[]{:S(2)}) async-start(), calls=%async_computation.35 | async-start | bytes 393216
  817.0 491.2 %reduce-scatter.49.cloned.1.call-start = ((), (), s32[]{:S(2)}) async-start(), calls=%async_computation.31 | async-start | bytes 589824
  889.8 433.7 %reduce-scatter.53.cloned.1.call-start = ((), (), s32[]{:S(2)}) async-start(), calls=%async_computation.33 | async-start | bytes 589824
  968.0 369.8 %reduce-scatter.43.cloned.1.call-start = ((), (), s32[]{:S(2)}) async-start(), calls=%async_computation.28 | async-start | bytes 442368 | tf_op jit(solution)/shard_map/reduce_scatter | solution.py:358
  1045.0 310.4 %reduce-scatter.45.cloned.1.call-start = ((), (), s32[]{:S(2)}) async-start(), calls=%async_computation.29 | async-start | bytes 884736
  (93 other events, 584.0 us)
Sparse Core Ops, SparseCore 0:
  14.3 41.3 all-gather.11
  58.6 38.7 all-gather.13
  99.7 65.4 all-gather.15
  167.3 45.6 all-gather.17
  215.1 37.3 all-gather.19
  254.6 52.3 all-gather.21
  309.3 51.9 all-gather.23
  600.1 56.5 reduce-scatter.36
  695.9 57.9 reduce-scatter.30
  758.4 58.5 reduce-scatter.28
  820.9 66.9 reduce-scatter.34
  891.6 74.3 reduce-scatter.38
  970.4 74.5 reduce-scatter.40
  1048.9 89.1 reduce-scatter.32
  1142.3 53.0 reduce-scatter.46
  1199.3 55.5 reduce-scatter.54
  1257.5 9.9 reduce-scatter.50
  1269.7 22.4 all-reduce.73
  1295.0 13.1 reduce-scatter.48
  1310.4 13.1 reduce-scatter.52
  1325.8 12.0 reduce-scatter.42
  1340.1 15.2 reduce-scatter.44
where the time goes:
time: 1380 us; the launch traced here: 1360 us
  waiting for transfers between devices  637 us (46%)
  other arithmetic  230 us (17%)
  matrix products  211 us (15%)
  local copies, waits for them, and re-layouts  175 us (13%)
  blocking collectives  92.9 us (7%)
  between operations  18.2 us (1%)
    unnamed x29, waiting for transfers between devices  178 us
    dot_general x5, matrix products, against(): lax.dot_general(left, right, (((1,), (1,)), ((), ())), preferred_element_...  93.7 us
    reduce_scatter x1, waiting for transfers between devices, body(): lax.psum_scatter(mod_term.astype(jnp.bfloat16), 'dp', scatter_dimension=1...  87.5 us
    reduce_scatter x1, waiting for transfers between devices, body(): lax.psum_scatter(expand_term.astype(jnp.bfloat16), 'dp', scatter_dimensio...  76.2 us
    reduce_scatter x1, waiting for transfers between devices, body(): lax.psum_scatter(shrink_term.astype(jnp.bfloat16), 'dp', scatter_dimensio...  75.7 us
    reduce_scatter x1, waiting for transfers between devices, body(): lax.psum_scatter(qkv_term.astype(jnp.bfloat16), 'dp', scatter_dimension=1...  70.8 us
    all_gather x1, waiting for transfers between devices, fetch_forward(): lax.all_gather(gathered[2], 'dp', axis=1, tiled=True)  63.7 us
    convert_element_type x5, local copies, waits for them, and re-layouts, body(): d_qkv = from_groups(stacked).astype(jnp.bfloat16)  61.8 us
  transfers between devices with their start and end apart: 22, of which 16 were waited for; matrix products, arithmetic and copies ran while one was open for 27% of the time, Pallas kernels for 0%

commit v1 on v0

v1 whole, which is shorter than its diff:
```python
import functools

import jax
import jax.numpy as jnp
from jax import lax
from jax.experimental import pallas as pl
from jax.experimental.pallas import tpu as pltpu
from jax.sharding import PartitionSpec as P

D = 768
H = 12
HD = 64
FF = 3072
SIDE = 32
GROUP = 256
TOK = SIDE * SIDE
EPS = 1e-06
NJ, NK, UR, UC = 16, 2, 48, 384
UNITS = 12
CHUNK = 384
MIB = 1024 * 1024
BF = jnp.bfloat16
F32 = jnp.float32
GELU_A = 0.7978845608028654
GELU_B = GELU_A * 0.044715


def dot(left, right, left_dim, right_dim):
    return lax.dot_general(
        left, right, (((left_dim,), (right_dim,)), ((), ())), preferred_element_type=F32
    )


def params(limit=56):
    return pltpu.CompilerParams(vmem_limit_bytes=limit * MIB)


def whole(shape):
    zeros = (0,) * len(shape)
    return pl.BlockSpec(shape, lambda *ids: zeros, pipeline_mode=pl.Buffered(1))


SMEM_SPEC = pl.BlockSpec(memory_space=pltpu.SMEM)


def group_place(natural):
    pair, odd_row = natural // 64, (natural // 32) % 2
    column, odd_column = (natural % 32) // 2, natural % 2
    return (2 * odd_row + odd_column) * 64 + pair * 16 + column


def ungroup_matrix():
    natural = lax.broadcasted_iota(jnp.int32, (256, 256), 0)
    grouped = lax.broadcasted_iota(jnp.int32, (256, 256), 1)
    return jnp.where(group_place(natural) == grouped, 1.0, 0.0).astype(BF)


def group_matrix():
    natural = lax.broadcasted_iota(jnp.int32, (256, 256), 1)
    grouped = lax.broadcasted_iota(jnp.int32, (256, 256), 0)
    return jnp.where(group_place(natural) == grouped, 1.0, 0.0).astype(BF)


def norm_stats(values):
    centre = values - jnp.mean(values, axis=-1, keepdims=True)
    variance = jnp.mean(centre * centre, axis=-1, keepdims=True)
    scale = lax.rsqrt(variance + EPS)
    return centre * scale, scale


def prepare_kernel(latents, cotangent, tokens, gradient, norm, scale):
    order = group_matrix()
    gathered = dot(order, latents[...], 1, 0)
    gradient[...] = dot(order, cotangent[...], 1, 0).reshape(4, 64, D).astype(BF)
    tokens[...] = gathered.reshape(4, 64, D).astype(BF)
    normal, factor = norm_stats(gathered)
    norm[...] = normal.reshape(4, 64, D)
    scale[...] = factor.reshape(4, 64, 1)


def prepare(latents, cotangent):
    flat = pl.BlockSpec((256, D), lambda i: (i, 0))
    split = pl.BlockSpec((4, 64, D), lambda i: (0, i, 0))
    return pl.pallas_call(
        prepare_kernel,
        grid=(4,),
        in_specs=[flat, flat],
        out_specs=[split, split, split, pl.BlockSpec((4, 64, 1), lambda i: (0, i, 0))],
        out_shape=[
            jax.ShapeDtypeStruct((4, GROUP, D), BF),
            jax.ShapeDtypeStruct((4, GROUP, D), BF),
            jax.ShapeDtypeStruct((4, GROUP, D), F32),
            jax.ShapeDtypeStruct((4, GROUP, 1), F32),
        ],
        compiler_params=params(),
        name="prepare",
    )(latents, cotangent)


def edge_columns(tag):
    place = lax.broadcasted_iota(jnp.int32, (16, 128), 0)
    left = jnp.where((place == 0) | ((place == 8) & (tag == 1)), 0.0, 1.0)
    right = jnp.where((place == 15) | ((place == 7) & (tag == 1)), 0.0, 1.0)
    return left, right


def neighbours(even, odd, left, right):
    return pltpu.roll(odd, 1, 0) * left, pltpu.roll(even, 15, 0) * right


def conv_rows(load, kernel, left, right, keep, emit):
    above = None
    partial = None
    for row in range(SIDE + 1):
        taps = None
        if row < SIDE:
            a, p = row % 2, row // 2
            even, odd = load(2 * a, p), load(2 * a + 1, p)
            odd_left, even_right = neighbours(even, odd, left, right)
            taps = []
            for tap in range(3):
                k = [kernel[3 * tap + b] for b in range(3)]
                taps.append(
                    (
                        k[0] * odd_left + k[1] * even + k[2] * odd,
                        k[0] * even + k[1] * odd + k[2] * even_right,
                    )
                )
        crossing = row == SIDE // 2
        if partial is not None:
            a, p = (row - 1) % 2, (row - 1) // 2
            for b in range(2):
                value = partial[b]
                if taps is not None:
                    below = taps[2][b]
                    value = value + (below * keep if crossing else below)
                emit(2 * a + b, p, value)
        if taps is not None:
            partial = []
            for b in range(2):
                value = taps[1][b]
                if above is not None:
                    value = value + (above[b] * keep if crossing else above[b])
                partial.append(value)
            above = taps[0]


def conv_back_rows(load_grad, load_field, kernel, left, right, keep, emit):
    sums = [jnp.zeros((16, 128), F32) for _ in range(9)]
    from_above = None
    partial = None
    field_above = None
    field = (load_field(0, 0), load_field(1, 0))
    for row in range(SIDE + 1):
        crossing = row == SIDE // 2
        taps = None
        if row < SIDE:
            a, p = row % 2, row // 2
            even, odd = load_grad(2 * a, p), load_grad(2 * a + 1, p)
            odd_left, even_right = neighbours(even, odd, left, right)
            picks = ((odd, even, odd_left), (even_right, odd, even))
            taps = []
            for tap in range(3):
                k = [kernel[3 * tap + b] for b in range(3)]
                taps.append(
                    tuple(k[0] * x[0] + k[1] * x[1] + k[2] * x[2] for x in picks)
                )
            field_below = None
            if row + 1 < SIDE:
                a, p = (row + 1) % 2, (row + 1) // 2
                field_below = (load_field(2 * a, p), load_field(2 * a + 1, p))
            for tap, rows in enumerate((field_above, field, field_below)):
                if rows is None:
                    continue
                if (tap == 0 and crossing) or (tap == 2 and row + 1 == SIDE // 2):
                    rows = (rows[0] * keep, rows[1] * keep)
                for b in range(3):
                    sums[3 * tap + b] = (
                        sums[3 * tap + b] + rows[0] * picks[0][b] + rows[1] * picks[1][b]
                    )
            field_above, field = field, field_below
        if partial is not None:
            a, p = (row - 1) % 2, (row - 1) // 2
            for b in range(2):
                value = partial[b]
                if taps is not None:
                    value = value + (taps[0][b] * keep if crossing else taps[0][b])
                emit(2 * a + b, p, value)
        if taps is not None:
            partial = []
            for b in range(2):
                value = taps[1][b]
                if from_above is not None:
                    value = value + (from_above[b] * keep if crossing else from_above[b])
                partial.append(value)
            from_above = taps[2]
    return sums


def first_conv_kernel(tag_ref, norm, mods, kernel, out):
    tag = tag_ref[0]
    left, right = edge_columns(tag)
    keep = 1.0 - tag.astype(F32)
    taps = [jnp.broadcast_to(kernel[i : i + 1, :], (16, 128)) for i in range(9)]

    def load(g, p):
        q = 2 * (p // 8)
        shift = mods[0, q : q + 2].reshape(16, 128)
        scale = mods[1, q : q + 2].reshape(16, 128)
        return norm[g, p * 16 : p * 16 + 16, :] * (1.0 + scale) + shift

    def emit(g, p, value):
        out[g, p * 16 : p * 16 + 16, :] = value.astype(BF)

    conv_rows(load, taps, left, right, keep, emit)


def first_conv(tag, norm, mods, kernel):
    return pl.pallas_call(
        first_conv_kernel,
        grid=(D // 128,),
        in_specs=[
            SMEM_SPEC,
            pl.BlockSpec((4, GROUP, 128), lambda i: (0, 0, i)),
            pl.BlockSpec((6, 4, 8, 128), lambda i: (0, 0, 0, i)),
            pl.BlockSpec((9, 128), lambda i: (0, i)),
        ],
        out_specs=pl.BlockSpec((4, GROUP, 128), lambda i: (0, 0, i)),
        out_shape=jax.ShapeDtypeStruct((4, GROUP, D), BF),
        compiler_params=params(),
        name="first_conv",
    )(tag, norm, mods, kernel)


def join_rows(block, target):
    rows = block.shape[0] * block.shape[2] * UR
    for k in range(NK):
        target[:, k * UC : (k + 1) * UC] = block[:, k].reshape(rows, UC)


def quadrant_rows(mods, index, half):
    return mods[index, pl.ds(2 * half, 2)].reshape(1, 2, 8, D)


def item_bias(tag):
    def label(dim):
        place = lax.broadcasted_iota(jnp.int32, (GROUP, GROUP), dim)
        return 2 * (place // 128) + (place % 16) // 8

    return jnp.where((label(0) == label(1)) | (tag == 0), 0.0, -1e30)


def attend_kernel(
    tag_ref, conv_in, tokens, mods, w_qkv, w_proj, qkv, merged, attn, resid, second, lse,
    full_qkv, full_proj, bias, mixed_t,
):
    @pl.when(pl.program_id(0) == 0)
    def _():
        join_rows(w_qkv, full_qkv)
        join_rows(w_proj, full_proj)
        bias[...] = item_bias(tag_ref[0])

    qkv[0] = dot(full_qkv[...], conv_in[0], 1, 1).astype(BF)

    def head(h, _):
        rows = pl.ds(pl.multiple_of(h * HD, HD), HD)
        queries = qkv[0, rows, :] * jnp.asarray(HD**-0.5, BF)
        keys = qkv[0, pl.ds(pl.multiple_of(D + h * HD, HD), HD), :]
        values = qkv[0, pl.ds(pl.multiple_of(2 * D + h * HD, HD), HD), :]
        scores = dot(keys, queries, 0, 0) + bias[...]
        highest = jnp.max(scores, axis=0, keepdims=True)
        raised = jnp.exp(scores - highest)
        total = jnp.sum(raised, axis=0, keepdims=True)
        probs = (raised * (1.0 / total)).astype(BF)
        lse[0, pl.ds(h, 1), :] = highest + jnp.log(total)
        mixed_t[rows, :] = dot(values, probs, 1, 0).astype(BF)
        return 0

    lax.fori_loop(0, H, head, 0)
    merged[0] = mixed_t[...].T
    projected = dot(merged[0], full_proj[...], 1, 1)
    attn[0] = projected.astype(BF)
    gate = mods[2].reshape(2, 1, 2, 8, D)
    resid[0] = (
        tokens[0].astype(F32) + (projected.reshape(2, 8, 2, 8, D) * gate).reshape(GROUP, D)
    )

    def rows_norm(i, _):
        rows = pl.ds(pl.multiple_of(i * 64, 64), 64)
        normal, _ = norm_stats(resid[0, rows, :])
        half = i // 2
        scaled = normal.reshape(4, 2, 8, D) * (1.0 + quadrant_rows(mods, 4, half))
        value = scaled + quadrant_rows(mods, 3, half)
        second[0, rows, :] = value.reshape(64, D).astype(BF)
        return 0

    lax.fori_loop(0, 4, rows_norm, 0)


def group_spec(*shape):
    return pl.BlockSpec((1,) + shape, lambda g: (g,) + (0,) * len(shape))


def unit_spec(units, start):
    shape = (NJ, NK, units, UR, UC)
    return pl.BlockSpec(
        shape, lambda g: (0, 0, start // units, 0, 0), pipeline_mode=pl.Buffered(1)
    )


def attend(tag, conv_in, tokens, mods, packed):
    return pl.pallas_call(
        attend_kernel,
        grid=(4,),
        in_specs=[
            SMEM_SPEC,
            group_spec(GROUP, D),
            group_spec(GROUP, D),
            whole((6, 4, 8, D)),
            unit_spec(3, 0),
            unit_spec(1, 3),
        ],
        out_specs=[
            group_spec(3 * D, GROUP),
            group_spec(GROUP, D),
            group_spec(GROUP, D),
            group_spec(GROUP, D),
            group_spec(GROUP, D),
            group_spec(16, GROUP),
        ],
        out_shape=[
            jax.ShapeDtypeStruct((4, 3 * D, GROUP), BF),
            jax.ShapeDtypeStruct((4, GROUP, D), BF),
            jax.ShapeDtypeStruct((4, GROUP, D), BF),
            jax.ShapeDtypeStruct((4, GROUP, D), F32),
            jax.ShapeDtypeStruct((4, GROUP, D), BF),
            jax.ShapeDtypeStruct((4, 16, GROUP), F32),
        ],
        scratch_shapes=[
            pltpu.VMEM((3 * D, D), BF),
            pltpu.VMEM((D, D), BF),
            pltpu.VMEM((GROUP, GROUP), F32),
            pltpu.VMEM((D, GROUP), BF),
        ],
        compiler_params=params(),
        name="attend",
    )(tag, conv_in, tokens, mods, packed, packed)


def feed_kernel(
    tag_ref, second, gradient, mods, w_expand, w_shrink, kernel,
    shrunk, d_second, g_expand, g_shrink, g_kernel,
    d_shrunk, d_shrunk_t, weight, field, slope, hidden, d_field,
):
    step = pl.program_id(0)
    tag = tag_ref[0]

    @pl.when(step == 0)
    def _():
        gate = mods[5].reshape(1, 2, 1, 2, 8, D)
        value = gradient[...].astype(F32).reshape(4, 2, 8, 2, 8, D) * gate
        d_shrunk[...] = value.reshape(TOK, D).astype(BF)
        d_shrunk_t[...] = d_shrunk[...].T
        shrunk[...] = jnp.zeros_like(shrunk)
        d_second[...] = jnp.zeros_like(d_second)

    join_rows(w_expand, weight)
    shrink = w_shrink[...].reshape(D, CHUNK)
    left, right = edge_columns(tag)
    keep = 1.0 - tag.astype(F32)
    field[...] = dot(second[...].reshape(TOK, D), weight[...], 1, 1).reshape(4, GROUP, CHUNK)
    slope[...] = dot(d_shrunk[...], shrink, 1, 0).reshape(4, GROUP, CHUNK)

    def lanes(i, _):
        cols = pl.ds(pl.multiple_of(i * 128, 128), 128)
        taps = [jnp.broadcast_to(kernel[t : t + 1, cols], (16, 128)) for t in range(9)]

        def load(g, p):
            return field[g, p * 16 : p * 16 + 16, cols]

        def load_slope(g, p):
            return slope[g, p * 16 : p * 16 + 16, cols]

        def emit(g, p, value):
            square = value * value
            half = 0.5 + 0.5 * jnp.tanh(value * (GELU_A + GELU_B * square))
            out = value * half
            hidden[g, p * 16 : p * 16 + 16, cols] = out.astype(BF)
            rate = half + out * (1.0 - half) * (2.0 * GELU_A + 6.0 * GELU_B * square)
            slope[g, p * 16 : p * 16 + 16, cols] = load_slope(g, p) * rate

        conv_rows(load, taps, left, right, keep, emit)

        def emit_back(g, p, value):
            d_field[g, p * 16 : p * 16 + 16, cols] = value.astype(BF)

        sums = conv_back_rows(load_slope, load, taps, left, right, keep, emit_back)
        for t in range(9):
            g_kernel[t : t + 1, cols] = jnp.sum(sums[t], axis=0, keepdims=True)
        return 0

    lax.fori_loop(0, CHUNK // 128, lanes, 0)
    hid = hidden[...].reshape(TOK, CHUNK)
    d_fld = d_field[...].reshape(TOK, CHUNK)
    shrunk[...] += dot(hid, shrink, 1, 1).reshape(4, GROUP, D)
    d_second[...] += dot(d_fld, weight[...], 1, 0).reshape(4, GROUP, D)
    g_shrink[...] = dot(d_shrunk_t[...], hid, 1, 0).astype(BF).reshape(NJ, 1, 1, UR, UC)
    grad = dot(d_fld, second[...].reshape(TOK, D), 0, 0).astype(BF)
    for k in range(NK):
        g_expand[:, k] = grad[:, k * UC : (k + 1) * UC].reshape(2, 4, UR, UC)


def feed(tag, second, gradient, mods, packed, kernel):
    steps = FF // CHUNK
    return pl.pallas_call(
        feed_kernel,
        grid=(steps,),
        in_specs=[
            SMEM_SPEC,
            whole((4, GROUP, D)),
            whole((4, GROUP, D)),
            whole((6, 4, 8, D)),
            pl.BlockSpec((2, NK, 4, UR, UC), lambda c: (c, 0, 1, 0, 0)),
            pl.BlockSpec((NJ, 1, 1, UR, UC), lambda c: (0, c // 4, 8 + c % 4, 0, 0)),
            pl.BlockSpec((9, CHUNK), lambda c: (0, c)),
        ],
        out_specs=[
            pl.BlockSpec((4, GROUP, D), lambda c: (0, 0, 0)),
            pl.BlockSpec((4, GROUP, D), lambda c: (0, 0, 0)),
            pl.BlockSpec((2, NK, 4, UR, UC), lambda c: (c, 0, 0, 0, 0)),
            pl.BlockSpec((NJ, 1, 1, UR, UC), lambda c: (0, c // 4, c % 4, 0, 0)),
            pl.BlockSpec((9, CHUNK), lambda c: (0, c)),
        ],
        out_shape=[
            jax.ShapeDtypeStruct((4, GROUP, D), F32),
            jax.ShapeDtypeStruct((4, GROUP, D), F32),
            jax.ShapeDtypeStruct((NJ, NK, 4, UR, UC), BF),
            jax.ShapeDtypeStruct((NJ, NK, 4, UR, UC), BF),
            jax.ShapeDtypeStruct((9, FF), F32),
        ],
        scratch_shapes=[
            pltpu.VMEM((TOK, D), BF),
            pltpu.VMEM((D, TOK), BF),
            pltpu.VMEM((CHUNK, D), BF),
            pltpu.VMEM((4, GROUP, CHUNK), F32),
            pltpu.VMEM((4, GROUP, CHUNK), F32),
            pltpu.VMEM((4, GROUP, CHUNK), BF),
            pltpu.VMEM((4, GROUP, CHUNK), BF),
        ],
        compiler_params=params(60),
        name="feed",
    )(tag, second, gradient, mods, packed, packed, kernel)


def attend_back_kernel(
    tag_ref, resid, shrunk, d_second, gradient, attn, mods, qkv, merged, conv_in, lse, w_qkv, w_proj,
    output, d_resid, g_qkv, g_proj, d_conv, sums,
    full_qkv, full_proj, proj_t, bias, d_mixed, d_qkv, acc_qkv, acc_proj, d_attn,
):
    step = pl.program_id(0)

    @pl.when(step == 0)
    def _():
        join_rows(w_qkv, full_qkv)
        join_rows(w_proj, full_proj)
        proj_t[...] = full_proj[...].T
        bias[...] = item_bias(tag_ref[0])
        acc_qkv[...] = jnp.zeros_like(acc_qkv)
        acc_proj[...] = jnp.zeros_like(acc_proj)
        sums[...] = jnp.zeros_like(sums)

    def rows_norm(i, _):
        rows = pl.ds(pl.multiple_of(i * 64, 64), 64)
        half = i // 2
        base = resid[0, rows, :]
        normal, factor = norm_stats(base)
        shrunk_rows = shrunk[0, rows, :]
        outward = gradient[0, rows, :].astype(F32)
        d_sec = d_second[0, rows, :]

        def by_item(value):
            return value.reshape(4, 2, 8, D)

        def add(index, value):
            sums[index, pl.ds(2 * half, 2)] += jnp.sum(by_item(value), axis=0)

        gated = (by_item(shrunk_rows) * quadrant_rows(mods, 5, half)).reshape(64, D)
        output[0, rows, :] = (base + gated).astype(BF)
        add(3, outward * shrunk_rows)
        add(1, d_sec)
        add(2, d_sec * normal)
        inner = (by_item(d_sec) * (1.0 + quadrant_rows(mods, 4, half))).reshape(64, D)
        mean = jnp.mean(inner, axis=-1, keepdims=True)
        along = jnp.mean(inner * normal, axis=-1, keepdims=True)
        back = outward + (inner - mean - normal * along) * factor
        d_resid[0, rows, :] = back
        add(0, back * attn[0, rows, :].astype(F32))
        gated = (by_item(back) * quadrant_rows(mods, 2, half)).reshape(64, D)
        d_attn[rows, :] = gated.astype(BF)
        return 0

    lax.fori_loop(0, 4, rows_norm, 0)
    acc_proj[...] += dot(d_attn[...], merged[0], 0, 0)
    d_mixed[...] = dot(proj_t[...], d_attn[...], 1, 1).astype(BF)

    def head(h, _):
        rows = pl.ds(pl.multiple_of(h * HD, HD), HD)
        key_rows = pl.ds(pl.multiple_of(D + h * HD, HD), HD)
        value_rows = pl.ds(pl.multiple_of(2 * D + h * HD, HD), HD)
        queries = qkv[0, rows, :] * jnp.asarray(HD**-0.5, BF)
        keys = qkv[0, key_rows, :]
        values = qkv[0, value_rows, :]
        d_mix = d_mixed[rows, :]
        probs = jnp.exp(dot(keys, queries, 0, 0) + (bias[...] - lse[0, pl.ds(h, 1), :]))
        d_probs = dot(values, d_mix, 0, 0)
        d_qkv[value_rows, :] = dot(d_mix, probs.astype(BF), 1, 1).astype(BF)
        weighted = probs * d_probs
        inner = jnp.sum(weighted, axis=0, keepdims=True)
        d_scores = (weighted - probs * inner).astype(BF)
        d_qkv[rows, :] = (dot(keys, d_scores, 1, 0) * HD**-0.5).astype(BF)
        d_qkv[key_rows, :] = dot(queries, d_scores, 1, 1).astype(BF)
        return 0

    lax.fori_loop(0, H, head, 0)
    acc_qkv[...] += dot(d_qkv[...], conv_in[0], 1, 0)
    d_conv[0] = dot(d_qkv[...], full_qkv[...], 0, 0)

    @pl.when(step == pl.num_programs(0) - 1)
    def _():
        for k in range(NK):
            cols = slice(k * UC, (k + 1) * UC)
            g_qkv[:, k] = acc_qkv[:, cols].astype(BF).reshape(NJ, 3, UR, UC)
            g_proj[:, k] = acc_proj[:, cols].astype(BF).reshape(NJ, 1, UR, UC)


def attend_back(tag, resid, shrunk, d_second, gradient, attn, mods, qkv, merged, conv_in, lse, packed):
    return pl.pallas_call(
        attend_back_kernel,
        grid=(4,),
        in_specs=[
            SMEM_SPEC,
            group_spec(GROUP, D),
            group_spec(GROUP, D),
            group_spec(GROUP, D),
            group_spec(GROUP, D),
            group_spec(GROUP, D),
            whole((6, 4, 8, D)),
            group_spec(3 * D, GROUP),
            group_spec(GROUP, D),
            group_spec(GROUP, D),
            group_spec(16, GROUP),
            unit_spec(3, 0),
            unit_spec(1, 3),
        ],
        out_specs=[
            group_spec(GROUP, D),
            group_spec(GROUP, D),
            whole((NJ, NK, 3, UR, UC)),
            whole((NJ, NK, 1, UR, UC)),
            group_spec(GROUP, D),
            whole((4, 4, 8, D)),
        ],
        out_shape=[
            jax.ShapeDtypeStruct((4, GROUP, D), BF),
            jax.ShapeDtypeStruct((4, GROUP, D), F32),
            jax.ShapeDtypeStruct((NJ, NK, 3, UR, UC), BF),
            jax.ShapeDtypeStruct((NJ, NK, 1, UR, UC), BF),
            jax.ShapeDtypeStruct((4, GROUP, D), F32),
            jax.ShapeDtypeStruct((4, 4, 8, D), F32),
        ],
        scratch_shapes=[
            pltpu.VMEM((3 * D, D), BF),
            pltpu.VMEM((D, D), BF),
            pltpu.VMEM((D, D), BF),
            pltpu.VMEM((GROUP, GROUP), F32),
            pltpu.VMEM((D, GROUP), BF),
            pltpu.VMEM((3 * D, GROUP), BF),
            pltpu.VMEM((3 * D, D), F32),
            pltpu.VMEM((D, D), F32),
            pltpu.VMEM((GROUP, D), BF),
        ],
        compiler_params=params(60),
        name="attend_back",
    )(tag, resid, shrunk, d_second, gradient, attn, mods, qkv, merged, conv_in, lse, packed, packed)


def finish_kernel(
    tag_ref, d_conv, norm, factor, d_resid, output, mods, kernel,
    block_output, input_grad, g_kernel, sums, d_first, total,
):
    tag = tag_ref[0]
    left, right = edge_columns(tag)
    keep = 1.0 - tag.astype(F32)

    def lanes(i, _):
        cols = pl.ds(pl.multiple_of(i * 128, 128), 128)
        taps = [jnp.broadcast_to(kernel[t : t + 1, cols], (16, 128)) for t in range(9)]

        def load_grad(g, p):
            return d_conv[g, p * 16 : p * 16 + 16, cols]

        def load_field(g, p):
            q = 2 * (p // 8)
            shift = mods[0, q : q + 2, :, cols].reshape(16, 128)
            scale = mods[1, q : q + 2, :, cols].reshape(16, 128)
            return norm[g, p * 16 : p * 16 + 16, cols] * (1.0 + scale) + shift

        def emit(g, p, value):
            d_first[g, p * 16 : p * 16 + 16, cols] = value

        grads = conv_back_rows(load_grad, load_field, taps, left, right, keep, emit)
        for t in range(9):
            g_kernel[t : t + 1, cols] = jnp.sum(grads[t], axis=0, keepdims=True)
        return 0

    lax.fori_loop(0, D // 128, lanes, 0)
    sums[...] = jnp.zeros_like(sums)

    def rows_back(i, _):
        g, part = i // 4, i % 4
        rows = pl.ds(pl.multiple_of(part * 64, 64), 64)
        half = part // 2
        value = d_first[g, rows, :]
        normal = norm[g, rows, :]
        sums[0, pl.ds(2 * half, 2)] += jnp.sum(value.reshape(4, 2, 8, D), axis=0)
        sums[1, pl.ds(2 * half, 2)] += jnp.sum((value * normal).reshape(4, 2, 8, D), axis=0)
        inner = (value.reshape(4, 2, 8, D) * (1.0 + quadrant_rows(mods, 1, half))).reshape(64, D)
        mean = jnp.mean(inner, axis=-1, keepdims=True)
        along = jnp.mean(inner * normal, axis=-1, keepdims=True)
        total[g, rows, :] = (
            d_resid[g, rows, :] + (inner - mean - normal * along) * factor[g, rows, :]
        )
        return 0

    lax.fori_loop(0, 16, rows_back, 0)
    order = ungroup_matrix()

    def place(i, _):
        rows = pl.ds(pl.multiple_of(i * 64, 64), 64)
        target = pl.ds(pl.multiple_of(i * 256, 256), 256)
        grouped = total[:, rows, :].reshape(256, D)
        high = grouped.astype(BF)
        rest = (grouped - high.astype(F32)).astype(BF)
        input_grad[target, :] = dot(order, high, 1, 0) + dot(order, rest, 1, 0)
        block_output[target, :] = dot(order, output[:, rows, :].reshape(256, D), 1, 0).astype(BF)
        return 0

    lax.fori_loop(0, 4, place, 0)


def finish(tag, d_conv, norm, factor, d_resid, output, mods, kernel):
    return pl.pallas_call(
        finish_kernel,
        in_specs=[SMEM_SPEC] + [pl.BlockSpec(memory_space=pltpu.VMEM)] * 7,
        out_specs=[pl.BlockSpec(memory_space=pltpu.VMEM)] * 4,
        out_shape=[
            jax.ShapeDtypeStruct((TOK, D), BF),
            jax.ShapeDtypeStruct((TOK, D), F32),
            jax.ShapeDtypeStruct((9, D), F32),
            jax.ShapeDtypeStruct((2, 4, 8, D), F32),
        ],
        scratch_shapes=[pltpu.VMEM((4, GROUP, D), F32), pltpu.VMEM((4, GROUP, D), F32)],
        compiler_params=params(60),
        name="finish",
    )(tag, d_conv, norm, factor, d_resid, output, mods, kernel)


BOTH = ("dp", "fsdp")


def exchange(pieces):
    return lax.all_to_all(pieces, BOTH, 0, 0, tiled=True)


def pack_shards(qkv, proj, expand, shrink):
    low = shrink.T.reshape(UR, 4, UC).transpose(1, 0, 2).reshape(4 * UR, UC)
    return jnp.concatenate([qkv.T, proj.T, expand.T, low], axis=0)


def gather_packed(nd, nf, qkv, proj, expand, shrink):
    if (nd, nf) == (NJ, NK):
        rows = lax.all_gather(pack_shards(qkv, proj, expand, shrink), BOTH)
        return rows.reshape(NJ, NK, UNITS, UR, UC)

    def full(shard):
        rows = lax.all_gather(shard.T, "fsdp", axis=1, tiled=True)
        return lax.all_gather(rows, "dp", axis=0, tiled=True)

    def split(weight, units):
        return weight.reshape(NJ, units, UR, NK, UC).transpose(0, 3, 1, 2, 4)

    low = full(shrink).reshape(NJ, UR, NK, 4, UC).transpose(0, 2, 3, 1, 4)
    return jnp.concatenate(
        [split(full(qkv), 3), split(full(proj), 1), split(full(expand), 4), low], axis=2
    )


def scatter_packed(nd, nf, parts):
    kinds = [kind for kind, _ in parts]
    if (nd, nf) == (NJ, NK):
        joined = jnp.concatenate([grad for _, grad in parts], axis=2)
        rows = lax.psum_scatter(
            joined.reshape(NJ * NK, -1, UC), BOTH, scatter_dimension=0, tiled=True
        )[0].astype(F32)
        out, start = [], 0
        for kind, grad in parts:
            size = grad.shape[2] * UR
            piece = rows[start : start + size]
            start += size
            if kind == "shrink":
                piece = piece.reshape(4, UR, UC).transpose(1, 0, 2).reshape(UR, 4 * UC)
            out.append(piece.T)
        return out
    out = []
    for kind, grad in parts:
        if kind == "shrink":
            weight = grad.transpose(0, 3, 1, 2, 4).reshape(NJ * UR, -1)
        else:
            weight = grad.transpose(0, 2, 3, 1, 4).reshape(-1, NK * UC)
        columns = lax.psum_scatter(weight, "dp", scatter_dimension=0, tiled=True)
        piece = lax.psum_scatter(columns, "fsdp", scatter_dimension=1, tiled=True)
        out.append(piece.astype(F32).T)
    return out


def condition(nd, nf, timesteps, classes, step_table, class_table, attn_kernel, ffn_kernel):
    slots = nd * nf
    mine = jnp.concatenate([timesteps[0], classes[0]])[None]
    ids = exchange(jnp.broadcast_to(mine, (slots, 8)))
    first_row = lax.axis_index("fsdp") * step_table.shape[0]
    own = first_row + jnp.arange(step_table.shape[0], dtype=jnp.int32)
    step_hot = (ids[:, :4].reshape(-1, 1) == own[None, :]).astype(BF)
    class_hot = (ids[:, 4:].reshape(-1, 1) == own[None, :]).astype(BF)
    part = jnp.dot(step_hot, step_table, preferred_element_type=F32) + jnp.dot(
        class_hot, class_table, preferred_element_type=F32
    )
    cond = lax.psum(part, "fsdp")
    act = jax.nn.silu(cond).astype(BF)
    items, width = act.shape
    filters = jnp.concatenate([attn_kernel, ffn_kernel], axis=1).reshape(-1, width)
    sent = lax.all_gather(jnp.concatenate([act, filters], axis=0), "dp")
    act_all = sent[:, :items].transpose(1, 0, 2).reshape(items, nd * width)
    filters = sent[:, items:].reshape(nd, 9, -1).astype(F32)
    attn_full = filters[:, :, : attn_kernel.shape[1]].transpose(1, 0, 2).reshape(9, -1)
    ffn_full = filters[:, :, attn_kernel.shape[1] :].transpose(1, 0, 2).reshape(9, -1)
    return step_hot, class_hot, cond, act_all, attn_full, ffn_full


def body(
    latents, size_tags, timesteps, classes, step_table, class_table, modulation_weight,
    attn_kernel, qkv_weight, proj_weight, expand_weight, ffn_kernel, shrink_weight, cotangent,
    *, nd, nf,
):
    slots = nd * nf
    tag = size_tags[0]
    packed = gather_packed(nd, nf, qkv_weight, proj_weight, expand_weight, shrink_weight)
    tokens, gradient, norm, factor = prepare(latents, cotangent)
    step_hot, class_hot, cond, act_all, attn_full, ffn_full = condition(
        nd, nf, timesteps, classes, step_table, class_table, attn_kernel, ffn_kernel
    )
    height, width = modulation_weight.shape
    act_rows = lax.dynamic_slice_in_dim(
        act_all, lax.axis_index("fsdp") * height, height, axis=1
    )
    part = jnp.dot(act_rows, modulation_weight, preferred_element_type=F32)
    part = exchange(part.reshape(slots, 4, width)).reshape(nd, nf, 4, width)
    mod_rows = part.sum(axis=1).transpose(1, 0, 2).reshape(4, nd * width)
    chosen = jnp.where(tag == 1, mod_rows, mod_rows[:1])
    mods = jnp.broadcast_to(chosen.reshape(4, 6, 1, D).transpose(1, 0, 2, 3), (6, 4, 8, D))

    conv_in = first_conv(size_tags, norm, mods, attn_full)
    qkv, merged, attn, resid, second, lse = attend(size_tags, conv_in, tokens, mods, packed)
    shrunk, d_second, g_expand, g_shrink, g_ffn = feed(
        size_tags, second, gradient, mods, packed, ffn_full
    )
    expand_grad, shrink_grad = scatter_packed(
        nd, nf, [("expand", g_expand), ("shrink", g_shrink)]
    )
    output, d_resid, g_qkv, g_proj, d_conv, later = attend_back(
        size_tags, resid, shrunk, d_second, gradient, attn, mods, qkv, merged, conv_in, lse, packed
    )
    qkv_grad, proj_grad = scatter_packed(nd, nf, [("qkv", g_qkv), ("proj", g_proj)])
    block_output, input_grad, g_attn, early = finish(
        size_tags, d_conv, norm, factor, d_resid, output, mods, attn_full
    )
    rows = jnp.concatenate([early, later], axis=0).sum(axis=2)
    rows = rows.transpose(1, 0, 2).reshape(4, 6 * D)
    alone = jnp.concatenate([rows.sum(axis=0, keepdims=True), jnp.zeros((3, 6 * D), F32)])
    d_mod = jnp.where(tag == 1, rows, alone).astype(BF)
    pieces = d_mod.reshape(4, nd, 1, width).transpose(1, 2, 0, 3)
    d_mod_all = exchange(jnp.broadcast_to(pieces, (nd, nf, 4, width)).reshape(slots, 4, width))
    d_mod_all = d_mod_all.reshape(slots * 4, width)
    modulation_grad = dot(act_rows, d_mod_all, 0, 0)
    d_act = dot(d_mod_all, modulation_weight, 1, 1)
    spread = lax.dynamic_update_slice_in_dim(
        jnp.zeros((slots * 4, D), F32), d_act, lax.axis_index("fsdp") * height, axis=1
    )
    spread = spread.reshape(slots * 4, nd, 1, -1).transpose(1, 2, 0, 3)
    spread = jnp.broadcast_to(spread, (nd, nf) + spread.shape[2:])
    d_act = exchange(spread.reshape((slots,) + spread.shape[2:])).sum(axis=0)
    gate = jax.nn.sigmoid(cond)
    d_cond = d_act * (gate * (1.0 + cond * (1.0 - gate)))

    def table_grad(hot):
        return lax.dot_general(
            hot.astype(F32), d_cond, (((0,), (0,)), ((), ())), precision=lax.Precision.HIGHEST
        )

    filters = jnp.concatenate([g_attn.reshape(9, nd, -1), g_ffn.reshape(9, nd, -1)], axis=2)
    filters = lax.psum_scatter(filters.transpose(1, 0, 2), "dp", scatter_dimension=0, tiled=True)
    filters = lax.psum(filters[0], "fsdp")
    cut = attn_kernel.shape[1]
    return (
        block_output,
        input_grad,
        table_grad(step_hot),
        table_grad(class_hot),
        modulation_grad,
        filters[:, :cut],
        qkv_grad,
        proj_grad,
        expand_grad,
        filters[:, cut:],
        shrink_grad,
    )


def solution(mesh):
    matrix = P("fsdp", "dp")
    rows = P(BOTH, None)
    filters = P(None, "dp")
    in_specs = (
        rows, P(BOTH), rows, rows, matrix, matrix, matrix, filters, matrix, matrix, matrix,
        filters, matrix, rows,
    )
    out_specs = (
        rows, rows, matrix, matrix, matrix, filters, matrix, matrix, matrix, filters, matrix,
    )
    run = functools.partial(body, nd=mesh.shape["dp"], nf=mesh.shape["fsdp"])
    return jax.shard_map(run, mesh=mesh, in_specs=in_specs, out_specs=out_specs, check_vma=False)
```

time: 1380 us -> 622 us (0.45); the launches traced: 1360 us -> 621 us
  waiting for transfers between devices: 637 us -> 309 us
  other arithmetic: 230 us -> 19.1 us
  matrix products: 211 us -> 3.93 us
  Pallas kernels: 0 us -> 195 us
  local copies, waits for them, and re-layouts: 175 us -> 14.8 us
  blocking collectives: 92.9 us -> 51.6 us
    dot_general x25 -> x7, matrix products: 211 us -> 3.93 us  [the longest x2 1.85 us: table_grad(): lax.dot_general(hot.astype(F32), d_cond, (((0,), (0,)), ((), ())), precis...]
    pallas_call x0 -> x6, Pallas kernels: none -> 195 us  [the longest x1 79.8 us: feed(): pl.pallas_call(feed_kernel, grid=(steps,), in_specs=[SMEM_SPEC, whole((4,...]
    unnamed x29 -> x4, waiting for transfers between devices: 178 us -> 0.07 us
    reduce_scatter x8 -> x3, waiting for transfers between devices: 358 us -> 264 us  [the longest x2 239 us: scatter_packed(): lax.psum_scatter(joined.reshape(NJ * NK, -1, UC), BOTH, scatter_dimension...]
    convert_element_type x11 -> x2, local copies, waits for them, and re-layouts: 77.6 us -> 0.19 us  [condition(): filters = sent[:, items:].reshape(nd, 9, -1).astype(F32)]
    all_gather x7 -> x1, waiting for transfers between devices: 101 us -> 37.7 us  [gather_packed(): rows = lax.all_gather(pack_shards(qkv, proj, expand, shrink), BOTH)]
    all_gather x9 -> x1, blocking collectives: 84 us -> 23.9 us  [condition(): sent = lax.all_gather(jnp.concatenate([act, filters], axis=0), 'dp')]
    reduce_sum x9 -> x4, other arithmetic: 56 us -> 0.32 us  [the longest x1 0.16 us: body(): rows = jnp.concatenate([early, later], axis=0).sum(axis=2)]
  transfers between devices with their start and end apart: 22 -> 7, of which waited for: 16 -> 5; matrix products, arithmetic and copies ran while one was open for 27% -> 5% of each run, Pallas kernels for 0% -> 2%
where the time goes in v1:
time: 622 us; the launch traced here: 621 us
  waiting for transfers between devices  309 us (50%)
  Pallas kernels  195 us (31%)
  blocking collectives  51.6 us (8%)
  other arithmetic  19.1 us (3%)
  local copies, waits for them, and re-layouts  14.8 us (2%)
  between operations  14.8 us (2%)
  starting transfers between devices  12.8 us (2%)
    reduce_scatter x2, waiting for transfers between devices, scatter_packed(): lax.psum_scatter(joined.reshape(NJ * NK, -1, UC), BOTH, scatter_dimension...  239 us
    pallas_call x1, Pallas kernels, feed(): pl.pallas_call(feed_kernel, grid=(steps,), in_specs=[SMEM_SPEC, whole((4,...  79.8 us
    pallas_call x1, Pallas kernels, attend_back(): pl.pallas_call(attend_back_kernel, grid=(4,), in_specs=[SMEM_SPEC, group_...  48.6 us
    pallas_call x1, Pallas kernels, attend(): pl.pallas_call(attend_kernel, grid=(4,), in_specs=[SMEM_SPEC, group_spec(...  38 us
    all_gather x1, waiting for transfers between devices, gather_packed(): rows = lax.all_gather(pack_shards(qkv, proj, expand, shrink), BOTH)  37.7 us
    reduce_scatter x1, waiting for transfers between devices, body(): lax.psum_scatter(filters.transpose(1, 0, 2), 'dp', scatter_dimension=0, t...  25.6 us
    all_gather x1, blocking collectives, condition(): sent = lax.all_gather(jnp.concatenate([act, filters], axis=0), 'dp')  23.9 us
    pallas_call x1, Pallas kernels, finish(): pl.pallas_call(finish_kernel, in_specs=[SMEM_SPEC] + [pl.BlockSpec(memory...  16.3 us
  transfers between devices with their start and end apart: 7, of which 5 were waited for; matrix products, arithmetic and copies ran while one was open for 5% of the time, Pallas kernels for 2%

profile of v1, /device:TPU:0, one launch (start us, length us, event | category | flops | bytes accessed | tf_op | source)
XLA Modules:
  0.0 621.0 jit_solution(17697437476866350291)
XLA Ops:
  7.3 1.0 reshape.142
  8.3 1.8 pad_maximum_fusion.2
  10.1 0.7 pad_add_fusion
  10.8 0.6 broadcast_in_dim.46
  11.5 7.3 %all-to-all-start = ((s32[32,1,8]{2,1,0:T(1,128)}), s32[32,1,8]{2,1,0:T(1,128)S(1)}, u32[]{:S(2)}, u32[]{:S(2)}) async-start(s32[32,1,8]{2,1,0:T(1,128)} %broadcast_in_dim.46), calls=%async_computation | async-start | bytes 32768 | tf_op jit(solution)/shard_map/all_to_all | solution.py:672
  18.8 0.8 pad_maximum_fusion.3
  19.6 0.1 reshape.136
  19.7 0.1 copy.56
  20.4 6.0 prepare.1
  26.5 0.1 eq.37
  26.6 0.1 eq.41
  26.7 0.2 fusion.5
  27.0 0.2 convolution_add_fusion
  27.2 8.6 %psum.14 = f32[128,48]{0,1:T(8,128)S(1)} all-reduce(f32[128,48]{0,1:T(8,128)S(1)} %convolution_add_fusion), channel_id=1, replica_groups=mesh['dp'=16,'fsdp'=2] {'fsdp'}, use_global_device_ids=true, to_apply=%region_0.0 | all-reduce | flops 6144 | bytes 49152 | tf_op jit(solution)/shard_map/psum | solution.py:737
  35.8 23.9 %all-gather.2 = bf16[16,173,48]{1,2,0:T(8,128)(2,1)S(1)} all-gather(bf16[1,173,48]{1,2,0:T(8,128)(2,1)S(1)} %maximum_bitcast_fusion.1), channel_id=2, replica_groups=mesh['dp'=16,'fsdp'=2] {'dp'}, dimensions={0}, use_global_device_ids=true | all-gather | bytes 282336 | tf_op jit(solution)/shard_map/all_gather | solution.py:741
  59.8 0.3 fusion.17
  60.1 0.7 reshape.138
  60.8 2.6 all-to-all-start.1
  63.4 0.2 reduce-scatter.4.cloned.1.call-start
  63.6 0.2 copy.72
  63.9 0.1 reshape.158
  64.1 0.7 reshape.141.kernel
  64.8 0.1 slice_bitcast_fusion.1
  65.0 0.1 copy.64
  65.1 0.8 reshape.145.kernel
  65.9 7.2 %all-to-all-done.1 = f32[32,4,288]{2,1,0:T(4,128)S(1)} async-done(((f32[32,4,288]{2,1,0:T(4,128)}), f32[32,4,288]{2,1,0:T(4,128)S(1)}, u32[]{:S(2)}, u32[]{:S(2)}) %all-to-all-start.1) | async-done | bytes 147488 | tf_op jit(solution)/shard_map/all_to_all | solution.py:672
  73.1 0.1 reshape.140
  73.4 0.9 broadcast_in_dim.50.mods
  74.3 6.1 first_conv.1.conv_in
  80.4 37.7 %all-gather.5.cloned.1.call-done = bf16[18432,384]{1,0:T(8,128)(2,1)} async-done(((bf16[576,384]{1,0:T(8,128)(2,1)}), bf16[18432,384]{1,0:T(8,128)(2,1)}) %all-gather.5.cloned.1.call-update) | async-done | bytes 14155792 | tf_op jit(solution)/shard_map/all_gather | solution.py:682
  118.1 38.0 %attend.1 = (bf16[4,2304,256]{2,1,0:T(8,128)(2,1)}, bf16[4,256,768]{2,1,0:T(8,128)(2,1)}, bf16[4,256,768]{2,1,0:T(8,128)(2,1)}, f32[4,256,768]{2,1,0:T(8,128)}, ...) custom-call(s32[1]{0:T(128)S(6)} %copy.76.tag_ref, bf16[4,256,768]{2,1,0:T(8,128)(2,1)} %first_conv.1.conv_in, ...), custom_call_target="tpu_custom_call" | custom-call | tf_op jit(solution)/shard_map/attend/pallas_call | solution.py:312
  156.1 79.8 %feed.1 = (f32[4,256,768]{2,1,0:T(8,128)}, f32[4,256,768]{2,1,0:T(8,128)}, bf16[16,2,4,48,384]{4,3,2,1,0:T(8,128)(2,1)}, bf16[16,2,4,48,384]{4,3,2,1,0:T(8,128)(2,1)}, f32[9,3072]{1,0:T(8,128)}) custom-call(s32[1]{0:T(128)S(6)} %copy.76.tag_ref, bf16[4,256,768]{2,1,0:T(8,128)(2,1)} %get-tuple-element.39.second, ...), custom_call_target="tpu_custom_call" | custom-call | tf_op jit(solution)/shard_map/feed/pallas_call | solution.py:415
  235.8 48.6 %attend_back.1 = (bf16[4,256,768]{2,1,0:T(8,128)(2,1)}, f32[4,256,768]{2,1,0:T(8,128)}, bf16[16,2,3,48,384]{4,3,2,1,0:T(8,128)(2,1)}, bf16[16,2,1,48,384]{4,3,2,...) custom-call(s32[1]{0:T(128)S(6)} %copy.76.tag_ref, f32[4,256,768]{2,1,0:T(8,128)} %get-tuple-element.38.resid, ...), custom_call_target="tpu_custom_call" | custom-call | tf_op jit(solution)/shard_map/attend_back/pallas_call | solution.py:537
  284.5 16.3 %finish.1 = (bf16[1024,768]{1,0:T(8,128)(2,1)}, f32[1024,768]{1,0:T(8,128)}, f32[9,768]{1,0:T(8,128)}, f32[2,4,8,768]{3,2,1,0:T(8,128)}) custom-call(s32[1]{0:T(128)S(6)} %copy.76.tag_ref, f32[4,256,768]{2,1,0:T(8,128)} %get-tuple-element.47.d_conv, f32[4,256,768]{2,1,0:T(8,128)} %get-tuple-element.36.norm, f32[4,256,1]{2,1,0:T(8,128)} %get-tuple-element.48.factor, ...), custom_call_target="tpu_custom_call" | custom-call | tf_op jit(solution)/shard_map/finish/pallas_call | solution.py:652
  300.8 0.9 reshape.152
  301.7 0.1 reshape.153
  301.8 0.1 copy.68
  301.9 0.8 maximum_bitcast_fusion
  302.8 4.8 pad_maximum_fusion.1
  307.7 7.8 %pad_maximum_fusion = bf16[16,2,8,48,384]{4,3,2,1,0:T(8,128)(2,1)} fusion(bf16[16,2,4,48,384]{4,3,2,1,0:T(8,128)(2,1)} %get-tuple-element.60, bf16[16,2,4,48,384]{4,3,2,1,0:T(8,128)(2,1)} %get-tuple-element.59), kind=kLoop, calls=%fused_computation | loop fusion | flops 4718592 | bytes 18874368 | tf_op jit(solution)/shard_map/concatenate | solution.py:701
  315.6 1.0 copy-done.2
  316.6 0.2 maximum_reduce_fusion
  316.9 0.1 reshape.147
  317.1 10.7 %all_to_all.24 = bf16[32,4,288]{2,1,0:T(4,128)(2,1)S(1)} all-to-all(bf16[32,4,288]{2,1,0:T(4,128)(2,1)S(1)} %bitcast.91), channel_id=1, replica_groups=mesh['dp'=16,'fsdp'=2] {'dp','fsdp'}, dimensions={0} | all-to-all | bytes 147456 | tf_op jit(solution)/shard_map/all_to_all | solution.py:672
  327.8 0.3 convolution_dynamic-update-slice_fusion
  328.1 0.9 broadcast_in_dim.56
  329.0 2.6 all-to-all-start.3
  331.7 1.0 fusion.15
  332.7 25.6 %reduce-scatter.4.cloned.1.call-done = f32[1,9,240]{2,1,0:T(8,128)} async-done(((f32[16,9,240]{2,1,0:T(8,128)}), f32[1,9,240]{2,1,0:T(8,128)}) %reduce-scatter.4.cloned.1.call-update) | async-done | bytes 8656 | tf_op jit(solution)/shard_map/reduce_scatter | solution.py:810
  358.3 8.6 %psum.15 = f32[9,240]{1,0:T(8,128)S(1)} all-reduce(f32[9,240]{1,0:T(8,128)} %bitcast.101), channel_id=1, replica_groups=mesh['dp'=16,'fsdp'=2] {'fsdp'}, use_global_device_ids=true, to_apply=%region_6.7 | all-reduce | flops 2160 | bytes 17280 | tf_op jit(solution)/shard_map/psum | solution.py:811
  366.8 0.7 slice.77
  367.5 0.6 slice.73
  368.2 0.9 fusion
  369.1 0.9 fusion.3
  370.0 99.5 %reduce-scatter.6.cloned.1.call-done = bf16[1,192,384]{2,1,0:T(8,128)(2,1)} async-done(((bf16[32,192,384]{2,1,0:T(8,128)(2,1)}), bf16[1,192,384]{2,1,0:T(8,128)(2,1)}) %reduce-scatter.6.cloned.1.call-update) | async-done | bytes 147472 | tf_op jit(solution)/shard_map/reduce_scatter | solution.py:702
  469.6 0.9 convert_element_type.28
  470.5 0.6 slice_bitcast_fusion.4
  471.1 0.7 slice_bitcast_fusion.2
  471.8 139.1 %reduce-scatter.8.cloned.1.call-done = bf16[1,384,384]{2,1,0:T(8,128)(2,1)} async-done(((bf16[32,384,384]{2,1,0:T(8,128)(2,1)}), bf16[1,384,384]{2,1,0:T(8,128)(2,1)}) %reduce-scatter.8.cloned.1.call-update) | async-done | bytes 294928 | tf_op jit(solution)/shard_map/reduce_scatter | solution.py:702
  610.9 0.9 slice.78
  611.8 0.1 copy.69
  612.0 0.7 copy.74
  612.7 1.0 convert_element_type.29
  613.7 0.7 slice_bitcast_fusion
  (47 shorter events, 1.1 us)
Async XLA Ops:
  7.2 52.6 %copy-start = (bf16[384,288]{0,1:T(8,128)(2,1)S(1)}, bf16[384,288]{0,1:T(8,128)(2,1)}, u32[]{:S(2)}) copy-start(bf16[384,288]{0,1:T(8,128)(2,1)} %param.20) | copy-start | bytes 663556
  7.2 19.5 %copy-start.5 = (bf16[500,48]{0,1:T(8,128)(2,1)S(1)}, bf16[500,48]{0,1:T(8,128)(2,1)}, u32[]{:S(2)}) copy-start(bf16[500,48]{0,1:T(8,128)(2,1)} %param.18) | copy-start | bytes 144004
  7.2 19.8 %copy-start.6 = (bf16[500,48]{0,1:T(8,128)(2,1)S(1)}, bf16[500,48]{0,1:T(8,128)(2,1)}, u32[]{:S(2)}) copy-start(bf16[500,48]{0,1:T(8,128)(2,1)} %param.19) | copy-start | bytes 144004
  7.2 110.9 %all-gather.5.cloned.1.call-start = ((), (), s32[]{:S(2)}) async-start(), calls=%async_computation.10 | async-start | bytes 14598144 | tf_op jit(solution)/shard_map/all_gather | solution.py:682
  11.5 15.0 %all-to-all-start = ((s32[32,1,8]{2,1,0:T(1,128)}), s32[32,1,8]{2,1,0:T(1,128)S(1)}, u32[]{:S(2)}, u32[]{:S(2)}) async-start(s32[32,1,8]{2,1,0:T(1,128)} %broadcast_in_dim.46), calls=%async_computation | async-start | bytes 32768 | tf_op jit(solution)/shard_map/all_to_all | solution.py:672
  60.8 12.2 %all-to-all-start.1 = ((f32[32,4,288]{2,1,0:T(4,128)}), f32[32,4,288]{2,1,0:T(4,128)S(1)}, u32[]{:S(2)}, u32[]{:S(2)}) async-start(f32[32,4,288]{2,1,0:T(4,128)} %reshape.138), calls=%async_computation.1 | async-start | bytes 393216 | tf_op jit(solution)/shard_map/all_to_all | solution.py:672
  63.4 294.9 %reduce-scatter.4.cloned.1.call-start = ((), (), s32[]{:S(2)}) async-start(), calls=%async_computation.7 | async-start | bytes 278528 | tf_op jit(solution)/shard_map/reduce_scatter | solution.py:810
  284.5 17.3 %copy-start.3 = (f32[9,3072]{1,0:T(8,128)S(1)}, f32[9,3072]{1,0:T(8,128)}, u32[]{:S(2)}) copy-start(f32[9,3072]{1,0:T(8,128)} %get-tuple-element.56) | copy-start | bytes 331780
  284.5 18.4 %copy-start.1 = (bf16[16,2,1,48,384]{4,3,2,1,0:T(8,128)(2,1)S(1)}, bf16[16,2,1,48,384]{4,3,2,1,0:T(8,128)(2,1)}, u32[]{:S(2)}) copy-start(bf16[16,2,1,48,384]{4,3,2,1,0:T(8,128)(2,1)} %get-tuple-element.58) | copy-start | bytes 3538948
  302.8 166.8 %reduce-scatter.6.cloned.1.call-start = ((), (), s32[]{:S(2)}) async-start(), calls=%async_computation.8 | async-start | bytes 4866048 | tf_op jit(solution)/shard_map/reduce_scatter | solution.py:702
  307.6 303.3 %reduce-scatter.8.cloned.1.call-start = ((), (), s32[]{:S(2)}) async-start(), calls=%async_computation.9 | async-start | bytes 9732096 | tf_op jit(solution)/shard_map/reduce_scatter | solution.py:702
  315.5 1.0 copy-start.2
  315.5 1.0 copy-start.4
  329.0 39.1 %all-to-all-start.3 = ((f32[32,128,48]{1,2,0:T(8,128)}), f32[32,128,48]{1,2,0:T(8,128)S(1)}, u32[]{:S(2)}, u32[]{:S(2)}) async-start(f32[32,128,48]{1,2,0:T(8,128)} %bitcast.28), calls=%async_computation.3 | async-start | bytes 1572864 | tf_op jit(solution)/shard_map/all_to_all | solution.py:672
Sparse Core Ops, SparseCore 0:
  11.5 106.5 all-gather.4
  302.9 55.3 reduce-scatter.3
  363.8 105.7 reduce-scatter.5
  476.3 134.5 reduce-scatter.7

commit v2 on v1

--- a/solution.py
+++ b/solution.py
@@ -35,6 +35,10 @@
     return pltpu.CompilerParams(vmem_limit_bytes=limit * MIB)
 
 
+def cost(micros):
+    return pl.CostEstimate(flops=int(micros * 1.1e9), transcendentals=0, bytes_accessed=4 * MIB)
+
+
 def whole(shape):
     zeros = (0,) * len(shape)
     return pl.BlockSpec(shape, lambda *ids: zeros, pipeline_mode=pl.Buffered(1))
@@ -93,6 +97,7 @@
             jax.ShapeDtypeStruct((4, GROUP, 1), F32),
         ],
         compiler_params=params(),
+        cost_estimate=cost(6),
         name="prepare",
     )(latents, cotangent)
 
@@ -228,6 +233,7 @@
         out_specs=pl.BlockSpec((4, GROUP, 128), lambda i: (0, 0, i)),
         out_shape=jax.ShapeDtypeStruct((4, GROUP, D), BF),
         compiler_params=params(),
+        cost_estimate=cost(6),
         name="first_conv",
     )(tag, norm, mods, kernel)
 
@@ -236,6 +242,20 @@
     rows = block.shape[0] * block.shape[2] * UR
     for k in range(NK):
         target[:, k * UC : (k + 1) * UC] = block[:, k].reshape(rows, UC)
+
+
+def share_out(rows, core, units, keep, send):
+    first, count = units
+    for k in range(NK):
+        part = rows[:, k * UC : (k + 1) * UC].astype(BF)
+        part = part.reshape(-1, 2, part.shape[0] // (keep.shape[0] * 2), UC)
+        even, odd = part[:, 0], part[:, 1]
+        for target, value in (
+            (keep, jnp.where(core == 0, even, odd)),
+            (send, jnp.where(core == 0, odd, even)),
+        ):
+            whole_units = value.reshape(value.shape[0], -1, UR, UC)
+            target[:, k] = whole_units[:, first : first + count]
 
 
 def quadrant_rows(mods, index, half):
@@ -343,13 +363,14 @@
             pltpu.VMEM((D, GROUP), BF),
         ],
         compiler_params=params(),
+        cost_estimate=cost(38),
         name="attend",
     )(tag, conv_in, tokens, mods, packed, packed)
 
 
 def feed_kernel(
     tag_ref, second, gradient, mods, w_expand, w_shrink, kernel,
-    shrunk, d_second, g_expand, g_shrink, g_kernel,
+    shrunk, d_second, keep_expand, send_expand, keep_shrink, send_shrink, g_kernel,
     d_shrunk, d_shrunk_t, weight, field, slope, hidden, d_field,
 ):
     step = pl.program_id(0)
@@ -404,10 +425,16 @@
     d_fld = d_field[...].reshape(TOK, CHUNK)
     shrunk[...] += dot(hid, shrink, 1, 1).reshape(4, GROUP, D)
     d_second[...] += dot(d_fld, weight[...], 1, 0).reshape(4, GROUP, D)
-    g_shrink[...] = dot(d_shrunk_t[...], hid, 1, 0).astype(BF).reshape(NJ, 1, 1, UR, UC)
-    grad = dot(d_fld, second[...].reshape(TOK, D), 0, 0).astype(BF)
-    for k in range(NK):
-        g_expand[:, k] = grad[:, k * UC : (k + 1) * UC].reshape(2, 4, UR, UC)
+    core = tag_ref[1]
+    grad = dot(d_shrunk_t[...], hid, 1, 0).astype(BF).reshape(NJ // 2, 2, UR, UC)
+    own, other = jnp.where(core == 0, grad[:, 0], grad[:, 1]), jnp.where(core == 0, grad[:, 1], grad[:, 0])
+    keep_shrink[...] = own.reshape(NJ // 2, 1, 1, UR, UC)
+    send_shrink[...] = other.reshape(NJ // 2, 1, 1, UR, UC)
+    share_out(dot(d_fld, second[...].reshape(TOK, D), 0, 0), core, (0, 4), keep_expand, send_expand)
+
+
+def packed_half(units):
+    return jax.ShapeDtypeStruct((NJ // 2, NK, units, UR, UC), BF)
 
 
 def feed(tag, second, gradient, mods, packed, kernel):
@@ -427,15 +454,19 @@
         out_specs=[
             pl.BlockSpec((4, GROUP, D), lambda c: (0, 0, 0)),
             pl.BlockSpec((4, GROUP, D), lambda c: (0, 0, 0)),
-            pl.BlockSpec((2, NK, 4, UR, UC), lambda c: (c, 0, 0, 0, 0)),
-            pl.BlockSpec((NJ, 1, 1, UR, UC), lambda c: (0, c // 4, c % 4, 0, 0)),
+            pl.BlockSpec((1, NK, 4, UR, UC), lambda c: (c, 0, 0, 0, 0)),
+            pl.BlockSpec((1, NK, 4, UR, UC), lambda c: (c, 0, 0, 0, 0)),
+            pl.BlockSpec((NJ // 2, 1, 1, UR, UC), lambda c: (0, c // 4, c % 4, 0, 0)),
+            pl.BlockSpec((NJ // 2, 1, 1, UR, UC), lambda c: (0, c // 4, c % 4, 0, 0)),
             pl.BlockSpec((9, CHUNK), lambda c: (0, c)),
         ],
         out_shape=[
             jax.ShapeDtypeStruct((4, GROUP, D), F32),
             jax.ShapeDtypeStruct((4, GROUP, D), F32),
-            jax.ShapeDtypeStruct((NJ, NK, 4, UR, UC), BF),
-            jax.ShapeDtypeStruct((NJ, NK, 4, UR, UC), BF),
+            packed_half(4),
+            packed_half(4),
+            packed_half(4),
+            packed_half(4),
             jax.ShapeDtypeStruct((9, FF), F32),
         ],
         scratch_shapes=[
@@ -448,13 +479,14 @@
             pltpu.VMEM((4, GROUP, CHUNK), BF),
         ],
         compiler_params=params(60),
+        cost_estimate=cost(80),
         name="feed",
     )(tag, second, gradient, mods, packed, packed, kernel)
 
 
 def attend_back_kernel(
     tag_ref, resid, shrunk, d_second, gradient, attn, mods, qkv, merged, conv_in, lse, w_qkv, w_proj,
-    output, d_resid, g_qkv, g_proj, d_conv, sums,
+    output, d_resid, keep_a, send_a, keep_b, send_b, d_conv, sums,
     full_qkv, full_proj, proj_t, bias, d_mixed, d_qkv, acc_qkv, acc_proj, d_attn,
 ):
     step = pl.program_id(0)
@@ -527,10 +559,10 @@
 
     @pl.when(step == pl.num_programs(0) - 1)
     def _():
-        for k in range(NK):
-            cols = slice(k * UC, (k + 1) * UC)
-            g_qkv[:, k] = acc_qkv[:, cols].astype(BF).reshape(NJ, 3, UR, UC)
-            g_proj[:, k] = acc_proj[:, cols].astype(BF).reshape(NJ, 1, UR, UC)
+        core = tag_ref[1]
+        share_out(acc_qkv, core, (0, 2), keep_a, send_a)
+        share_out(acc_qkv, core, (2, 1), keep_b.at[:, :, 0:1], send_b.at[:, :, 0:1])
+        share_out(acc_proj, core, (0, 1), keep_b.at[:, :, 1:2], send_b.at[:, :, 1:2])
 
 
 def attend_back(tag, resid, shrunk, d_second, gradient, attn, mods, qkv, merged, conv_in, lse, packed):
@@ -555,16 +587,20 @@
         out_specs=[
             group_spec(GROUP, D),
             group_spec(GROUP, D),
-            whole((NJ, NK, 3, UR, UC)),
-            whole((NJ, NK, 1, UR, UC)),
+            whole((NJ // 2, NK, 2, UR, UC)),
+            whole((NJ // 2, NK, 2, UR, UC)),
+            whole((NJ // 2, NK, 2, UR, UC)),
+            whole((NJ // 2, NK, 2, UR, UC)),
             group_spec(GROUP, D),
             whole((4, 4, 8, D)),
         ],
         out_shape=[
             jax.ShapeDtypeStruct((4, GROUP, D), BF),
             jax.ShapeDtypeStruct((4, GROUP, D), F32),
-            jax.ShapeDtypeStruct((NJ, NK, 3, UR, UC), BF),
-            jax.ShapeDtypeStruct((NJ, NK, 1, UR, UC), BF),
+            packed_half(2),
+            packed_half(2),
+            packed_half(2),
+            packed_half(2),
             jax.ShapeDtypeStruct((4, GROUP, D), F32),
             jax.ShapeDtypeStruct((4, 4, 8, D), F32),
         ],
@@ -580,6 +616,7 @@
             pltpu.VMEM((GROUP, D), BF),
         ],
         compiler_params=params(60),
+        cost_estimate=cost(49),
         name="attend_back",
     )(tag, resid, shrunk, d_second, gradient, attn, mods, qkv, merged, conv_in, lse, packed, packed)
 
@@ -661,6 +698,7 @@
         ],
         scratch_shapes=[pltpu.VMEM((4, GROUP, D), F32), pltpu.VMEM((4, GROUP, D), F32)],
         compiler_params=params(60),
+        cost_estimate=cost(16),
         name="finish",
     )(tag, d_conv, norm, factor, d_resid, output, mods, kernel)
 
@@ -695,32 +733,59 @@
     )
 
 
-def scatter_packed(nd, nf, parts):
-    kinds = [kind for kind, _ in parts]
+def pick(grads, index, axis):
+    return lax.dynamic_index_in_dim(grads, index, axis, keepdims=False)
+
+
+def swap(value, bit):
+    if bit is None:
+        return lax.ppermute(value, "fsdp", [(0, 1), (1, 0)])
+    return lax.ppermute(value, "dp", [(i, i ^ bit) for i in range(NJ)])
+
+
+def halve(keep, got, axis, bit):
+    mine = lax.axis_index("fsdp") if bit is None else (lax.axis_index("dp") // bit) % 2
+    sent = pick(keep, 1 - mine, axis) + pick(got, 1 - mine, axis)
+    kept = pick(keep, mine, axis) + pick(got, mine, axis)
+    return kept, swap(sent, bit)
+
+
+def last_sum(keep, got):
+    place = lax.axis_index("dp") // 4
+    total = (pick(keep, place, 0) + pick(got, place, 0)).astype(F32)
+    for step in range(1, 4):
+        target = (place + step) % 4
+        sent = pick(keep, target, 0) + pick(got, target, 0)
+        moved = [(i, (i + 4 * step) % NJ) for i in range(NJ)]
+        total = total + lax.ppermute(sent, "dp", moved).astype(F32)
+    return total
+
+
+def scatter_packed(nd, nf, keep_a, send_a, keep_b, send_b):
     if (nd, nf) == (NJ, NK):
-        joined = jnp.concatenate([grad for _, grad in parts], axis=2)
-        rows = lax.psum_scatter(
-            joined.reshape(NJ * NK, -1, UC), BOTH, scatter_dimension=0, tiled=True
-        )[0].astype(F32)
-        out, start = [], 0
-        for kind, grad in parts:
-            size = grad.shape[2] * UR
-            piece = rows[start : start + size]
-            start += size
-            if kind == "shrink":
-                piece = piece.reshape(4, UR, UC).transpose(1, 0, 2).reshape(UR, 4 * UC)
-            out.append(piece.T)
-        return out
-    out = []
-    for kind, grad in parts:
+        a, b = (x.reshape((4, 2) + x.shape[1:]) for x in (keep_a, keep_b))
+        got_a, got_b = swap(send_a, 1).reshape(a.shape), swap(send_b, 1).reshape(b.shape)
+        a, got_a = halve(a, got_a, 2, None)
+        b, got_b = halve(b, got_b, 1, 2)
+        a, got_a = halve(a, got_a, 1, 2)
+        b, got_b = halve(b, got_b, 1, None)
+        return last_sum(a, got_a), last_sum(b, got_b)
+    return jnp.stack([keep_a, send_a], axis=1), jnp.stack([keep_b, send_b], axis=1)
+
+
+def own_shard(nd, nf, kind, units):
+    if (nd, nf) == (NJ, NK):
         if kind == "shrink":
-            weight = grad.transpose(0, 3, 1, 2, 4).reshape(NJ * UR, -1)
-        else:
-            weight = grad.transpose(0, 2, 3, 1, 4).reshape(-1, NK * UC)
-        columns = lax.psum_scatter(weight, "dp", scatter_dimension=0, tiled=True)
-        piece = lax.psum_scatter(columns, "fsdp", scatter_dimension=1, tiled=True)
-        out.append(piece.astype(F32).T)
-    return out
+            return units.transpose(1, 0, 2).reshape(UR, 4 * UC).T
+        return units.reshape(-1, UC).T
+    units = units.reshape((NJ,) + units.shape[2:])
+    if kind == "shrink":
+        weight = units.transpose(0, 3, 1, 2, 4).reshape(NJ * UR, -1)
+    else:
+        weight = units.transpose(0, 2, 3, 1, 4).reshape(-1, NK * UC)
+    columns = lax.psum_scatter(weight, "dp", scatter_dimension=0, tiled=True)
+    piece = lax.psum_scatter(columns, "fsdp", scatter_dimension=1, tiled=True)
+    return piece.astype(F32).T
 
 
 def condition(nd, nf, timesteps, classes, step_table, class_table, attn_kernel, ffn_kernel):
@@ -753,6 +818,8 @@
 ):
     slots = nd * nf
     tag = size_tags[0]
+    core = lax.axis_index("dp") % 2 if (nd, nf) == (NJ, NK) else jnp.int32(0)
+    where = jnp.stack([tag, core])
     packed = gather_packed(nd, nf, qkv_weight, proj_weight, expand_weight, shrink_weight)
     tokens, gradient, norm, factor = prepare(latents, cotangent)
     step_hot, class_hot, cond, act_all, attn_full, ffn_full = condition(
@@ -770,16 +837,15 @@
 
     conv_in = first_conv(size_tags, norm, mods, attn_full)
     qkv, merged, attn, resid, second, lse = attend(size_tags, conv_in, tokens, mods, packed)
-    shrunk, d_second, g_expand, g_shrink, g_ffn = feed(
-        size_tags, second, gradient, mods, packed, ffn_full
-    )
-    expand_grad, shrink_grad = scatter_packed(
-        nd, nf, [("expand", g_expand), ("shrink", g_shrink)]
-    )
-    output, d_resid, g_qkv, g_proj, d_conv, later = attend_back(
-        size_tags, resid, shrunk, d_second, gradient, attn, mods, qkv, merged, conv_in, lse, packed
-    )
-    qkv_grad, proj_grad = scatter_packed(nd, nf, [("qkv", g_qkv), ("proj", g_proj)])
+    shrunk, d_second, *grads, g_ffn = feed(where, second, gradient, mods, packed, ffn_full)
+    expand, shrink = scatter_packed(nd, nf, *grads)
+    output, d_resid, *grads, d_conv, later = attend_back(
+        where, resid, shrunk, d_second, gradient, attn, mods, qkv, merged, conv_in, lse, packed
+    )
+    first, rest = scatter_packed(nd, nf, *grads)
+    units = rest.ndim - 3
+    proj = lax.slice_in_dim(rest, 1, 2, axis=units)
+    joined = jnp.concatenate([first, lax.slice_in_dim(rest, 0, 1, axis=units)], axis=units)
     block_output, input_grad, g_attn, early = finish(
         size_tags, d_conv, norm, factor, d_resid, output, mods, attn_full
     )
@@ -787,9 +853,18 @@
     rows = rows.transpose(1, 0, 2).reshape(4, 6 * D)
     alone = jnp.concatenate([rows.sum(axis=0, keepdims=True), jnp.zeros((3, 6 * D), F32)])
     d_mod = jnp.where(tag == 1, rows, alone).astype(BF)
-    pieces = d_mod.reshape(4, nd, 1, width).transpose(1, 2, 0, 3)
-    d_mod_all = exchange(jnp.broadcast_to(pieces, (nd, nf, 4, width)).reshape(slots, 4, width))
-    d_mod_all = d_mod_all.reshape(slots * 4, width)
+    filters = jnp.concatenate([g_attn.reshape(9, nd, -1), g_ffn.reshape(9, nd, -1)], axis=2)
+    pieces = jnp.concatenate(
+        [
+            d_mod.astype(F32).reshape(4, nd, width).transpose(1, 0, 2).reshape(nd, -1),
+            filters.transpose(1, 0, 2).reshape(nd, -1),
+        ],
+        axis=1,
+    )
+    pieces = jnp.broadcast_to(pieces[:, None], (nd, nf, pieces.shape[1])).reshape(slots, 1, -1)
+    got = exchange(pieces)[:, 0]
+    d_mod_all = got[:, : 4 * width].reshape(slots * 4, width).astype(BF)
+    filters = got[:, 4 * width :].sum(axis=0).reshape(9, -1)
     modulation_grad = dot(act_rows, d_mod_all, 0, 0)
     d_act = dot(d_mod_all, modulation_weight, 1, 1)
     spread = lax.dynamic_update_slice_in_dim(
@@ -806,9 +881,6 @@
             hot.astype(F32), d_cond, (((0,), (0,)), ((), ())), precision=lax.Precision.HIGHEST
         )
 
-    filters = jnp.concatenate([g_attn.reshape(9, nd, -1), g_ffn.reshape(9, nd, -1)], axis=2)
-    filters = lax.psum_scatter(filters.transpose(1, 0, 2), "dp", scatter_dimension=0, tiled=True)
-    filters = lax.psum(filters[0], "fsdp")
     cut = attn_kernel.shape[1]
     return (
         block_output,
@@ -817,11 +889,11 @@
         table_grad(class_hot),
         modulation_grad,
         filters[:, :cut],
-        qkv_grad,
-        proj_grad,
-        expand_grad,
+        own_shard(nd, nf, "qkv", joined),
+        own_shard(nd, nf, "proj", proj),
+        own_shard(nd, nf, "expand", expand),
         filters[:, cut:],
-        shrink_grad,
+        own_shard(nd, nf, "shrink", shrink),
     )
 
 

time: 622 us -> 441 us (0.71)
  waiting for transfers between devices: 309 us -> 104 us
  starting transfers between devices: 12.8 us -> 46.6 us
  blocking collectives: 51.6 us -> 32.3 us
  other arithmetic: 19.1 us -> 28 us
    reduce_scatter x3 -> x0, waiting for transfers between devices: 264 us -> none  [the longest x2 239 us: scatter_packed(): lax.psum_scatter(joined.reshape(NJ * NK, -1, UC), BOTH, scatter_dimension...]
    ppermute x0 -> x24, waiting for transfers between devices: none -> 54.2 us  [the longest x8 29.7 us: swap(): return lax.ppermute(value, 'dp', [(i, i ^ bit) for i in range(NJ)])]
    ppermute x0 -> x24, starting transfers between devices: none -> 30.5 us  [the longest x12 19.9 us: last_sum(): total = total + lax.ppermute(sent, 'dp', moved).astype(F32)]
    add x0 -> x15, other arithmetic: none -> 22.2 us  [the longest x8 17.4 us: halve(): kept = pick(keep, mine, axis) + pick(got, mine, axis)]
    concatenate x2, other arithmetic: 12.6 us -> 0.72 us  [the longest x1 0.7 us: body(): jnp.concatenate([first, lax.slice_in_dim(rest, 0, 1, axis=units)], axis=u...]
    all_to_all x1 -> x0, blocking collectives: 10.7 us -> none  [exchange(): return lax.all_to_all(pieces, BOTH, 0, 0, tiled=True)]
    psum x1 -> x0, blocking collectives: 8.55 us -> none  [body(): filters = lax.psum(filters[0], 'fsdp')]
    all_to_all x3 -> x4, waiting for transfers between devices: 7.2 us -> 12.5 us  [exchange(): return lax.all_to_all(pieces, BOTH, 0, 0, tiled=True)]
  transfers between devices with their start and end apart: 7 -> 29, of which waited for: 5 -> 13; matrix products, arithmetic and copies ran while one was open for 5% -> 9% of each run, Pallas kernels for 2% -> 18%
where the time goes in v2:
time: 441 us; the launch traced here: 440 us
  Pallas kernels  195 us (44%)
  waiting for transfers between devices  104 us (24%)
  starting transfers between devices  46.6 us (11%)
  blocking collectives  32.3 us (7%)
  other arithmetic  28 us (6%)
  between operations  15.4 us (3%)
  local copies, waits for them, and re-layouts  14.8 us (3%)
    pallas_call x1, Pallas kernels, feed(): pl.pallas_call(feed_kernel, grid=(steps,), in_specs=[SMEM_SPEC, whole((4,...  79.9 us
    pallas_call x1, Pallas kernels, attend_back(): pl.pallas_call(attend_back_kernel, grid=(4,), in_specs=[SMEM_SPEC, group_...  48.9 us
    pallas_call x1, Pallas kernels, attend(): pl.pallas_call(attend_kernel, grid=(4,), in_specs=[SMEM_SPEC, group_spec(...  37.9 us
    all_gather x1, waiting for transfers between devices, gather_packed(): rows = lax.all_gather(pack_shards(qkv, proj, expand, shrink), BOTH)  37.1 us
    ppermute x8, waiting for transfers between devices, swap(): return lax.ppermute(value, 'dp', [(i, i ^ bit) for i in range(NJ)])  29.7 us
    all_gather x1, blocking collectives, condition(): sent = lax.all_gather(jnp.concatenate([act, filters], axis=0), 'dp')  23.8 us
    ppermute x12, starting transfers between devices, last_sum(): total = total + lax.ppermute(sent, 'dp', moved).astype(F32)  19.9 us
    ppermute x12, waiting for transfers between devices, last_sum(): total = total + lax.ppermute(sent, 'dp', moved).astype(F32)  18.7 us
  transfers between devices with their start and end apart: 29, of which 13 were waited for; matrix products, arithmetic and copies ran while one was open for 9% of the time, Pallas kernels for 18%

profile of v2, /device:TPU:0, one launch (start us, length us, event | category | flops | bytes accessed | tf_op | source)
XLA Modules:
  0.0 439.6 jit_solution(18184843728509802309)
XLA Ops:
  7.3 1.0 reshape.236
  8.3 1.8 pad_maximum_fusion
  10.8 7.3 %all-to-all-start = ((s32[32,1,8]{2,1,0:T(1,128)}), s32[32,1,8]{2,1,0:T(1,128)S(1)}, u32[]{:S(2)}, u32[]{:S(2)}) async-start(s32[32,1,8]{2,1,0:T(1,128)} %broadcast_in_dim.45), calls=%async_computation | async-start | bytes 32768 | tf_op jit(solution)/shard_map/all_to_all | solution.py:710
  18.9 6.1 %prepare.1 = (bf16[4,256,768]{2,1,0:T(8,128)(2,1)}, bf16[4,256,768]{2,1,0:T(8,128)(2,1)}, f32[4,256,768]{2,1,0:T(8,128)}, f32[4,256,1]{2,1,0:T(8,128)}) custom-call(bf16[1024,768]{1,0:T(8,128)(2,1)} %latents.1, bf16[1024,768]{1,0:T(8,128)(2,1)} %cotangent.1), custom_call_target="tpu_custom_call" | custom-call | flops 6600000000 | bytes 4194304 | tf_op jit(solution)/shard_map/prepare/pallas_call | solution.py:88
  26.9 8.6 %psum.7 = f32[128,48]{0,1:T(8,128)S(1)} all-reduce(f32[128,48]{0,1:T(8,128)S(1)} %convolution_add_fusion), channel_id=1, replica_groups=mesh['dp'=16,'fsdp'=2] {'fsdp'}, use_global_device_ids=true, to_apply=%region_0.1 | all-reduce | flops 6144 | bytes 49152 | tf_op jit(solution)/shard_map/psum | solution.py:802
  35.5 23.8 %all-gather.2 = bf16[16,173,48]{1,2,0:T(8,128)(2,1)S(1)} all-gather(bf16[1,173,48]{1,2,0:T(8,128)(2,1)S(1)} %maximum_bitcast_fusion.1), channel_id=2, replica_groups=mesh['dp'=16,'fsdp'=2] {'dp'}, dimensions={0}, use_global_device_ids=true | all-gather | bytes 282336 | tf_op jit(solution)/shard_map/all_gather | solution.py:806
  60.3 0.7 reshape.232
  61.0 2.8 all-to-all-start.1
  64.3 0.7 reshape.235.kernel
  65.2 0.8 reshape.239.kernel
  66.0 7.2 %all-to-all-done.1 = f32[32,4,288]{2,1,0:T(4,128)S(1)} async-done(((f32[32,4,288]{2,1,0:T(4,128)}), f32[32,4,288]{2,1,0:T(4,128)S(1)}, u32[]{:S(2)}, u32[]{:S(2)}) %all-to-all-start.1) | async-done | bytes 147488 | tf_op jit(solution)/shard_map/all_to_all | solution.py:710
  73.6 0.8 broadcast_in_dim.49.mods
  74.5 6.2 %first_conv.1.conv_in = bf16[4,256,768]{2,1,0:T(8,128)(2,1)} custom-call(s32[1]{0:T(128)S(6)} %copy.92.tag_ref, f32[4,256,768]{2,1,0:T(8,128)} %get-tuple-element.40.norm, f32[6,4,8,768]{3,2,1,0:T(8,128)} %broadcast_in_dim.49.mods, f32[9,768]{1,0:T(8,128)} %reshape.235.kernel), custom_call_target="tpu_custom_call" | custom-call | flops 6600000000 | bytes 4194304 | tf_op jit(solution)/shard_map/first_conv/pallas_call | solution.py:224
  80.6 37.1 %all-gather.5.cloned.1.call-done = bf16[18432,384]{1,0:T(8,128)(2,1)} async-done(((bf16[576,384]{1,0:T(8,128)(2,1)}), bf16[18432,384]{1,0:T(8,128)(2,1)}) %all-gather.5.cloned.1.call-update) | async-done | bytes 14155792 | tf_op jit(solution)/shard_map/all_gather | solution.py:720
  117.7 37.9 %attend.1 = (bf16[4,2304,256]{2,1,0:T(8,128)(2,1)}, bf16[4,256,768]{2,1,0:T(8,128)(2,1)}, bf16[4,256,768]{2,1,0:T(8,128)(2,1)}, f32[4,256,768]{2,1,0:T(8,128)}, ...) custom-call(s32[1]{0:T(128)S(6)} %copy.92.tag_ref, bf16[4,256,768]{2,1,0:T(8,128)(2,1)} %first_conv.1.conv_in, ...), custom_call_target="tpu_custom_call" | custom-call | flops 41799999488 | bytes 4194304 | tf_op jit(solution)/shard_map/attend/pallas_call | solution.py:332
  155.5 79.9 %feed.1 = (f32[4,256,768]{2,1,0:T(8,128)}, f32[4,256,768]{2,1,0:T(8,128)}, bf16[8,2,4,48,384]{4,3,2,1,0:T(8,128)(2,1)}, bf16[8,2,4,48,384]{4,3,2,1,0:T(8,128)(2,...) custom-call(s32[2]{0:T(128)} %pad_add_fusion.tag_ref, ...), custom_call_target="tpu_custom_call" | custom-call | flops 88000004096 | bytes 4194304 | tf_op jit(solution)/shard_map/feed/pallas_call | solution.py:442
  236.0 48.9 %attend_back.1 = (bf16[4,256,768]{2,1,0:T(8,128)(2,1)}, f32[4,256,768]{2,1,0:T(8,128)}, bf16[8,2,2,48,384]{4,3,2,1,0:T(8,128)(2,1)}, bf16[8,2,2,48,384]{4,3,2,1,...) custom-call(s32[2]{0:T(128)} %pad_add_fusion.tag_ref, ...), custom_call_target="tpu_custom_call" | custom-call | flops 53900001280 | bytes 4194304 | tf_op jit(solution)/shard_map/attend_back/pallas_call | solution.py:569
  285.5 16.0 %finish.1 = (bf16[1024,768]{1,0:T(8,128)(2,1)}, f32[1024,768]{1,0:T(8,128)}, f32[9,768]{1,0:T(8,128)}, f32[2,4,8,768]{3,2,1,0:T(8,128)}) custom-call(s32[1]{0:T(128)S(6)} %copy.92.tag_ref, f32[4,256,768]{2,1,0:T(8,128)} %get-tuple-element.51.d_conv, f32[4,256,768]{2,1,0:T(8,128)} %get-tuple-element.40.norm, f32[4,256,1]{2,1,0:T(8,128)} %get-tuple-element.52.factor, ...), custom_call_target="tpu_custom_call" | custom-call | flops 17600000000 | bytes 4194304 | tf_op jit(solution)/shard_map/finish/pallas_call | solution.py:689
  301.5 1.1 maximum_reduce_fusion
  303.8 1.4 reshape.247
  305.2 2.7 all-to-all-start.2
  308.0 2.3 dynamic-slice_add_fusion.3
  310.4 1.8 collective-permute-start.1
  312.1 1.5 dynamic-slice_add_fusion.2
  313.6 0.9 fusion
  314.5 1.5 collective-permute-start.7
  316.0 5.3 %all-to-all-done.2 = f32[32,1,3312]{2,1,0:T(1,128)S(1)} async-done(((f32[32,1,3312]{2,1,0:T(1,128)}), f32[32,1,3312]{2,1,0:T(1,128)S(1)}, u32[]{:S(2)}, u32[]{:S(2)}) %all-to-all-start.2) | async-done | bytes 423968 | tf_op jit(solution)/shard_map/all_to_all | solution.py:710
  321.3 0.7 copy-done.3
  322.5 0.9 broadcast_in_dim.54
  323.5 3.2 all-to-all-start.3
  326.7 3.6 dynamic-slice_add_fusion
  330.3 1.8 collective-permute-start.19
  332.1 1.3 bitcast_add_fusion.7
  333.9 1.1 bitcast_add_fusion.5
  335.0 1.7 collective-permute-start.8
  336.7 3.0 dynamic-slice_add_fusion.1
  340.1 1.0 fusion.35
  341.1 29.5 %collective-permute-done.2 = bf16[4,2,48,384]{3,2,1,0:T(8,128)(2,1)S(1)} collective-permute-done((bf16[4,2,48,384]{3,2,1,0:T(8,128)(2,1)S(1)}, bf16[4,2,48,384]{3,2,1,0:T(8,128)(2,1)S(1)}, u32[]{:S(2)}, u32[]{:S(2)}) %collective-permute-start.2) | collective-permute-done | bytes 294944 | tf_op jit(solution)/shard_map/ppermute | solution.py:743
  370.7 1.5 collective-permute-start.3
  372.3 2.1 collective-permute-start.4
  374.4 1.7 collective-permute-start.5
  376.8 1.1 collective-permute-done.3
  377.8 4.4 %collective-permute-start.10 = (bf16[2,48,384]{2,1,0:T(8,128)(2,1)}, bf16[2,48,384]{2,1,0:T(8,128)(2,1)}, u32[]{:S(2)}, u32[]{:S(2)}) collective-permute-start(bf16[2,48,384]{2,1,0:T(8,128)(2,1)} %get-tuple-element.97), channel_id=1, source_target_pairs={{0,16},{2,18},{4,20},{6,22},{8,24},{10,26},{12,28},{14,30},{16,0},... | collective-permute-start | bytes 221192 | tf_op jit(solution)/shard_map/ppermute | solution.py:760
  382.2 2.5 collective-permute-start.11
  387.0 4.2 collective-permute-done.9
  391.2 1.2 fusion.18
  392.4 2.4 bitcast_add_fusion.1
  394.8 1.1 collective-permute-start.20
  396.6 2.2 bitcast_add_fusion.3
  398.8 0.9 collective-permute-start.14
  400.5 0.9 fusion.3
  401.4 5.8 %collective-permute-done.20 = bf16[4,4,48,384]{3,2,1,0:T(8,128)(2,1)} collective-permute-done((bf16[4,4,48,384]{3,2,1,0:T(8,128)(2,1)}, bf16[4,4,48,384]{3,2,1,0:T(8,128)(2,1)}, u32[]{:S(2)}, u32[]{:S(2)}) %collective-permute-start.20) | collective-permute-done | bytes 589856 | tf_op jit(solution)/shard_map/ppermute | solution.py:742
  407.2 1.1 fusion.23
  408.4 1.3 collective-permute-start.22
  409.7 2.4 collective-permute-start.23
  412.2 0.9 fusion.6
  413.8 1.5 collective-permute-start.16
  415.3 1.8 collective-permute-done.21
  417.1 1.7 collective-permute-start.17
  418.7 3.8 collective-permute-done.22
  422.5 1.0 fusion.12
  423.5 0.7 copy.81
  424.7 7.3 %collective-permute-done.16 = bf16[4,48,384]{2,1,0:T(8,128)(2,1)S(1)} collective-permute-done((bf16[4,48,384]{2,1,0:T(8,128)(2,1)S(1)}, bf16[4,48,384]{2,1,0:T(8,128)(2,1)S(1)}, u32[]{:S(2)}, u32[]{:S(2)}) %collective-permute-start.16) | collective-permute-done | bytes 147488 | tf_op jit(solution)/shard_map/ppermute | solution.py:760
  432.0 0.8 fusion.14
  (152 shorter events, 14.1 us)
Async XLA Ops:
  7.2 52.8 %copy-start = (bf16[384,288]{0,1:T(8,128)(2,1)S(1)}, bf16[384,288]{0,1:T(8,128)(2,1)}, u32[]{:S(2)}) copy-start(bf16[384,288]{0,1:T(8,128)(2,1)} %param.20) | copy-start | bytes 663556
  7.2 2.9 copy-start.30
  7.2 2.9 copy-start.29
  7.2 11.6 %copy-start.20 = (bf16[9,48]{1,0:T(8,128)(2,1)S(1)}, bf16[9,48]{1,0:T(8,128)(2,1)}, u32[]{:S(2)}) copy-start(bf16[9,48]{1,0:T(8,128)(2,1)} %param.21) | copy-start | bytes 2596
  7.2 11.6 %copy-start.19 = (bf16[9,192]{1,0:T(8,128)(2,1)S(1)}, bf16[9,192]{1,0:T(8,128)(2,1)}, u32[]{:S(2)}) copy-start(bf16[9,192]{1,0:T(8,128)(2,1)} %param.25) | copy-start | bytes 10372
  7.2 110.4 %all-gather.5.cloned.1.call-start = ((), (), s32[]{:S(2)}) async-start(), calls=%async_computation.4 | async-start | bytes 14598144 | tf_op jit(solution)/shard_map/all_gather | solution.py:720
  10.8 15.0 %all-to-all-start = ((s32[32,1,8]{2,1,0:T(1,128)}), s32[32,1,8]{2,1,0:T(1,128)S(1)}, u32[]{:S(2)}, u32[]{:S(2)}) async-start(s32[32,1,8]{2,1,0:T(1,128)} %broadcast_in_dim.45), calls=%async_computation | async-start | bytes 32768 | tf_op jit(solution)/shard_map/all_to_all | solution.py:710
  18.8 7.5 %copy-start.21 = (s32[500]{0:T(512)}, s32[500]{0:T(512)S(1)}, u32[]{:S(2)}) copy-start(s32[500]{0:T(512)S(1)} %iota_add_fusion) | copy-start | bytes 6004
  18.9 7.2 %copy-start.27 = (bf16[500,48]{0,1:T(8,128)(2,1)S(1)}, bf16[500,48]{0,1:T(8,128)(2,1)}, u32[]{:S(2)}) copy-start(bf16[500,48]{0,1:T(8,128)(2,1)} %param.18) | copy-start | bytes 144004
  18.9 7.7 %copy-start.28 = (bf16[500,48]{0,1:T(8,128)(2,1)S(1)}, bf16[500,48]{0,1:T(8,128)(2,1)}, u32[]{:S(2)}) copy-start(bf16[500,48]{0,1:T(8,128)(2,1)} %param.19) | copy-start | bytes 144004
  26.0 0.5 copy-start.23
  26.1 0.6 copy-start.25
  35.5 23.8 %copy-start.15 = (f32[128,48]{0,1:T(8,128)}, f32[128,48]{0,1:T(8,128)S(1)}, u32[]{:S(2)}) copy-start(f32[128,48]{0,1:T(8,128)S(1)} %psum.7) | copy-start | bytes 73732
  59.3 0.7 copy-start.9
  61.0 12.2 %all-to-all-start.1 = ((f32[32,4,288]{2,1,0:T(4,128)}), f32[32,4,288]{2,1,0:T(4,128)S(1)}, u32[]{:S(2)}, u32[]{:S(2)}) async-start(f32[32,4,288]{2,1,0:T(4,128)} %reshape.232), calls=%async_computation.1 | async-start | bytes 393216 | tf_op jit(solution)/shard_map/all_to_all | solution.py:710
  235.4 91.3 %collective-permute-start.18 = (bf16[8,2,4,48,384]{4,3,2,1,0:T(8,128)(2,1)}, bf16[8,2,4,48,384]{4,3,2,1,0:T(8,128)(2,1)}, u32[]{:S(2)}, u32[]{:S(2)}) collective-permute-start(bf16[8,2,4,48,384]{4,3,2,1,0:T(8,128)(2,1)} %get-tuple-element.68), channel_id=1, source_target_pairs={{0,2},{2,0},{4,6},{6,4},{8,10},{10,8},{12,14},{14,12},{16,18},{18,... | collective-permute-start | bytes 7077896 | tf_op jit(solution)/shard_map/ppermute | solution.py:743
  235.8 101.0 %collective-permute-start.12 = (bf16[8,2,4,48,384]{4,3,2,1,0:T(8,128)(2,1)}, bf16[8,2,4,48,384]{4,3,2,1,0:T(8,128)(2,1)}, u32[]{:S(2)}, u32[]{:S(2)}) collective-permute-start(bf16[8,2,4,48,384]{4,3,2,1,0:T(8,128)(2,1)} %get-tuple-element.66), channel_id=1, source_target_pairs={{0,2},{2,0},{4,6},{6,4},{8,10},{10,8},{12,14},{14,12},{16,18},{18,... | collective-permute-start | bytes 7077896 | tf_op jit(solution)/shard_map/ppermute | solution.py:743
  284.9 23.1 %collective-permute-start = (bf16[8,2,2,48,384]{4,3,2,1,0:T(8,128)(2,1)}, bf16[8,2,2,48,384]{4,3,2,1,0:T(8,128)(2,1)}, u32[]{:S(2)}, u32[]{:S(2)}) collective-permute-start(bf16[8,2,2,48,384]{4,3,2,1,0:T(8,128)(2,1)} %get-tuple-element.62), channel_id=1, source_target_pairs={{0,2},{2,0},{4,6},{6,4},{8,10},{10,8},{12,14},{14,12},{16,18},{18,... | collective-permute-start | bytes 3538952 | tf_op jit(solution)/shard_map/ppermute | solution.py:743
  285.2 26.9 %collective-permute-start.6 = (bf16[8,2,2,48,384]{4,3,2,1,0:T(8,128)(2,1)}, bf16[8,2,2,48,384]{4,3,2,1,0:T(8,128)(2,1)}, u32[]{:S(2)}, u32[]{:S(2)}) collective-permute-start(bf16[8,2,2,48,384]{4,3,2,1,0:T(8,128)(2,1)} %get-tuple-element.64), channel_id=1, source_target_pairs={{0,2},{2,0},{4,6},{6,4},{8,10},{10,8},{12,14},{14,12},{16,18},{18,... | collective-permute-start | bytes 3538952 | tf_op jit(solution)/shard_map/ppermute | solution.py:743
  285.5 16.0 %copy-start.11 = (f32[4,4,8,768]{3,2,1,0:T(8,128)S(1)}, f32[4,4,8,768]{3,2,1,0:T(8,128)}, u32[]{:S(2)}) copy-start(f32[4,4,8,768]{3,2,1,0:T(8,128)} %get-tuple-element.58) | copy-start | bytes 1179652
  301.4 1.6 copy-start.18
  301.4 1.7 copy-start.14
  303.6 4.4 copy-start.8
  305.2 16.0 %all-to-all-start.2 = ((f32[32,1,3312]{2,1,0:T(1,128)}), f32[32,1,3312]{2,1,0:T(1,128)S(1)}, u32[]{:S(2)}, u32[]{:S(2)}) async-start(f32[32,1,3312]{2,1,0:T(1,128)} %reshape.247), calls=%async_computation.2 | async-start | bytes 851968 | tf_op jit(solution)/shard_map/all_to_all | solution.py:710
  308.0 4.1 copy-start.5
  310.4 21.7 %collective-permute-start.1 = (bf16[4,2,2,48,384]{4,3,2,1,0:T(8,128)(2,1)}, bf16[4,2,2,48,384]{4,3,2,1,0:T(8,128)(2,1)}, u32[]{:S(2)}, u32[]{:S(2)}) collective-permute-start(bf16[4,2,2,48,384]{4,3,2,1,0:T(8,128)(2,1)} %get-tuple-element.78), channel_id=1, source_target_pairs={{0,1},{1,0},{2,3},{3,2},{4,5},{5,4},{6,7},{7,6},{8,9},{9,8},{10,11... | collective-permute-start | bytes 1769480 | tf_op jit(solution)/shard_map/ppermute | solution.py:742
  314.5 19.4 %collective-permute-start.7 = (bf16[4,2,2,48,384]{4,3,2,0,1:T(8,128)(2,1)}, bf16[4,2,2,48,384]{4,3,2,0,1:T(8,128)(2,1)}, u32[]{:S(2)}, u32[]{:S(2)}) collective-permute-start(bf16[4,2,2,48,384]{4,3,2,0,1:T(8,128)(2,1)} %fusion), channel_id=1, source_target_pairs={{0,4},{2,6},{4,0},{6,2},{8,12},{10,14},{12,8},{14,10},{16,20},{18,... | collective-permute-start | bytes 1769480 | tf_op jit(solution)/shard_map/ppermute | solution.py:743
  321.3 0.8 copy-start.3
  323.5 76.9 %all-to-all-start.3 = ((f32[32,128,48]{1,2,0:T(8,128)}), f32[32,128,48]{1,2,0:T(8,128)S(1)}, u32[]{:S(2)}, u32[]{:S(2)}) async-start(f32[32,128,48]{1,2,0:T(8,128)} %bitcast.28), calls=%async_computation.3 | async-start | bytes 1572864 | tf_op jit(solution)/shard_map/all_to_all | solution.py:710
  330.3 62.1 %collective-permute-start.19 = (bf16[4,2,4,48,384]{4,3,2,1,0:T(8,128)(2,1)}, bf16[4,2,4,48,384]{4,3,2,1,0:T(8,128)(2,1)}, u32[]{:S(2)}, u32[]{:S(2)}) collective-permute-start(bf16[4,2,4,48,384]{4,3,2,1,0:T(8,128)(2,1)} %get-tuple-element.70), channel_id=1, source_target_pairs={{0,4},{2,6},{4,0},{6,2},{8,12},{10,14},{12,8},{14,10},{16,20},{18,... | collective-permute-start | bytes 3538952 | tf_op jit(solution)/shard_map/ppermute | solution.py:743
  332.1 4.6 %copy-start.2 = (bf16[8,2,4,48,384]{4,3,2,1,0:T(8,128)(2,1)S(1)}, bf16[8,2,4,48,384]{4,3,2,1,0:T(8,128)(2,1)}, u32[]{:S(2)}) copy-start(bf16[8,2,4,48,384]{4,3,2,1,0:T(8,128)(2,1)} %get-tuple-element.65) | copy-start | bytes 7077892
  333.4 37.3 %copy-start.6 = (bf16[4,1,2,48,384]{4,3,2,1,0:T(8,128)(2,1)}, bf16[4,1,2,48,384]{4,3,2,1,0:T(8,128)(2,1)S(1)}, u32[]{:S(2)}) copy-start(bf16[4,1,2,48,384]{4,3,2,1,0:T(8,128)(2,1)S(1)} %get-tuple-element.85) | copy-start | bytes 884740
  333.4 37.3 %collective-permute-start.2 = (bf16[4,2,48,384]{3,2,1,0:T(8,128)(2,1)S(1)}, bf16[4,2,48,384]{3,2,1,0:T(8,128)(2,1)S(1)}, u32[]{:S(2)}, u32[]{:S(2)}) collective-permute-start(bf16[4,2,48,384]{3,2,1,0:T(8,128)(2,1)S(1)} %get-tuple-element.86), channel_id=1, source_target_pairs={{0,4},{2,6},{4,0},{6,2},{8,12},{10,14},{12,8},{14,10},{16,20},{18,... | collective-permute-start | bytes 884744 | tf_op jit(solution)/shard_map/ppermute | solution.py:743
  335.0 41.1 %copy-start.7 = (bf16[4,1,2,48,384]{4,3,2,0,1:T(8,128)(2,1)}, bf16[4,1,2,48,384]{4,3,2,0,1:T(8,128)(2,1)S(1)}, u32[]{:S(2)}) copy-start(bf16[4,1,2,48,384]{4,3,2,0,1:T(8,128)(2,1)S(1)} %get-tuple-element.87) | copy-start | bytes 884740
  335.0 39.4 %collective-permute-start.8 = (bf16[4,2,48,384]{3,2,1,0:T(8,128)(2,1)S(1)}, bf16[4,2,48,384]{3,2,1,0:T(8,128)(2,1)S(1)}, u32[]{:S(2)}, u32[]{:S(2)}) collective-permute-start(bf16[4,2,48,384]{3,2,1,0:T(8,128)(2,1)S(1)} %get-tuple-element.88), channel_id=1, source_target_pairs={{0,1},{1,0},{2,3},{3,2},{4,5},{5,4},{6,7},{7,6},{8,9},{9,8},{10,11... | collective-permute-start | bytes 884744 | tf_op jit(solution)/shard_map/ppermute | solution.py:742
  336.7 3.4 copy-start.10
  339.7 45.6 %copy-start.4 = (f32[32,1,3312]{2,0,1:T(8,128)S(1)}, f32[32,1,3312]{2,0,1:T(8,128)}, u32[]{:S(2)}) copy-start(f32[32,1,3312]{2,0,1:T(8,128)} %copy-done.3) | copy-start | bytes 1271812
  339.7 56.9 %collective-permute-start.13 = (bf16[4,2,4,48,384]{4,3,2,1,0:T(8,128)(2,1)}, bf16[4,2,4,48,384]{4,3,2,1,0:T(8,128)(2,1)}, u32[]{:S(2)}, u32[]{:S(2)}) collective-permute-start(bf16[4,2,4,48,384]{4,3,2,1,0:T(8,128)(2,1)} %get-tuple-element.72), channel_id=1, source_target_pairs={{0,1},{1,0},{2,3},{3,2},{4,5},{5,4},{6,7},{7,6},{8,9},{9,8},{10,11... | collective-permute-start | bytes 3538952 | tf_op jit(solution)/shard_map/ppermute | solution.py:742
  370.7 6.1 %copy-start.12 = (bf16[4,2,48,384]{3,2,1,0:T(8,128)(2,1)}, bf16[4,2,48,384]{3,2,1,0:T(8,128)(2,1)S(1)}, u32[]{:S(2)}) copy-start(bf16[4,2,48,384]{3,2,1,0:T(8,128)(2,1)S(1)} %collective-permute-done.2) | copy-start | bytes 884740
  370.7 7.1 %collective-permute-start.3 = (bf16[2,48,384]{2,1,0:T(8,128)(2,1)S(1)}, bf16[2,48,384]{2,1,0:T(8,128)(2,1)S(1)}, u32[]{:S(2)}, u32[]{:S(2)}) collective-permute-start(bf16[2,48,384]{2,1,0:T(8,128)(2,1)S(1)} %get-tuple-element.92), channel_id=1, source_target_pairs={{0,8},{2,10},{4,12},{6,14},{8,16},{10,18},{12,20},{14,22},{16,24},... | collective-permute-start | bytes 221192 | tf_op jit(solution)/shard_map/ppermute | solution.py:760
  372.3 10.0 %collective-permute-start.4 = (bf16[2,48,384]{2,1,0:T(8,128)(2,1)S(1)}, bf16[2,48,384]{2,1,0:T(8,128)(2,1)S(1)}, u32[]{:S(2)}, u32[]{:S(2)}) collective-permute-start(bf16[2,48,384]{2,1,0:T(8,128)(2,1)S(1)} %get-tuple-element.94), channel_id=1, source_target_pairs={{0,16},{2,18},{4,20},{6,22},{8,24},{10,26},{12,28},{14,30},{16,0},... | collective-permute-start | bytes 221192 | tf_op jit(solution)/shard_map/ppermute | solution.py:760
  374.4 3.4 copy-start.13
  374.4 10.3 %collective-permute-start.5 = (bf16[2,48,384]{2,1,0:T(8,128)(2,1)S(1)}, bf16[2,48,384]{2,1,0:T(8,128)(2,1)S(1)}, u32[]{:S(2)}, u32[]{:S(2)}) collective-permute-start(bf16[2,48,384]{2,1,0:T(8,128)(2,1)S(1)} %get-tuple-element.93), channel_id=1, source_target_pairs={{0,24},{2,26},{4,28},{6,30},{8,0},{10,2},{12,4},{14,6},{16,8},{18,... | collective-permute-start | bytes 221192 | tf_op jit(solution)/shard_map/ppermute | solution.py:760
  377.8 8.9 %collective-permute-start.10 = (bf16[2,48,384]{2,1,0:T(8,128)(2,1)}, bf16[2,48,384]{2,1,0:T(8,128)(2,1)}, u32[]{:S(2)}, u32[]{:S(2)}) collective-permute-start(bf16[2,48,384]{2,1,0:T(8,128)(2,1)} %get-tuple-element.97), channel_id=1, source_target_pairs={{0,16},{2,18},{4,20},{6,22},{8,24},{10,26},{12,28},{14,30},{16,0},... | collective-permute-start | bytes 221192 | tf_op jit(solution)/shard_map/ppermute | solution.py:760
  382.2 4.8 %collective-permute-start.11 = (bf16[2,48,384]{2,1,0:T(8,128)(2,1)}, bf16[2,48,384]{2,1,0:T(8,128)(2,1)}, u32[]{:S(2)}, u32[]{:S(2)}) collective-permute-start(bf16[2,48,384]{2,1,0:T(8,128)(2,1)} %get-tuple-element.96), channel_id=1, source_target_pairs={{0,24},{2,26},{4,28},{6,30},{8,0},{10,2},{12,4},{14,6},{16,8},{18,... | collective-permute-start | bytes 221192 | tf_op jit(solution)/shard_map/ppermute | solution.py:760
  384.7 0.6 copy-start.17
  384.7 6.5 %collective-permute-start.9 = (bf16[2,48,384]{2,1,0:T(8,128)(2,1)}, bf16[2,48,384]{2,1,0:T(8,128)(2,1)}, u32[]{:S(2)}, u32[]{:S(2)}) collective-permute-start(bf16[2,48,384]{2,1,0:T(8,128)(2,1)} %get-tuple-element.95), channel_id=1, source_target_pairs={{0,8},{2,10},{4,12},{6,14},{8,16},{10,18},{12,20},{14,22},{16,24},... | collective-permute-start | bytes 221192 | tf_op jit(solution)/shard_map/ppermute | solution.py:760
  394.8 12.3 %collective-permute-start.20 = (bf16[4,4,48,384]{3,2,1,0:T(8,128)(2,1)}, bf16[4,4,48,384]{3,2,1,0:T(8,128)(2,1)}, u32[]{:S(2)}, u32[]{:S(2)}) collective-permute-start(bf16[4,4,48,384]{3,2,1,0:T(8,128)(2,1)} %get-tuple-element.74), channel_id=1, source_target_pairs={{0,1},{1,0},{2,3},{3,2},{4,5},{5,4},{6,7},{7,6},{8,9},{9,8},{10,11... | collective-permute-start | bytes 1769480 | tf_op jit(solution)/shard_map/ppermute | solution.py:742
  398.8 1.6 copy-start.16
  398.8 1.6 copy-start.22
  398.8 1.7 copy-start.26
  398.8 8.4 %copy-start.1 = (bf16[4,1,4,48,384]{4,3,2,1,0:T(8,128)(2,1)S(1)}, bf16[4,1,4,48,384]{4,3,2,1,0:T(8,128)(2,1)}, u32[]{:S(2)}) copy-start(bf16[4,1,4,48,384]{4,3,2,1,0:T(8,128)(2,1)} %get-tuple-element.73) | copy-start | bytes 1769476
  398.8 14.3 %collective-permute-start.14 = (bf16[4,4,48,384]{3,2,1,0:T(8,128)(2,1)}, bf16[4,4,48,384]{3,2,1,0:T(8,128)(2,1)S(1)}, u32[]{:S(2)}, u32[]{:S(2)}) collective-permute-start(bf16[4,4,48,384]{3,2,1,0:T(8,128)(2,1)} %get-tuple-element.76), channel_id=1, source_target_pairs={{0,4},{2,6},{4,0},{6,2},{8,12},{10,14},{12,8},{14,10},{16,20},{18,... | collective-permute-start | bytes 1769480 | tf_op jit(solution)/shard_map/ppermute | solution.py:743
  400.4 11.8 %copy-start.24 = (s32[128]{0:T(128)S(1)}, s32[128]{0:T(128)}, u32[]{:S(2)}) copy-start(s32[128]{0:T(128)} %copy-done.23) | copy-start | bytes 1540
  408.3 8.8 %collective-permute-start.21 = (bf16[4,48,384]{2,1,0:T(8,128)(2,1)S(1)}, bf16[4,48,384]{2,1,0:T(8,128)(2,1)S(1)}, u32[]{:S(2)}, u32[]{:S(2)}) collective-permute-start(bf16[4,48,384]{2,1,0:T(8,128)(2,1)S(1)} %get-tuple-element.79), channel_id=1, source_target_pairs={{0,8},{2,10},{4,12},{6,14},{8,16},{10,18},{12,20},{14,22},{16,24},... | collective-permute-start | bytes 442376 | tf_op jit(solution)/shard_map/ppermute | solution.py:760
  408.4 14.1 %collective-permute-start.22 = (bf16[4,48,384]{2,1,0:T(8,128)(2,1)S(1)}, bf16[4,48,384]{2,1,0:T(8,128)(2,1)S(1)}, u32[]{:S(2)}, u32[]{:S(2)}) collective-permute-start(bf16[4,48,384]{2,1,0:T(8,128)(2,1)S(1)} %get-tuple-element.81), channel_id=1, source_target_pairs={{0,16},{2,18},{4,20},{6,22},{8,24},{10,26},{12,28},{14,30},{16,0},... | collective-permute-start | bytes 442376 | tf_op jit(solution)/shard_map/ppermute | solution.py:760
  409.7 12.8 %collective-permute-start.23 = (bf16[4,48,384]{2,1,0:T(8,128)(2,1)S(1)}, bf16[4,48,384]{2,1,0:T(8,128)(2,1)S(1)}, u32[]{:S(2)}, u32[]{:S(2)}) collective-permute-start(bf16[4,48,384]{2,1,0:T(8,128)(2,1)S(1)} %get-tuple-element.80), channel_id=1, source_target_pairs={{0,24},{2,26},{4,28},{6,30},{8,0},{10,2},{12,4},{14,6},{16,8},{18,... | collective-permute-start | bytes 442376 | tf_op jit(solution)/shard_map/ppermute | solution.py:760
  413.2 11.5 %collective-permute-start.15 = (bf16[4,48,384]{2,1,0:T(8,128)(2,1)S(1)}, bf16[4,48,384]{2,1,0:T(8,128)(2,1)S(1)}, u32[]{:S(2)}, u32[]{:S(2)}) collective-permute-start(bf16[4,48,384]{2,1,0:T(8,128)(2,1)S(1)} %get-tuple-element.82), channel_id=1, source_target_pairs={{0,8},{2,10},{4,12},{6,14},{8,16},{10,18},{12,20},{14,22},{16,24},... | collective-permute-start | bytes 442376 | tf_op jit(solution)/shard_map/ppermute | solution.py:760
  413.8 18.2 %collective-permute-start.16 = (bf16[4,48,384]{2,1,0:T(8,128)(2,1)S(1)}, bf16[4,48,384]{2,1,0:T(8,128)(2,1)S(1)}, u32[]{:S(2)}, u32[]{:S(2)}) collective-permute-start(bf16[4,48,384]{2,1,0:T(8,128)(2,1)S(1)} %get-tuple-element.84), channel_id=1, source_target_pairs={{0,16},{2,18},{4,20},{6,22},{8,24},{10,26},{12,28},{14,30},{16,0},... | collective-permute-start | bytes 442376 | tf_op jit(solution)/shard_map/ppermute | solution.py:760
  417.1 14.9 %collective-permute-start.17 = (bf16[4,48,384]{2,1,0:T(8,128)(2,1)S(1)}, bf16[4,48,384]{2,1,0:T(8,128)(2,1)S(1)}, u32[]{:S(2)}, u32[]{:S(2)}) collective-permute-start(bf16[4,48,384]{2,1,0:T(8,128)(2,1)S(1)} %get-tuple-element.83), channel_id=1, source_target_pairs={{0,24},{2,26},{4,28},{6,30},{8,0},{10,2},{12,4},{14,6},{16,8},{18,... | collective-permute-start | bytes 442376 | tf_op jit(solution)/shard_map/ppermute | solution.py:760
Sparse Core Ops, SparseCore 0:
  11.6 106.0 all-gather.4

commit v3 on v2

--- a/solution.py
+++ b/solution.py
@@ -17,7 +17,7 @@
 EPS = 1e-06
 NJ, NK, UR, UC = 16, 2, 48, 384
 UNITS = 12
-CHUNK = 384
+CHUNK = 768
 MIB = 1024 * 1024
 BF = jnp.bfloat16
 F32 = jnp.float32
@@ -36,7 +36,7 @@
 
 
 def cost(micros):
-    return pl.CostEstimate(flops=int(micros * 1.1e9), transcendentals=0, bytes_accessed=4 * MIB)
+    return pl.CostEstimate(flops=int(micros * 1e8), transcendentals=0, bytes_accessed=4 * MIB)
 
 
 def whole(shape):
@@ -271,13 +271,14 @@
 
 
 def attend_kernel(
-    tag_ref, conv_in, tokens, mods, w_qkv, w_proj, qkv, merged, attn, resid, second, lse,
+    tag_ref, conv_in, tokens, mods, w_qkv, w_proj, qkv, merged, attn, resid, second, lse, proj_t,
     full_qkv, full_proj, bias, mixed_t,
 ):
     @pl.when(pl.program_id(0) == 0)
     def _():
         join_rows(w_qkv, full_qkv)
         join_rows(w_proj, full_proj)
+        proj_t[...] = full_proj[...].T
         bias[...] = item_bias(tag_ref[0])
 
     qkv[0] = dot(full_qkv[...], conv_in[0], 1, 1).astype(BF)
@@ -296,7 +297,7 @@
         mixed_t[rows, :] = dot(values, probs, 1, 0).astype(BF)
         return 0
 
-    lax.fori_loop(0, H, head, 0)
+    lax.fori_loop(0, H, head, 0, unroll=6)
     merged[0] = mixed_t[...].T
     projected = dot(merged[0], full_proj[...], 1, 1)
     attn[0] = projected.astype(BF)
@@ -347,6 +348,7 @@
             group_spec(GROUP, D),
             group_spec(GROUP, D),
             group_spec(16, GROUP),
+            whole((D, D)),
         ],
         out_shape=[
             jax.ShapeDtypeStruct((4, 3 * D, GROUP), BF),
@@ -355,6 +357,7 @@
             jax.ShapeDtypeStruct((4, GROUP, D), F32),
             jax.ShapeDtypeStruct((4, GROUP, D), BF),
             jax.ShapeDtypeStruct((4, 16, GROUP), F32),
+            jax.ShapeDtypeStruct((D, D), BF),
         ],
         scratch_shapes=[
             pltpu.VMEM((3 * D, D), BF),
@@ -369,12 +372,14 @@
 
 
 def feed_kernel(
-    tag_ref, second, gradient, mods, w_expand, w_shrink, kernel,
-    shrunk, d_second, keep_expand, send_expand, keep_shrink, send_shrink, g_kernel,
-    d_shrunk, d_shrunk_t, weight, field, slope, hidden, d_field,
+    tag_ref, second, gradient, mods, w_expand, w_shrink, kernel, *rest,
 ):
+    (
+        shrunk, d_second, keep_expand, send_expand, keep_shrink, send_shrink, g_kernel,
+        d_shrunk, d_shrunk_t, expand, shrink, field, slope, hidden, d_field,
+    ) = rest[-15:]
     step = pl.program_id(0)
-    tag = tag_ref[0]
+    tag, core = tag_ref[0], tag_ref[1]
 
     @pl.when(step == 0)
     def _():
@@ -382,15 +387,20 @@
         value = gradient[...].astype(F32).reshape(4, 2, 8, 2, 8, D) * gate
         d_shrunk[...] = value.reshape(TOK, D).astype(BF)
         d_shrunk_t[...] = d_shrunk[...].T
-        shrunk[...] = jnp.zeros_like(shrunk)
-        d_second[...] = jnp.zeros_like(d_second)
-
-    join_rows(w_expand, weight)
-    shrink = w_shrink[...].reshape(D, CHUNK)
+        if len(rest) > 15:
+            shrunk[...] = rest[0][...]
+            d_second[...] = rest[1][...]
+        else:
+            shrunk[...] = jnp.zeros_like(shrunk)
+            d_second[...] = jnp.zeros_like(d_second)
+
+    join_rows(w_expand, expand)
+    for q in range(2):
+        shrink[:, q * UC : (q + 1) * UC] = w_shrink[:, 0, q].reshape(D, UC)
     left, right = edge_columns(tag)
     keep = 1.0 - tag.astype(F32)
-    field[...] = dot(second[...].reshape(TOK, D), weight[...], 1, 1).reshape(4, GROUP, CHUNK)
-    slope[...] = dot(d_shrunk[...], shrink, 1, 0).reshape(4, GROUP, CHUNK)
+    field[...] = dot(second[...].reshape(TOK, D), expand[...], 1, 1).reshape(4, GROUP, CHUNK)
+    slope[...] = dot(d_shrunk[...], shrink[...], 1, 0).reshape(4, GROUP, CHUNK)
 
     def lanes(i, _):
         cols = pl.ds(pl.multiple_of(i * 128, 128), 128)
@@ -407,7 +417,7 @@
             half = 0.5 + 0.5 * jnp.tanh(value * (GELU_A + GELU_B * square))
             out = value * half
             hidden[g, p * 16 : p * 16 + 16, cols] = out.astype(BF)
-            rate = half + out * (1.0 - half) * (2.0 * GELU_A + 6.0 * GELU_B * square)
+            rate = half + (out - out * half) * (2.0 * GELU_A + 6.0 * GELU_B * square)
             slope[g, p * 16 : p * 16 + 16, cols] = load_slope(g, p) * rate
 
         conv_rows(load, taps, left, right, keep, emit)
@@ -423,82 +433,80 @@
     lax.fori_loop(0, CHUNK // 128, lanes, 0)
     hid = hidden[...].reshape(TOK, CHUNK)
     d_fld = d_field[...].reshape(TOK, CHUNK)
-    shrunk[...] += dot(hid, shrink, 1, 1).reshape(4, GROUP, D)
-    d_second[...] += dot(d_fld, weight[...], 1, 0).reshape(4, GROUP, D)
-    core = tag_ref[1]
-    grad = dot(d_shrunk_t[...], hid, 1, 0).astype(BF).reshape(NJ // 2, 2, UR, UC)
-    own, other = jnp.where(core == 0, grad[:, 0], grad[:, 1]), jnp.where(core == 0, grad[:, 1], grad[:, 0])
-    keep_shrink[...] = own.reshape(NJ // 2, 1, 1, UR, UC)
-    send_shrink[...] = other.reshape(NJ // 2, 1, 1, UR, UC)
+    grad = dot(d_shrunk_t[...], hid, 1, 0).astype(BF)
+    for q in range(2):
+        part = grad[:, q * UC : (q + 1) * UC].reshape(NJ // 2, 2, UR, UC)
+        keep_shrink[:, 0, q] = jnp.where(core == 0, part[:, 0], part[:, 1])
+        send_shrink[:, 0, q] = jnp.where(core == 0, part[:, 1], part[:, 0])
     share_out(dot(d_fld, second[...].reshape(TOK, D), 0, 0), core, (0, 4), keep_expand, send_expand)
+    shrunk[...] += dot(hid, shrink[...], 1, 1).reshape(4, GROUP, D)
+    d_second[...] += dot(d_fld, expand[...], 1, 0).reshape(4, GROUP, D)
 
 
 def packed_half(units):
     return jax.ShapeDtypeStruct((NJ // 2, NK, units, UR, UC), BF)
 
 
-def feed(tag, second, gradient, mods, packed, kernel):
-    steps = FF // CHUNK
+def feed(part, tag, second, gradient, mods, packed, kernel, before=()):
+    half = NJ // 2
+    expand_spec = pl.BlockSpec((2, NK, 4, UR, UC), lambda c: (c, 0, 0, 0, 0))
+    shrink_spec = pl.BlockSpec((half, 1, 2, UR, UC), lambda c: (0, c, 0, 0, 0))
+    expand_shape = jax.ShapeDtypeStruct((half // 2, NK, 4, UR, UC), BF)
     return pl.pallas_call(
         feed_kernel,
-        grid=(steps,),
+        grid=(2,),
         in_specs=[
             SMEM_SPEC,
             whole((4, GROUP, D)),
             whole((4, GROUP, D)),
             whole((6, 4, 8, D)),
-            pl.BlockSpec((2, NK, 4, UR, UC), lambda c: (c, 0, 1, 0, 0)),
-            pl.BlockSpec((NJ, 1, 1, UR, UC), lambda c: (0, c // 4, 8 + c % 4, 0, 0)),
-            pl.BlockSpec((9, CHUNK), lambda c: (0, c)),
-        ],
+            pl.BlockSpec((4, NK, 4, UR, UC), lambda c: (2 * c + part, 0, 1, 0, 0)),
+            pl.BlockSpec((NJ, 1, 2, UR, UC), lambda c: (0, c, 4 + part, 0, 0)),
+            pl.BlockSpec((9, CHUNK), lambda c: (0, 2 * c + part)),
+        ]
+        + [whole((4, GROUP, D)) for _ in before],
         out_specs=[
-            pl.BlockSpec((4, GROUP, D), lambda c: (0, 0, 0)),
-            pl.BlockSpec((4, GROUP, D), lambda c: (0, 0, 0)),
-            pl.BlockSpec((1, NK, 4, UR, UC), lambda c: (c, 0, 0, 0, 0)),
-            pl.BlockSpec((1, NK, 4, UR, UC), lambda c: (c, 0, 0, 0, 0)),
-            pl.BlockSpec((NJ // 2, 1, 1, UR, UC), lambda c: (0, c // 4, c % 4, 0, 0)),
-            pl.BlockSpec((NJ // 2, 1, 1, UR, UC), lambda c: (0, c // 4, c % 4, 0, 0)),
+            whole((4, GROUP, D)),
+            whole((4, GROUP, D)),
+            expand_spec,
+            expand_spec,
+            shrink_spec,
+            shrink_spec,
             pl.BlockSpec((9, CHUNK), lambda c: (0, c)),
         ],
         out_shape=[
             jax.ShapeDtypeStruct((4, GROUP, D), F32),
             jax.ShapeDtypeStruct((4, GROUP, D), F32),
-            packed_half(4),
-            packed_half(4),
-            packed_half(4),
-            packed_half(4),
-            jax.ShapeDtypeStruct((9, FF), F32),
+            expand_shape,
+            expand_shape,
+            packed_half(2),
+            packed_half(2),
+            jax.ShapeDtypeStruct((9, FF // 2), F32),
         ],
         scratch_shapes=[
             pltpu.VMEM((TOK, D), BF),
             pltpu.VMEM((D, TOK), BF),
             pltpu.VMEM((CHUNK, D), BF),
+            pltpu.VMEM((D, CHUNK), BF),
             pltpu.VMEM((4, GROUP, CHUNK), F32),
             pltpu.VMEM((4, GROUP, CHUNK), F32),
             pltpu.VMEM((4, GROUP, CHUNK), BF),
             pltpu.VMEM((4, GROUP, CHUNK), BF),
         ],
         compiler_params=params(60),
-        cost_estimate=cost(80),
-        name="feed",
-    )(tag, second, gradient, mods, packed, packed, kernel)
+        cost_estimate=cost(38),
+        name=f"feed_{part}",
+    )(tag, second, gradient, mods, packed, packed, kernel, *before)
 
 
 def attend_back_kernel(
-    tag_ref, resid, shrunk, d_second, gradient, attn, mods, qkv, merged, conv_in, lse, w_qkv, w_proj,
-    output, d_resid, keep_a, send_a, keep_b, send_b, d_conv, sums,
-    full_qkv, full_proj, proj_t, bias, d_mixed, d_qkv, acc_qkv, acc_proj, d_attn,
+    tag_ref, resid, shrunk, d_second, gradient, attn, mods, qkv, lse, proj_t,
+    output, d_resid, d_qkv, d_attn_t, sums,
+    bias, d_mixed, d_attn,
 ):
-    step = pl.program_id(0)
-
-    @pl.when(step == 0)
+    @pl.when(pl.program_id(0) == 0)
     def _():
-        join_rows(w_qkv, full_qkv)
-        join_rows(w_proj, full_proj)
-        proj_t[...] = full_proj[...].T
         bias[...] = item_bias(tag_ref[0])
-        acc_qkv[...] = jnp.zeros_like(acc_qkv)
-        acc_proj[...] = jnp.zeros_like(acc_proj)
         sums[...] = jnp.zeros_like(sums)
 
     def rows_norm(i, _):
@@ -532,7 +540,7 @@
         return 0
 
     lax.fori_loop(0, 4, rows_norm, 0)
-    acc_proj[...] += dot(d_attn[...], merged[0], 0, 0)
+    d_attn_t[...] = d_attn[...].T
     d_mixed[...] = dot(proj_t[...], d_attn[...], 1, 1).astype(BF)
 
     def head(h, _):
@@ -553,154 +561,209 @@
         d_qkv[key_rows, :] = dot(queries, d_scores, 1, 1).astype(BF)
         return 0
 
-    lax.fori_loop(0, H, head, 0)
-    acc_qkv[...] += dot(d_qkv[...], conv_in[0], 1, 0)
-    d_conv[0] = dot(d_qkv[...], full_qkv[...], 0, 0)
-
-    @pl.when(step == pl.num_programs(0) - 1)
-    def _():
-        core = tag_ref[1]
-        share_out(acc_qkv, core, (0, 2), keep_a, send_a)
-        share_out(acc_qkv, core, (2, 1), keep_b.at[:, :, 0:1], send_b.at[:, :, 0:1])
-        share_out(acc_proj, core, (0, 1), keep_b.at[:, :, 1:2], send_b.at[:, :, 1:2])
-
-
-def attend_back(tag, resid, shrunk, d_second, gradient, attn, mods, qkv, merged, conv_in, lse, packed):
+    lax.fori_loop(0, H, head, 0, unroll=6)
+
+
+def attend_back(part, tag, resid, shrunk, d_second, gradient, attn, mods, qkv, lse, proj_t):
+    def pick_group(*shape):
+        return pl.BlockSpec((1,) + shape, lambda g: (2 * part + g,) + (0,) * len(shape))
+
     return pl.pallas_call(
         attend_back_kernel,
-        grid=(4,),
+        grid=(2,),
         in_specs=[
             SMEM_SPEC,
-            group_spec(GROUP, D),
-            group_spec(GROUP, D),
-            group_spec(GROUP, D),
-            group_spec(GROUP, D),
-            group_spec(GROUP, D),
+            pick_group(GROUP, D),
+            pick_group(GROUP, D),
+            pick_group(GROUP, D),
+            pick_group(GROUP, D),
+            pick_group(GROUP, D),
             whole((6, 4, 8, D)),
-            group_spec(3 * D, GROUP),
-            group_spec(GROUP, D),
-            group_spec(GROUP, D),
-            group_spec(16, GROUP),
-            unit_spec(3, 0),
-            unit_spec(1, 3),
+            pick_group(3 * D, GROUP),
+            pick_group(16, GROUP),
+            whole((D, D)),
         ],
         out_specs=[
             group_spec(GROUP, D),
             group_spec(GROUP, D),
-            whole((NJ // 2, NK, 2, UR, UC)),
-            whole((NJ // 2, NK, 2, UR, UC)),
-            whole((NJ // 2, NK, 2, UR, UC)),
-            whole((NJ // 2, NK, 2, UR, UC)),
-            group_spec(GROUP, D),
+            pl.BlockSpec((3 * D, GROUP), lambda g: (0, g)),
+            pl.BlockSpec((D, GROUP), lambda g: (0, g)),
             whole((4, 4, 8, D)),
         ],
         out_shape=[
-            jax.ShapeDtypeStruct((4, GROUP, D), BF),
-            jax.ShapeDtypeStruct((4, GROUP, D), F32),
-            packed_half(2),
-            packed_half(2),
-            packed_half(2),
-            packed_half(2),
-            jax.ShapeDtypeStruct((4, GROUP, D), F32),
+            jax.ShapeDtypeStruct((2, GROUP, D), BF),
+            jax.ShapeDtypeStruct((2, GROUP, D), F32),
+            jax.ShapeDtypeStruct((3 * D, 2 * GROUP), BF),
+            jax.ShapeDtypeStruct((D, 2 * GROUP), BF),
             jax.ShapeDtypeStruct((4, 4, 8, D), F32),
         ],
         scratch_shapes=[
-            pltpu.VMEM((3 * D, D), BF),
-            pltpu.VMEM((D, D), BF),
-            pltpu.VMEM((D, D), BF),
             pltpu.VMEM((GROUP, GROUP), F32),
             pltpu.VMEM((D, GROUP), BF),
-            pltpu.VMEM((3 * D, GROUP), BF),
-            pltpu.VMEM((3 * D, D), F32),
-            pltpu.VMEM((D, D), F32),
             pltpu.VMEM((GROUP, D), BF),
         ],
-        compiler_params=params(60),
-        cost_estimate=cost(49),
-        name="attend_back",
-    )(tag, resid, shrunk, d_second, gradient, attn, mods, qkv, merged, conv_in, lse, packed, packed)
+        compiler_params=params(),
+        cost_estimate=cost(16),
+        name=f"attend_back_{part}",
+    )(tag, resid, shrunk, d_second, gradient, attn, mods, qkv, lse, proj_t)
+
+
+PAIRS = 2
+ROWS = 288 * PAIRS
+
+
+def project_grads_kernel(
+    tag_ref, d_qkv0, d_qkv1, d_attn0, d_attn1, conv_in, merged, keep_a, send_a, keep_b, send_b
+):
+    core = tag_ref[1]
+
+    def against(low, high, field):
+        return dot(low[...], field[0:2].reshape(2 * GROUP, D), 1, 0) + dot(
+            high[...], field[2:4].reshape(2 * GROUP, D), 1, 0
+        )
+
+    grad = against(d_qkv0, d_qkv1, conv_in)
+    share_out(grad, core, (0, 2), keep_a, send_a)
+    share_out(grad, core, (2, 1), keep_b.at[:, :, 0:1], send_b.at[:, :, 0:1])
+    grad = against(d_attn0, d_attn1, merged)
+    share_out(grad, core, (0, 1), keep_b.at[:, :, 1:2], send_b.at[:, :, 1:2])
+
+
+def project_grads(tag, d_qkv, d_attn, conv_in, merged):
+    packed_spec = pl.BlockSpec((PAIRS, NK, 2, UR, UC), lambda i: (i, 0, 0, 0, 0))
+    tall = pl.BlockSpec((ROWS, 2 * GROUP), lambda i: (i, 0))
+    short = pl.BlockSpec((96 * PAIRS, 2 * GROUP), lambda i: (i, 0))
+    return pl.pallas_call(
+        project_grads_kernel,
+        grid=(8 // PAIRS,),
+        in_specs=[SMEM_SPEC, tall, tall, short, short, whole((4, GROUP, D)), whole((4, GROUP, D))],
+        out_specs=[packed_spec] * 4,
+        out_shape=[packed_half(2)] * 4,
+        compiler_params=params(),
+        cost_estimate=cost(8),
+        name="project_grads",
+    )(tag, *d_qkv, *d_attn, conv_in, merged)
+
+
+def conv_back_kernel(
+    tag_ref, d_qkv0, d_qkv1, w_qkv, norm, mods, kernel, d_first, g_kernel, weight, d_conv
+):
+    step = pl.program_id(0)
+
+    @pl.when(step == 0)
+    def _():
+        d_conv[...] = jnp.zeros_like(d_conv)
+
+    join_rows(w_qkv, weight)
+    d_conv[0:2] += dot(d_qkv0[...], weight[...], 0, 0).reshape(2, GROUP, D)
+    d_conv[2:4] += dot(d_qkv1[...], weight[...], 0, 0).reshape(2, GROUP, D)
+
+    @pl.when(step == pl.num_programs(0) - 1)
+    def _():
+        tag = tag_ref[0]
+        left, right = edge_columns(tag)
+        keep = 1.0 - tag.astype(F32)
+
+        def lanes(i, _):
+            cols = pl.ds(pl.multiple_of(i * 128, 128), 128)
+            taps = [jnp.broadcast_to(kernel[t : t + 1, cols], (16, 128)) for t in range(9)]
+
+            def load_grad(g, p):
+                return d_conv[g, p * 16 : p * 16 + 16, cols]
+
+            def load_field(g, p):
+                q = 2 * (p // 8)
+                shift = mods[0, q : q + 2, :, cols].reshape(16, 128)
+                scale = mods[1, q : q + 2, :, cols].reshape(16, 128)
+                return norm[g, p * 16 : p * 16 + 16, cols] * (1.0 + scale) + shift
+
+            def emit(g, p, value):
+                d_first[g, p * 16 : p * 16 + 16, cols] = value
+
+            grads = conv_back_rows(load_grad, load_field, taps, left, right, keep, emit)
+            for t in range(9):
+                g_kernel[t : t + 1, cols] = jnp.sum(grads[t], axis=0, keepdims=True)
+            return 0
+
+        lax.fori_loop(0, D // 128, lanes, 0)
+
+
+def conv_back(tag, d_qkv, packed, norm, mods, kernel):
+    tall = pl.BlockSpec((ROWS, 2 * GROUP), lambda i: (i, 0))
+    return pl.pallas_call(
+        conv_back_kernel,
+        grid=(8 // PAIRS,),
+        in_specs=[
+            SMEM_SPEC,
+            tall,
+            tall,
+            pl.BlockSpec((2 * PAIRS, NK, 3, UR, UC), lambda i: (i, 0, 0, 0, 0)),
+            whole((4, GROUP, D)),
+            whole((6, 4, 8, D)),
+            whole((9, D)),
+        ],
+        out_specs=[whole((4, GROUP, D)), whole((9, D))],
+        out_shape=[
+            jax.ShapeDtypeStruct((4, GROUP, D), F32),
+            jax.ShapeDtypeStruct((9, D), F32),
+        ],
+        scratch_shapes=[pltpu.VMEM((ROWS, D), BF), pltpu.VMEM((4, GROUP, D), F32)],
+        compiler_params=params(),
+        cost_estimate=cost(15),
+        name="conv_back",
+    )(tag, *d_qkv, packed, norm, mods, kernel)
 
 
 def finish_kernel(
-    tag_ref, d_conv, norm, factor, d_resid, output, mods, kernel,
-    block_output, input_grad, g_kernel, sums, d_first, total,
+    d_first, norm, factor, d_resid0, d_resid1, output0, output1, mods,
+    block_output, input_grad, sums, total,
 ):
-    tag = tag_ref[0]
-    left, right = edge_columns(tag)
-    keep = 1.0 - tag.astype(F32)
-
-    def lanes(i, _):
-        cols = pl.ds(pl.multiple_of(i * 128, 128), 128)
-        taps = [jnp.broadcast_to(kernel[t : t + 1, cols], (16, 128)) for t in range(9)]
-
-        def load_grad(g, p):
-            return d_conv[g, p * 16 : p * 16 + 16, cols]
-
-        def load_field(g, p):
-            q = 2 * (p // 8)
-            shift = mods[0, q : q + 2, :, cols].reshape(16, 128)
-            scale = mods[1, q : q + 2, :, cols].reshape(16, 128)
-            return norm[g, p * 16 : p * 16 + 16, cols] * (1.0 + scale) + shift
-
-        def emit(g, p, value):
-            d_first[g, p * 16 : p * 16 + 16, cols] = value
-
-        grads = conv_back_rows(load_grad, load_field, taps, left, right, keep, emit)
-        for t in range(9):
-            g_kernel[t : t + 1, cols] = jnp.sum(grads[t], axis=0, keepdims=True)
-        return 0
-
-    lax.fori_loop(0, D // 128, lanes, 0)
-    sums[...] = jnp.zeros_like(sums)
-
-    def rows_back(i, _):
-        g, part = i // 4, i % 4
-        rows = pl.ds(pl.multiple_of(part * 64, 64), 64)
-        half = part // 2
-        value = d_first[g, rows, :]
-        normal = norm[g, rows, :]
+    half = pl.program_id(0) // 2
+
+    @pl.when(pl.program_id(0) == 0)
+    def _():
+        sums[...] = jnp.zeros_like(sums)
+
+    for g in range(4):
+        base = (d_resid0, d_resid1)[g // 2]
+        value = d_first[g]
+        normal = norm[g]
         sums[0, pl.ds(2 * half, 2)] += jnp.sum(value.reshape(4, 2, 8, D), axis=0)
         sums[1, pl.ds(2 * half, 2)] += jnp.sum((value * normal).reshape(4, 2, 8, D), axis=0)
         inner = (value.reshape(4, 2, 8, D) * (1.0 + quadrant_rows(mods, 1, half))).reshape(64, D)
         mean = jnp.mean(inner, axis=-1, keepdims=True)
         along = jnp.mean(inner * normal, axis=-1, keepdims=True)
-        total[g, rows, :] = (
-            d_resid[g, rows, :] + (inner - mean - normal * along) * factor[g, rows, :]
-        )
-        return 0
-
-    lax.fori_loop(0, 16, rows_back, 0)
+        total[g] = base[g % 2] + (inner - mean - normal * along) * factor[g]
     order = ungroup_matrix()
-
-    def place(i, _):
-        rows = pl.ds(pl.multiple_of(i * 64, 64), 64)
-        target = pl.ds(pl.multiple_of(i * 256, 256), 256)
-        grouped = total[:, rows, :].reshape(256, D)
-        high = grouped.astype(BF)
-        rest = (grouped - high.astype(F32)).astype(BF)
-        input_grad[target, :] = dot(order, high, 1, 0) + dot(order, rest, 1, 0)
-        block_output[target, :] = dot(order, output[:, rows, :].reshape(256, D), 1, 0).astype(BF)
-        return 0
-
-    lax.fori_loop(0, 4, place, 0)
-
-
-def finish(tag, d_conv, norm, factor, d_resid, output, mods, kernel):
+    grouped = total[...].reshape(256, D)
+    high = grouped.astype(BF)
+    rest = (grouped - high.astype(F32)).astype(BF)
+    input_grad[...] = dot(order, high, 1, 0) + dot(order, rest, 1, 0)
+    low_half = dot(order[:, 0:128], output0[...].reshape(128, D), 1, 0)
+    high_half = dot(order[:, 128:256], output1[...].reshape(128, D), 1, 0)
+    block_output[...] = (low_half + high_half).astype(BF)
+
+
+def finish(d_first, norm, factor, d_resid, output, mods):
+    def split(groups, width):
+        return pl.BlockSpec((groups, 64, width), lambda i: (0, i, 0))
+
+    flat = pl.BlockSpec((256, D), lambda i: (i, 0))
     return pl.pallas_call(
         finish_kernel,
-        in_specs=[SMEM_SPEC] + [pl.BlockSpec(memory_space=pltpu.VMEM)] * 7,
-        out_specs=[pl.BlockSpec(memory_space=pltpu.VMEM)] * 4,
+        grid=(4,),
+        in_specs=[split(4, D), split(4, D), split(4, 1)] + [split(2, D)] * 4 + [whole((6, 4, 8, D))],
+        out_specs=[flat, flat, whole((2, 4, 8, D))],
         out_shape=[
             jax.ShapeDtypeStruct((TOK, D), BF),
             jax.ShapeDtypeStruct((TOK, D), F32),
-            jax.ShapeDtypeStruct((9, D), F32),
             jax.ShapeDtypeStruct((2, 4, 8, D), F32),
         ],
-        scratch_shapes=[pltpu.VMEM((4, GROUP, D), F32), pltpu.VMEM((4, GROUP, D), F32)],
-        compiler_params=params(60),
-        cost_estimate=cost(16),
+        scratch_shapes=[pltpu.VMEM((4, 64, D), F32)],
+        compiler_params=params(),
+        cost_estimate=cost(8),
         name="finish",
-    )(tag, d_conv, norm, factor, d_resid, output, mods, kernel)
+    )(d_first, norm, factor, *d_resid, *output, mods)
 
 
 BOTH = ("dp", "fsdp")
@@ -745,32 +808,25 @@
 
 def halve(keep, got, axis, bit):
     mine = lax.axis_index("fsdp") if bit is None else (lax.axis_index("dp") // bit) % 2
-    sent = pick(keep, 1 - mine, axis) + pick(got, 1 - mine, axis)
     kept = pick(keep, mine, axis) + pick(got, mine, axis)
-    return kept, swap(sent, bit)
-
-
-def last_sum(keep, got):
+    return kept, pick(keep, 1 - mine, axis) + pick(got, 1 - mine, axis)
+
+
+def last_sends(total):
     place = lax.axis_index("dp") // 4
-    total = (pick(keep, place, 0) + pick(got, place, 0)).astype(F32)
-    for step in range(1, 4):
-        target = (place + step) % 4
-        sent = pick(keep, target, 0) + pick(got, target, 0)
+    return [pick(total, (place + step) % 4, 0) for step in range(1, 4)]
+
+
+def last_sum(total, sends):
+    own = pick(total, lax.axis_index("dp") // 4, 0).astype(F32)
+    for step, sent in enumerate(sends, 1):
         moved = [(i, (i + 4 * step) % NJ) for i in range(NJ)]
-        total = total + lax.ppermute(sent, "dp", moved).astype(F32)
-    return total
-
-
-def scatter_packed(nd, nf, keep_a, send_a, keep_b, send_b):
-    if (nd, nf) == (NJ, NK):
-        a, b = (x.reshape((4, 2) + x.shape[1:]) for x in (keep_a, keep_b))
-        got_a, got_b = swap(send_a, 1).reshape(a.shape), swap(send_b, 1).reshape(b.shape)
-        a, got_a = halve(a, got_a, 2, None)
-        b, got_b = halve(b, got_b, 1, 2)
-        a, got_a = halve(a, got_a, 1, 2)
-        b, got_b = halve(b, got_b, 1, None)
-        return last_sum(a, got_a), last_sum(b, got_b)
-    return jnp.stack([keep_a, send_a], axis=1), jnp.stack([keep_b, send_b], axis=1)
+        own = own + lax.ppermute(sent, "dp", moved).astype(F32)
+    return own
+
+
+def tie(value, *others):
+    return lax.optimization_barrier((value,) + others)
 
 
 def own_shard(nd, nf, kind, units):
@@ -778,7 +834,6 @@
         if kind == "shrink":
             return units.transpose(1, 0, 2).reshape(UR, 4 * UC).T
         return units.reshape(-1, UC).T
-    units = units.reshape((NJ,) + units.shape[2:])
     if kind == "shrink":
         weight = units.transpose(0, 3, 1, 2, 4).reshape(NJ * UR, -1)
     else:
@@ -786,6 +841,10 @@
     columns = lax.psum_scatter(weight, "dp", scatter_dimension=0, tiled=True)
     piece = lax.psum_scatter(columns, "fsdp", scatter_dimension=1, tiled=True)
     return piece.astype(F32).T
+
+
+def both_cores(keep, send):
+    return jnp.stack([keep, send], axis=1).reshape((-1,) + keep.shape[1:])
 
 
 def condition(nd, nf, timesteps, classes, step_table, class_table, attn_kernel, ffn_kernel):
@@ -836,19 +895,98 @@
     mods = jnp.broadcast_to(chosen.reshape(4, 6, 1, D).transpose(1, 0, 2, 3), (6, 4, 8, D))
 
     conv_in = first_conv(size_tags, norm, mods, attn_full)
-    qkv, merged, attn, resid, second, lse = attend(size_tags, conv_in, tokens, mods, packed)
-    shrunk, d_second, *grads, g_ffn = feed(where, second, gradient, mods, packed, ffn_full)
-    expand, shrink = scatter_packed(nd, nf, *grads)
-    output, d_resid, *grads, d_conv, later = attend_back(
-        where, resid, shrunk, d_second, gradient, attn, mods, qkv, merged, conv_in, lse, packed
-    )
-    first, rest = scatter_packed(nd, nf, *grads)
-    units = rest.ndim - 3
-    proj = lax.slice_in_dim(rest, 1, 2, axis=units)
-    joined = jnp.concatenate([first, lax.slice_in_dim(rest, 0, 1, axis=units)], axis=units)
-    block_output, input_grad, g_attn, early = finish(
-        size_tags, d_conv, norm, factor, d_resid, output, mods, attn_full
-    )
+    qkv, merged, attn, resid, second, lse, proj_t = attend(
+        size_tags, conv_in, tokens, mods, packed
+    )
+    common = (second, gradient, mods, packed, ffn_full)
+    square = (nd, nf) == (NJ, NK)
+    shrunk, d_second, keep_e0, send_e0, keep_s0, send_s0, g_ffn0 = feed(0, where, *common)
+    if square:
+        got_e0, got_s0 = swap(send_e0, 1), swap(send_s0, 1)
+    shrunk, d_second, keep_e1, send_e1, keep_s1, send_s1, g_ffn1 = feed(
+        1, where, *common, (shrunk, d_second)
+    )
+    g_ffn = jnp.stack([g_ffn0.reshape(9, 2, -1), g_ffn1.reshape(9, 2, -1)], axis=2).reshape(9, FF)
+    if square:
+        got_e1, got_s1 = swap(send_e1, 1), swap(send_s1, 1)
+
+        def grid(value, outer):
+            return value.reshape((outer, 2) + value.shape[1:])
+
+        keep_e0, out_e0 = halve(grid(keep_e0, 2), grid(got_e0, 2), 2, None)
+        keep_s0, out_s0 = halve(grid(keep_s0, 4), grid(got_s0, 4), 1, 2)
+        d_second, out_e0, out_s0 = tie(d_second, out_e0, out_s0)
+        got_e0, got_s0 = swap(out_e0, None), swap(out_s0, 2)
+    back = (gradient, attn, mods, qkv, lse)
+    output0, d_resid0, d_qkv0, d_attn0, later0 = attend_back(
+        0, where, resid, shrunk, d_second, *back, proj_t
+    )
+    if square:
+        d_qkv0, got_e0, got_s0, got_e1, got_s1 = tie(d_qkv0, got_e0, got_s0, got_e1, got_s1)
+        keep_e0, out_e0 = halve(keep_e0, got_e0, 1, 2)
+        keep_s0, out_s0 = halve(keep_s0, got_s0, 1, None)
+        keep_e1, out_e1 = halve(grid(keep_e1, 2), grid(got_e1, 2), 2, None)
+        keep_s1, out_s1 = halve(grid(keep_s1, 4), grid(got_s1, 4), 1, 2)
+        d_second, d_qkv0, out_e0, out_s0, out_e1, out_s1 = tie(
+            d_second, d_qkv0, out_e0, out_s0, out_e1, out_s1
+        )
+        got_e0, got_s0 = swap(out_e0, 2), swap(out_s0, None)
+        got_e1, got_s1 = swap(out_e1, None), swap(out_s1, 2)
+    output1, d_resid1, d_qkv1, d_attn1, later1 = attend_back(
+        1, where, resid, shrunk, d_second, *back, proj_t
+    )
+    d_qkv = (d_qkv0, d_qkv1)
+    keep_a, send_a, keep_b, send_b = project_grads(
+        where, d_qkv, (d_attn0, d_attn1), conv_in, merged
+    )
+    if square:
+        got_a, got_b = swap(send_a, 1), swap(send_b, 1)
+        keep_a, got_e1, got_s1 = tie(keep_a, got_e1, got_s1)
+        keep_e1, out_e1 = halve(keep_e1, got_e1, 1, 2)
+        keep_s1, out_s1 = halve(keep_s1, got_s1, 1, None)
+        norm, out_e1, out_s1 = tie(norm, out_e1, out_s1)
+        got_e1, got_s1 = swap(out_e1, 2), swap(out_s1, None)
+    d_first, g_attn = conv_back(where, d_qkv, packed, norm, mods, attn_full)
+    if square:
+        d_first, got_e1, got_s1, got_a, got_b = tie(d_first, got_e1, got_s1, got_a, got_b)
+        expand = jnp.stack([keep_e0 + got_e0, keep_e1 + got_e1], axis=1).reshape(4, 4, UR, UC)
+        total = jnp.concatenate([expand, keep_s0 + got_s0, keep_s1 + got_s1], axis=1)
+        sends = last_sends(total)
+        keep_a, out_a = halve(grid(keep_a, 4), grid(got_a, 4), 2, None)
+        keep_b, out_b = halve(grid(keep_b, 4), grid(got_b, 4), 1, 2)
+        d_first, out_a, out_b, *sends = tie(d_first, out_a, out_b, *sends)
+        feeding = last_sum(total, sends)
+        got_a, got_b = swap(out_a, None), swap(out_b, 2)
+    block_output, input_grad, early = finish(
+        d_first, norm, factor, (d_resid0, d_resid1), (output0, output1), mods
+    )
+    later = later0 + later1
+    if square:
+        keep_a, out_a = halve(keep_a, got_a, 1, 2)
+        keep_b, out_b = halve(keep_b, got_b, 1, None)
+        got_a, got_b = swap(out_a, 2), swap(out_b, None)
+        total = jnp.concatenate([keep_a + got_a, keep_b + got_b], axis=1)
+        packed_grads = (last_sum(total, last_sends(total)), feeding)
+        packed_grads = jnp.concatenate(packed_grads, axis=0)
+        cuts = [packed_grads[i:j] for i, j in ((0, 3), (3, 4), (4, 8), (8, 12))]
+    else:
+        first, rest = both_cores(keep_a, send_a), both_cores(keep_b, send_b)
+        expand = jnp.stack(
+            [both_cores(k, s).reshape((2, 4, NK, 4, UR, UC)) for k, s in
+             ((keep_e0, send_e0), (keep_e1, send_e1))],
+            axis=1,
+        ).reshape(NJ, NK, 4, UR, UC)
+        shrink = [both_cores(keep_s0, send_s0), both_cores(keep_s1, send_s1)]
+        cuts = [
+            jnp.concatenate([first, rest[:, :, :1]], axis=2),
+            rest[:, :, 1:],
+            expand,
+            jnp.concatenate(shrink, axis=2),
+        ]
+    shards = [
+        own_shard(nd, nf, kind, cut)
+        for kind, cut in zip(("qkv", "proj", "expand", "shrink"), cuts)
+    ]
     rows = jnp.concatenate([early, later], axis=0).sum(axis=2)
     rows = rows.transpose(1, 0, 2).reshape(4, 6 * D)
     alone = jnp.concatenate([rows.sum(axis=0, keepdims=True), jnp.zeros((3, 6 * D), F32)])
@@ -889,11 +1027,11 @@
         table_grad(class_hot),
         modulation_grad,
         filters[:, :cut],
-        own_shard(nd, nf, "qkv", joined),
-        own_shard(nd, nf, "proj", proj),
-        own_shard(nd, nf, "expand", expand),
+        shards[0],
+        shards[1],
+        shards[2],
         filters[:, cut:],
-        own_shard(nd, nf, "shrink", shrink),
+        shards[3],
     )
 
 

time: 441 us -> 421 us (0.955); the launches traced: 440 us -> 413 us
  waiting for transfers between devices: 104 us -> 80.5 us
  Pallas kernels: 195 us -> 189 us
    add x8 -> x6, other arithmetic: 17.4 us -> 4.83 us  [halve(): kept = pick(keep, mine, axis) + pick(got, mine, axis)]
    add x7 -> x19, other arithmetic: 4.82 us -> 16.7 us  [the longest x12 10.7 us: halve(): return (kept, pick(keep, 1 - mine, axis) + pick(got, 1 - mine, axis))]
    ppermute x12 -> x6, starting transfers between devices: 19.9 us -> 10 us  [last_sum(): own = own + lax.ppermute(sent, 'dp', moved).astype(F32)]
    ppermute x12 -> x6, waiting for transfers between devices: 18.7 us -> 9.14 us  [last_sum(): own = own + lax.ppermute(sent, 'dp', moved).astype(F32)]
    pallas_call x1, Pallas kernels: 37.9 us -> 31.9 us  [attend(): pl.pallas_call(attend_kernel, grid=(4,), in_specs=[SMEM_SPEC, group_spec(...]
    ppermute x8 -> x12, waiting for transfers between devices: 29.7 us -> 24.3 us  [swap(): return lax.ppermute(value, 'dp', [(i, i ^ bit) for i in range(NJ)])]
    all_to_all x4, waiting for transfers between devices: 12.5 us -> 7.43 us  [exchange(): return lax.all_to_all(pieces, BOTH, 0, 0, tiled=True)]
    ppermute x8 -> x12, starting transfers between devices: 5.58 us -> 10.3 us  [swap(): return lax.ppermute(value, 'dp', [(i, i ^ bit) for i in range(NJ)])]
  transfers between devices with their start and end apart: 29 -> 29, of which waited for: 13 -> 8; matrix products, arithmetic and copies ran while one was open for 9% -> 8% of each run, Pallas kernels for 18% -> 29%
where the time goes in v3:
time: 421 us; the launch traced here: 413 us
  Pallas kernels  189 us (45%)
  waiting for transfers between devices  80.5 us (19%)
  starting transfers between devices  43.2 us (10%)
  blocking collectives  32.3 us (8%)
  other arithmetic  29 us (7%)
  local copies, waits for them, and re-layouts  19.1 us (5%)
  between operations  15.9 us (4%)
    pallas_call x2, Pallas kernels, feed(): pl.pallas_call(feed_kernel, grid=(2,), in_specs=[SMEM_SPEC, whole((4, GRO...  77.4 us
    all_gather x1, waiting for transfers between devices, gather_packed(): rows = lax.all_gather(pack_shards(qkv, proj, expand, shrink), BOTH)  38.5 us
    pallas_call x2, Pallas kernels, attend_back(): pl.pallas_call(attend_back_kernel, grid=(2,), in_specs=[SMEM_SPEC, pick_g...  34.3 us
    pallas_call x1, Pallas kernels, attend(): pl.pallas_call(attend_kernel, grid=(4,), in_specs=[SMEM_SPEC, group_spec(...  31.9 us
    ppermute x12, waiting for transfers between devices, swap(): return lax.ppermute(value, 'dp', [(i, i ^ bit) for i in range(NJ)])  24.3 us
    all_gather x1, blocking collectives, condition(): sent = lax.all_gather(jnp.concatenate([act, filters], axis=0), 'dp')  23.7 us
    all_to_all x4, starting transfers between devices, exchange(): return lax.all_to_all(pieces, BOTH, 0, 0, tiled=True)  16.7 us
    pallas_call x1, Pallas kernels, conv_back(): pl.pallas_call(conv_back_kernel, grid=(8 // PAIRS,), in_specs=[SMEM_SPEC,...  15.2 us
  transfers between devices with their start and end apart: 29, of which 8 were waited for; matrix products, arithmetic and copies ran while one was open for 8% of the time, Pallas kernels for 29%

profile of v3, /device:TPU:0, one launch (start us, length us, event | category | flops | bytes accessed | tf_op | source)
XLA Modules:
  0.0 413.2 jit_solution(7244988024792904704)
XLA Ops:
  7.3 1.0 reshape.224
  8.3 1.8 pad_maximum_fusion.2
  10.8 7.3 %all-to-all-start = ((s32[32,1,8]{2,1,0:T(1,128)}), s32[32,1,8]{2,1,0:T(1,128)S(1)}, u32[]{:S(2)}, u32[]{:S(2)}) async-start(s32[32,1,8]{2,1,0:T(1,128)} %broadcast_in_dim.45), calls=%async_computation | async-start | bytes 32768 | tf_op jit(solution)/shard_map/all_to_all | solution.py:773
  19.5 6.1 %prepare.1 = (bf16[4,256,768]{2,1,0:T(8,128)(2,1)}, bf16[4,256,768]{2,1,0:T(8,128)(2,1)}, f32[4,256,768]{2,1,0:T(8,128)}, f32[4,256,1]{2,1,0:T(8,128)}) custom-call(bf16[1024,768]{1,0:T(8,128)(2,1)} %latents.1, bf16[1024,768]{1,0:T(8,128)(2,1)} %cotangent.1), custom_call_target="tpu_custom_call" | custom-call | flops 600000000 | bytes 4194304 | tf_op jit(solution)/shard_map/prepare/pallas_call | solution.py:88
  26.6 8.6 %psum.7 = f32[128,48]{0,1:T(8,128)S(1)} all-reduce(f32[128,48]{0,1:T(8,128)S(1)} %convolution_add_fusion), channel_id=1, replica_groups=mesh['dp'=16,'fsdp'=2] {'fsdp'}, use_global_device_ids=true, to_apply=%region_0.1 | all-reduce | flops 6144 | bytes 49152 | tf_op jit(solution)/shard_map/psum | solution.py:861
  35.2 23.7 %all-gather.2 = bf16[16,173,48]{1,2,0:T(8,128)(2,1)S(1)} all-gather(bf16[1,173,48]{1,2,0:T(8,128)(2,1)S(1)} %maximum_bitcast_fusion.1), channel_id=2, replica_groups=mesh['dp'=16,'fsdp'=2] {'dp'}, dimensions={0}, use_global_device_ids=true | all-gather | bytes 282336 | tf_op jit(solution)/shard_map/all_gather | solution.py:865
  60.6 2.6 all-to-all-start.1
  65.4 7.4 %all-to-all-done.1 = f32[32,4,288]{2,1,0:T(4,128)S(1)} async-done(((f32[32,4,288]{2,1,0:T(4,128)}), f32[32,4,288]{2,1,0:T(4,128)S(1)}, u32[]{:S(2)}, u32[]{:S(2)}) %all-to-all-start.1) | async-done | bytes 147488 | tf_op jit(solution)/shard_map/all_to_all | solution.py:773
  73.2 0.9 broadcast_in_dim.49.mods
  74.1 6.1 %first_conv.1.conv_in = bf16[4,256,768]{2,1,0:T(8,128)(2,1)} custom-call(s32[1]{0:T(128)S(6)} %copy.189.tag_ref, f32[4,256,768]{2,1,0:T(8,128)} %get-tuple-element.127.norm, f32[6,4,8,768]{3,2,1,0:T(8,128)} %broadcast_in_dim.49.mods, f32[9,768]{1,0:T(8,128)} %reshape.223.kernel), custom_call_target="tpu_custom_call" | custom-call | flops 600000000 | bytes 4194304 | tf_op jit(solution)/shard_map/first_conv/pallas_call | solution.py:224
  80.2 38.5 %all-gather.5.cloned.1.call-done = bf16[18432,384]{1,0:T(8,128)(2,1)} async-done(((bf16[576,384]{1,0:T(8,128)(2,1)}), bf16[18432,384]{1,0:T(8,128)(2,1)}) %all-gather.5.cloned.1.call-update) | async-done | bytes 14155792 | tf_op jit(solution)/shard_map/all_gather | solution.py:783
  118.7 31.9 %attend.1 = (bf16[4,2304,256]{2,1,0:T(8,128)(2,1)}, bf16[4,256,768]{2,1,0:T(8,128)(2,1)}, bf16[4,256,768]{2,1,0:T(8,128)(2,1)}, f32[4,256,768]{2,1,0:T(8,128)}, ...) custom-call(s32[1]{0:T(128)S(6)} %copy.189.tag_ref, ...), custom_call_target="tpu_custom_call" | custom-call | flops 3800000000 | bytes 4194304 | tf_op jit(solution)/shard_map/attend/pallas_call | solution.py:333
  150.6 37.7 %feed_0.1 = (f32[4,256,768]{2,1,0:T(8,128)}, f32[4,256,768]{2,1,0:T(8,128)}, bf16[4,2,4,48,384]{4,3,2,1,0:T(8,128)(2,1)}, bf16[4,2,4,48,384]{4,3,2,1,0:T(8,128)(...) custom-call(s32[2]{0:T(128)} %pad_add_fusion.tag_ref, ...), custom_call_target="tpu_custom_call" | custom-call | flops 3800000000 | bytes 4194304 | tf_op jit(solution)/shard_map/feed_0/pallas_call | solution.py:455
  188.9 39.7 %feed_1.1 = (f32[4,256,768]{2,1,0:T(8,128)}, f32[4,256,768]{2,1,0:T(8,128)}, bf16[4,2,4,48,384]{4,3,2,1,0:T(8,128)(2,1)}, bf16[4,2,4,48,384]{4,3,2,1,0:T(8,128)(...) custom-call(s32[2]{0:T(128)} %pad_add_fusion.tag_ref, ...), custom_call_target="tpu_custom_call" | custom-call | flops 3800000000 | bytes 4194304 | tf_op jit(solution)/shard_map/feed_1/pallas_call | solution.py:455
  229.4 1.1 copy-done.3
  230.5 1.4 dynamic-slice_add_fusion.5
  232.1 1.5 collective-permute-start.2
  234.2 17.1 %attend_back_0.1 = (bf16[2,256,768]{2,1,0:T(8,128)(2,1)}, f32[2,256,768]{2,1,0:T(8,128)}, bf16[2304,512]{1,0:T(8,128)(2,1)}, bf16[768,512]{1,0:T(8,128)(2,1)}, f32[4,4,8,768]{3,2,1,0:T(8,128)}) custom-call(s32[2]{0:T(128)} %pad_add_fusion.tag_ref, f32[4,256,768]{2,1,0:T(8,128)} %get-tuple-element.98.resid, f32[4,256,768]{2,1,0:T(8,128)} %get-tuple-element.99.shrunk, ...), custom_call_target="tpu_custom_call" | custom-call | flops 1600000000 | bytes 4194304 | tf_op jit(solution)/shard_map/attend_back_0/pallas_call | solution.py:571
  253.4 0.9 fusion.3
  255.1 1.4 collective-permute-start.12
  257.1 1.5 collective-permute-start.7
  258.6 17.3 %attend_back_1.1 = (bf16[2,256,768]{2,1,0:T(8,128)(2,1)}, f32[2,256,768]{2,1,0:T(8,128)}, bf16[2304,512]{1,0:T(8,128)(2,1)}, bf16[768,512]{1,0:T(8,128)(2,1)}, f32[4,4,8,768]{3,2,1,0:T(8,128)}) custom-call(s32[2]{0:T(128)} %pad_add_fusion.tag_ref, f32[4,256,768]{2,1,0:T(8,128)} %get-tuple-element.98.resid, f32[4,256,768]{2,1,0:T(8,128)} %get-tuple-element.99.shrunk, ...), custom_call_target="tpu_custom_call" | custom-call | flops 1600000000 | bytes 4194304 | tf_op jit(solution)/shard_map/attend_back_1/pallas_call | solution.py:571
  275.9 9.7 %project_grads.1 = (bf16[8,2,2,48,384]{4,3,2,1,0:T(8,128)(2,1)}, bf16[8,2,2,48,384]{4,3,2,1,0:T(8,128)(2,1)}, bf16[8,2,2,48,384]{4,3,2,1,0:T(8,128)(2,1)}, bf16[8,2,2,48,384]{4,3,2,1,0:T(8,128)(2,1)}) custom-call(s32[2]{0:T(128)} %pad_add_fusion.tag_ref, bf16[2304,512]{1,0:T(8,128)(2,1)} %get-tuple-element.116.d_qkv0, ...), custom_call_target="tpu_custom_call" | custom-call | flops 800000000 | bytes 4194304 | tf_op jit(solution)/shard_map/project_grads/pallas_call | solution.py:636
  286.6 1.2 add.375
  288.4 1.8 fusion.20
  290.2 1.8 fusion.21
  292.0 1.7 fusion.22
  293.7 1.4 collective-permute-start.8
  295.7 1.1 collective-permute-done.13
  296.9 15.2 %conv_back.1 = (f32[4,256,768]{2,1,0:T(8,128)}, f32[9,768]{1,0:T(8,128)}) custom-call(s32[2]{0:T(128)} %pad_add_fusion.tag_ref, bf16[2304,512]{1,0:T(8,128)(2,1)} %get-tuple-element.116.d_qkv0, bf16[2304,512]{1,0:T(8,128)(2,1)} %get-tuple-element.118.d_qkv1, bf16[16,2,12,48,384]{4,3,2,1,0:T(8,128)(2,1)} %bitcast.202, ...), custom_call_target="tpu_custom_call" | custom-call | flops 1500000000 | bytes 4194304 | tf_op jit(solution)/shard_map/conv_back/pallas_call | solution.py:693
  313.4 1.2 fusion.19
  314.6 1.2 bitcast_add_fusion.6
  316.0 1.4 dynamic-slice_add_fusion
  317.5 0.9 fusion
  318.9 1.4 dynamic-slice_add_fusion.1
  320.4 0.9 fusion.1
  321.5 1.0 dynamic-slice_bitcast_fusion
  323.0 1.4 collective-permute-start.22
  324.4 2.4 collective-permute-start.23
  326.8 8.6 %finish.1 = (bf16[1024,768]{1,0:T(8,128)(2,1)}, f32[1024,768]{1,0:T(8,128)}, f32[2,4,8,768]{3,2,1,0:T(8,128)}) custom-call(f32[4,256,768]{2,1,0:T(8,128)} %get-tuple-element.142.d_first, f32[4,256,768]{2,1,0:T(8,128)} %get-tuple-element.127.norm, f32[4,256,1]{2,1,0:T(8,128)} %get-tuple-element.143.factor, f32[2,256,768]{2,1,0:T(8,128)} %get-tuple-element.144.d_resid0, ...), custom_call_target="tpu_custom_call" | custom-call | flops 800000000 | bytes 4194304 | tf_op jit(solution)/shard_map/finish/pallas_call | solution.py:752
  335.4 1.1 maximum_reduce_fusion
  337.1 1.4 reshape.247
  338.5 2.7 all-to-all-start.2
  341.2 1.8 collective-permute-start.16
  343.0 1.5 collective-permute-start.14
  344.5 1.0 collective-permute-done.22
  345.6 1.3 fusion.7
  348.3 13.1 %collective-permute-done.16 = bf16[4,2,2,48,384]{4,3,2,0,1:T(8,128)(2,1)} collective-permute-done((bf16[4,2,2,48,384]{4,3,2,0,1:T(8,128)(2,1)}, bf16[4,2,2,48,384]{4,3,2,0,1:T(8,128)(2,1)}, u32[]{:S(2)}, u32[]{:S(2)}) %collective-permute-start.16) | collective-permute-done | bytes 589856 | tf_op jit(solution)/shard_map/ppermute | solution.py:806
  361.4 1.7 fusion.17
  363.1 1.5 collective-permute-start.17
  365.1 0.9 broadcast_in_dim.54
  366.1 4.1 all-to-all-start.3
  370.2 1.0 fusion.18
  371.2 1.8 collective-permute-start.15
  374.4 1.1 bitcast_add_fusion.1
  375.6 11.2 %collective-permute-done.15 = bf16[4,2,48,384]{3,2,1,0:T(8,128)(2,1)S(1)} collective-permute-done((bf16[4,2,48,384]{3,2,1,0:T(8,128)(2,1)S(1)}, bf16[4,2,48,384]{3,2,1,0:T(8,128)(2,1)S(1)}, u32[]{:S(2)}, u32[]{:S(2)}) %collective-permute-start.15) | collective-permute-done | bytes 294944 | tf_op jit(solution)/shard_map/ppermute | solution.py:806
  386.7 1.0 bitcast_add_fusion.4
  387.8 2.1 collective-permute-start.18
  389.9 2.8 collective-permute-start.19
  393.5 1.0 fusion.41
  394.5 2.4 collective-permute-done.18
  396.9 5.7 %collective-permute-done.19 = bf16[4,48,384]{2,1,0:T(8,128)(2,1)S(1)} collective-permute-done((bf16[4,48,384]{2,1,0:T(8,128)(2,1)S(1)}, bf16[4,48,384]{2,1,0:T(8,128)(2,1)S(1)}, u32[]{:S(2)}, u32[]{:S(2)}) %collective-permute-start.19) | collective-permute-done | bytes 147488 | tf_op jit(solution)/shard_map/ppermute | solution.py:824
  404.1 0.9 fusion.8
  405.0 0.9 fusion.11
  (154 shorter events, 23.4 us)
Async XLA Ops:
  7.2 52.4 %copy-start = (bf16[384,288]{0,1:T(8,128)(2,1)S(1)}, bf16[384,288]{0,1:T(8,128)(2,1)}, u32[]{:S(2)}) copy-start(bf16[384,288]{0,1:T(8,128)(2,1)} %param.20) | copy-start | bytes 663556
  7.2 2.9 copy-start.20
  7.2 2.9 copy-start.19
  7.2 12.2 %copy-start.16 = (bf16[9,48]{1,0:T(8,128)(2,1)S(1)}, bf16[9,48]{1,0:T(8,128)(2,1)}, u32[]{:S(2)}) copy-start(bf16[9,48]{1,0:T(8,128)(2,1)} %param.21) | copy-start | bytes 2596
  7.2 12.2 %copy-start.15 = (bf16[9,192]{1,0:T(8,128)(2,1)S(1)}, bf16[9,192]{1,0:T(8,128)(2,1)}, u32[]{:S(2)}) copy-start(bf16[9,192]{1,0:T(8,128)(2,1)} %param.25) | copy-start | bytes 10372
  7.2 111.5 %all-gather.5.cloned.1.call-start = ((), (), s32[]{:S(2)}) async-start(), calls=%async_computation.4 | async-start | bytes 14598144 | tf_op jit(solution)/shard_map/all_gather | solution.py:783
  10.8 14.9 %all-to-all-start = ((s32[32,1,8]{2,1,0:T(1,128)}), s32[32,1,8]{2,1,0:T(1,128)S(1)}, u32[]{:S(2)}, u32[]{:S(2)}) async-start(s32[32,1,8]{2,1,0:T(1,128)} %broadcast_in_dim.45), calls=%async_computation | async-start | bytes 32768 | tf_op jit(solution)/shard_map/all_to_all | solution.py:773
  19.5 6.6 %copy-start.17 = (bf16[500,48]{0,1:T(8,128)(2,1)S(1)}, bf16[500,48]{0,1:T(8,128)(2,1)}, u32[]{:S(2)}) copy-start(bf16[500,48]{0,1:T(8,128)(2,1)} %param.18) | copy-start | bytes 144004
  19.5 6.8 %copy-start.18 = (bf16[500,48]{0,1:T(8,128)(2,1)S(1)}, bf16[500,48]{0,1:T(8,128)(2,1)}, u32[]{:S(2)}) copy-start(bf16[500,48]{0,1:T(8,128)(2,1)} %param.19) | copy-start | bytes 144004
  58.9 0.7 copy-start.8
  60.6 12.2 %all-to-all-start.1 = ((f32[32,4,288]{2,1,0:T(4,128)}), f32[32,4,288]{2,1,0:T(4,128)S(1)}, u32[]{:S(2)}, u32[]{:S(2)}) async-start(f32[32,4,288]{2,1,0:T(4,128)} %reshape.220), calls=%async_computation.1 | async-start | bytes 393216 | tf_op jit(solution)/shard_map/all_to_all | solution.py:773
  188.3 40.9 %collective-permute-start.1 = (bf16[8,2,2,48,384]{4,3,2,1,0:T(8,128)(2,1)}, bf16[8,2,2,48,384]{4,3,2,1,0:T(8,128)(2,1)S(1)}, u32[]{:S(2)}, u32[]{:S(2)}) collective-permute-start(bf16[8,2,2,48,384]{4,3,2,1,0:T(8,128)(2,1)} %get-tuple-element.96), channel_id=1, source_target_pairs={{0,2},{2,0},{4,6},{6,4},{8,10},{10,8},{12,14},{14,12},{16,18},{18,... | collective-permute-start | bytes 3538952 | tf_op jit(solution)/shard_map/ppermute | solution.py:806
  188.7 40.8 %collective-permute-start = (bf16[4,2,4,48,384]{4,3,2,1,0:T(8,128)(2,1)}, bf16[4,2,4,48,384]{4,3,2,1,0:T(8,128)(2,1)}, u32[]{:S(2)}, u32[]{:S(2)}) collective-permute-start(bf16[4,2,4,48,384]{4,3,2,1,0:T(8,128)(2,1)} %get-tuple-element.94), channel_id=1, source_target_pairs={{0,2},{2,0},{4,6},{6,4},{8,10},{10,8},{12,14},{14,12},{16,18},{18,... | collective-permute-start | bytes 3538952 | tf_op jit(solution)/shard_map/ppermute | solution.py:806
  188.9 40.3 %copy-start.4 = (bf16[8,2,2,48,384]{4,3,2,1,0:T(8,128)(2,1)S(1)}, bf16[8,2,2,48,384]{4,3,2,1,0:T(8,128)(2,1)}, u32[]{:S(2)}) copy-start(bf16[8,2,2,48,384]{4,3,2,1,0:T(8,128)(2,1)} %get-tuple-element.95) | copy-start | bytes 3538948
  228.7 22.6 %collective-permute-start.4 = (bf16[4,2,4,48,384]{4,3,2,1,0:T(8,128)(2,1)}, bf16[4,2,4,48,384]{4,3,2,1,0:T(8,128)(2,1)S(1)}, u32[]{:S(2)}, u32[]{:S(2)}) collective-permute-start(bf16[4,2,4,48,384]{4,3,2,1,0:T(8,128)(2,1)} %get-tuple-element.107), channel_id=1, source_target_pairs={{0,2},{2,0},{4,6},{6,4},{8,10},{10,8},{12,14},{14,12},{16,18},{18,... | collective-permute-start | bytes 3538952 | tf_op jit(solution)/shard_map/ppermute | solution.py:806
  229.0 22.3 %collective-permute-start.5 = (bf16[8,2,2,48,384]{4,3,2,1,0:T(8,128)(2,1)}, bf16[8,2,2,48,384]{4,3,2,1,0:T(8,128)(2,1)S(1)}, u32[]{:S(2)}, u32[]{:S(2)}) collective-permute-start(bf16[8,2,2,48,384]{4,3,2,1,0:T(8,128)(2,1)} %get-tuple-element.108), channel_id=1, source_target_pairs={{0,2},{2,0},{4,6},{6,4},{8,10},{10,8},{12,14},{14,12},{16,18},{18,... | collective-permute-start | bytes 3538952 | tf_op jit(solution)/shard_map/ppermute | solution.py:806
  229.2 1.3 copy-start.3
  232.1 19.2 %collective-permute-start.2 = (bf16[2,2,4,48,384]{4,3,2,0,1:T(8,128)(2,1)S(1)}, bf16[2,2,4,48,384]{4,3,2,0,1:T(8,128)(2,1)S(1)}, u32[]{:S(2)}, u32[]{:S(2)}) collective-permute-start(bf16[2,2,4,48,384]{4,3,2,0,1:T(8,128)(2,1)S(1)} %fusion.5), channel_id=1, source_target_pairs={{0,1},{1,0},{2,3},{3,2},{4,5},{5,4},{6,7},{7,6},{8,9},{9,8},{10,11... | collective-permute-start | bytes 1769480 | tf_op jit(solution)/shard_map/ppermute | solution.py:805
  233.6 17.7 %collective-permute-start.3 = (bf16[4,2,2,48,384]{4,3,2,0,1:T(8,128)(2,1)S(1)}, bf16[4,2,2,48,384]{4,3,2,0,1:T(8,128)(2,1)S(1)}, u32[]{:S(2)}, u32[]{:S(2)}) collective-permute-start(bf16[4,2,2,48,384]{4,3,2,0,1:T(8,128)(2,1)S(1)} %fusion.4), channel_id=1, source_target_pairs={{0,4},{2,6},{4,0},{6,2},{8,12},{10,14},{12,8},{14,10},{16,20},{18,... | collective-permute-start | bytes 1769480 | tf_op jit(solution)/shard_map/ppermute | solution.py:806
  234.2 17.1 %copy-start.6 = (bf16[8,2,2,48,384]{4,3,2,1,0:T(8,128)(2,1)S(1)}, bf16[8,2,2,48,384]{4,3,2,1,0:T(8,128)(2,1)}, u32[]{:S(2)}) copy-start(bf16[8,2,2,48,384]{4,3,2,1,0:T(8,128)(2,1)} %get-tuple-element.114) | copy-start | bytes 3538948
  251.3 3.0 copy-start.12
  251.3 3.0 copy-start.10
  251.5 1.7 copy-start.5
  255.1 32.6 %collective-permute-start.12 = (bf16[2,4,48,384]{3,2,1,0:T(8,128)(2,1)}, bf16[2,4,48,384]{3,2,1,0:T(8,128)(2,1)}, u32[]{:S(2)}, u32[]{:S(2)}) collective-permute-start(bf16[2,4,48,384]{3,2,1,0:T(8,128)(2,1)} %fusion.24), channel_id=1, source_target_pairs={{0,4},{2,6},{4,0},{6,2},{8,12},{10,14},{12,8},{14,10},{16,20},{18,... | collective-permute-start | bytes 884744 | tf_op jit(solution)/shard_map/ppermute | solution.py:806
  256.5 33.7 %collective-permute-start.6 = (bf16[2,2,4,48,384]{4,3,2,0,1:T(8,128)(2,1)}, bf16[2,2,4,48,384]{4,3,2,0,1:T(8,128)(2,1)}, u32[]{:S(2)}, u32[]{:S(2)}) collective-permute-start(bf16[2,2,4,48,384]{4,3,2,0,1:T(8,128)(2,1)} %fusion.3), channel_id=1, source_target_pairs={{0,1},{1,0},{2,3},{3,2},{4,5},{5,4},{6,7},{7,6},{8,9},{9,8},{10,11... | collective-permute-start | bytes 1769480 | tf_op jit(solution)/shard_map/ppermute | solution.py:805
  257.1 33.1 %collective-permute-start.7 = (bf16[4,2,2,48,384]{4,3,2,0,1:T(8,128)(2,1)}, bf16[4,2,2,48,384]{4,3,2,0,1:T(8,128)(2,1)}, u32[]{:S(2)}, u32[]{:S(2)}) collective-permute-start(bf16[4,2,2,48,384]{4,3,2,0,1:T(8,128)(2,1)} %fusion.2), channel_id=1, source_target_pairs={{0,4},{2,6},{4,0},{6,2},{8,12},{10,14},{12,8},{14,10},{16,20},{18,... | collective-permute-start | bytes 1769480 | tf_op jit(solution)/shard_map/ppermute | solution.py:806
  275.9 10.3 %copy-start.14 = (f32[9,1536]{1,0:T(8,128)S(1)}, f32[9,1536]{1,0:T(8,128)}, u32[]{:S(2)}) copy-start(f32[9,1536]{1,0:T(8,128)} %get-tuple-element.155) | copy-start | bytes 165892
  275.9 10.4 %copy-start.13 = (f32[9,1536]{1,0:T(8,128)S(1)}, f32[9,1536]{1,0:T(8,128)}, u32[]{:S(2)}) copy-start(f32[9,1536]{1,0:T(8,128)} %get-tuple-element.154) | copy-start | bytes 165892
  285.6 27.7 %collective-permute-start.10 = (bf16[8,2,2,48,384]{4,3,2,1,0:T(8,128)(2,1)}, bf16[8,2,2,48,384]{4,3,2,1,0:T(8,128)(2,1)}, u32[]{:S(2)}, u32[]{:S(2)}) collective-permute-start(bf16[8,2,2,48,384]{4,3,2,1,0:T(8,128)(2,1)} %get-tuple-element.131), channel_id=1, source_target_pairs={{0,2},{2,0},{4,6},{6,4},{8,10},{10,8},{12,14},{14,12},{16,18},{18,... | collective-permute-start | bytes 3538952 | tf_op jit(solution)/shard_map/ppermute | solution.py:806
  285.7 27.7 %collective-permute-start.11 = (bf16[8,2,2,48,384]{4,3,2,1,0:T(8,128)(2,1)}, bf16[8,2,2,48,384]{4,3,2,1,0:T(8,128)(2,1)}, u32[]{:S(2)}, u32[]{:S(2)}) collective-permute-start(bf16[8,2,2,48,384]{4,3,2,1,0:T(8,128)(2,1)} %get-tuple-element.132), channel_id=1, source_target_pairs={{0,2},{2,0},{4,6},{6,4},{8,10},{10,8},{12,14},{14,12},{16,18},{18,... | collective-permute-start | bytes 3538952 | tf_op jit(solution)/shard_map/ppermute | solution.py:806
  287.8 9.1 %collective-permute-start.13 = (bf16[4,2,48,384]{3,2,1,0:T(8,128)(2,1)S(1)}, bf16[4,2,48,384]{3,2,1,0:T(8,128)(2,1)S(1)}, u32[]{:S(2)}, u32[]{:S(2)}) collective-permute-start(bf16[4,2,48,384]{3,2,1,0:T(8,128)(2,1)S(1)} %fusion.23), channel_id=1, source_target_pairs={{0,1},{1,0},{2,3},{3,2},{4,5},{5,4},{6,7},{7,6},{8,9},{9,8},{10,11... | collective-permute-start | bytes 884744 | tf_op jit(solution)/shard_map/ppermute | solution.py:805
  290.2 6.6 %copy-start.11 = (bf16[4,2,2,48,384]{4,3,2,0,1:T(8,128)(2,1)S(1)}, bf16[4,2,2,48,384]{4,3,2,0,1:T(8,128)(2,1)}, u32[]{:S(2)}) copy-start(bf16[4,2,2,48,384]{4,3,2,0,1:T(8,128)(2,1)} %copy-done.10) | copy-start | bytes 1769476
  293.7 19.6 %collective-permute-start.8 = (bf16[2,4,48,384]{3,2,1,0:T(8,128)(2,1)}, bf16[2,4,48,384]{3,2,1,0:T(8,128)(2,1)}, u32[]{:S(2)}, u32[]{:S(2)}) collective-permute-start(bf16[2,4,48,384]{3,2,1,0:T(8,128)(2,1)} %fusion.22), channel_id=1, source_target_pairs={{0,4},{2,6},{4,0},{6,2},{8,12},{10,14},{12,8},{14,10},{16,20},{18,... | collective-permute-start | bytes 884744 | tf_op jit(solution)/shard_map/ppermute | solution.py:806
  295.2 18.2 %collective-permute-start.9 = (bf16[4,2,48,384]{3,2,1,0:T(8,128)(2,1)}, bf16[4,2,48,384]{3,2,1,0:T(8,128)(2,1)}, u32[]{:S(2)}, u32[]{:S(2)}) collective-permute-start(bf16[4,2,48,384]{3,2,1,0:T(8,128)(2,1)} %fusion.21), channel_id=1, source_target_pairs={{0,1},{1,0},{2,3},{3,2},{4,5},{5,4},{6,7},{7,6},{8,9},{9,8},{10,11... | collective-permute-start | bytes 884744 | tf_op jit(solution)/shard_map/ppermute | solution.py:805
  313.4 2.4 copy-start.7
  314.6 1.4 copy-start.2
  317.5 1.5 copy-start.1
  322.4 22.1 %collective-permute-start.21 = (bf16[8,48,384]{2,1,0:T(8,128)(2,1)}, bf16[8,48,384]{2,1,0:T(8,128)(2,1)}, u32[]{:S(2)}, u32[]{:S(2)}) collective-permute-start(bf16[8,48,384]{2,1,0:T(8,128)(2,1)} %get-tuple-element.158), channel_id=1, source_target_pairs={{0,8},{2,10},{4,12},{6,14},{8,16},{10,18},{12,20},{14,22},{16,24},... | collective-permute-start | bytes 884744 | tf_op jit(solution)/shard_map/ppermute | solution.py:824
  323.0 22.5 %collective-permute-start.22 = (bf16[8,48,384]{2,1,0:T(8,128)(2,1)}, bf16[8,48,384]{2,1,0:T(8,128)(2,1)}, u32[]{:S(2)}, u32[]{:S(2)}) collective-permute-start(bf16[8,48,384]{2,1,0:T(8,128)(2,1)} %get-tuple-element.159), channel_id=1, source_target_pairs={{0,16},{2,18},{4,20},{6,22},{8,24},{10,26},{12,28},{14,30},{16,0},... | collective-permute-start | bytes 884744 | tf_op jit(solution)/shard_map/ppermute | solution.py:824
  324.4 21.1 %collective-permute-start.23 = (bf16[8,48,384]{2,1,0:T(8,128)(2,1)}, bf16[8,48,384]{2,1,0:T(8,128)(2,1)}, u32[]{:S(2)}, u32[]{:S(2)}) collective-permute-start(bf16[8,48,384]{2,1,0:T(8,128)(2,1)} %get-tuple-element.160), channel_id=1, source_target_pairs={{0,24},{2,26},{4,28},{6,30},{8,0},{10,2},{12,4},{14,6},{16,8},{18,... | collective-permute-start | bytes 884744 | tf_op jit(solution)/shard_map/ppermute | solution.py:824
  338.5 26.1 %all-to-all-start.2 = ((f32[32,1,3312]{2,1,0:T(1,128)}), f32[32,1,3312]{2,1,0:T(1,128)S(1)}, u32[]{:S(2)}, u32[]{:S(2)}) async-start(f32[32,1,3312]{2,1,0:T(1,128)} %reshape.247), calls=%async_computation.2 | async-start | bytes 851968 | tf_op jit(solution)/shard_map/all_to_all | solution.py:773
  341.2 20.2 %collective-permute-start.16 = (bf16[4,2,2,48,384]{4,3,2,0,1:T(8,128)(2,1)}, bf16[4,2,2,48,384]{4,3,2,0,1:T(8,128)(2,1)}, u32[]{:S(2)}, u32[]{:S(2)}) collective-permute-start(bf16[4,2,2,48,384]{4,3,2,0,1:T(8,128)(2,1)} %fusion), channel_id=1, source_target_pairs={{0,4},{2,6},{4,0},{6,2},{8,12},{10,14},{12,8},{14,10},{16,20},{18,... | collective-permute-start | bytes 1769480 | tf_op jit(solution)/shard_map/ppermute | solution.py:806
  343.0 27.1 %collective-permute-start.14 = (bf16[4,2,2,48,384]{4,3,2,0,1:T(8,128)(2,1)}, bf16[4,2,2,48,384]{4,3,2,0,1:T(8,128)(2,1)}, u32[]{:S(2)}, u32[]{:S(2)}) collective-permute-start(bf16[4,2,2,48,384]{4,3,2,0,1:T(8,128)(2,1)} %fusion.1), channel_id=1, source_target_pairs={{0,1},{1,0},{2,3},{3,2},{4,5},{5,4},{6,7},{7,6},{8,9},{9,8},{10,11... | collective-permute-start | bytes 1769480 | tf_op jit(solution)/shard_map/ppermute | solution.py:805
  363.1 11.3 %collective-permute-start.17 = (bf16[4,2,48,384]{3,2,1,0:T(8,128)(2,1)}, bf16[4,2,48,384]{3,2,1,0:T(8,128)(2,1)}, u32[]{:S(2)}, u32[]{:S(2)}) collective-permute-start(bf16[4,2,48,384]{3,2,1,0:T(8,128)(2,1)} %fusion.17), channel_id=1, source_target_pairs={{0,1},{1,0},{2,3},{3,2},{4,5},{5,4},{6,7},{7,6},{8,9},{9,8},{10,11... | collective-permute-start | bytes 884744 | tf_op jit(solution)/shard_map/ppermute | solution.py:805
  366.1 38.0 %all-to-all-start.3 = ((f32[32,128,48]{1,2,0:T(8,128)}), f32[32,128,48]{1,2,0:T(8,128)S(1)}, u32[]{:S(2)}, u32[]{:S(2)}) async-start(f32[32,128,48]{1,2,0:T(8,128)} %bitcast.68), calls=%async_computation.3 | async-start | bytes 1572864 | tf_op jit(solution)/shard_map/all_to_all | solution.py:773
  371.2 15.6 %collective-permute-start.15 = (bf16[4,2,48,384]{3,2,1,0:T(8,128)(2,1)S(1)}, bf16[4,2,48,384]{3,2,1,0:T(8,128)(2,1)S(1)}, u32[]{:S(2)}, u32[]{:S(2)}) collective-permute-start(bf16[4,2,48,384]{3,2,1,0:T(8,128)(2,1)S(1)} %fusion.18), channel_id=1, source_target_pairs={{0,4},{2,6},{4,0},{6,2},{8,12},{10,14},{12,8},{14,10},{16,20},{18,... | collective-permute-start | bytes 884744 | tf_op jit(solution)/shard_map/ppermute | solution.py:806
  375.5 17.9 %copy-start.9 = (bf16[16,128,48]{1,2,0:T(8,128)(2,1)S(1)}, bf16[16,128,48]{1,2,0:T(8,128)(2,1)}, u32[]{:S(2)}) copy-start(bf16[16,128,48]{1,2,0:T(8,128)(2,1)} %copy-done.8) | copy-start | bytes 589828
  387.8 9.0 %collective-permute-start.18 = (bf16[4,48,384]{2,1,0:T(8,128)(2,1)S(1)}, bf16[4,48,384]{2,1,0:T(8,128)(2,1)S(1)}, u32[]{:S(2)}, u32[]{:S(2)}) collective-permute-start(bf16[4,48,384]{2,1,0:T(8,128)(2,1)S(1)} %get-tuple-element.184), channel_id=1, source_target_pairs={{0,8},{2,10},{4,12},{6,14},{8,16},{10,18},{12,20},{14,22},{16,24},... | collective-permute-start | bytes 442376 | tf_op jit(solution)/shard_map/ppermute | solution.py:824
  389.9 12.7 %collective-permute-start.19 = (bf16[4,48,384]{2,1,0:T(8,128)(2,1)S(1)}, bf16[4,48,384]{2,1,0:T(8,128)(2,1)S(1)}, u32[]{:S(2)}, u32[]{:S(2)}) collective-permute-start(bf16[4,48,384]{2,1,0:T(8,128)(2,1)S(1)} %get-tuple-element.185), channel_id=1, source_target_pairs={{0,16},{2,18},{4,20},{6,22},{8,24},{10,26},{12,28},{14,30},{16,0},... | collective-permute-start | bytes 442376 | tf_op jit(solution)/shard_map/ppermute | solution.py:824
  392.7 9.9 %collective-permute-start.20 = (bf16[4,48,384]{2,1,0:T(8,128)(2,1)S(1)}, bf16[4,48,384]{2,1,0:T(8,128)(2,1)S(1)}, u32[]{:S(2)}, u32[]{:S(2)}) collective-permute-start(bf16[4,48,384]{2,1,0:T(8,128)(2,1)S(1)} %get-tuple-element.186), channel_id=1, source_target_pairs={{0,24},{2,26},{4,28},{6,30},{8,0},{10,2},{12,4},{14,6},{16,8},{18,... | collective-permute-start | bytes 442376 | tf_op jit(solution)/shard_map/ppermute | solution.py:824
Sparse Core Ops, SparseCore 0:
  11.6 107.1 all-gather.4

commit v4 on v3

--- a/solution.py
+++ b/solution.py
@@ -16,7 +16,6 @@
 TOK = SIDE * SIDE
 EPS = 1e-06
 NJ, NK, UR, UC = 16, 2, 48, 384
-UNITS = 12
 CHUNK = 768
 MIB = 1024 * 1024
 BF = jnp.bfloat16
@@ -271,15 +270,27 @@
 
 
 def attend_kernel(
-    tag_ref, conv_in, tokens, mods, w_qkv, w_proj, qkv, merged, attn, resid, second, lse, proj_t,
-    full_qkv, full_proj, bias, mixed_t,
+    where, conv_in, tokens, mods, own_a, own_b, peer_a, peer_b,
+    qkv, merged, attn, resid, second, lse, proj_t, full_qkv,
+    full_proj, bias, mixed_t,
 ):
     @pl.when(pl.program_id(0) == 0)
     def _():
-        join_rows(w_qkv, full_qkv)
-        join_rows(w_proj, full_proj)
+        core, z, y, x = (where[i] for i in range(1, 5))
+        for owner in range(NJ):
+            step = (owner // 4 - z + 4) % 4
+            side = (owner // 2) % 2 ^ y
+            mine = core == owner % 2
+            for k in range(NK):
+                cols = slice(k * UC, (k + 1) * UC)
+                a = jnp.where(mine, own_a[k ^ x, side, step], peer_a[k ^ x, side, step])
+                b = jnp.where(mine, own_b[side, k ^ x, step], peer_b[side, k ^ x, step])
+                start = owner * 3 * UR
+                full_qkv[start : start + 2 * UR, cols] = a.reshape(2 * UR, UC)
+                full_qkv[start + 2 * UR : start + 3 * UR, cols] = b[0]
+                full_proj[owner * UR : (owner + 1) * UR, cols] = b[1]
         proj_t[...] = full_proj[...].T
-        bias[...] = item_bias(tag_ref[0])
+        bias[...] = item_bias(where[0])
 
     qkv[0] = dot(full_qkv[...], conv_in[0], 1, 1).astype(BF)
 
@@ -322,14 +333,8 @@
     return pl.BlockSpec((1,) + shape, lambda g: (g,) + (0,) * len(shape))
 
 
-def unit_spec(units, start):
-    shape = (NJ, NK, units, UR, UC)
-    return pl.BlockSpec(
-        shape, lambda g: (0, 0, start // units, 0, 0), pipeline_mode=pl.Buffered(1)
-    )
-
-
-def attend(tag, conv_in, tokens, mods, packed):
+def attend(where, conv_in, tokens, mods, projections):
+    relative = (2, 2, 4, 2, UR, UC)
     return pl.pallas_call(
         attend_kernel,
         grid=(4,),
@@ -338,9 +343,8 @@
             group_spec(GROUP, D),
             group_spec(GROUP, D),
             whole((6, 4, 8, D)),
-            unit_spec(3, 0),
-            unit_spec(1, 3),
-        ],
+        ]
+        + [whole(relative)] * 4,
         out_specs=[
             group_spec(3 * D, GROUP),
             group_spec(GROUP, D),
@@ -349,6 +353,7 @@
             group_spec(GROUP, D),
             group_spec(16, GROUP),
             whole((D, D)),
+            whole((3 * D, D)),
         ],
         out_shape=[
             jax.ShapeDtypeStruct((4, 3 * D, GROUP), BF),
@@ -358,9 +363,9 @@
             jax.ShapeDtypeStruct((4, GROUP, D), BF),
             jax.ShapeDtypeStruct((4, 16, GROUP), F32),
             jax.ShapeDtypeStruct((D, D), BF),
+            jax.ShapeDtypeStruct((3 * D, D), BF),
         ],
         scratch_shapes=[
-            pltpu.VMEM((3 * D, D), BF),
             pltpu.VMEM((D, D), BF),
             pltpu.VMEM((GROUP, GROUP), F32),
             pltpu.VMEM((D, GROUP), BF),
@@ -368,16 +373,14 @@
         compiler_params=params(),
         cost_estimate=cost(38),
         name="attend",
-    )(tag, conv_in, tokens, mods, packed, packed)
+    )(where, conv_in, tokens, mods, *projections)
 
 
 def feed_kernel(
-    tag_ref, second, gradient, mods, w_expand, w_shrink, kernel, *rest,
+    tag_ref, second, gradient, mods, w_expand, w_shrink, kernel,
+    shrunk, d_second, keep_expand, send_expand, keep_shrink, send_shrink, g_kernel,
+    d_shrunk, d_shrunk_t, expand, shrink, field, slope, hidden, d_field,
 ):
-    (
-        shrunk, d_second, keep_expand, send_expand, keep_shrink, send_shrink, g_kernel,
-        d_shrunk, d_shrunk_t, expand, shrink, field, slope, hidden, d_field,
-    ) = rest[-15:]
     step = pl.program_id(0)
     tag, core = tag_ref[0], tag_ref[1]
 
@@ -387,12 +390,8 @@
         value = gradient[...].astype(F32).reshape(4, 2, 8, 2, 8, D) * gate
         d_shrunk[...] = value.reshape(TOK, D).astype(BF)
         d_shrunk_t[...] = d_shrunk[...].T
-        if len(rest) > 15:
-            shrunk[...] = rest[0][...]
-            d_second[...] = rest[1][...]
-        else:
-            shrunk[...] = jnp.zeros_like(shrunk)
-            d_second[...] = jnp.zeros_like(d_second)
+        shrunk[...] = jnp.zeros_like(shrunk)
+        d_second[...] = jnp.zeros_like(d_second)
 
     join_rows(w_expand, expand)
     for q in range(2):
@@ -447,24 +446,22 @@
     return jax.ShapeDtypeStruct((NJ // 2, NK, units, UR, UC), BF)
 
 
-def feed(part, tag, second, gradient, mods, packed, kernel, before=()):
+def feed(tag, second, gradient, mods, packed, kernel):
     half = NJ // 2
     expand_spec = pl.BlockSpec((2, NK, 4, UR, UC), lambda c: (c, 0, 0, 0, 0))
-    shrink_spec = pl.BlockSpec((half, 1, 2, UR, UC), lambda c: (0, c, 0, 0, 0))
-    expand_shape = jax.ShapeDtypeStruct((half // 2, NK, 4, UR, UC), BF)
+    shrink_spec = pl.BlockSpec((half, 1, 2, UR, UC), lambda c: (0, c // 2, c % 2, 0, 0))
     return pl.pallas_call(
         feed_kernel,
-        grid=(2,),
+        grid=(FF // CHUNK,),
         in_specs=[
             SMEM_SPEC,
             whole((4, GROUP, D)),
             whole((4, GROUP, D)),
             whole((6, 4, 8, D)),
-            pl.BlockSpec((4, NK, 4, UR, UC), lambda c: (2 * c + part, 0, 1, 0, 0)),
-            pl.BlockSpec((NJ, 1, 2, UR, UC), lambda c: (0, c, 4 + part, 0, 0)),
-            pl.BlockSpec((9, CHUNK), lambda c: (0, 2 * c + part)),
-        ]
-        + [whole((4, GROUP, D)) for _ in before],
+            pl.BlockSpec((4, NK, 4, UR, UC), lambda c: (c, 0, 0, 0, 0)),
+            pl.BlockSpec((NJ, 1, 2, UR, UC), lambda c: (0, c // 2, 2 + c % 2, 0, 0)),
+            pl.BlockSpec((9, CHUNK), lambda c: (0, c)),
+        ],
         out_specs=[
             whole((4, GROUP, D)),
             whole((4, GROUP, D)),
@@ -477,11 +474,11 @@
         out_shape=[
             jax.ShapeDtypeStruct((4, GROUP, D), F32),
             jax.ShapeDtypeStruct((4, GROUP, D), F32),
-            expand_shape,
-            expand_shape,
-            packed_half(2),
-            packed_half(2),
-            jax.ShapeDtypeStruct((9, FF // 2), F32),
+            packed_half(4),
+            packed_half(4),
+            packed_half(4),
+            packed_half(4),
+            jax.ShapeDtypeStruct((9, FF), F32),
         ],
         scratch_shapes=[
             pltpu.VMEM((TOK, D), BF),
@@ -495,8 +492,8 @@
         ],
         compiler_params=params(60),
         cost_estimate=cost(38),
-        name=f"feed_{part}",
-    )(tag, second, gradient, mods, packed, packed, kernel, *before)
+        name="feed",
+    )(tag, second, gradient, mods, packed, packed, kernel)
 
 
 def attend_back_kernel(
@@ -646,7 +643,7 @@
 
 
 def conv_back_kernel(
-    tag_ref, d_qkv0, d_qkv1, w_qkv, norm, mods, kernel, d_first, g_kernel, weight, d_conv
+    tag_ref, d_qkv0, d_qkv1, weight, norm, mods, kernel, d_first, g_kernel, d_conv
 ):
     step = pl.program_id(0)
 
@@ -654,7 +651,6 @@
     def _():
         d_conv[...] = jnp.zeros_like(d_conv)
 
-    join_rows(w_qkv, weight)
     d_conv[0:2] += dot(d_qkv0[...], weight[...], 0, 0).reshape(2, GROUP, D)
     d_conv[2:4] += dot(d_qkv1[...], weight[...], 0, 0).reshape(2, GROUP, D)
 
@@ -688,7 +684,7 @@
         lax.fori_loop(0, D // 128, lanes, 0)
 
 
-def conv_back(tag, d_qkv, packed, norm, mods, kernel):
+def conv_back(tag, d_qkv, weight, norm, mods, kernel):
     tall = pl.BlockSpec((ROWS, 2 * GROUP), lambda i: (i, 0))
     return pl.pallas_call(
         conv_back_kernel,
@@ -697,7 +693,7 @@
             SMEM_SPEC,
             tall,
             tall,
-            pl.BlockSpec((2 * PAIRS, NK, 3, UR, UC), lambda i: (i, 0, 0, 0, 0)),
+            pl.BlockSpec((ROWS, D), lambda i: (i, 0)),
             whole((4, GROUP, D)),
             whole((6, 4, 8, D)),
             whole((9, D)),
@@ -707,11 +703,11 @@
             jax.ShapeDtypeStruct((4, GROUP, D), F32),
             jax.ShapeDtypeStruct((9, D), F32),
         ],
-        scratch_shapes=[pltpu.VMEM((ROWS, D), BF), pltpu.VMEM((4, GROUP, D), F32)],
+        scratch_shapes=[pltpu.VMEM((4, GROUP, D), F32)],
         compiler_params=params(),
         cost_estimate=cost(15),
         name="conv_back",
-    )(tag, *d_qkv, packed, norm, mods, kernel)
+    )(tag, *d_qkv, weight, norm, mods, kernel)
 
 
 def finish_kernel(
@@ -773,27 +769,48 @@
     return lax.all_to_all(pieces, BOTH, 0, 0, tiled=True)
 
 
-def pack_shards(qkv, proj, expand, shrink):
-    low = shrink.T.reshape(UR, 4, UC).transpose(1, 0, 2).reshape(4 * UR, UC)
-    return jnp.concatenate([qkv.T, proj.T, expand.T, low], axis=0)
-
-
-def gather_packed(nd, nf, qkv, proj, expand, shrink):
+def units_of(weight):
+    return weight.T.reshape(-1, UR, UC)
+
+
+def low_units(shrink):
+    return shrink.T.reshape(UR, 4, UC).transpose(1, 0, 2)
+
+
+def gather_feed(nd, nf, expand, shrink):
     if (nd, nf) == (NJ, NK):
-        rows = lax.all_gather(pack_shards(qkv, proj, expand, shrink), BOTH)
-        return rows.reshape(NJ, NK, UNITS, UR, UC)
-
-    def full(shard):
-        rows = lax.all_gather(shard.T, "fsdp", axis=1, tiled=True)
-        return lax.all_gather(rows, "dp", axis=0, tiled=True)
-
-    def split(weight, units):
-        return weight.reshape(NJ, units, UR, NK, UC).transpose(0, 3, 1, 2, 4)
-
-    low = full(shrink).reshape(NJ, UR, NK, 4, UC).transpose(0, 2, 3, 1, 4)
-    return jnp.concatenate(
-        [split(full(qkv), 3), split(full(proj), 1), split(full(expand), 4), low], axis=2
-    )
+        rows = jnp.concatenate([units_of(expand), low_units(shrink)]).reshape(8 * UR, UC)
+        return lax.all_gather(rows, BOTH).reshape(NJ, NK, 8, UR, UC)
+    low = full_rows(shrink).reshape(NJ, UR, NK, 4, UC).transpose(0, 2, 3, 1, 4)
+    return jnp.concatenate([all_units(full_rows(expand), 4), low], axis=2)
+
+
+def full_rows(shard):
+    rows = lax.all_gather(shard.T, "fsdp", axis=1, tiled=True)
+    return lax.all_gather(rows, "dp", axis=0, tiled=True)
+
+
+def all_units(weight, units):
+    return weight.reshape(NJ, units, UR, NK, UC).transpose(0, 3, 1, 2, 4)
+
+
+def gather_projections(nd, nf, qkv, proj):
+    if (nd, nf) == (NJ, NK):
+        own = jnp.concatenate([units_of(qkv), units_of(proj)])
+        turns = [
+            lax.ppermute(own, "dp", [(i, (i - 4 * step) % NJ) for i in range(NJ)])
+            for step in range(1, 4)
+        ]
+        a = jnp.stack([own[:2]] + [turn[:2] for turn in turns])
+        b = jnp.stack([own[2:]] + [turn[2:] for turn in turns])
+        a, b = jnp.stack([a, swap(a, 2)]), jnp.stack([b, swap(b, None)])
+        a, b = jnp.stack([a, swap(a, None)]), jnp.stack([b, swap(b, 2)])
+        return a, b, swap(a, 1), swap(b, 1)
+    units = jnp.concatenate([all_units(full_rows(qkv), 3), all_units(full_rows(proj), 1)], axis=2)
+    units = units.reshape((4, 2, 2) + units.shape[1:])
+    first, rest = units[:, :, :, :, :2], units[:, :, :, :, 2:]
+    a, b = first.transpose(2, 3, 1, 0, 4, 5, 6), rest.transpose(2, 1, 3, 0, 4, 5, 6)
+    return a[0], b[0], a[1], b[1]
 
 
 def pick(grads, index, axis):
@@ -817,11 +834,17 @@
     return [pick(total, (place + step) % 4, 0) for step in range(1, 4)]
 
 
-def last_sum(total, sends):
+def last_swaps(sends):
+    return [
+        lax.ppermute(sent, "dp", [(i, (i + 4 * step) % NJ) for i in range(NJ)])
+        for step, sent in enumerate(sends, 1)
+    ]
+
+
+def last_sum(total, got):
     own = pick(total, lax.axis_index("dp") // 4, 0).astype(F32)
-    for step, sent in enumerate(sends, 1):
-        moved = [(i, (i + 4 * step) % NJ) for i in range(NJ)]
-        own = own + lax.ppermute(sent, "dp", moved).astype(F32)
+    for value in got:
+        own = own + value.astype(F32)
     return own
 
 
@@ -877,9 +900,15 @@
 ):
     slots = nd * nf
     tag = size_tags[0]
-    core = lax.axis_index("dp") % 2 if (nd, nf) == (NJ, NK) else jnp.int32(0)
-    where = jnp.stack([tag, core])
-    packed = gather_packed(nd, nf, qkv_weight, proj_weight, expand_weight, shrink_weight)
+    square = (nd, nf) == (NJ, NK)
+    if square:
+        place = lax.axis_index("dp")
+        where = [tag, place % 2, place // 4, (place // 2) % 2, lax.axis_index("fsdp")]
+        where = jnp.stack(where).astype(jnp.int32)
+    else:
+        where = jnp.stack([tag] + [jnp.int32(0)] * 4)
+    projections = gather_projections(nd, nf, qkv_weight, proj_weight)
+    packed = gather_feed(nd, nf, expand_weight, shrink_weight)
     tokens, gradient, norm, factor = prepare(latents, cotangent)
     step_hot, class_hot, cond, act_all, attn_full, ffn_full = condition(
         nd, nf, timesteps, classes, step_table, class_table, attn_kernel, ffn_kernel
@@ -895,43 +924,28 @@
     mods = jnp.broadcast_to(chosen.reshape(4, 6, 1, D).transpose(1, 0, 2, 3), (6, 4, 8, D))
 
     conv_in = first_conv(size_tags, norm, mods, attn_full)
-    qkv, merged, attn, resid, second, lse, proj_t = attend(
-        size_tags, conv_in, tokens, mods, packed
-    )
-    common = (second, gradient, mods, packed, ffn_full)
-    square = (nd, nf) == (NJ, NK)
-    shrunk, d_second, keep_e0, send_e0, keep_s0, send_s0, g_ffn0 = feed(0, where, *common)
+    qkv, merged, attn, resid, second, lse, proj_t, full_qkv = attend(
+        where, conv_in, tokens, mods, projections
+    )
+    shrunk, d_second, keep_e, send_e, keep_s, send_s, g_ffn = feed(
+        where, second, gradient, mods, packed, ffn_full
+    )
+    back = (gradient, attn, mods, qkv, lse)
     if square:
-        got_e0, got_s0 = swap(send_e0, 1), swap(send_s0, 1)
-    shrunk, d_second, keep_e1, send_e1, keep_s1, send_s1, g_ffn1 = feed(
-        1, where, *common, (shrunk, d_second)
-    )
-    g_ffn = jnp.stack([g_ffn0.reshape(9, 2, -1), g_ffn1.reshape(9, 2, -1)], axis=2).reshape(9, FF)
-    if square:
-        got_e1, got_s1 = swap(send_e1, 1), swap(send_s1, 1)
-
-        def grid(value, outer):
-            return value.reshape((outer, 2) + value.shape[1:])
-
-        keep_e0, out_e0 = halve(grid(keep_e0, 2), grid(got_e0, 2), 2, None)
-        keep_s0, out_s0 = halve(grid(keep_s0, 4), grid(got_s0, 4), 1, 2)
-        d_second, out_e0, out_s0 = tie(d_second, out_e0, out_s0)
-        got_e0, got_s0 = swap(out_e0, None), swap(out_s0, 2)
-    back = (gradient, attn, mods, qkv, lse)
+        got_e, got_s = swap(send_e, 1), swap(send_s, 1)
     output0, d_resid0, d_qkv0, d_attn0, later0 = attend_back(
         0, where, resid, shrunk, d_second, *back, proj_t
     )
+
+    def grid(value):
+        return value.reshape((4, 2) + value.shape[1:])
+
     if square:
-        d_qkv0, got_e0, got_s0, got_e1, got_s1 = tie(d_qkv0, got_e0, got_s0, got_e1, got_s1)
-        keep_e0, out_e0 = halve(keep_e0, got_e0, 1, 2)
-        keep_s0, out_s0 = halve(keep_s0, got_s0, 1, None)
-        keep_e1, out_e1 = halve(grid(keep_e1, 2), grid(got_e1, 2), 2, None)
-        keep_s1, out_s1 = halve(grid(keep_s1, 4), grid(got_s1, 4), 1, 2)
-        d_second, d_qkv0, out_e0, out_s0, out_e1, out_s1 = tie(
-            d_second, d_qkv0, out_e0, out_s0, out_e1, out_s1
-        )
-        got_e0, got_s0 = swap(out_e0, 2), swap(out_s0, None)
-        got_e1, got_s1 = swap(out_e1, None), swap(out_s1, 2)
+        d_qkv0, got_e, got_s = tie(d_qkv0, got_e, got_s)
+        keep_e, out_e = halve(grid(keep_e), grid(got_e), 2, None)
+        keep_s, out_s = halve(grid(keep_s), grid(got_s), 1, 2)
+        d_second, d_qkv0, out_e, out_s = tie(d_second, d_qkv0, out_e, out_s)
+        got_e, got_s = swap(out_e, None), swap(out_s, 2)
     output1, d_resid1, d_qkv1, d_attn1, later1 = attend_back(
         1, where, resid, shrunk, d_second, *back, proj_t
     )
@@ -941,47 +955,43 @@
     )
     if square:
         got_a, got_b = swap(send_a, 1), swap(send_b, 1)
-        keep_a, got_e1, got_s1 = tie(keep_a, got_e1, got_s1)
-        keep_e1, out_e1 = halve(keep_e1, got_e1, 1, 2)
-        keep_s1, out_s1 = halve(keep_s1, got_s1, 1, None)
-        norm, out_e1, out_s1 = tie(norm, out_e1, out_s1)
-        got_e1, got_s1 = swap(out_e1, 2), swap(out_s1, None)
-    d_first, g_attn = conv_back(where, d_qkv, packed, norm, mods, attn_full)
+        keep_a, got_e, got_s = tie(keep_a, got_e, got_s)
+        keep_e, out_e = halve(keep_e, got_e, 1, 2)
+        keep_s, out_s = halve(keep_s, got_s, 1, None)
+        norm, out_e, out_s = tie(norm, out_e, out_s)
+        got_e, got_s = swap(out_e, 2), swap(out_s, None)
+    d_first, g_attn = conv_back(where, d_qkv, full_qkv, norm, mods, attn_full)
     if square:
-        d_first, got_e1, got_s1, got_a, got_b = tie(d_first, got_e1, got_s1, got_a, got_b)
-        expand = jnp.stack([keep_e0 + got_e0, keep_e1 + got_e1], axis=1).reshape(4, 4, UR, UC)
-        total = jnp.concatenate([expand, keep_s0 + got_s0, keep_s1 + got_s1], axis=1)
-        sends = last_sends(total)
-        keep_a, out_a = halve(grid(keep_a, 4), grid(got_a, 4), 2, None)
-        keep_b, out_b = halve(grid(keep_b, 4), grid(got_b, 4), 1, 2)
+        d_first, got_e, got_s, got_a, got_b = tie(d_first, got_e, got_s, got_a, got_b)
+        keep_a, out_a = halve(grid(keep_a), grid(got_a), 2, None)
+        keep_b, out_b = halve(grid(keep_b), grid(got_b), 1, 2)
+        feeding = jnp.concatenate([keep_e + got_e, keep_s + got_s], axis=1)
+        sends = last_sends(feeding)
         d_first, out_a, out_b, *sends = tie(d_first, out_a, out_b, *sends)
-        feeding = last_sum(total, sends)
         got_a, got_b = swap(out_a, None), swap(out_b, 2)
+        got_feeding = last_swaps(sends)
     block_output, input_grad, early = finish(
         d_first, norm, factor, (d_resid0, d_resid1), (output0, output1), mods
     )
     later = later0 + later1
     if square:
+        later, got_a, got_b = tie(later, got_a, got_b)
         keep_a, out_a = halve(keep_a, got_a, 1, 2)
         keep_b, out_b = halve(keep_b, got_b, 1, None)
         got_a, got_b = swap(out_a, 2), swap(out_b, None)
         total = jnp.concatenate([keep_a + got_a, keep_b + got_b], axis=1)
-        packed_grads = (last_sum(total, last_sends(total)), feeding)
-        packed_grads = jnp.concatenate(packed_grads, axis=0)
-        cuts = [packed_grads[i:j] for i, j in ((0, 3), (3, 4), (4, 8), (8, 12))]
+        sends = last_sends(total)
+        sends[0], *got_feeding = tie(sends[0], *got_feeding)
+        feeding = last_sum(feeding, got_feeding)
+        total = last_sum(total, last_swaps(sends))
+        cuts = [total[:3], total[3:], feeding[:4], feeding[4:]]
     else:
         first, rest = both_cores(keep_a, send_a), both_cores(keep_b, send_b)
-        expand = jnp.stack(
-            [both_cores(k, s).reshape((2, 4, NK, 4, UR, UC)) for k, s in
-             ((keep_e0, send_e0), (keep_e1, send_e1))],
-            axis=1,
-        ).reshape(NJ, NK, 4, UR, UC)
-        shrink = [both_cores(keep_s0, send_s0), both_cores(keep_s1, send_s1)]
         cuts = [
             jnp.concatenate([first, rest[:, :, :1]], axis=2),
             rest[:, :, 1:],
-            expand,
-            jnp.concatenate(shrink, axis=2),
+            both_cores(keep_e, send_e),
+            both_cores(keep_s, send_s),
         ]
     shards = [
         own_shard(nd, nf, kind, cut)

time: 421 us -> 392 us (0.931); the launches traced: 413 us -> 391 us
  waiting for transfers between devices: 80.5 us -> 49.5 us
  starting transfers between devices: 43.2 us -> 56.2 us
  Pallas kernels: 189 us -> 182 us
    all_gather x1, waiting for transfers between devices: 38.5 us -> 0.02 us  [gather_feed(): return lax.all_gather(rows, BOTH).reshape(NJ, NK, 8, UR, UC)]
    ppermute x12, waiting for transfers between devices: 24.3 us -> 1.11 us  [swap(): return lax.ppermute(value, 'dp', [(i, i ^ bit) for i in range(NJ)])]
    all_to_all x4, waiting for transfers between devices: 7.43 us -> 24.2 us  [exchange(): return lax.all_to_all(pieces, BOTH, 0, 0, tiled=True)]
    ppermute x6 -> x9, starting transfers between devices: 10 us -> 26.7 us  [the longest x6 20.5 us: last_swaps(): lax.ppermute(sent, 'dp', [(i, (i + 4 * step) % NJ) for i in range(NJ)])]
    pallas_call x2 -> x1, Pallas kernels: 77.4 us -> 69 us  [feed(): pl.pallas_call(feed_kernel, grid=(FF // CHUNK,), in_specs=[SMEM_SPEC, who...]
    ppermute x6, waiting for transfers between devices: 1.09 us -> 9.44 us  [swap(): return lax.ppermute(value, 'fsdp', [(0, 1), (1, 0)])]
    ppermute x6 -> x9, waiting for transfers between devices: 9.14 us -> 14.7 us  [the longest x6 14.7 us: last_swaps(): lax.ppermute(sent, 'dp', [(i, (i + 4 * step) % NJ) for i in range(NJ)])]
    add x12 -> x7, other arithmetic: 10.7 us -> 7.72 us  [halve(): return (kept, pick(keep, 1 - mine, axis) + pick(got, 1 - mine, axis))]
  transfers between devices with their start and end apart: 29 -> 32, of which waited for: 8 -> 9; matrix products, arithmetic and copies ran while one was open for 8% -> 7% of each run, Pallas kernels for 29% -> 29%
where the time goes in v4:
time: 392 us; the launch traced here: 391 us
  Pallas kernels  182 us (46%)
  starting transfers between devices  56.2 us (14%)
  waiting for transfers between devices  49.5 us (13%)
  blocking collectives  35.8 us (9%)
  other arithmetic  26.8 us (7%)
  local copies, waits for them, and re-layouts  20.7 us (5%)
  between operations  15.5 us (4%)
  matrix products  3.92 us (1%)
    pallas_call x1, Pallas kernels, feed(): pl.pallas_call(feed_kernel, grid=(FF // CHUNK,), in_specs=[SMEM_SPEC, who...  69 us
    pallas_call x2, Pallas kernels, attend_back(): pl.pallas_call(attend_back_kernel, grid=(2,), in_specs=[SMEM_SPEC, pick_g...  34.3 us
    pallas_call x1, Pallas kernels, attend(): pl.pallas_call(attend_kernel, grid=(4,), in_specs=[SMEM_SPEC, group_spec(...  33.1 us
    all_gather x1, blocking collectives, condition(): sent = lax.all_gather(jnp.concatenate([act, filters], axis=0), 'dp')  27.7 us
    all_to_all x4, waiting for transfers between devices, exchange(): return lax.all_to_all(pieces, BOTH, 0, 0, tiled=True)  24.2 us
    ppermute x6, starting transfers between devices, last_swaps(): lax.ppermute(sent, 'dp', [(i, (i + 4 * step) % NJ) for i in range(NJ)])  20.5 us
    pallas_call x1, Pallas kernels, conv_back(): pl.pallas_call(conv_back_kernel, grid=(8 // PAIRS,), in_specs=[SMEM_SPEC,...  15.6 us
    ppermute x6, waiting for transfers between devices, last_swaps(): lax.ppermute(sent, 'dp', [(i, (i + 4 * step) % NJ) for i in range(NJ)])  14.7 us
  transfers between devices with their start and end apart: 32, of which 9 were waited for; matrix products, arithmetic and copies ran while one was open for 7% of the time, Pallas kernels for 29%

profile of v4, /device:TPU:0, one launch (start us, length us, event | category | flops | bytes accessed | tf_op | source)
XLA Modules:
  0.0 390.8 jit_solution(8274342451408910068)
XLA Ops:
  7.3 1.0 copy.128
  8.3 1.7 pad_maximum_fusion.6
  10.0 5.1 %collective-permute-start = (bf16[4,48,384]{2,1,0:T(8,128)(2,1)S(1)}, bf16[4,48,384]{2,1,0:T(8,128)(2,1)S(1)}, u32[]{:S(2)}, u32[]{:S(2)}) collective-permute-start(bf16[4,48,384]{2,1,0:T(8,128)(2,1)S(1)} %pad_maximum_fusion.8), channel_id=1, source_target_pairs={{0,24},{2,26},{4,28},{6,30},{8,0},{10,2},{12,4},{14,6},{16,8},{18,... | collective-permute-start | bytes 442376 | tf_op jit(solution)/shard_map/ppermute | solution.py:801
  15.1 1.0 collective-permute-start.2
  16.8 5.1 %all-to-all-start = ((s32[32,1,8]{2,1,0:T(1,128)}), s32[32,1,8]{2,1,0:T(1,128)S(1)}, u32[]{:S(2)}, u32[]{:S(2)}) async-start(s32[32,1,8]{2,1,0:T(1,128)} %broadcast_in_dim.45), calls=%async_computation | async-start | bytes 32768 | tf_op jit(solution)/shard_map/all_to_all | solution.py:769
  21.9 6.0 %prepare.1 = (bf16[4,256,768]{2,1,0:T(8,128)(2,1)}, bf16[4,256,768]{2,1,0:T(8,128)(2,1)}, f32[4,256,768]{2,1,0:T(8,128)}, f32[4,256,1]{2,1,0:T(8,128)}) custom-call(bf16[1024,768]{1,0:T(8,128)(2,1)} %latents.1, bf16[1024,768]{1,0:T(8,128)(2,1)} %cotangent.1), custom_call_target="tpu_custom_call" | custom-call | flops 600000000 | bytes 4194304 | tf_op jit(solution)/shard_map/prepare/pallas_call | solution.py:87
  29.6 2.5 all-to-all-done
  34.6 7.1 %collective-permute-done.5 = bf16[4,2,48,384]{3,2,1,0:T(8,128)(2,1)S(1)} collective-permute-done((bf16[4,2,48,384]{3,2,1,0:T(8,128)(2,1)S(1)}, bf16[4,2,48,384]{3,2,1,0:T(8,128)(2,1)S(1)}, u32[]{:S(2)}, u32[]{:S(2)}) %collective-permute-start.5) | collective-permute-done | bytes 294944 | tf_op jit(solution)/shard_map/ppermute | solution.py:822
  42.5 8.1 %psum.7 = f32[128,48]{0,1:T(8,128)S(1)} all-reduce(f32[128,48]{0,1:T(8,128)S(1)} %convolution_add_fusion), channel_id=1, replica_groups=mesh['dp'=16,'fsdp'=2] {'fsdp'}, use_global_device_ids=true, to_apply=%region_0.1 | all-reduce | flops 6144 | bytes 49152 | tf_op jit(solution)/shard_map/psum | solution.py:884
  50.7 1.4 collective-permute-start.4
  52.1 27.7 %all-gather.1 = bf16[16,173,48]{1,2,0:T(8,128)(2,1)S(1)} all-gather(bf16[1,173,48]{1,2,0:T(8,128)(2,1)S(1)} %maximum_bitcast_fusion.1), channel_id=2, replica_groups=mesh['dp'=16,'fsdp'=2] {'dp'}, dimensions={0}, use_global_device_ids=true | all-gather | bytes 282336 | tf_op jit(solution)/shard_map/all_gather | solution.py:888
  81.0 1.2 pad_maximum_fusion.own_a
  83.4 2.6 all-to-all-start.1
  88.2 10.4 %all-to-all-done.1 = f32[32,4,288]{2,1,0:T(4,128)S(1)} async-done(((f32[32,4,288]{2,1,0:T(4,128)}), f32[32,4,288]{2,1,0:T(4,128)S(1)}, u32[]{:S(2)}, u32[]{:S(2)}) %all-to-all-start.1) | async-done | bytes 147488 | tf_op jit(solution)/shard_map/all_to_all | solution.py:769
  99.9 6.1 %first_conv.1.conv_in = bf16[4,256,768]{2,1,0:T(8,128)(2,1)} custom-call(s32[1]{0:T(128)S(6)} %copy.131.tag_ref, f32[4,256,768]{2,1,0:T(8,128)} %get-tuple-element.111.norm, f32[6,4,8,768]{3,2,1,0:T(8,128)} %broadcast_in_dim.49.mods, f32[9,768]{1,0:T(8,128)} %reshape.207.kernel), custom_call_target="tpu_custom_call" | custom-call | flops 600000000 | bytes 4194304 | tf_op jit(solution)/shard_map/first_conv/pallas_call | solution.py:223
  106.0 33.1 %attend.1 = (bf16[4,2304,256]{2,1,0:T(8,128)(2,1)}, bf16[4,256,768]{2,1,0:T(8,128)(2,1)}, bf16[4,256,768]{2,1,0:T(8,128)(2,1)}, f32[4,256,768]{2,1,0:T(8,128)}, ...) custom-call(s32[5]{0:T(128)} %stack.85.where.tag_ref, ...), custom_call_target="tpu_custom_call" | custom-call | flops 3800000000 | bytes 4194304 | tf_op jit(solution)/shard_map/attend/pallas_call | solution.py:338
  139.1 69.0 %feed.1 = (f32[4,256,768]{2,1,0:T(8,128)}, f32[4,256,768]{2,1,0:T(8,128)}, bf16[8,2,4,48,384]{4,3,2,1,0:T(8,128)(2,1)}, bf16[8,2,4,48,384]{4,3,2,1,0:T(8,128)(2,...) custom-call(s32[5]{0:T(128)} %stack.85.where.tag_ref, ...), custom_call_target="tpu_custom_call" | custom-call | flops 3800000000 | bytes 4194304 | tf_op jit(solution)/shard_map/feed/pallas_call | solution.py:453
  208.7 17.0 %attend_back_0.1 = (bf16[2,256,768]{2,1,0:T(8,128)(2,1)}, f32[2,256,768]{2,1,0:T(8,128)}, bf16[2304,512]{1,0:T(8,128)(2,1)}, bf16[768,512]{1,0:T(8,128)(2,1)}, f32[4,4,8,768]{3,2,1,0:T(8,128)}) custom-call(s32[5]{0:T(128)} %stack.85.where.tag_ref, f32[4,256,768]{2,1,0:T(8,128)} %get-tuple-element.85.resid, f32[4,256,768]{2,1,0:T(8,128)} %get-tuple-element.86.shrunk, ...), custom_call_target="tpu_custom_call" | custom-call | flops 1600000000 | bytes 4194304 | tf_op jit(solution)/shard_map/attend_back_0/pallas_call | solution.py:568
  225.7 1.5 copy-done.5
  227.2 2.1 dynamic-slice_add_fusion.1
  229.3 1.2 fusion
  230.6 0.9 copy-done.3
  231.5 1.3 dynamic-slice_add_fusion
  232.8 1.4 collective-permute-start.11
  234.2 2.0 collective-permute-start.12
  236.2 17.2 %attend_back_1.1 = (bf16[2,256,768]{2,1,0:T(8,128)(2,1)}, f32[2,256,768]{2,1,0:T(8,128)}, bf16[2304,512]{1,0:T(8,128)(2,1)}, bf16[768,512]{1,0:T(8,128)(2,1)}, f32[4,4,8,768]{3,2,1,0:T(8,128)}) custom-call(s32[5]{0:T(128)} %stack.85.where.tag_ref, f32[4,256,768]{2,1,0:T(8,128)} %get-tuple-element.85.resid, f32[4,256,768]{2,1,0:T(8,128)} %get-tuple-element.86.shrunk, ...), custom_call_target="tpu_custom_call" | custom-call | flops 1600000000 | bytes 4194304 | tf_op jit(solution)/shard_map/attend_back_1/pallas_call | solution.py:568
  253.5 9.7 %project_grads.1 = (bf16[8,2,2,48,384]{4,3,2,1,0:T(8,128)(2,1)}, bf16[8,2,2,48,384]{4,3,2,1,0:T(8,128)(2,1)}, bf16[8,2,2,48,384]{4,3,2,1,0:T(8,128)(2,1)}, bf16[8,2,2,48,384]{4,3,2,1,0:T(8,128)(2,1)}) custom-call(s32[5]{0:T(128)} %stack.85.where.tag_ref, bf16[2304,512]{1,0:T(8,128)(2,1)} %get-tuple-element.99.d_qkv0, ...), custom_call_target="tpu_custom_call" | custom-call | flops 800000000 | bytes 4194304 | tf_op jit(solution)/shard_map/project_grads/pallas_call | solution.py:633
  263.7 1.0 fusion.6
  264.7 1.0 fusion.5
  266.3 15.6 %conv_back.1 = (f32[4,256,768]{2,1,0:T(8,128)}, f32[9,768]{1,0:T(8,128)}) custom-call(s32[5]{0:T(128)} %stack.85.where.tag_ref, bf16[2304,512]{1,0:T(8,128)(2,1)} %get-tuple-element.99.d_qkv0, bf16[2304,512]{1,0:T(8,128)(2,1)} %get-tuple-element.101.d_qkv1, bf16[2304,768]{1,0:T(8,128)(2,1)} %get-tuple-element.102.weight, ...), custom_call_target="tpu_custom_call" | custom-call | flops 1500000000 | bytes 4194304 | tf_op jit(solution)/shard_map/conv_back/pallas_call | solution.py:689
  282.8 1.4 bitcast_add_fusion
  284.2 1.4 dynamic-slice_add_fusion.2
  287.1 1.4 dynamic-slice_add_fusion.3
  289.4 0.9 fusion.21
  290.4 1.8 collective-permute-start.17
  292.1 1.6 collective-permute-start.18
  294.0 1.2 add.293
  296.1 1.1 reshape.228
  297.2 8.6 %finish.1 = (bf16[1024,768]{1,0:T(8,128)(2,1)}, f32[1024,768]{1,0:T(8,128)}, f32[2,4,8,768]{3,2,1,0:T(8,128)}) custom-call(f32[4,256,768]{2,1,0:T(8,128)} %get-tuple-element.124.d_first, f32[4,256,768]{2,1,0:T(8,128)} %get-tuple-element.111.norm, f32[4,256,1]{2,1,0:T(8,128)} %get-tuple-element.125.factor, f32[2,256,768]{2,1,0:T(8,128)} %get-tuple-element.126.d_resid0, ...), custom_call_target="tpu_custom_call" | custom-call | flops 800000000 | bytes 4194304 | tf_op jit(solution)/shard_map/finish/pallas_call | solution.py:748
  305.8 1.1 collective-permute-done.18
  306.9 1.1 maximum_reduce_fusion
  308.6 1.4 reshape.229
  310.0 3.2 all-to-all-start.2
  313.1 1.0 fusion.24
  314.2 1.8 collective-permute-start.20
  316.0 1.5 collective-permute-start.21
  317.5 2.4 collective-permute-start.22
  319.9 1.4 collective-permute-start.23
  321.3 1.7 fusion.25
  323.0 1.5 collective-permute-start.19
  324.5 2.3 collective-permute-done.20
  326.8 1.1 bitcast_add_fusion.7
  327.9 11.2 %all-to-all-done.2 = f32[32,1,3312]{2,1,0:T(1,128)S(1)} async-done(((f32[32,1,3312]{2,1,0:T(1,128)}), f32[32,1,3312]{2,1,0:T(1,128)S(1)}, u32[]{:S(2)}, u32[]{:S(2)}) %all-to-all-start.2) | async-done | bytes 423968 | tf_op jit(solution)/shard_map/all_to_all | solution.py:769
  340.4 1.0 broadcast_in_dim.54
  341.4 2.8 all-to-all-start.3
  344.2 1.1 bitcast_add_fusion.10
  345.6 11.9 %collective-permute-start.24 = (bf16[4,48,384]{2,1,0:T(8,128)(2,1)S(1)}, bf16[4,48,384]{2,1,0:T(8,128)(2,1)S(1)}, u32[]{:S(2)}, u32[]{:S(2)}) collective-permute-start(bf16[4,48,384]{2,1,0:T(8,128)(2,1)S(1)} %get-tuple-element.145), channel_id=1, source_target_pairs={{0,8},{2,10},{4,12},{6,14},{8,16},{10,18},{12,20},{14,22},{16,24},... | collective-permute-start | bytes 442376 | tf_op jit(solution)/shard_map/ppermute | solution.py:839
  357.5 3.4 collective-permute-start.25
  360.8 1.3 fusion.4
  363.6 1.6 collective-permute-done.24
  365.2 12.9 %collective-permute-done.25 = bf16[4,48,384]{2,1,0:T(8,128)(2,1)S(1)} collective-permute-done((bf16[4,48,384]{2,1,0:T(8,128)(2,1)S(1)}, bf16[4,48,384]{2,1,0:T(8,128)(2,1)S(1)}, u32[]{:S(2)}, u32[]{:S(2)}) %collective-permute-start.25) | collective-permute-done | bytes 147488 | tf_op jit(solution)/shard_map/ppermute | solution.py:839
  381.0 1.0 fusion.42
  382.1 0.9 fusion.7
  383.0 0.9 fusion.10
  (175 shorter events, 23.3 us)
Async XLA Ops:
  7.2 75.2 %copy-start = (bf16[384,288]{0,1:T(8,128)(2,1)S(1)}, bf16[384,288]{0,1:T(8,128)(2,1)}, u32[]{:S(2)}) copy-start(bf16[384,288]{0,1:T(8,128)(2,1)} %param.20) | copy-start | bytes 663556
  7.2 2.8 copy-start.17
  7.2 2.8 copy-start.22
  7.2 8.9 %copy-start.29 = (s32[1,4]{1,0:T(1,128)S(1)}, s32[1,4]{1,0:T(1,128)}, u32[]{:S(2)}) copy-start(s32[1,4]{1,0:T(1,128)} %param.16) | copy-start | bytes 52
  7.2 8.9 %copy-start.28 = (s32[1,4]{1,0:T(1,128)S(1)}, s32[1,4]{1,0:T(1,128)}, u32[]{:S(2)}) copy-start(s32[1,4]{1,0:T(1,128)} %param.17) | copy-start | bytes 52
  7.2 131.8 %all-gather.4.cloned.1.call-start = ((), (), s32[]{:S(2)}) async-start(), calls=%async_computation.4 | async-start | bytes 9732096 | tf_op jit(solution)/shard_map/all_gather | solution.py:783
  10.0 22.7 %collective-permute-start = (bf16[4,48,384]{2,1,0:T(8,128)(2,1)S(1)}, bf16[4,48,384]{2,1,0:T(8,128)(2,1)S(1)}, u32[]{:S(2)}, u32[]{:S(2)}) collective-permute-start(bf16[4,48,384]{2,1,0:T(8,128)(2,1)S(1)} %pad_maximum_fusion.8), channel_id=1, source_target_pairs={{0,24},{2,26},{4,28},{6,30},{8,0},{10,2},{12,4},{14,6},{16,8},{18,... | collective-permute-start | bytes 442376 | tf_op jit(solution)/shard_map/ppermute | solution.py:801
  15.1 17.7 %collective-permute-start.1 = (bf16[4,48,384]{2,1,0:T(8,128)(2,1)S(1)}, bf16[4,48,384]{2,1,0:T(8,128)(2,1)S(1)}, u32[]{:S(2)}, u32[]{:S(2)}) collective-permute-start(bf16[4,48,384]{2,1,0:T(8,128)(2,1)S(1)} %pad_maximum_fusion.8), channel_id=1, source_target_pairs={{0,16},{2,18},{4,20},{6,22},{8,24},{10,26},{12,28},{14,30},{16,0},... | collective-permute-start | bytes 442376 | tf_op jit(solution)/shard_map/ppermute | solution.py:801
  15.1 17.7 %collective-permute-start.2 = (bf16[4,48,384]{2,1,0:T(8,128)(2,1)S(1)}, bf16[4,48,384]{2,1,0:T(8,128)(2,1)S(1)}, u32[]{:S(2)}, u32[]{:S(2)}) collective-permute-start(bf16[4,48,384]{2,1,0:T(8,128)(2,1)S(1)} %pad_maximum_fusion.8), channel_id=1, source_target_pairs={{0,8},{2,10},{4,12},{6,14},{8,16},{10,18},{12,20},{14,22},{16,24},... | collective-permute-start | bytes 442376 | tf_op jit(solution)/shard_map/ppermute | solution.py:801
  16.8 15.3 %all-to-all-start = ((s32[32,1,8]{2,1,0:T(1,128)}), s32[32,1,8]{2,1,0:T(1,128)S(1)}, u32[]{:S(2)}, u32[]{:S(2)}) async-start(s32[32,1,8]{2,1,0:T(1,128)} %broadcast_in_dim.45), calls=%async_computation | async-start | bytes 32768 | tf_op jit(solution)/shard_map/all_to_all | solution.py:769
  21.9 6.1 %copy-start.24 = (bf16[9,192]{1,0:T(8,128)(2,1)S(1)}, bf16[9,192]{1,0:T(8,128)(2,1)}, u32[]{:S(2)}) copy-start(bf16[9,192]{1,0:T(8,128)(2,1)} %param.25) | copy-start | bytes 10372
  21.9 6.1 %copy-start.25 = (bf16[9,48]{1,0:T(8,128)(2,1)S(1)}, bf16[9,48]{1,0:T(8,128)(2,1)}, u32[]{:S(2)}) copy-start(bf16[9,48]{1,0:T(8,128)(2,1)} %param.21) | copy-start | bytes 2596
  21.9 10.5 %copy-start.26 = (bf16[500,48]{0,1:T(8,128)(2,1)S(1)}, bf16[500,48]{0,1:T(8,128)(2,1)}, u32[]{:S(2)}) copy-start(bf16[500,48]{0,1:T(8,128)(2,1)} %param.18) | copy-start | bytes 144004
  32.7 1.7 copy-start.27
  32.9 8.9 %collective-permute-start.5 = (bf16[4,2,48,384]{3,2,1,0:T(8,128)(2,1)S(1)}, bf16[4,2,48,384]{3,2,1,0:T(8,128)(2,1)S(1)}, u32[]{:S(2)}, u32[]{:S(2)}) collective-permute-start(bf16[4,2,48,384]{3,2,1,0:T(8,128)(2,1)S(1)} %get-tuple-element.173), channel_id=1, source_target_pairs={{0,1},{1,0},{2,3},{3,2},{4,5},{5,4},{6,7},{7,6},{8,9},{9,8},{10,11... | collective-permute-start | bytes 884744 | tf_op jit(solution)/shard_map/ppermute | solution.py:822
  33.6 17.0 %collective-permute-start.3 = (bf16[4,2,48,384]{3,2,1,0:T(8,128)(2,1)S(1)}, bf16[4,2,48,384]{3,2,1,0:T(8,128)(2,1)S(1)}, u32[]{:S(2)}, u32[]{:S(2)}) collective-permute-start(bf16[4,2,48,384]{3,2,1,0:T(8,128)(2,1)S(1)} %get-tuple-element.175), channel_id=1, source_target_pairs={{0,4},{2,6},{4,0},{6,2},{8,12},{10,14},{12,8},{14,10},{16,20},{18,... | collective-permute-start | bytes 884744 | tf_op jit(solution)/shard_map/ppermute | solution.py:823
  41.9 38.0 %collective-permute-start.6 = (bf16[2,4,2,48,384]{4,3,2,1,0:T(8,128)(2,1)S(1)}, bf16[2,4,2,48,384]{4,3,2,1,0:T(8,128)(2,1)S(1)}, u32[]{:S(2)}, u32[]{:S(2)}) collective-permute-start(bf16[2,4,2,48,384]{4,3,2,1,0:T(8,128)(2,1)S(1)} %get-tuple-element.169), channel_id=1, source_target_pairs={{0,4},{2,6},{4,0},{6,2},{8,12},{10,14},{12,8},{14,10},{16,20},{18,... | collective-permute-start | bytes 1769480 | tf_op jit(solution)/shard_map/ppermute | solution.py:823
  50.7 30.3 %collective-permute-start.4 = (bf16[2,4,2,48,384]{4,3,2,1,0:T(8,128)(2,1)S(1)}, bf16[2,4,2,48,384]{4,3,2,1,0:T(8,128)(2,1)S(1)}, u32[]{:S(2)}, u32[]{:S(2)}) collective-permute-start(bf16[2,4,2,48,384]{4,3,2,1,0:T(8,128)(2,1)S(1)} %get-tuple-element.171), channel_id=1, source_target_pairs={{0,1},{1,0},{2,3},{3,2},{4,5},{5,4},{6,7},{7,6},{8,9},{9,8},{10,11... | collective-permute-start | bytes 1769480 | tf_op jit(solution)/shard_map/ppermute | solution.py:822
  79.9 0.7 copy-start.7
  79.9 2.5 copy-start.18
  80.6 1.5 copy-start.16
  80.6 25.4 %collective-permute-start.8 = (bf16[2,2,4,2,48,384]{5,4,3,2,1,0:T(8,128)(2,1)S(1)}, bf16[2,2,4,2,48,384]{5,4,3,2,1,0:T(8,128)(2,1)}, u32[]{:S(2)}, u32[]{:S(2)}) collective-permute-start(bf16[2,2,4,2,48,384]{5,4,3,2,1,0:T(8,128)(2,1)S(1)} %pad_maximum_fusion.1.own_b), channel_id=1, source_target_pairs={{0,2},{2,0},{4,6},{6,4},{8,10},{10,8},{12,14},{14,12},{16,18},{18,... | collective-permute-start | bytes 3538952 | tf_op jit(solution)/shard_map/ppermute | solution.py:823
  82.1 3.9 slice-start
  82.1 23.9 %collective-permute-start.7 = (bf16[2,2,4,2,48,384]{5,4,3,2,1,0:T(8,128)(2,1)}, bf16[2,2,4,2,48,384]{5,4,3,2,1,0:T(8,128)(2,1)}, u32[]{:S(2)}, u32[]{:S(2)}) collective-permute-start(bf16[2,2,4,2,48,384]{5,4,3,2,1,0:T(8,128)(2,1)} %pad_maximum_fusion.own_a), channel_id=1, source_target_pairs={{0,2},{2,0},{4,6},{6,4},{8,10},{10,8},{12,14},{14,12},{16,18},{18,... | collective-permute-start | bytes 3538952 | tf_op jit(solution)/shard_map/ppermute | solution.py:823
  83.4 15.2 %all-to-all-start.1 = ((f32[32,4,288]{2,1,0:T(4,128)}), f32[32,4,288]{2,1,0:T(4,128)S(1)}, u32[]{:S(2)}, u32[]{:S(2)}) async-start(f32[32,4,288]{2,1,0:T(4,128)} %reshape.204), calls=%async_computation.1 | async-start | bytes 393216 | tf_op jit(solution)/shard_map/all_to_all | solution.py:769
  208.1 17.6 %collective-permute-start.10 = (bf16[8,2,4,48,384]{4,3,2,1,0:T(8,128)(2,1)}, bf16[8,2,4,48,384]{4,3,2,1,0:T(8,128)(2,1)S(1)}, u32[]{:S(2)}, u32[]{:S(2)}) collective-permute-start(bf16[8,2,4,48,384]{4,3,2,1,0:T(8,128)(2,1)} %get-tuple-element.93), channel_id=1, source_target_pairs={{0,2},{2,0},{4,6},{6,4},{8,10},{10,8},{12,14},{14,12},{16,18},{18,... | collective-permute-start | bytes 7077896 | tf_op jit(solution)/shard_map/ppermute | solution.py:823
  208.5 17.3 %collective-permute-start.9 = (bf16[8,2,4,48,384]{4,3,2,1,0:T(8,128)(2,1)}, bf16[8,2,4,48,384]{4,3,2,1,0:T(8,128)(2,1)}, u32[]{:S(2)}, u32[]{:S(2)}) collective-permute-start(bf16[8,2,4,48,384]{4,3,2,1,0:T(8,128)(2,1)} %get-tuple-element.92), channel_id=1, source_target_pairs={{0,2},{2,0},{4,6},{6,4},{8,10},{10,8},{12,14},{14,12},{16,18},{18,... | collective-permute-start | bytes 7077896 | tf_op jit(solution)/shard_map/ppermute | solution.py:823
  208.7 18.6 %copy-start.4 = (bf16[8,2,4,48,384]{4,3,2,1,0:T(8,128)(2,1)S(1)}, bf16[8,2,4,48,384]{4,3,2,1,0:T(8,128)(2,1)}, u32[]{:S(2)}) copy-start(bf16[8,2,4,48,384]{4,3,2,1,0:T(8,128)(2,1)} %get-tuple-element.95) | copy-start | bytes 7077892
  225.7 1.5 copy-start.5
  227.2 3.4 copy-start.6
  229.3 2.2 copy-start.3
  232.8 31.9 %copy-start.1 = (bf16[4,1,2,4,48,384]{5,4,3,2,1,0:T(8,128)(2,1)}, bf16[4,1,2,4,48,384]{5,4,3,2,1,0:T(8,128)(2,1)S(1)}, u32[]{:S(2)}) copy-start(bf16[4,1,2,4,48,384]{5,4,3,2,1,0:T(8,128)(2,1)S(1)} %get-tuple-element.149) | copy-start | bytes 3538948
  232.8 30.9 %collective-permute-start.11 = (bf16[4,2,4,48,384]{4,3,2,0,1:T(8,128)(2,1)}, bf16[4,2,4,48,384]{4,3,2,0,1:T(8,128)(2,1)S(1)}, u32[]{:S(2)}, u32[]{:S(2)}) collective-permute-start(bf16[4,2,4,48,384]{4,3,2,0,1:T(8,128)(2,1)} %fusion), channel_id=1, source_target_pairs={{0,1},{1,0},{2,3},{3,2},{4,5},{5,4},{6,7},{7,6},{8,9},{9,8},{10,11... | collective-permute-start | bytes 3538952 | tf_op jit(solution)/shard_map/ppermute | solution.py:822
  234.2 29.5 %collective-permute-start.12 = (bf16[4,2,4,48,384]{4,3,2,1,0:T(8,128)(2,1)}, bf16[4,2,4,48,384]{4,3,2,1,0:T(8,128)(2,1)S(1)}, u32[]{:S(2)}, u32[]{:S(2)}) collective-permute-start(bf16[4,2,4,48,384]{4,3,2,1,0:T(8,128)(2,1)} %get-tuple-element.108), channel_id=1, source_target_pairs={{0,4},{2,6},{4,0},{6,2},{8,12},{10,14},{12,8},{14,10},{16,20},{18,... | collective-permute-start | bytes 3538952 | tf_op jit(solution)/shard_map/ppermute | solution.py:823
  263.1 18.8 %collective-permute-start.15 = (bf16[8,2,2,48,384]{4,3,2,1,0:T(8,128)(2,1)}, bf16[8,2,2,48,384]{4,3,2,1,0:T(8,128)(2,1)}, u32[]{:S(2)}, u32[]{:S(2)}) collective-permute-start(bf16[8,2,2,48,384]{4,3,2,1,0:T(8,128)(2,1)} %get-tuple-element.115), channel_id=1, source_target_pairs={{0,2},{2,0},{4,6},{6,4},{8,10},{10,8},{12,14},{14,12},{16,18},{18,... | collective-permute-start | bytes 3538952 | tf_op jit(solution)/shard_map/ppermute | solution.py:823
  263.2 18.7 %collective-permute-start.16 = (bf16[8,2,2,48,384]{4,3,2,1,0:T(8,128)(2,1)}, bf16[8,2,2,48,384]{4,3,2,1,0:T(8,128)(2,1)}, u32[]{:S(2)}, u32[]{:S(2)}) collective-permute-start(bf16[8,2,2,48,384]{4,3,2,1,0:T(8,128)(2,1)} %get-tuple-element.116), channel_id=1, source_target_pairs={{0,2},{2,0},{4,6},{6,4},{8,10},{10,8},{12,14},{14,12},{16,18},{18,... | collective-permute-start | bytes 3538952 | tf_op jit(solution)/shard_map/ppermute | solution.py:823
  263.7 2.0 copy-start.10
  263.7 2.0 copy-start.12
  265.7 16.2 %collective-permute-start.13 = (bf16[4,4,48,384]{3,2,1,0:T(8,128)(2,1)}, bf16[4,4,48,384]{3,2,1,0:T(8,128)(2,1)S(1)}, u32[]{:S(2)}, u32[]{:S(2)}) collective-permute-start(bf16[4,4,48,384]{3,2,1,0:T(8,128)(2,1)} %fusion.6), channel_id=1, source_target_pairs={{0,4},{2,6},{4,0},{6,2},{8,12},{10,14},{12,8},{14,10},{16,20},{18,... | collective-permute-start | bytes 1769480 | tf_op jit(solution)/shard_map/ppermute | solution.py:823
  266.1 15.9 %collective-permute-start.14 = (bf16[4,4,48,384]{3,2,1,0:T(8,128)(2,1)}, bf16[4,4,48,384]{3,2,1,0:T(8,128)(2,1)S(1)}, u32[]{:S(2)}, u32[]{:S(2)}) collective-permute-start(bf16[4,4,48,384]{3,2,1,0:T(8,128)(2,1)} %fusion.5), channel_id=1, source_target_pairs={{0,1},{1,0},{2,3},{3,2},{4,5},{5,4},{6,7},{7,6},{8,9},{9,8},{10,11... | collective-permute-start | bytes 1769480 | tf_op jit(solution)/shard_map/ppermute | solution.py:822
  266.3 16.4 %copy-start.2 = (bf16[4,1,2,4,48,384]{5,4,3,2,1,0:T(8,128)(2,1)S(1)}, bf16[4,1,2,4,48,384]{5,4,3,2,1,0:T(8,128)(2,1)}, u32[]{:S(2)}) copy-start(bf16[4,1,2,4,48,384]{5,4,3,2,1,0:T(8,128)(2,1)} %copy-done.1) | copy-start | bytes 3538948
  266.3 16.4 %copy-start.11 = (bf16[4,2,4,48,384]{4,3,2,0,1:T(8,128)(2,1)S(1)}, bf16[4,2,4,48,384]{4,3,2,0,1:T(8,128)(2,1)}, u32[]{:S(2)}) copy-start(bf16[4,2,4,48,384]{4,3,2,0,1:T(8,128)(2,1)} %copy-done.10) | copy-start | bytes 3538948
  266.3 16.4 %copy-start.13 = (bf16[4,2,4,48,384]{4,3,2,1,0:T(8,128)(2,1)S(1)}, bf16[4,2,4,48,384]{4,3,2,1,0:T(8,128)(2,1)}, u32[]{:S(2)}) copy-start(bf16[4,2,4,48,384]{4,3,2,1,0:T(8,128)(2,1)} %copy-done.12) | copy-start | bytes 3538948
  281.9 0.8 copy-start.20
  282.8 1.4 copy-start.15
  285.6 1.5 copy-start.14
  289.4 4.3 %copy-start.21 = (f32[9,3072]{1,0:T(8,128)S(1)}, f32[9,3072]{1,0:T(8,128)}, u32[]{:S(2)}) copy-start(f32[9,3072]{1,0:T(8,128)} %get-tuple-element.139) | copy-start | bytes 331780
  290.4 4.8 %copy-start.23 = (f32[9,768]{1,0:T(8,128)S(1)}, f32[9,768]{1,0:T(8,128)}, u32[]{:S(2)}) copy-start(f32[9,768]{1,0:T(8,128)} %get-tuple-element.138) | copy-start | bytes 82948
  290.4 15.4 %collective-permute-start.17 = (bf16[4,2,2,48,384]{4,3,2,0,1:T(8,128)(2,1)}, bf16[4,2,2,48,384]{4,3,2,0,1:T(8,128)(2,1)}, u32[]{:S(2)}, u32[]{:S(2)}) collective-permute-start(bf16[4,2,2,48,384]{4,3,2,0,1:T(8,128)(2,1)} %fusion.2), channel_id=1, source_target_pairs={{0,1},{1,0},{2,3},{3,2},{4,5},{5,4},{6,7},{7,6},{8,9},{9,8},{10,11... | collective-permute-start | bytes 1769480 | tf_op jit(solution)/shard_map/ppermute | solution.py:822
  292.1 14.8 %collective-permute-start.18 = (bf16[4,2,2,48,384]{4,3,2,0,1:T(8,128)(2,1)}, bf16[4,2,2,48,384]{4,3,2,0,1:T(8,128)(2,1)}, u32[]{:S(2)}, u32[]{:S(2)}) collective-permute-start(bf16[4,2,2,48,384]{4,3,2,0,1:T(8,128)(2,1)} %fusion.1), channel_id=1, source_target_pairs={{0,4},{2,6},{4,0},{6,2},{8,12},{10,14},{12,8},{14,10},{16,20},{18,... | collective-permute-start | bytes 1769480 | tf_op jit(solution)/shard_map/ppermute | solution.py:823
  310.0 29.2 %all-to-all-start.2 = ((f32[32,1,3312]{2,1,0:T(1,128)}), f32[32,1,3312]{2,1,0:T(1,128)S(1)}, u32[]{:S(2)}, u32[]{:S(2)}) async-start(f32[32,1,3312]{2,1,0:T(1,128)} %reshape.229), calls=%async_computation.2 | async-start | bytes 851968 | tf_op jit(solution)/shard_map/all_to_all | solution.py:769
  314.2 12.7 %collective-permute-start.20 = (bf16[4,2,48,384]{3,2,1,0:T(8,128)(2,1)S(1)}, bf16[4,2,48,384]{3,2,1,0:T(8,128)(2,1)}, u32[]{:S(2)}, u32[]{:S(2)}) collective-permute-start(bf16[4,2,48,384]{3,2,1,0:T(8,128)(2,1)S(1)} %fusion.24), channel_id=1, source_target_pairs={{0,1},{1,0},{2,3},{3,2},{4,5},{5,4},{6,7},{7,6},{8,9},{9,8},{10,11... | collective-permute-start | bytes 884744 | tf_op jit(solution)/shard_map/ppermute | solution.py:822
  316.0 29.4 %collective-permute-start.21 = (bf16[8,48,384]{2,1,0:T(8,128)(2,1)}, bf16[8,48,384]{2,1,0:T(8,128)(2,1)}, u32[]{:S(2)}, u32[]{:S(2)}) collective-permute-start(bf16[8,48,384]{2,1,0:T(8,128)(2,1)} %get-tuple-element.142), channel_id=1, source_target_pairs={{0,8},{2,10},{4,12},{6,14},{8,16},{10,18},{12,20},{14,22},{16,24},... | collective-permute-start | bytes 884744 | tf_op jit(solution)/shard_map/ppermute | solution.py:839
  317.5 28.1 %collective-permute-start.22 = (bf16[8,48,384]{2,1,0:T(8,128)(2,1)}, bf16[8,48,384]{2,1,0:T(8,128)(2,1)}, u32[]{:S(2)}, u32[]{:S(2)}) collective-permute-start(bf16[8,48,384]{2,1,0:T(8,128)(2,1)} %get-tuple-element.143), channel_id=1, source_target_pairs={{0,16},{2,18},{4,20},{6,22},{8,24},{10,26},{12,28},{14,30},{16,0},... | collective-permute-start | bytes 884744 | tf_op jit(solution)/shard_map/ppermute | solution.py:839
  319.9 25.7 %collective-permute-start.23 = (bf16[8,48,384]{2,1,0:T(8,128)(2,1)}, bf16[8,48,384]{2,1,0:T(8,128)(2,1)}, u32[]{:S(2)}, u32[]{:S(2)}) collective-permute-start(bf16[8,48,384]{2,1,0:T(8,128)(2,1)} %get-tuple-element.144), channel_id=1, source_target_pairs={{0,24},{2,26},{4,28},{6,30},{8,0},{10,2},{12,4},{14,6},{16,8},{18,... | collective-permute-start | bytes 884744 | tf_op jit(solution)/shard_map/ppermute | solution.py:839
  323.0 21.2 %collective-permute-start.19 = (bf16[4,2,48,384]{3,2,1,0:T(8,128)(2,1)}, bf16[4,2,48,384]{3,2,1,0:T(8,128)(2,1)}, u32[]{:S(2)}, u32[]{:S(2)}) collective-permute-start(bf16[4,2,48,384]{3,2,1,0:T(8,128)(2,1)} %fusion.25), channel_id=1, source_target_pairs={{0,4},{2,6},{4,0},{6,2},{8,12},{10,14},{12,8},{14,10},{16,20},{18,... | collective-permute-start | bytes 884744 | tf_op jit(solution)/shard_map/ppermute | solution.py:823
  339.2 0.8 copy-start.8
  341.4 40.6 %all-to-all-start.3 = ((f32[32,128,48]{1,2,0:T(8,128)}), f32[32,128,48]{1,2,0:T(8,128)S(1)}, u32[]{:S(2)}, u32[]{:S(2)}) async-start(f32[32,128,48]{1,2,0:T(8,128)} %bitcast.73), calls=%async_computation.3 | async-start | bytes 1572864 | tf_op jit(solution)/shard_map/all_to_all | solution.py:769
  345.6 19.6 %collective-permute-start.24 = (bf16[4,48,384]{2,1,0:T(8,128)(2,1)S(1)}, bf16[4,48,384]{2,1,0:T(8,128)(2,1)S(1)}, u32[]{:S(2)}, u32[]{:S(2)}) collective-permute-start(bf16[4,48,384]{2,1,0:T(8,128)(2,1)S(1)} %get-tuple-element.145), channel_id=1, source_target_pairs={{0,8},{2,10},{4,12},{6,14},{8,16},{10,18},{12,20},{14,22},{16,24},... | collective-permute-start | bytes 442376 | tf_op jit(solution)/shard_map/ppermute | solution.py:839
  357.5 20.7 %collective-permute-start.25 = (bf16[4,48,384]{2,1,0:T(8,128)(2,1)S(1)}, bf16[4,48,384]{2,1,0:T(8,128)(2,1)S(1)}, u32[]{:S(2)}, u32[]{:S(2)}) collective-permute-start(bf16[4,48,384]{2,1,0:T(8,128)(2,1)S(1)} %get-tuple-element.166), channel_id=1, source_target_pairs={{0,16},{2,18},{4,20},{6,22},{8,24},{10,26},{12,28},{14,30},{16,0},... | collective-permute-start | bytes 442376 | tf_op jit(solution)/shard_map/ppermute | solution.py:839
  360.8 17.4 %collective-permute-start.26 = (bf16[4,48,384]{2,1,0:T(8,128)(2,1)S(1)}, bf16[4,48,384]{2,1,0:T(8,128)(2,1)S(1)}, u32[]{:S(2)}, u32[]{:S(2)}) collective-permute-start(bf16[4,48,384]{2,1,0:T(8,128)(2,1)S(1)} %get-tuple-element.167), channel_id=1, source_target_pairs={{0,24},{2,26},{4,28},{6,30},{8,0},{10,2},{12,4},{14,6},{16,8},{18,... | collective-permute-start | bytes 442376 | tf_op jit(solution)/shard_map/ppermute | solution.py:839
  362.9 16.7 %copy-start.9 = (f32[32,1,3312]{2,0,1:T(8,128)S(1)}, f32[32,1,3312]{2,0,1:T(8,128)}, u32[]{:S(2)}) copy-start(f32[32,1,3312]{2,0,1:T(8,128)} %copy-done.8) | copy-start | bytes 1271812
  363.6 17.4 %copy-start.19 = (bf16[16,128,48]{1,2,0:T(8,128)(2,1)S(1)}, bf16[16,128,48]{1,2,0:T(8,128)(2,1)}, u32[]{:S(2)}) copy-start(bf16[16,128,48]{1,2,0:T(8,128)(2,1)} %copy-done.18) | copy-start | bytes 589828
Sparse Core Ops, SparseCore 0:
  11.6 92.9 all-gather.3

commit v5 on v4

--- a/solution.py
+++ b/solution.py
@@ -17,6 +17,7 @@
 EPS = 1e-06
 NJ, NK, UR, UC = 16, 2, 48, 384
 CHUNK = 768
+HEADS = 3
 MIB = 1024 * 1024
 BF = jnp.bfloat16
 F32 = jnp.float32
@@ -308,7 +309,7 @@
         mixed_t[rows, :] = dot(values, probs, 1, 0).astype(BF)
         return 0
 
-    lax.fori_loop(0, H, head, 0, unroll=6)
+    lax.fori_loop(0, H, head, 0, unroll=HEADS)
     merged[0] = mixed_t[...].T
     projected = dot(merged[0], full_proj[...], 1, 1)
     attn[0] = projected.astype(BF)
@@ -498,8 +499,8 @@
 
 def attend_back_kernel(
     tag_ref, resid, shrunk, d_second, gradient, attn, mods, qkv, lse, proj_t,
-    output, d_resid, d_qkv, d_attn_t, sums,
-    bias, d_mixed, d_attn,
+    output, d_resid, d_qkv, d_attn_t, item_sums,
+    bias, d_mixed, d_attn, sums,
 ):
     @pl.when(pl.program_id(0) == 0)
     def _():
@@ -558,7 +559,11 @@
         d_qkv[key_rows, :] = dot(queries, d_scores, 1, 1).astype(BF)
         return 0
 
-    lax.fori_loop(0, H, head, 0, unroll=6)
+    lax.fori_loop(0, H, head, 0, unroll=HEADS)
+
+    @pl.when(pl.program_id(0) == pl.num_programs(0) - 1)
+    def _():
+        item_sums[...] = jnp.sum(sums[...], axis=2)
 
 
 def attend_back(part, tag, resid, shrunk, d_second, gradient, attn, mods, qkv, lse, proj_t):
@@ -585,19 +590,20 @@
             group_spec(GROUP, D),
             pl.BlockSpec((3 * D, GROUP), lambda g: (0, g)),
             pl.BlockSpec((D, GROUP), lambda g: (0, g)),
-            whole((4, 4, 8, D)),
+            whole((4, 4, D)),
         ],
         out_shape=[
             jax.ShapeDtypeStruct((2, GROUP, D), BF),
             jax.ShapeDtypeStruct((2, GROUP, D), F32),
             jax.ShapeDtypeStruct((3 * D, 2 * GROUP), BF),
             jax.ShapeDtypeStruct((D, 2 * GROUP), BF),
-            jax.ShapeDtypeStruct((4, 4, 8, D), F32),
+            jax.ShapeDtypeStruct((4, 4, D), F32),
         ],
         scratch_shapes=[
             pltpu.VMEM((GROUP, GROUP), F32),
             pltpu.VMEM((D, GROUP), BF),
             pltpu.VMEM((GROUP, D), BF),
+            pltpu.VMEM((4, 4, 8, D), F32),
         ],
         compiler_params=params(),
         cost_estimate=cost(16),
@@ -643,7 +649,7 @@
 
 
 def conv_back_kernel(
-    tag_ref, d_qkv0, d_qkv1, weight, norm, mods, kernel, d_first, g_kernel, d_conv
+    tag_ref, d_qkv0, d_qkv1, weight, norm, mods, kernel, d_first, g_kernel, item_sums, d_conv
 ):
     step = pl.program_id(0)
 
@@ -663,6 +669,7 @@
         def lanes(i, _):
             cols = pl.ds(pl.multiple_of(i * 128, 128), 128)
             taps = [jnp.broadcast_to(kernel[t : t + 1, cols], (16, 128)) for t in range(9)]
+            sums = [[jnp.zeros((16, 128), F32) for _ in range(2)] for _ in range(2)]
 
             def load_grad(g, p):
                 return d_conv[g, p * 16 : p * 16 + 16, cols]
@@ -674,11 +681,18 @@
                 return norm[g, p * 16 : p * 16 + 16, cols] * (1.0 + scale) + shift
 
             def emit(g, p, value):
-                d_first[g, p * 16 : p * 16 + 16, cols] = value
+                rows = slice(p * 16, p * 16 + 16)
+                d_first[g, rows, cols] = value
+                sums[0][p // 8] += value
+                sums[1][p // 8] += value * norm[g, rows, cols]
 
             grads = conv_back_rows(load_grad, load_field, taps, left, right, keep, emit)
             for t in range(9):
                 g_kernel[t : t + 1, cols] = jnp.sum(grads[t], axis=0, keepdims=True)
+            for kind in range(2):
+                for item in range(4):
+                    part = sums[kind][item // 2][8 * (item % 2) : 8 * (item % 2) + 8]
+                    item_sums[kind, item : item + 1, cols] = jnp.sum(part, axis=0, keepdims=True)
             return 0
 
         lax.fori_loop(0, D // 128, lanes, 0)
@@ -698,10 +712,11 @@
             whole((6, 4, 8, D)),
             whole((9, D)),
         ],
-        out_specs=[whole((4, GROUP, D)), whole((9, D))],
+        out_specs=[whole((4, GROUP, D)), whole((9, D)), whole((2, 4, D))],
         out_shape=[
             jax.ShapeDtypeStruct((4, GROUP, D), F32),
             jax.ShapeDtypeStruct((9, D), F32),
+            jax.ShapeDtypeStruct((2, 4, D), F32),
         ],
         scratch_shapes=[pltpu.VMEM((4, GROUP, D), F32)],
         compiler_params=params(),
@@ -712,20 +727,14 @@
 
 def finish_kernel(
     d_first, norm, factor, d_resid0, d_resid1, output0, output1, mods,
-    block_output, input_grad, sums, total,
+    block_output, input_grad, total,
 ):
     half = pl.program_id(0) // 2
-
-    @pl.when(pl.program_id(0) == 0)
-    def _():
-        sums[...] = jnp.zeros_like(sums)
 
     for g in range(4):
         base = (d_resid0, d_resid1)[g // 2]
         value = d_first[g]
         normal = norm[g]
-        sums[0, pl.ds(2 * half, 2)] += jnp.sum(value.reshape(4, 2, 8, D), axis=0)
-        sums[1, pl.ds(2 * half, 2)] += jnp.sum((value * normal).reshape(4, 2, 8, D), axis=0)
         inner = (value.reshape(4, 2, 8, D) * (1.0 + quadrant_rows(mods, 1, half))).reshape(64, D)
         mean = jnp.mean(inner, axis=-1, keepdims=True)
         along = jnp.mean(inner * normal, axis=-1, keepdims=True)
@@ -749,11 +758,10 @@
         finish_kernel,
         grid=(4,),
         in_specs=[split(4, D), split(4, D), split(4, 1)] + [split(2, D)] * 4 + [whole((6, 4, 8, D))],
-        out_specs=[flat, flat, whole((2, 4, 8, D))],
+        out_specs=[flat, flat],
         out_shape=[
             jax.ShapeDtypeStruct((TOK, D), BF),
             jax.ShapeDtypeStruct((TOK, D), F32),
-            jax.ShapeDtypeStruct((2, 4, 8, D), F32),
         ],
         scratch_shapes=[pltpu.VMEM((4, 64, D), F32)],
         compiler_params=params(),
@@ -794,18 +802,19 @@
     return weight.reshape(NJ, units, UR, NK, UC).transpose(0, 3, 1, 2, 4)
 
 
-def gather_projections(nd, nf, qkv, proj):
-    if (nd, nf) == (NJ, NK):
-        own = jnp.concatenate([units_of(qkv), units_of(proj)])
-        turns = [
-            lax.ppermute(own, "dp", [(i, (i - 4 * step) % NJ) for i in range(NJ)])
-            for step in range(1, 4)
-        ]
-        a = jnp.stack([own[:2]] + [turn[:2] for turn in turns])
-        b = jnp.stack([own[2:]] + [turn[2:] for turn in turns])
-        a, b = jnp.stack([a, swap(a, 2)]), jnp.stack([b, swap(b, None)])
-        a, b = jnp.stack([a, swap(a, None)]), jnp.stack([b, swap(b, 2)])
-        return a, b, swap(a, 1), swap(b, 1)
+def project_turns(own):
+    turns = [
+        lax.ppermute(own, "dp", [(i, (i - 4 * step) % NJ) for i in range(NJ)])
+        for step in range(1, 4)
+    ]
+    return turns
+
+
+def widen(a, b, bit_a, bit_b):
+    return jnp.stack([a, swap(a, bit_a)]), jnp.stack([b, swap(b, bit_b)])
+
+
+def all_projections(qkv, proj):
     units = jnp.concatenate([all_units(full_rows(qkv), 3), all_units(full_rows(proj), 1)], axis=2)
     units = units.reshape((4, 2, 2) + units.shape[1:])
     first, rest = units[:, :, :, :, :2], units[:, :, :, :, 2:]
@@ -848,8 +857,8 @@
     return own
 
 
-def tie(value, *others):
-    return lax.optimization_barrier((value,) + others)
+def after(value, *others):
+    return lax.optimization_barrier((value,) + others)[0]
 
 
 def own_shard(nd, nf, kind, units):
@@ -870,27 +879,47 @@
     return jnp.stack([keep, send], axis=1).reshape((-1,) + keep.shape[1:])
 
 
-def condition(nd, nf, timesteps, classes, step_table, class_table, attn_kernel, ffn_kernel):
-    slots = nd * nf
-    mine = jnp.concatenate([timesteps[0], classes[0]])[None]
-    ids = exchange(jnp.broadcast_to(mine, (slots, 8)))
+def look_up(ids, step_table, class_table):
     first_row = lax.axis_index("fsdp") * step_table.shape[0]
     own = first_row + jnp.arange(step_table.shape[0], dtype=jnp.int32)
     step_hot = (ids[:, :4].reshape(-1, 1) == own[None, :]).astype(BF)
     class_hot = (ids[:, 4:].reshape(-1, 1) == own[None, :]).astype(BF)
-    part = jnp.dot(step_hot, step_table, preferred_element_type=F32) + jnp.dot(
-        class_hot, class_table, preferred_element_type=F32
-    )
-    cond = lax.psum(part, "fsdp")
+    return step_hot, class_hot, dot(step_hot, step_table, 1, 0) + dot(class_hot, class_table, 1, 0)
+
+
+def share_act(nd, cond, attn_kernel, ffn_kernel):
+    items, width = cond.shape
     act = jax.nn.silu(cond).astype(BF)
-    items, width = act.shape
     filters = jnp.concatenate([attn_kernel, ffn_kernel], axis=1).reshape(-1, width)
     sent = lax.all_gather(jnp.concatenate([act, filters], axis=0), "dp")
     act_all = sent[:, :items].transpose(1, 0, 2).reshape(items, nd * width)
     filters = sent[:, items:].reshape(nd, 9, -1).astype(F32)
     attn_full = filters[:, :, : attn_kernel.shape[1]].transpose(1, 0, 2).reshape(9, -1)
     ffn_full = filters[:, :, attn_kernel.shape[1] :].transpose(1, 0, 2).reshape(9, -1)
-    return step_hot, class_hot, cond, act_all, attn_full, ffn_full
+    return act_all, attn_full, ffn_full
+
+
+def exchange_columns(nd, nf, d_act):
+    rows, items = d_act.shape
+    if (nd, nf) == (NJ, NK):
+        return lax.all_to_all(d_act.reshape(nd, rows // nd, items), "dp", 0, 0, tiled=True)
+    spread = lax.dynamic_update_slice_in_dim(
+        jnp.zeros((rows * nf, items), F32), d_act, lax.axis_index("fsdp") * rows, axis=0
+    )
+    spread = spread.reshape(nd, 1, -1, items)
+    spread = jnp.broadcast_to(spread, (nd, nf) + spread.shape[2:])
+    return exchange(spread.reshape((nd * nf,) + spread.shape[2:]))
+
+
+def own_columns(nd, nf, terms):
+    part = terms.sum(axis=0)
+    if (nd, nf) != (NJ, NK):
+        return part
+    order = [(j * NK + k, k * NJ + j) for j in range(NJ) for k in range(NK)]
+    own = lax.ppermute(part, BOTH, order)
+    other = lax.ppermute(part, BOTH, [(i, o ^ 1) for i, o in order])
+    first = lax.axis_index("fsdp") == 0
+    return jnp.concatenate([jnp.where(first, own, other), jnp.where(first, other, own)])
 
 
 def body(
@@ -907,19 +936,42 @@
         where = jnp.stack(where).astype(jnp.int32)
     else:
         where = jnp.stack([tag] + [jnp.int32(0)] * 4)
-    projections = gather_projections(nd, nf, qkv_weight, proj_weight)
     packed = gather_feed(nd, nf, expand_weight, shrink_weight)
     tokens, gradient, norm, factor = prepare(latents, cotangent)
-    step_hot, class_hot, cond, act_all, attn_full, ffn_full = condition(
-        nd, nf, timesteps, classes, step_table, class_table, attn_kernel, ffn_kernel
-    )
+    mine = jnp.concatenate([timesteps[0], classes[0]])[None]
+    mine = jnp.broadcast_to(mine, (slots, 8))
+    if square:
+        own = jnp.concatenate([units_of(qkv_weight), units_of(proj_weight)])
+        own = after(own, mine)
+        turns = project_turns(own)
+    ids = exchange(mine)
+    if square:
+        ids = after(ids, norm)
+    step_hot, class_hot, part = look_up(ids, step_table, class_table)
+    if square:
+        cond = part + swap(part, None)
+        a = jnp.stack([own[:2]] + [turn[:2] for turn in turns])
+        b = jnp.stack([own[2:]] + [turn[2:] for turn in turns])
+        a, b = widen(a, b, 2, None)
+        cond = after(cond, a, b)
+        next_a, next_b = swap(a, None), swap(b, 2)
+    else:
+        cond = lax.psum(part, "fsdp")
+    act_all, attn_full, ffn_full = share_act(nd, cond, attn_kernel, ffn_kernel)
+    if square:
+        next_a, next_b = after(next_a, act_all), after(next_b, act_all)
     height, width = modulation_weight.shape
     act_rows = lax.dynamic_slice_in_dim(
         act_all, lax.axis_index("fsdp") * height, height, axis=1
     )
-    part = jnp.dot(act_rows, modulation_weight, preferred_element_type=F32)
-    part = exchange(part.reshape(slots, 4, width)).reshape(nd, nf, 4, width)
-    mod_rows = part.sum(axis=1).transpose(1, 0, 2).reshape(4, nd * width)
+    terms = dot(act_rows, modulation_weight, 1, 0)
+    terms = exchange(terms.reshape(slots, 1, 4 * width)).reshape(nd, nf, 4, width)
+    if square:
+        a, b = jnp.stack([a, next_a]), jnp.stack([b, next_b])
+        projections = (a, b, swap(a, 1), swap(b, 1))
+    else:
+        projections = all_projections(qkv_weight, proj_weight)
+    mod_rows = terms.sum(axis=1).transpose(1, 0, 2).reshape(4, nd * width)
     chosen = jnp.where(tag == 1, mod_rows, mod_rows[:1])
     mods = jnp.broadcast_to(chosen.reshape(4, 6, 1, D).transpose(1, 0, 2, 3), (6, 4, 8, D))
 
@@ -941,10 +993,10 @@
         return value.reshape((4, 2) + value.shape[1:])
 
     if square:
-        d_qkv0, got_e, got_s = tie(d_qkv0, got_e, got_s)
+        got_e, got_s = after(got_e, d_qkv0), after(got_s, d_qkv0)
         keep_e, out_e = halve(grid(keep_e), grid(got_e), 2, None)
         keep_s, out_s = halve(grid(keep_s), grid(got_s), 1, 2)
-        d_second, d_qkv0, out_e, out_s = tie(d_second, d_qkv0, out_e, out_s)
+        d_second = after(d_second, out_e, out_s)
         got_e, got_s = swap(out_e, None), swap(out_s, 2)
     output1, d_resid1, d_qkv1, d_attn1, later1 = attend_back(
         1, where, resid, shrunk, d_second, *back, proj_t
@@ -955,35 +1007,61 @@
     )
     if square:
         got_a, got_b = swap(send_a, 1), swap(send_b, 1)
-        keep_a, got_e, got_s = tie(keep_a, got_e, got_s)
+        got_e, got_s = after(got_e, keep_a), after(got_s, keep_a)
         keep_e, out_e = halve(keep_e, got_e, 1, 2)
         keep_s, out_s = halve(keep_s, got_s, 1, None)
-        norm, out_e, out_s = tie(norm, out_e, out_s)
+        full_qkv = after(full_qkv, out_e, out_s)
         got_e, got_s = swap(out_e, 2), swap(out_s, None)
-    d_first, g_attn = conv_back(where, d_qkv, full_qkv, norm, mods, attn_full)
-    if square:
-        d_first, got_e, got_s, got_a, got_b = tie(d_first, got_e, got_s, got_a, got_b)
+    d_first, g_attn, early = conv_back(where, d_qkv, full_qkv, norm, mods, attn_full)
+    if square:
+        got_e, got_s, got_a, got_b = (after(x, d_first) for x in (got_e, got_s, got_a, got_b))
+        early, g_attn = after(early, got_e, got_s), after(g_attn, got_e, got_s)
+    later = later0 + later1
+    rows = jnp.concatenate([early, later], axis=0)
+    rows = rows.transpose(1, 0, 2).reshape(4, 6 * D)
+    alone = jnp.concatenate([rows.sum(axis=0, keepdims=True), jnp.zeros((3, 6 * D), F32)])
+    d_mod = jnp.where(tag == 1, rows, alone).astype(BF)
+    filters = jnp.concatenate([g_attn.reshape(9, nd, -1), g_ffn.reshape(9, nd, -1)], axis=2)
+    pieces = jnp.concatenate(
+        [
+            d_mod.reshape(4, nd, width).transpose(1, 0, 2).reshape(nd, -1),
+            filters.astype(BF).transpose(1, 0, 2).reshape(nd, -1),
+        ],
+        axis=1,
+    )
+    pieces = jnp.broadcast_to(pieces[:, None], (nd, nf, pieces.shape[1])).reshape(slots, 1, -1)
+    if square:
         keep_a, out_a = halve(grid(keep_a), grid(got_a), 2, None)
         keep_b, out_b = halve(grid(keep_b), grid(got_b), 1, 2)
-        feeding = jnp.concatenate([keep_e + got_e, keep_s + got_s], axis=1)
-        sends = last_sends(feeding)
-        d_first, out_a, out_b, *sends = tie(d_first, out_a, out_b, *sends)
+        e = halve(keep_e.reshape((2, 2) + keep_e.shape[1:]), got_e.reshape((2, 2) + got_e.shape[1:]), 1, 4)
+        s = halve(keep_s.reshape((2, 2) + keep_s.shape[1:]), got_s.reshape((2, 2) + got_s.shape[1:]), 1, 4)
+        feeding, out_f = (jnp.concatenate(pair, axis=1) for pair in zip(e, s))
+        d_first = after(d_first, out_a, out_b, out_f, pieces)
         got_a, got_b = swap(out_a, None), swap(out_b, 2)
-        got_feeding = last_swaps(sends)
-    block_output, input_grad, early = finish(
+        got_f = swap(out_f, 4)
+    got = exchange(pieces)[:, 0]
+    block_output, input_grad = finish(
         d_first, norm, factor, (d_resid0, d_resid1), (output0, output1), mods
     )
-    later = later0 + later1
-    if square:
-        later, got_a, got_b = tie(later, got_a, got_b)
+    if square:
+        got = after(got, input_grad)
+        got_a, got_b, got_f = (after(x, got) for x in (got_a, got_b, got_f))
         keep_a, out_a = halve(keep_a, got_a, 1, 2)
         keep_b, out_b = halve(keep_b, got_b, 1, None)
         got_a, got_b = swap(out_a, 2), swap(out_b, None)
+    d_mod_all = got[:, : 4 * width].reshape(slots * 4, width)
+    d_act = dot(modulation_weight, d_mod_all, 1, 1)
+    own_act = exchange_columns(nd, nf, d_act)
+    if square:
+        feeding, out_f = halve(feeding, got_f, 0, 8)
         total = jnp.concatenate([keep_a + got_a, keep_b + got_b], axis=1)
         sends = last_sends(total)
-        sends[0], *got_feeding = tie(sends[0], *got_feeding)
-        feeding = last_sum(feeding, got_feeding)
-        total = last_sum(total, last_swaps(sends))
+        sends[1] = jnp.concatenate([sends[1], out_f])
+        own_act = after(own_act, *sends)
+        last = last_swaps(sends)
+        last[1], got_f = last[1][:4], last[1][4:]
+        total = last_sum(total, last)
+        feeding = feeding.astype(F32) + got_f.astype(F32)
         cuts = [total[:3], total[3:], feeding[:4], feeding[4:]]
     else:
         first, rest = both_cores(keep_a, send_a), both_cores(keep_b, send_b)
@@ -997,36 +1075,15 @@
         own_shard(nd, nf, kind, cut)
         for kind, cut in zip(("qkv", "proj", "expand", "shrink"), cuts)
     ]
-    rows = jnp.concatenate([early, later], axis=0).sum(axis=2)
-    rows = rows.transpose(1, 0, 2).reshape(4, 6 * D)
-    alone = jnp.concatenate([rows.sum(axis=0, keepdims=True), jnp.zeros((3, 6 * D), F32)])
-    d_mod = jnp.where(tag == 1, rows, alone).astype(BF)
-    filters = jnp.concatenate([g_attn.reshape(9, nd, -1), g_ffn.reshape(9, nd, -1)], axis=2)
-    pieces = jnp.concatenate(
-        [
-            d_mod.astype(F32).reshape(4, nd, width).transpose(1, 0, 2).reshape(nd, -1),
-            filters.transpose(1, 0, 2).reshape(nd, -1),
-        ],
-        axis=1,
-    )
-    pieces = jnp.broadcast_to(pieces[:, None], (nd, nf, pieces.shape[1])).reshape(slots, 1, -1)
-    got = exchange(pieces)[:, 0]
-    d_mod_all = got[:, : 4 * width].reshape(slots * 4, width).astype(BF)
-    filters = got[:, 4 * width :].sum(axis=0).reshape(9, -1)
+    filters = got[:, 4 * width :].astype(F32).sum(axis=0).reshape(9, -1)
     modulation_grad = dot(act_rows, d_mod_all, 0, 0)
-    d_act = dot(d_mod_all, modulation_weight, 1, 1)
-    spread = lax.dynamic_update_slice_in_dim(
-        jnp.zeros((slots * 4, D), F32), d_act, lax.axis_index("fsdp") * height, axis=1
-    )
-    spread = spread.reshape(slots * 4, nd, 1, -1).transpose(1, 2, 0, 3)
-    spread = jnp.broadcast_to(spread, (nd, nf) + spread.shape[2:])
-    d_act = exchange(spread.reshape((slots,) + spread.shape[2:])).sum(axis=0)
     gate = jax.nn.sigmoid(cond)
-    d_cond = d_act * (gate * (1.0 + cond * (1.0 - gate)))
+    d_cond = own_columns(nd, nf, own_act)
+    d_cond = d_cond * (gate * (1.0 + cond * (1.0 - gate))).T
 
     def table_grad(hot):
         return lax.dot_general(
-            hot.astype(F32), d_cond, (((0,), (0,)), ((), ())), precision=lax.Precision.HIGHEST
+            hot.astype(F32), d_cond, (((0,), (1,)), ((), ())), precision=lax.Precision.HIGHEST
         )
 
     cut = attn_kernel.shape[1]

time: 392 us -> 374 us (0.954)
  starting transfers between devices: 56.2 us -> 44.4 us
  waiting for transfers between devices: 49.5 us -> 43.1 us
    ppermute x6 -> x3, starting transfers between devices: 20.5 us -> 4.66 us  [last_swaps(): lax.ppermute(sent, 'dp', [(i, (i + 4 * step) % NJ) for i in range(NJ)])]
    all_to_all x4 -> x3, waiting for transfers between devices: 24.2 us -> 13.3 us  [exchange(): return lax.all_to_all(pieces, BOTH, 0, 0, tiled=True)]
    psum x1 -> x0, blocking collectives: 8.1 us -> none  [condition(): cond = lax.psum(part, 'fsdp')]
    all_gather x1, blocking collectives: 27.7 us -> 34.4 us  [share_act(): sent = lax.all_gather(jnp.concatenate([act, filters], axis=0), 'dp')]
    add x4 -> x7, other arithmetic: 6.24 us -> 10.9 us  [halve(): kept = pick(keep, mine, axis) + pick(got, mine, axis)]
    all_to_all x0 -> x1, waiting for transfers between devices: none -> 4.51 us  [exchange_columns(): lax.all_to_all(d_act.reshape(nd, rows // nd, items), 'dp', 0, 0, tiled=True)]
    ppermute x6 -> x3, waiting for transfers between devices: 14.7 us -> 19.2 us  [last_swaps(): lax.ppermute(sent, 'dp', [(i, (i + 4 * step) % NJ) for i in range(NJ)])]
    ppermute x3 -> x5, starting transfers between devices: 6.11 us -> 10.3 us  [the longest x3 6.11 us: project_turns(): lax.ppermute(own, 'dp', [(i, (i - 4 * step) % NJ) for i in range(NJ)])]
  transfers between devices with their start and end apart: 32 -> 33, of which waited for: 9 -> 6; matrix products, arithmetic and copies ran while one was open for 7% -> 10% of each run, Pallas kernels for 29% -> 31%
where the time goes in v5:
time: 374 us; the launch traced here: 372 us
  Pallas kernels  185 us (49%)
  starting transfers between devices  44.4 us (12%)
  waiting for transfers between devices  43.1 us (12%)
  blocking collectives  34.4 us (9%)
  other arithmetic  28.5 us (8%)
  local copies, waits for them, and re-layouts  17.7 us (5%)
  between operations  15.6 us (4%)
  matrix products  3.83 us (1%)
    pallas_call x1, Pallas kernels, feed(): pl.pallas_call(feed_kernel, grid=(FF // CHUNK,), in_specs=[SMEM_SPEC, who...  69.1 us
    pallas_call x2, Pallas kernels, attend_back(): pl.pallas_call(attend_back_kernel, grid=(2,), in_specs=[SMEM_SPEC, pick_g...  35.9 us
    all_gather x1, blocking collectives, share_act(): sent = lax.all_gather(jnp.concatenate([act, filters], axis=0), 'dp')  34.4 us
    pallas_call x1, Pallas kernels, attend(): pl.pallas_call(attend_kernel, grid=(4,), in_specs=[SMEM_SPEC, group_spec(...  33.9 us
    ppermute x3, waiting for transfers between devices, last_swaps(): lax.ppermute(sent, 'dp', [(i, (i + 4 * step) % NJ) for i in range(NJ)])  19.2 us
    pallas_call x1, Pallas kernels, conv_back(): pl.pallas_call(conv_back_kernel, grid=(8 // PAIRS,), in_specs=[SMEM_SPEC,...  16 us
    all_to_all x3, waiting for transfers between devices, exchange(): return lax.all_to_all(pieces, BOTH, 0, 0, tiled=True)  13.3 us
    add x7, other arithmetic, halve(): kept = pick(keep, mine, axis) + pick(got, mine, axis)  10.9 us
  transfers between devices with their start and end apart: 33, of which 6 were waited for; matrix products, arithmetic and copies ran while one was open for 10% of the time, Pallas kernels for 31%

profile of v5, /device:TPU:0, one launch (start us, length us, event | category | flops | bytes accessed | tf_op | source)
XLA Modules:
  0.0 372.5 jit_solution(10881679577616338809)
XLA Ops:
  7.3 1.0 copy.210
  8.3 1.7 pad_maximum_fusion.8
  10.0 5.1 %collective-permute-start.1 = (bf16[4,48,384]{2,1,0:T(8,128)(2,1)S(1)}, bf16[4,48,384]{2,1,0:T(8,128)(2,1)S(1)}, u32[]{:S(2)}, u32[]{:S(2)}) collective-permute-start(bf16[4,48,384]{2,1,0:T(8,128)(2,1)S(1)} %pad_maximum_fusion.9), channel_id=1, source_target_pairs={{0,24},{2,26},{4,28},{6,30},{8,0},{10,2},{12,4},{14,6},{16,8},{18,... | collective-permute-start | bytes 442376 | tf_op jit(solution)/shard_map/ppermute | solution.py:807
  15.1 1.0 collective-permute-start.3
  16.8 5.1 %all-to-all-start = ((s32[32,1,8]{2,1,0:T(1,128)}), s32[32,1,8]{2,1,0:T(1,128)S(1)}, u32[]{:S(2)}, u32[]{:S(2)}) async-start(s32[32,1,8]{2,1,0:T(1,128)} %broadcast_in_dim.20), calls=%async_computation | async-start | bytes 32768 | tf_op jit(solution)/shard_map/all_to_all | solution.py:777
  21.9 6.0 %prepare.1 = (bf16[4,256,768]{2,1,0:T(8,128)(2,1)}, bf16[4,256,768]{2,1,0:T(8,128)(2,1)}, f32[4,256,768]{2,1,0:T(8,128)}, f32[4,256,1]{2,1,0:T(8,128)}) custom-call(bf16[1024,768]{1,0:T(8,128)(2,1)} %latents.1, bf16[1024,768]{1,0:T(8,128)(2,1)} %cotangent.1), custom_call_target="tpu_custom_call" | custom-call | flops 600000000 | bytes 4194304 | tf_op jit(solution)/shard_map/prepare/pallas_call | solution.py:88
  27.9 4.2 %all-to-all-done = s32[32,1,8]{2,1,0:T(1,128)S(1)} async-done(((s32[32,1,8]{2,1,0:T(1,128)}), s32[32,1,8]{2,1,0:T(1,128)S(1)}, u32[]{:S(2)}, u32[]{:S(2)}) %all-to-all-start) | async-done | bytes 1056 | tf_op jit(solution)/shard_map/all_to_all | solution.py:777
  34.6 1.4 collective-permute-start
  36.0 6.0 %collective-permute-done.5 = bf16[4,2,48,384]{3,2,1,0:T(8,128)(2,1)S(1)} collective-permute-done((bf16[4,2,48,384]{3,2,1,0:T(8,128)(2,1)S(1)}, bf16[4,2,48,384]{3,2,1,0:T(8,128)(2,1)S(1)}, u32[]{:S(2)}, u32[]{:S(2)}) %collective-permute-start.5) | collective-permute-done | bytes 294944 | tf_op jit(solution)/shard_map/ppermute | solution.py:831
  43.2 0.8 collective-permute-start.6
  44.0 34.4 %all-gather.1 = bf16[16,173,48]{1,2,0:T(8,128)(2,1)S(1)} all-gather(bf16[1,173,48]{1,2,0:T(8,128)(2,1)S(1)} %maximum_bitcast_fusion.1), channel_id=2, replica_groups=mesh['dp'=16,'fsdp'=2] {'dp'}, dimensions={0}, use_global_device_ids=true | all-gather | bytes 282336 | tf_op jit(solution)/shard_map/all_gather | solution.py:894
  79.0 1.2 pad_maximum_fusion.own_a
  82.0 0.9 reshape.257
  82.9 2.6 all-to-all-start.1
  86.9 0.8 reshape.225.kernel
  87.7 9.1 %all-to-all-done.1 = f32[32,1,1152]{2,1,0:T(1,128)S(1)} async-done(((f32[32,1,1152]{2,1,0:T(1,128)}), f32[32,1,1152]{2,1,0:T(1,128)S(1)}, u32[]{:S(2)}, u32[]{:S(2)}) %all-to-all-start.1) | async-done | bytes 147488 | tf_op jit(solution)/shard_map/all_to_all | solution.py:777
  97.7 0.9 broadcast_in_dim.39.mods
  98.6 6.1 %first_conv.1.conv_in = bf16[4,256,768]{2,1,0:T(8,128)(2,1)} custom-call(s32[1]{0:T(128)S(6)} %copy.212.tag_ref, f32[4,256,768]{2,1,0:T(8,128)} %get-tuple-element.71.norm, f32[6,4,8,768]{3,2,1,0:T(8,128)} %broadcast_in_dim.39.mods, f32[9,768]{1,0:T(8,128)} %reshape.221.kernel), custom_call_target="tpu_custom_call" | custom-call | flops 600000000 | bytes 4194304 | tf_op jit(solution)/shard_map/first_conv/pallas_call | solution.py:224
  104.7 33.9 %attend.1 = (bf16[4,2304,256]{2,1,0:T(8,128)(2,1)}, bf16[4,256,768]{2,1,0:T(8,128)(2,1)}, bf16[4,256,768]{2,1,0:T(8,128)(2,1)}, f32[4,256,768]{2,1,0:T(8,128)}, ...) custom-call(s32[5]{0:T(128)} %stack.85.where.tag_ref, ...), custom_call_target="tpu_custom_call" | custom-call | flops 3800000000 | bytes 4194304 | tf_op jit(solution)/shard_map/attend/pallas_call | solution.py:339
  138.7 69.1 %feed.1 = (f32[4,256,768]{2,1,0:T(8,128)}, f32[4,256,768]{2,1,0:T(8,128)}, bf16[8,2,4,48,384]{4,3,2,1,0:T(8,128)(2,1)}, bf16[8,2,4,48,384]{4,3,2,1,0:T(8,128)(2,...) custom-call(s32[5]{0:T(128)} %stack.85.where.tag_ref, ...), custom_call_target="tpu_custom_call" | custom-call | flops 3800000000 | bytes 4194304 | tf_op jit(solution)/shard_map/feed/pallas_call | solution.py:454
  208.3 17.9 %attend_back_0.1 = (bf16[2,256,768]{2,1,0:T(8,128)(2,1)}, f32[2,256,768]{2,1,0:T(8,128)}, bf16[2304,512]{1,0:T(8,128)(2,1)}, bf16[768,512]{1,0:T(8,128)(2,1)}, f32[4,4,768]{2,1,0:T(4,128)}) custom-call(s32[5]{0:T(128)} %stack.85.where.tag_ref, f32[4,256,768]{2,1,0:T(8,128)} %get-tuple-element.77.resid, f32[4,256,768]{2,1,0:T(8,128)} %get-tuple-element.80.shrunk, ...), custom_call_target="tpu_custom_call" | custom-call | flops 1600000000 | bytes 4194304 | tf_op jit(solution)/shard_map/attend_back_0/pallas_call | solution.py:573
  226.2 1.5 copy-done.3
  227.7 2.4 dynamic-slice_add_fusion.1
  230.1 1.2 fusion.1
  232.5 1.2 fusion
  234.0 18.0 %attend_back_1.1 = (bf16[2,256,768]{2,1,0:T(8,128)(2,1)}, f32[2,256,768]{2,1,0:T(8,128)}, bf16[2304,512]{1,0:T(8,128)(2,1)}, bf16[768,512]{1,0:T(8,128)(2,1)}, f32[4,4,768]{2,1,0:T(4,128)}) custom-call(s32[5]{0:T(128)} %stack.85.where.tag_ref, f32[4,256,768]{2,1,0:T(8,128)} %get-tuple-element.77.resid, f32[4,256,768]{2,1,0:T(8,128)} %get-tuple-element.80.shrunk, ...), custom_call_target="tpu_custom_call" | custom-call | flops 1600000000 | bytes 4194304 | tf_op jit(solution)/shard_map/attend_back_1/pallas_call | solution.py:573
  252.0 9.7 %project_grads.1 = (bf16[8,2,2,48,384]{4,3,2,1,0:T(8,128)(2,1)}, bf16[8,2,2,48,384]{4,3,2,1,0:T(8,128)(2,1)}, bf16[8,2,2,48,384]{4,3,2,1,0:T(8,128)(2,1)}, bf16[8,2,2,48,384]{4,3,2,1,0:T(8,128)(2,1)}) custom-call(s32[5]{0:T(128)} %stack.85.where.tag_ref, bf16[2304,512]{1,0:T(8,128)(2,1)} %get-tuple-element.86.d_qkv0, ...), custom_call_target="tpu_custom_call" | custom-call | flops 800000000 | bytes 4194304 | tf_op jit(solution)/shard_map/project_grads/pallas_call | solution.py:639
  262.5 3.0 bitcast_add_fusion
  265.5 1.8 collective-permute-start.16
  267.2 1.1 collective-permute-start.17
  268.4 16.0 %conv_back.1 = (f32[4,256,768]{2,1,0:T(8,128)}, f32[9,768]{1,0:T(8,128)}, f32[2,4,768]{2,1,0:T(4,128)}) custom-call(s32[5]{0:T(128)} %stack.85.where.tag_ref, bf16[2304,512]{1,0:T(8,128)(2,1)} %get-tuple-element.86.d_qkv0, bf16[2304,512]{1,0:T(8,128)(2,1)} %get-tuple-element.94.d_qkv1, bf16[2304,768]{1,0:T(8,128)(2,1)} %get-tuple-element.102.weight, ...), custom_call_target="tpu_custom_call" | custom-call | flops 1500000000 | bytes 4194304 | tf_op jit(solution)/shard_map/conv_back/pallas_call | solution.py:703
  284.3 1.6 dynamic-slice_add_fusion.2
  285.9 0.9 fusion.2
  287.4 1.4 dynamic-slice_add_fusion.3
  288.9 0.9 fusion.3
  289.7 0.9 collective-permute-start.18
  293.0 1.0 reshape.260
  294.0 2.6 all-to-all-start.2
  296.6 1.2 fusion.19
  297.7 1.0 fusion.21
  298.8 0.9 pad_maximum_fusion.4
  299.7 1.7 collective-permute-start.22
  301.4 8.4 %finish.1 = (bf16[1024,768]{1,0:T(8,128)(2,1)}, f32[1024,768]{1,0:T(8,128)}) custom-call(f32[4,256,768]{2,1,0:T(8,128)} %get-tuple-element.118.d_first, f32[4,256,768]{2,1,0:T(8,128)} %get-tuple-element.71.norm, f32[4,256,1]{2,1,0:T(8,128)} %get-tuple-element.119.factor, f32[2,256,768]{2,1,0:T(8,128)} %get-tuple-element.120.d_resid0, ...), custom_call_target="tpu_custom_call" | custom-call | flops 800000000 | bytes 4194304 | tf_op jit(solution)/shard_map/finish/pallas_call | solution.py:757
  309.7 1.0 add_bitcast_fusion
  311.1 1.0 fusion.24
  312.1 1.6 collective-permute-start.21
  313.7 1.0 fusion.25
  314.7 1.6 collective-permute-start.19
  316.7 0.8 copy.167
  317.5 3.9 %all-to-all-start.3 = ((f32[16,24,128]{2,1,0:T(8,128)}), f32[16,24,128]{2,1,0:T(8,128)S(1)}, u32[]{:S(2)}, u32[]{:S(2)}) async-start(f32[16,24,128]{2,1,0:T(8,128)} %bitcast.72), calls=%async_computation.3 | async-start | bytes 393216 | tf_op jit(solution)/shard_map/all_to_all | solution.py:905
  321.4 1.0 fusion.42
  322.4 1.0 fusion.18
  323.4 1.1 bitcast_add_fusion.8
  324.6 1.1 bitcast_add_fusion.11
  325.8 4.5 %all-to-all-done.3 = f32[16,24,128]{2,1,0:T(8,128)S(1)} async-done(((f32[16,24,128]{2,1,0:T(8,128)}), f32[16,24,128]{2,1,0:T(8,128)S(1)}, u32[]{:S(2)}, u32[]{:S(2)}) %all-to-all-start.3) | async-done | bytes 196640 | tf_op jit(solution)/shard_map/all_to_all | solution.py:905
  331.0 3.5 collective-permute-start.24
  335.9 0.8 collective-permute-start.26
  336.8 1.4 collective-permute-start.25
  338.1 2.4 collective-permute-start.27
  340.6 0.9 fusion.6
  341.5 0.9 fusion.9
  342.5 11.4 %collective-permute-done.25 = bf16[4,48,384]{2,1,0:T(8,128)(2,1)S(1)} collective-permute-done((bf16[4,48,384]{2,1,0:T(8,128)(2,1)S(1)}, bf16[4,48,384]{2,1,0:T(8,128)(2,1)S(1)}, u32[]{:S(2)}, u32[]{:S(2)}) %collective-permute-start.25) | collective-permute-done | bytes 147488 | tf_op jit(solution)/shard_map/ppermute | solution.py:848
  353.9 7.7 %collective-permute-done.26 = bf16[12,48,384]{2,1,0:T(8,128)(2,1)S(1)} collective-permute-done((bf16[12,48,384]{2,1,0:T(8,128)(2,1)S(1)}, bf16[12,48,384]{2,1,0:T(8,128)(2,1)S(1)}, u32[]{:S(2)}, u32[]{:S(2)}) %collective-permute-start.26) | collective-permute-done | bytes 442400 | tf_op jit(solution)/shard_map/ppermute | solution.py:848
  363.0 1.1 convert_add_fusion
  (178 shorter events, 19.9 us)
Async XLA Ops:
  7.2 74.5 %copy-start = (bf16[384,288]{0,1:T(8,128)(2,1)S(1)}, bf16[384,288]{0,1:T(8,128)(2,1)}, u32[]{:S(2)}) copy-start(bf16[384,288]{0,1:T(8,128)(2,1)} %param.20) | copy-start | bytes 663556
  7.2 2.8 copy-start.18
  7.2 2.8 copy-start.13
  7.2 8.9 %copy-start.24 = (s32[1,4]{1,0:T(1,128)S(1)}, s32[1,4]{1,0:T(1,128)}, u32[]{:S(2)}) copy-start(s32[1,4]{1,0:T(1,128)} %param.16) | copy-start | bytes 52
  7.2 8.9 %copy-start.23 = (s32[1,4]{1,0:T(1,128)S(1)}, s32[1,4]{1,0:T(1,128)}, u32[]{:S(2)}) copy-start(s32[1,4]{1,0:T(1,128)} %param.17) | copy-start | bytes 52
  7.2 131.4 %all-gather.4.cloned.1.call-start = ((), (), s32[]{:S(2)}) async-start(), calls=%async_computation.4 | async-start | bytes 9732096 | tf_op jit(solution)/shard_map/all_gather | solution.py:791
  10.0 22.7 %collective-permute-start.1 = (bf16[4,48,384]{2,1,0:T(8,128)(2,1)S(1)}, bf16[4,48,384]{2,1,0:T(8,128)(2,1)S(1)}, u32[]{:S(2)}, u32[]{:S(2)}) collective-permute-start(bf16[4,48,384]{2,1,0:T(8,128)(2,1)S(1)} %pad_maximum_fusion.9), channel_id=1, source_target_pairs={{0,24},{2,26},{4,28},{6,30},{8,0},{10,2},{12,4},{14,6},{16,8},{18,... | collective-permute-start | bytes 442376 | tf_op jit(solution)/shard_map/ppermute | solution.py:807
  15.1 17.7 %collective-permute-start.2 = (bf16[4,48,384]{2,1,0:T(8,128)(2,1)S(1)}, bf16[4,48,384]{2,1,0:T(8,128)(2,1)S(1)}, u32[]{:S(2)}, u32[]{:S(2)}) collective-permute-start(bf16[4,48,384]{2,1,0:T(8,128)(2,1)S(1)} %pad_maximum_fusion.9), channel_id=1, source_target_pairs={{0,16},{2,18},{4,20},{6,22},{8,24},{10,26},{12,28},{14,30},{16,0},... | collective-permute-start | bytes 442376 | tf_op jit(solution)/shard_map/ppermute | solution.py:807
  15.1 17.7 %collective-permute-start.3 = (bf16[4,48,384]{2,1,0:T(8,128)(2,1)S(1)}, bf16[4,48,384]{2,1,0:T(8,128)(2,1)S(1)}, u32[]{:S(2)}, u32[]{:S(2)}) collective-permute-start(bf16[4,48,384]{2,1,0:T(8,128)(2,1)S(1)} %pad_maximum_fusion.9), channel_id=1, source_target_pairs={{0,8},{2,10},{4,12},{6,14},{8,16},{10,18},{12,20},{14,22},{16,24},... | collective-permute-start | bytes 442376 | tf_op jit(solution)/shard_map/ppermute | solution.py:807
  16.8 15.3 %all-to-all-start = ((s32[32,1,8]{2,1,0:T(1,128)}), s32[32,1,8]{2,1,0:T(1,128)S(1)}, u32[]{:S(2)}, u32[]{:S(2)}) async-start(s32[32,1,8]{2,1,0:T(1,128)} %broadcast_in_dim.20), calls=%async_computation | async-start | bytes 32768 | tf_op jit(solution)/shard_map/all_to_all | solution.py:777
  21.9 10.5 %copy-start.21 = (bf16[500,48]{0,1:T(8,128)(2,1)S(1)}, bf16[500,48]{0,1:T(8,128)(2,1)}, u32[]{:S(2)}) copy-start(bf16[500,48]{0,1:T(8,128)(2,1)} %param.18) | copy-start | bytes 144004
  32.7 1.7 copy-start.22
  32.9 9.1 %collective-permute-start.5 = (bf16[4,2,48,384]{3,2,1,0:T(8,128)(2,1)S(1)}, bf16[4,2,48,384]{3,2,1,0:T(8,128)(2,1)S(1)}, u32[]{:S(2)}, u32[]{:S(2)}) collective-permute-start(bf16[4,2,48,384]{3,2,1,0:T(8,128)(2,1)S(1)} %get-tuple-element.159), channel_id=1, source_target_pairs={{0,1},{1,0},{2,3},{3,2},{4,5},{5,4},{6,7},{7,6},{8,9},{9,8},{10,11... | collective-permute-start | bytes 884744 | tf_op jit(solution)/shard_map/ppermute | solution.py:831
  33.5 9.2 %copy-start.19 = (bf16[9,192]{1,0:T(8,128)(2,1)S(1)}, bf16[9,192]{1,0:T(8,128)(2,1)}, u32[]{:S(2)}) copy-start(bf16[9,192]{1,0:T(8,128)(2,1)} %param.25) | copy-start | bytes 10372
  33.5 9.2 %copy-start.20 = (bf16[9,48]{1,0:T(8,128)(2,1)S(1)}, bf16[9,48]{1,0:T(8,128)(2,1)}, u32[]{:S(2)}) copy-start(bf16[9,48]{1,0:T(8,128)(2,1)} %param.21) | copy-start | bytes 2596
  33.6 9.4 %collective-permute-start.4 = (bf16[4,2,48,384]{3,2,1,0:T(8,128)(2,1)S(1)}, bf16[4,2,48,384]{3,2,1,0:T(8,128)(2,1)S(1)}, u32[]{:S(2)}, u32[]{:S(2)}) collective-permute-start(bf16[4,2,48,384]{3,2,1,0:T(8,128)(2,1)S(1)} %get-tuple-element.161), channel_id=1, source_target_pairs={{0,4},{2,6},{4,0},{6,2},{8,12},{10,14},{12,8},{14,10},{16,20},{18,... | collective-permute-start | bytes 884744 | tf_op jit(solution)/shard_map/ppermute | solution.py:832
  34.6 8.4 %collective-permute-start = (f32[128,48]{0,1:T(8,128)S(1)}, f32[128,48]{0,1:T(8,128)S(1)}, u32[]{:S(2)}, u32[]{:S(2)}) collective-permute-start(f32[128,48]{0,1:T(8,128)S(1)} %convolution_add_fusion), channel_id=1, source_target_pairs={{0,1},{1,0},{2,3},{3,2},{4,5},{5,4},{6,7},{7,6},{8,9},{9,8},{10,11... | collective-permute-start | bytes 73736 | tf_op jit(solution)/shard_map/ppermute | solution.py:831
  42.1 36.3 %collective-permute-start.7 = (bf16[2,4,2,48,384]{4,3,2,1,0:T(8,128)(2,1)S(1)}, bf16[2,4,2,48,384]{4,3,2,1,0:T(8,128)(2,1)S(1)}, u32[]{:S(2)}, u32[]{:S(2)}) collective-permute-start(bf16[2,4,2,48,384]{4,3,2,1,0:T(8,128)(2,1)S(1)} %get-tuple-element.155), channel_id=1, source_target_pairs={{0,4},{2,6},{4,0},{6,2},{8,12},{10,14},{12,8},{14,10},{16,20},{18,... | collective-permute-start | bytes 1769480 | tf_op jit(solution)/shard_map/ppermute | solution.py:832
  43.2 35.9 %collective-permute-start.6 = (bf16[2,4,2,48,384]{4,3,2,1,0:T(8,128)(2,1)S(1)}, bf16[2,4,2,48,384]{4,3,2,1,0:T(8,128)(2,1)S(1)}, u32[]{:S(2)}, u32[]{:S(2)}) collective-permute-start(bf16[2,4,2,48,384]{4,3,2,1,0:T(8,128)(2,1)S(1)} %get-tuple-element.157), channel_id=1, source_target_pairs={{0,1},{1,0},{2,3},{3,2},{4,5},{5,4},{6,7},{7,6},{8,9},{9,8},{10,11... | collective-permute-start | bytes 1769480 | tf_op jit(solution)/shard_map/ppermute | solution.py:831
  78.4 3.3 copy-start.6
  78.4 3.2 copy-start.10
  78.6 1.6 copy-start.9
  78.6 26.1 %collective-permute-start.9 = (bf16[2,2,4,2,48,384]{5,4,3,2,1,0:T(8,128)(2,1)S(1)}, bf16[2,2,4,2,48,384]{5,4,3,2,1,0:T(8,128)(2,1)}, u32[]{:S(2)}, u32[]{:S(2)}) collective-permute-start(bf16[2,2,4,2,48,384]{5,4,3,2,1,0:T(8,128)(2,1)S(1)} %pad_maximum_fusion.1.own_b), channel_id=1, source_target_pairs={{0,2},{2,0},{4,6},{6,4},{8,10},{10,8},{12,14},{14,12},{16,18},{18,... | collective-permute-start | bytes 3538952 | tf_op jit(solution)/shard_map/ppermute | solution.py:832
  80.2 24.5 %collective-permute-start.8 = (bf16[2,2,4,2,48,384]{5,4,3,2,1,0:T(8,128)(2,1)}, bf16[2,2,4,2,48,384]{5,4,3,2,1,0:T(8,128)(2,1)}, u32[]{:S(2)}, u32[]{:S(2)}) collective-permute-start(bf16[2,2,4,2,48,384]{5,4,3,2,1,0:T(8,128)(2,1)} %pad_maximum_fusion.own_a), channel_id=1, source_target_pairs={{0,2},{2,0},{4,6},{6,4},{8,10},{10,8},{12,14},{14,12},{16,18},{18,... | collective-permute-start | bytes 3538952 | tf_op jit(solution)/shard_map/ppermute | solution.py:832
  81.7 3.8 %slice-start = ((bf16[16,173,48]{1,2,0:T(8,128)(2,1)}), bf16[16,45,48]{1,2,0:T(8,128)(2,1)S(1)}, s32[]{:S(2)}) async-start(bf16[16,173,48]{1,2,0:T(8,128)(2,1)} %copy-done.6), calls=%async_computation.5 | async-start | bytes 393216 | tf_op jit(solution)/shard_map/slice | solution.py:896
  82.9 13.9 %all-to-all-start.1 = ((f32[32,1,1152]{2,1,0:T(1,128)}), f32[32,1,1152]{2,1,0:T(1,128)S(1)}, u32[]{:S(2)}, u32[]{:S(2)}) async-start(f32[32,1,1152]{2,1,0:T(1,128)} %reshape.257), calls=%async_computation.1 | async-start | bytes 294912 | tf_op jit(solution)/shard_map/all_to_all | solution.py:777
  207.7 18.5 %collective-permute-start.11 = (bf16[8,2,4,48,384]{4,3,2,1,0:T(8,128)(2,1)}, bf16[8,2,4,48,384]{4,3,2,1,0:T(8,128)(2,1)S(1)}, u32[]{:S(2)}, u32[]{:S(2)}) collective-permute-start(bf16[8,2,4,48,384]{4,3,2,1,0:T(8,128)(2,1)} %get-tuple-element.91), channel_id=1, source_target_pairs={{0,2},{2,0},{4,6},{6,4},{8,10},{10,8},{12,14},{14,12},{16,18},{18,... | collective-permute-start | bytes 7077896 | tf_op jit(solution)/shard_map/ppermute | solution.py:832
  207.8 18.4 %collective-permute-start.10 = (bf16[8,2,4,48,384]{4,3,2,1,0:T(8,128)(2,1)}, bf16[8,2,4,48,384]{4,3,2,1,0:T(8,128)(2,1)}, u32[]{:S(2)}, u32[]{:S(2)}) collective-permute-start(bf16[8,2,4,48,384]{4,3,2,1,0:T(8,128)(2,1)} %get-tuple-element.88), channel_id=1, source_target_pairs={{0,2},{2,0},{4,6},{6,4},{8,10},{10,8},{12,14},{14,12},{16,18},{18,... | collective-permute-start | bytes 7077896 | tf_op jit(solution)/shard_map/ppermute | solution.py:832
  208.3 19.4 %copy-start.5 = (bf16[8,2,4,48,384]{4,3,2,1,0:T(8,128)(2,1)S(1)}, bf16[8,2,4,48,384]{4,3,2,1,0:T(8,128)(2,1)}, u32[]{:S(2)}) copy-start(bf16[8,2,4,48,384]{4,3,2,1,0:T(8,128)(2,1)} %get-tuple-element.87) | copy-start | bytes 7077892
  226.2 1.5 copy-start.3
  227.7 3.9 %copy-start.4 = (bf16[8,2,4,48,384]{4,3,2,1,0:T(8,128)(2,1)S(1)}, bf16[8,2,4,48,384]{4,3,2,1,0:T(8,128)(2,1)}, u32[]{:S(2)}) copy-start(bf16[8,2,4,48,384]{4,3,2,1,0:T(8,128)(2,1)} %copy-done.3) | copy-start | bytes 7077892
  230.1 2.1 copy-start.2
  231.3 31.2 %collective-permute-start.12 = (bf16[4,2,4,48,384]{4,3,2,0,1:T(8,128)(2,1)}, bf16[4,2,4,48,384]{4,3,2,0,1:T(8,128)(2,1)}, u32[]{:S(2)}, u32[]{:S(2)}) collective-permute-start(bf16[4,2,4,48,384]{4,3,2,0,1:T(8,128)(2,1)} %fusion.1), channel_id=1, source_target_pairs={{0,1},{1,0},{2,3},{3,2},{4,5},{5,4},{6,7},{7,6},{8,9},{9,8},{10,11... | collective-permute-start | bytes 3538952 | tf_op jit(solution)/shard_map/ppermute | solution.py:831
  233.7 28.8 %collective-permute-start.13 = (bf16[4,2,4,48,384]{4,3,2,0,1:T(8,128)(2,1)}, bf16[4,2,4,48,384]{4,3,2,0,1:T(8,128)(2,1)}, u32[]{:S(2)}, u32[]{:S(2)}) collective-permute-start(bf16[4,2,4,48,384]{4,3,2,0,1:T(8,128)(2,1)} %fusion), channel_id=1, source_target_pairs={{0,4},{2,6},{4,0},{6,2},{8,12},{10,14},{12,8},{14,10},{16,20},{18,... | collective-permute-start | bytes 3538952 | tf_op jit(solution)/shard_map/ppermute | solution.py:832
  251.9 10.3 %copy-start.12 = (f32[9,3072]{1,0:T(8,128)S(1)}, f32[9,3072]{1,0:T(8,128)}, u32[]{:S(2)}) copy-start(f32[9,3072]{1,0:T(8,128)} %get-tuple-element.117) | copy-start | bytes 331780
  251.9 10.5 %copy-start.16 = (f32[4,4,768]{2,1,0:T(4,128)S(1)}, f32[4,4,768]{2,1,0:T(4,128)}, u32[]{:S(2)}) copy-start(f32[4,4,768]{2,1,0:T(4,128)} %get-tuple-element.113) | copy-start | bytes 147460
  252.0 10.5 %copy-start.17 = (f32[4,4,768]{2,1,0:T(4,128)S(1)}, f32[4,4,768]{2,1,0:T(4,128)}, u32[]{:S(2)}) copy-start(f32[4,4,768]{2,1,0:T(4,128)} %get-tuple-element.114) | copy-start | bytes 147460
  261.7 22.6 %collective-permute-start.15 = (bf16[8,2,2,48,384]{4,3,2,1,0:T(8,128)(2,1)}, bf16[8,2,2,48,384]{4,3,2,1,0:T(8,128)(2,1)}, u32[]{:S(2)}, u32[]{:S(2)}) collective-permute-start(bf16[8,2,2,48,384]{4,3,2,1,0:T(8,128)(2,1)} %get-tuple-element.107), channel_id=1, source_target_pairs={{0,2},{2,0},{4,6},{6,4},{8,10},{10,8},{12,14},{14,12},{16,18},{18,... | collective-permute-start | bytes 3538952 | tf_op jit(solution)/shard_map/ppermute | solution.py:832
  261.8 22.6 %collective-permute-start.14 = (bf16[8,2,2,48,384]{4,3,2,1,0:T(8,128)(2,1)}, bf16[8,2,2,48,384]{4,3,2,1,0:T(8,128)(2,1)}, u32[]{:S(2)}, u32[]{:S(2)}) collective-permute-start(bf16[8,2,2,48,384]{4,3,2,1,0:T(8,128)(2,1)} %get-tuple-element.104), channel_id=1, source_target_pairs={{0,2},{2,0},{4,6},{6,4},{8,10},{10,8},{12,14},{14,12},{16,18},{18,... | collective-permute-start | bytes 3538952 | tf_op jit(solution)/shard_map/ppermute | solution.py:832
  265.5 25.2 %collective-permute-start.16 = (bf16[4,4,48,384]{3,2,1,0:T(8,128)(2,1)S(1)}, bf16[4,4,48,384]{3,2,1,0:T(8,128)(2,1)}, u32[]{:S(2)}, u32[]{:S(2)}) collective-permute-start(bf16[4,4,48,384]{3,2,1,0:T(8,128)(2,1)S(1)} %get-tuple-element.174), channel_id=1, source_target_pairs={{0,4},{2,6},{4,0},{6,2},{8,12},{10,14},{12,8},{14,10},{16,20},{18,... | collective-permute-start | bytes 1769480 | tf_op jit(solution)/shard_map/ppermute | solution.py:832
  267.2 23.4 %collective-permute-start.17 = (bf16[4,4,48,384]{3,2,1,0:T(8,128)(2,1)S(1)}, bf16[4,4,48,384]{3,2,1,0:T(8,128)(2,1)}, u32[]{:S(2)}, u32[]{:S(2)}) collective-permute-start(bf16[4,4,48,384]{3,2,1,0:T(8,128)(2,1)S(1)} %get-tuple-element.134), channel_id=1, source_target_pairs={{0,1},{1,0},{2,3},{3,2},{4,5},{5,4},{6,7},{7,6},{8,9},{9,8},{10,11... | collective-permute-start | bytes 1769480 | tf_op jit(solution)/shard_map/ppermute | solution.py:831
  268.4 16.0 %copy-start.8 = (bf16[8,2,2,48,384]{4,3,2,1,0:T(8,128)(2,1)S(1)}, bf16[8,2,2,48,384]{4,3,2,1,0:T(8,128)(2,1)}, u32[]{:S(2)}) copy-start(bf16[8,2,2,48,384]{4,3,2,1,0:T(8,128)(2,1)} %get-tuple-element.106) | copy-start | bytes 3538948
  285.9 1.5 copy-start.7
  286.8 24.3 %collective-permute-start.20 = (bf16[4,2,2,48,384]{4,3,2,0,1:T(8,128)(2,1)}, bf16[4,2,2,48,384]{4,3,2,0,1:T(8,128)(2,1)}, u32[]{:S(2)}, u32[]{:S(2)}) collective-permute-start(bf16[4,2,2,48,384]{4,3,2,0,1:T(8,128)(2,1)} %fusion.2), channel_id=1, source_target_pairs={{0,4},{2,6},{4,0},{6,2},{8,12},{10,14},{12,8},{14,10},{16,20},{18,... | collective-permute-start | bytes 1769480 | tf_op jit(solution)/shard_map/ppermute | solution.py:832
  288.8 1.8 copy-start.14
  288.8 2.2 copy-start.15
  289.7 23.9 %collective-permute-start.18 = (bf16[4,2,2,48,384]{4,3,2,0,1:T(8,128)(2,1)}, bf16[4,2,2,48,384]{4,3,2,0,1:T(8,128)(2,1)}, u32[]{:S(2)}, u32[]{:S(2)}) collective-permute-start(bf16[4,2,2,48,384]{4,3,2,0,1:T(8,128)(2,1)} %fusion.3), channel_id=1, source_target_pairs={{0,1},{1,0},{2,3},{3,2},{4,5},{5,4},{6,7},{7,6},{8,9},{9,8},{10,11... | collective-permute-start | bytes 1769480 | tf_op jit(solution)/shard_map/ppermute | solution.py:831
  291.3 5.2 %copy-start.1 = (bf16[4,1,4,48,384]{4,3,2,0,1:T(8,128)(2,1)S(1)}, bf16[4,1,4,48,384]{4,3,2,0,1:T(8,128)(2,1)}, u32[]{:S(2)}) copy-start(bf16[4,1,4,48,384]{4,3,2,0,1:T(8,128)(2,1)} %get-tuple-element.133) | copy-start | bytes 1769476
  294.0 16.8 %all-to-all-start.2 = ((bf16[32,2,1656]{2,1,0:T(2,128)(2,1)}), bf16[32,2,1656]{2,1,0:T(2,128)(2,1)S(1)}, u32[]{:S(2)}, u32[]{:S(2)}) async-start(bf16[32,2,1656]{2,1,0:T(2,128)(2,1)} %reshape.260), calls=%async_computation.2 | async-start | bytes 425984 | tf_op jit(solution)/shard_map/all_to_all | solution.py:777
  299.7 22.7 %collective-permute-start.22 = (bf16[2,8,48,384]{3,2,1,0:T(8,128)(2,1)}, bf16[2,8,48,384]{3,2,1,0:T(8,128)(2,1)}, u32[]{:S(2)}, u32[]{:S(2)}) collective-permute-start(bf16[2,8,48,384]{3,2,1,0:T(8,128)(2,1)} %pad_maximum_fusion.4), channel_id=1, source_target_pairs={{0,8},{2,10},{4,12},{6,14},{8,0},{10,2},{12,4},{14,6},{16,24},{18,... | collective-permute-start | bytes 1769480 | tf_op jit(solution)/shard_map/ppermute | solution.py:832
  312.1 11.3 %collective-permute-start.21 = (bf16[4,2,48,384]{3,2,1,0:T(8,128)(2,1)S(1)}, bf16[4,2,48,384]{3,2,1,0:T(8,128)(2,1)}, u32[]{:S(2)}, u32[]{:S(2)}) collective-permute-start(bf16[4,2,48,384]{3,2,1,0:T(8,128)(2,1)S(1)} %fusion.24), channel_id=1, source_target_pairs={{0,1},{1,0},{2,3},{3,2},{4,5},{5,4},{6,7},{7,6},{8,9},{9,8},{10,11... | collective-permute-start | bytes 884744 | tf_op jit(solution)/shard_map/ppermute | solution.py:831
  313.7 7.7 %copy-start.11 = (bf16[16,128,48]{1,2,0:T(8,128)(2,1)S(1)}, bf16[16,128,48]{1,2,0:T(8,128)(2,1)}, u32[]{:S(2)}) copy-start(bf16[16,128,48]{1,2,0:T(8,128)(2,1)} %copy-done.10) | copy-start | bytes 589828
  314.7 9.8 %collective-permute-start.19 = (bf16[4,2,48,384]{3,2,1,0:T(8,128)(2,1)S(1)}, bf16[4,2,48,384]{3,2,1,0:T(8,128)(2,1)}, u32[]{:S(2)}, u32[]{:S(2)}) collective-permute-start(bf16[4,2,48,384]{3,2,1,0:T(8,128)(2,1)S(1)} %fusion.25), channel_id=1, source_target_pairs={{0,4},{2,6},{4,0},{6,2},{8,12},{10,14},{12,8},{14,10},{16,20},{18,... | collective-permute-start | bytes 884744 | tf_op jit(solution)/shard_map/ppermute | solution.py:832
  317.5 12.9 %all-to-all-start.3 = ((f32[16,24,128]{2,1,0:T(8,128)}), f32[16,24,128]{2,1,0:T(8,128)S(1)}, u32[]{:S(2)}, u32[]{:S(2)}) async-start(f32[16,24,128]{2,1,0:T(8,128)} %bitcast.72), calls=%async_computation.3 | async-start | bytes 393216 | tf_op jit(solution)/shard_map/all_to_all | solution.py:905
  330.4 10.2 %collective-permute-start.23 = (f32[24,128]{1,0:T(8,128)S(1)}, f32[24,128]{1,0:T(8,128)S(1)}, u32[]{:S(2)}, u32[]{:S(2)}) collective-permute-start(f32[24,128]{1,0:T(8,128)S(1)} %reduce_sum.38), channel_id=1, source_target_pairs={{0,0},{1,16},{2,1},{3,17},{4,2},{5,18},{6,3},{7,19},{8,4},{9,20},{... | collective-permute-start | bytes 36872 | tf_op jit(solution)/shard_map/ppermute | solution.py:919
  331.0 9.5 %collective-permute-start.24 = (f32[24,128]{1,0:T(8,128)S(1)}, f32[24,128]{1,0:T(8,128)S(1)}, u32[]{:S(2)}, u32[]{:S(2)}) collective-permute-start(f32[24,128]{1,0:T(8,128)S(1)} %reduce_sum.38), channel_id=1, source_target_pairs={{0,1},{1,17},{2,0},{3,16},{4,3},{5,19},{6,2},{7,18},{8,5},{9,21},{... | collective-permute-start | bytes 36872 | tf_op jit(solution)/shard_map/ppermute | solution.py:920
  335.9 25.7 %collective-permute-start.26 = (bf16[12,48,384]{2,1,0:T(8,128)(2,1)S(1)}, bf16[12,48,384]{2,1,0:T(8,128)(2,1)S(1)}, u32[]{:S(2)}, u32[]{:S(2)}) collective-permute-start(bf16[12,48,384]{2,1,0:T(8,128)(2,1)S(1)} %pad_maximum_fusion.5), channel_id=1, source_target_pairs={{0,16},{2,18},{4,20},{6,22},{8,24},{10,26},{12,28},{14,30},{16,0},... | collective-permute-start | bytes 1327112 | tf_op jit(solution)/shard_map/ppermute | solution.py:848
  336.8 17.1 %collective-permute-start.25 = (bf16[4,48,384]{2,1,0:T(8,128)(2,1)S(1)}, bf16[4,48,384]{2,1,0:T(8,128)(2,1)S(1)}, u32[]{:S(2)}, u32[]{:S(2)}) collective-permute-start(bf16[4,48,384]{2,1,0:T(8,128)(2,1)S(1)} %get-tuple-element.152), channel_id=1, source_target_pairs={{0,8},{2,10},{4,12},{6,14},{8,16},{10,18},{12,20},{14,22},{16,24},... | collective-permute-start | bytes 442376 | tf_op jit(solution)/shard_map/ppermute | solution.py:848
  338.1 15.8 %collective-permute-start.27 = (bf16[4,48,384]{2,1,0:T(8,128)(2,1)S(1)}, bf16[4,48,384]{2,1,0:T(8,128)(2,1)S(1)}, u32[]{:S(2)}, u32[]{:S(2)}) collective-permute-start(bf16[4,48,384]{2,1,0:T(8,128)(2,1)S(1)} %get-tuple-element.151), channel_id=1, source_target_pairs={{0,24},{2,26},{4,28},{6,30},{8,0},{10,2},{12,4},{14,6},{16,8},{18,... | collective-permute-start | bytes 442376 | tf_op jit(solution)/shard_map/ppermute | solution.py:848
Sparse Core Ops, SparseCore 0:
  11.6 93.8 all-gather.3

commit v6 on v5

--- a/solution.py
+++ b/solution.py
@@ -17,7 +17,8 @@
 EPS = 1e-06
 NJ, NK, UR, UC = 16, 2, 48, 384
 CHUNK = 768
-HEADS = 3
+HEADS = 6
+PARTS = ((0, 1), (1, 3))
 MIB = 1024 * 1024
 BF = jnp.bfloat16
 F32 = jnp.float32
@@ -567,12 +568,14 @@
 
 
 def attend_back(part, tag, resid, shrunk, d_second, gradient, attn, mods, qkv, lse, proj_t):
+    first, count = PARTS[part]
+
     def pick_group(*shape):
-        return pl.BlockSpec((1,) + shape, lambda g: (2 * part + g,) + (0,) * len(shape))
+        return pl.BlockSpec((1,) + shape, lambda g: (first + g,) + (0,) * len(shape))
 
     return pl.pallas_call(
         attend_back_kernel,
-        grid=(2,),
+        grid=(count,),
         in_specs=[
             SMEM_SPEC,
             pick_group(GROUP, D),
@@ -593,10 +596,10 @@
             whole((4, 4, D)),
         ],
         out_shape=[
-            jax.ShapeDtypeStruct((2, GROUP, D), BF),
-            jax.ShapeDtypeStruct((2, GROUP, D), F32),
-            jax.ShapeDtypeStruct((3 * D, 2 * GROUP), BF),
-            jax.ShapeDtypeStruct((D, 2 * GROUP), BF),
+            jax.ShapeDtypeStruct((count, GROUP, D), BF),
+            jax.ShapeDtypeStruct((count, GROUP, D), F32),
+            jax.ShapeDtypeStruct((3 * D, count * GROUP), BF),
+            jax.ShapeDtypeStruct((D, count * GROUP), BF),
             jax.ShapeDtypeStruct((4, 4, D), F32),
         ],
         scratch_shapes=[
@@ -606,7 +609,7 @@
             pltpu.VMEM((4, 4, 8, D), F32),
         ],
         compiler_params=params(),
-        cost_estimate=cost(16),
+        cost_estimate=cost(9 * count),
         name=f"attend_back_{part}",
     )(tag, resid, shrunk, d_second, gradient, attn, mods, qkv, lse, proj_t)
 
@@ -621,8 +624,8 @@
     core = tag_ref[1]
 
     def against(low, high, field):
-        return dot(low[...], field[0:2].reshape(2 * GROUP, D), 1, 0) + dot(
-            high[...], field[2:4].reshape(2 * GROUP, D), 1, 0
+        return dot(low[...], field[0], 1, 0) + dot(
+            high[...], field[1:4].reshape(3 * GROUP, D), 1, 0
         )
 
     grad = against(d_qkv0, d_qkv1, conv_in)
@@ -632,14 +635,18 @@
     share_out(grad, core, (0, 1), keep_b.at[:, :, 1:2], send_b.at[:, :, 1:2])
 
 
+def column_specs(rows):
+    return [pl.BlockSpec((rows, count * GROUP), lambda i: (i, 0)) for _, count in PARTS]
+
+
 def project_grads(tag, d_qkv, d_attn, conv_in, merged):
     packed_spec = pl.BlockSpec((PAIRS, NK, 2, UR, UC), lambda i: (i, 0, 0, 0, 0))
-    tall = pl.BlockSpec((ROWS, 2 * GROUP), lambda i: (i, 0))
-    short = pl.BlockSpec((96 * PAIRS, 2 * GROUP), lambda i: (i, 0))
+    tall = column_specs(ROWS)
+    short = column_specs(96 * PAIRS)
     return pl.pallas_call(
         project_grads_kernel,
         grid=(8 // PAIRS,),
-        in_specs=[SMEM_SPEC, tall, tall, short, short, whole((4, GROUP, D)), whole((4, GROUP, D))],
+        in_specs=[SMEM_SPEC, *tall, *short, whole((4, GROUP, D)), whole((4, GROUP, D))],
         out_specs=[packed_spec] * 4,
         out_shape=[packed_half(2)] * 4,
         compiler_params=params(),
@@ -649,7 +656,8 @@
 
 
 def conv_back_kernel(
-    tag_ref, d_qkv0, d_qkv1, weight, norm, mods, kernel, d_first, g_kernel, item_sums, d_conv
+    tag_ref, d_qkv0, d_qkv1, weight, norm, mods, kernel, later0, later1, g_ffn,
+    d_first, pieces, d_conv, g_kernel, item_sums,
 ):
     step = pl.program_id(0)
 
@@ -657,8 +665,8 @@
     def _():
         d_conv[...] = jnp.zeros_like(d_conv)
 
-    d_conv[0:2] += dot(d_qkv0[...], weight[...], 0, 0).reshape(2, GROUP, D)
-    d_conv[2:4] += dot(d_qkv1[...], weight[...], 0, 0).reshape(2, GROUP, D)
+    d_conv[0] += dot(d_qkv0[...], weight[...], 0, 0)
+    d_conv[1:4] += dot(d_qkv1[...], weight[...], 0, 0).reshape(3, GROUP, D)
 
     @pl.when(step == pl.num_programs(0) - 1)
     def _():
@@ -696,33 +704,58 @@
             return 0
 
         lax.fori_loop(0, D // 128, lanes, 0)
-
-
-def conv_back(tag, d_qkv, weight, norm, mods, kernel):
-    tall = pl.BlockSpec((ROWS, 2 * GROUP), lambda i: (i, 0))
+        later = later0[...] + later1[...]
+        rows = [item_sums[i] for i in range(2)] + [later[i] for i in range(4)]
+        rows = jnp.concatenate(rows, axis=1)
+        alone = jnp.concatenate([jnp.sum(rows, axis=0, keepdims=True), jnp.zeros((3, 6 * D), F32)])
+        rows = jnp.where(tag == 1, rows, alone)
+        slots, _, width = pieces.shape
+        owners = 6 * D // width
+        short, long = D // owners, FF // owners
+        for j in range(owners):
+            filters = jnp.concatenate(
+                [
+                    g_kernel[:, j * short : (j + 1) * short],
+                    g_ffn[:, j * long : (j + 1) * long],
+                    jnp.zeros((9, width - short - long), F32),
+                ],
+                axis=1,
+            )
+            part = [rows[:, j * width : (j + 1) * width], filters, jnp.zeros((3, width), F32)]
+            part = jnp.concatenate(part, axis=0).astype(BF)
+            for copy in range(slots // owners):
+                pieces[j * (slots // owners) + copy] = part
+
+
+def conv_back(slots, width, tag, d_qkv, weight, norm, mods, kernel, later, g_ffn):
     return pl.pallas_call(
         conv_back_kernel,
         grid=(8 // PAIRS,),
         in_specs=[
             SMEM_SPEC,
-            tall,
-            tall,
+            *column_specs(ROWS),
             pl.BlockSpec((ROWS, D), lambda i: (i, 0)),
             whole((4, GROUP, D)),
             whole((6, 4, 8, D)),
             whole((9, D)),
-        ],
-        out_specs=[whole((4, GROUP, D)), whole((9, D)), whole((2, 4, D))],
+            whole((4, 4, D)),
+            whole((4, 4, D)),
+            whole((9, FF)),
+        ],
+        out_specs=[whole((4, GROUP, D)), whole((slots, 16, width))],
         out_shape=[
             jax.ShapeDtypeStruct((4, GROUP, D), F32),
-            jax.ShapeDtypeStruct((9, D), F32),
-            jax.ShapeDtypeStruct((2, 4, D), F32),
-        ],
-        scratch_shapes=[pltpu.VMEM((4, GROUP, D), F32)],
+            jax.ShapeDtypeStruct((slots, 16, width), BF),
+        ],
+        scratch_shapes=[
+            pltpu.VMEM((4, GROUP, D), F32),
+            pltpu.VMEM((9, D), F32),
+            pltpu.VMEM((2, 4, D), F32),
+        ],
         compiler_params=params(),
         cost_estimate=cost(15),
         name="conv_back",
-    )(tag, *d_qkv, weight, norm, mods, kernel)
+    )(tag, *d_qkv, weight, norm, mods, kernel, *later, g_ffn)
 
 
 def finish_kernel(
@@ -732,21 +765,20 @@
     half = pl.program_id(0) // 2
 
     for g in range(4):
-        base = (d_resid0, d_resid1)[g // 2]
+        base = d_resid1[g - 1] if g else d_resid0[0]
         value = d_first[g]
         normal = norm[g]
         inner = (value.reshape(4, 2, 8, D) * (1.0 + quadrant_rows(mods, 1, half))).reshape(64, D)
         mean = jnp.mean(inner, axis=-1, keepdims=True)
         along = jnp.mean(inner * normal, axis=-1, keepdims=True)
-        total[g] = base[g % 2] + (inner - mean - normal * along) * factor[g]
+        total[g] = base + (inner - mean - normal * along) * factor[g]
     order = ungroup_matrix()
     grouped = total[...].reshape(256, D)
     high = grouped.astype(BF)
     rest = (grouped - high.astype(F32)).astype(BF)
     input_grad[...] = dot(order, high, 1, 0) + dot(order, rest, 1, 0)
-    low_half = dot(order[:, 0:128], output0[...].reshape(128, D), 1, 0)
-    high_half = dot(order[:, 128:256], output1[...].reshape(128, D), 1, 0)
-    block_output[...] = (low_half + high_half).astype(BF)
+    grouped = jnp.concatenate([output0[...], output1[...]], axis=0).reshape(256, D)
+    block_output[...] = dot(order, grouped, 1, 0).astype(BF)
 
 
 def finish(d_first, norm, factor, d_resid, output, mods):
@@ -757,7 +789,9 @@
     return pl.pallas_call(
         finish_kernel,
         grid=(4,),
-        in_specs=[split(4, D), split(4, D), split(4, 1)] + [split(2, D)] * 4 + [whole((6, 4, 8, D))],
+        in_specs=[split(4, D), split(4, D), split(4, 1)]
+        + [split(count, D) for _, count in PARTS] * 2
+        + [whole((6, 4, 8, D))],
         out_specs=[flat, flat],
         out_shape=[
             jax.ShapeDtypeStruct((TOK, D), BF),
@@ -891,7 +925,8 @@
     items, width = cond.shape
     act = jax.nn.silu(cond).astype(BF)
     filters = jnp.concatenate([attn_kernel, ffn_kernel], axis=1).reshape(-1, width)
-    sent = lax.all_gather(jnp.concatenate([act, filters], axis=0), "dp")
+    sent = jnp.concatenate([act, filters], axis=0)[None]
+    sent = lax.all_to_all(jnp.broadcast_to(sent, (nd,) + sent.shape[1:]), "dp", 0, 0, tiled=True)
     act_all = sent[:, :items].transpose(1, 0, 2).reshape(items, nd * width)
     filters = sent[:, items:].reshape(nd, 9, -1).astype(F32)
     attn_full = filters[:, :, : attn_kernel.shape[1]].transpose(1, 0, 2).reshape(9, -1)
@@ -1001,65 +1036,53 @@
     output1, d_resid1, d_qkv1, d_attn1, later1 = attend_back(
         1, where, resid, shrunk, d_second, *back, proj_t
     )
+    if square:
+        got_e, got_s = after(got_e, d_attn1), after(got_s, d_attn1)
+        keep_e, out_e = halve(keep_e, got_e, 1, 2)
+        keep_s, out_s = halve(keep_s, got_s, 1, None)
+        d_attn0 = after(d_attn0, out_e, out_s)
+        got_e, got_s = swap(out_e, 2), swap(out_s, None)
     d_qkv = (d_qkv0, d_qkv1)
     keep_a, send_a, keep_b, send_b = project_grads(
         where, d_qkv, (d_attn0, d_attn1), conv_in, merged
     )
     if square:
+        got_e, got_s = after(got_e, keep_a), after(got_s, keep_a)
         got_a, got_b = swap(send_a, 1), swap(send_b, 1)
-        got_e, got_s = after(got_e, keep_a), after(got_s, keep_a)
-        keep_e, out_e = halve(keep_e, got_e, 1, 2)
-        keep_s, out_s = halve(keep_s, got_s, 1, None)
-        full_qkv = after(full_qkv, out_e, out_s)
-        got_e, got_s = swap(out_e, 2), swap(out_s, None)
-    d_first, g_attn, early = conv_back(where, d_qkv, full_qkv, norm, mods, attn_full)
-    if square:
-        got_e, got_s, got_a, got_b = (after(x, d_first) for x in (got_e, got_s, got_a, got_b))
-        early, g_attn = after(early, got_e, got_s), after(g_attn, got_e, got_s)
-    later = later0 + later1
-    rows = jnp.concatenate([early, later], axis=0)
-    rows = rows.transpose(1, 0, 2).reshape(4, 6 * D)
-    alone = jnp.concatenate([rows.sum(axis=0, keepdims=True), jnp.zeros((3, 6 * D), F32)])
-    d_mod = jnp.where(tag == 1, rows, alone).astype(BF)
-    filters = jnp.concatenate([g_attn.reshape(9, nd, -1), g_ffn.reshape(9, nd, -1)], axis=2)
-    pieces = jnp.concatenate(
-        [
-            d_mod.reshape(4, nd, width).transpose(1, 0, 2).reshape(nd, -1),
-            filters.astype(BF).transpose(1, 0, 2).reshape(nd, -1),
-        ],
-        axis=1,
-    )
-    pieces = jnp.broadcast_to(pieces[:, None], (nd, nf, pieces.shape[1])).reshape(slots, 1, -1)
-    if square:
-        keep_a, out_a = halve(grid(keep_a), grid(got_a), 2, None)
-        keep_b, out_b = halve(grid(keep_b), grid(got_b), 1, 2)
         e = halve(keep_e.reshape((2, 2) + keep_e.shape[1:]), got_e.reshape((2, 2) + got_e.shape[1:]), 1, 4)
         s = halve(keep_s.reshape((2, 2) + keep_s.shape[1:]), got_s.reshape((2, 2) + got_s.shape[1:]), 1, 4)
         feeding, out_f = (jnp.concatenate(pair, axis=1) for pair in zip(e, s))
+        keep_a, out_a = halve(grid(keep_a), grid(got_a), 2, None)
+        keep_b, out_b = halve(grid(keep_b), grid(got_b), 1, 2)
+        full_qkv = after(full_qkv, out_a, out_b, out_f)
+        got_a, got_b, got_f = swap(out_a, None), swap(out_b, 2), swap(out_f, 4)
+    d_first, pieces = conv_back(
+        slots, width, where, d_qkv, full_qkv, norm, mods, attn_full, (later0, later1), g_ffn
+    )
+    if square:
+        got_a, got_b, got_f = (after(x, d_first) for x in (got_a, got_b, got_f))
+        keep_a, out_a = halve(keep_a, got_a, 1, 2)
+        keep_b, out_b = halve(keep_b, got_b, 1, None)
+        feeding, out_f = halve(feeding, got_f, 0, 8)
+    if square:
         d_first = after(d_first, out_a, out_b, out_f, pieces)
-        got_a, got_b = swap(out_a, None), swap(out_b, 2)
-        got_f = swap(out_f, 4)
-    got = exchange(pieces)[:, 0]
+        got_a, got_b, got_f = swap(out_a, 2), swap(out_b, None), swap(out_f, 8)
+    got = exchange(pieces)
     block_output, input_grad = finish(
         d_first, norm, factor, (d_resid0, d_resid1), (output0, output1), mods
     )
     if square:
         got = after(got, input_grad)
-        got_a, got_b, got_f = (after(x, got) for x in (got_a, got_b, got_f))
-        keep_a, out_a = halve(keep_a, got_a, 1, 2)
-        keep_b, out_b = halve(keep_b, got_b, 1, None)
-        got_a, got_b = swap(out_a, 2), swap(out_b, None)
-    d_mod_all = got[:, : 4 * width].reshape(slots * 4, width)
+    d_mod_all = got[:, :4].reshape(slots * 4, width)
     d_act = dot(modulation_weight, d_mod_all, 1, 1)
-    own_act = exchange_columns(nd, nf, d_act)
-    if square:
-        feeding, out_f = halve(feeding, got_f, 0, 8)
+    if square:
+        got_a, got_b = after(got_a, d_act), after(got_b, d_act)
         total = jnp.concatenate([keep_a + got_a, keep_b + got_b], axis=1)
         sends = last_sends(total)
-        sends[1] = jnp.concatenate([sends[1], out_f])
-        own_act = after(own_act, *sends)
         last = last_swaps(sends)
-        last[1], got_f = last[1][:4], last[1][4:]
+    own_act = exchange_columns(nd, nf, d_act)
+    if square:
+        got_f = after(got_f, own_act)
         total = last_sum(total, last)
         feeding = feeding.astype(F32) + got_f.astype(F32)
         cuts = [total[:3], total[3:], feeding[:4], feeding[4:]]
@@ -1075,7 +1098,8 @@
         own_shard(nd, nf, kind, cut)
         for kind, cut in zip(("qkv", "proj", "expand", "shrink"), cuts)
     ]
-    filters = got[:, 4 * width :].astype(F32).sum(axis=0).reshape(9, -1)
+    cut = attn_kernel.shape[1]
+    filters = got[:, 4:13, : cut + ffn_kernel.shape[1]].astype(F32).sum(axis=0)
     modulation_grad = dot(act_rows, d_mod_all, 0, 0)
     gate = jax.nn.sigmoid(cond)
     d_cond = own_columns(nd, nf, own_act)
@@ -1086,7 +1110,6 @@
             hot.astype(F32), d_cond, (((0,), (1,)), ((), ())), precision=lax.Precision.HIGHEST
         )
 
-    cut = attn_kernel.shape[1]
     return (
         block_output,
         input_grad,

time: 374 us -> 354 us (0.947)
  blocking collectives: 34.4 us -> 0 us
  starting transfers between devices: 44.4 us -> 67.6 us
    all_gather x1 -> x0, blocking collectives: 34.4 us -> none  [share_act(): sent = lax.all_gather(jnp.concatenate([act, filters], axis=0), 'dp')]
    ppermute x3, waiting for transfers between devices: 19.2 us -> 0.01 us  [last_swaps(): lax.ppermute(sent, 'dp', [(i, (i + 4 * step) % NJ) for i in range(NJ)])]
    all_to_all x0 -> x1, waiting for transfers between devices: none -> 12.4 us  [share_act(): lax.all_to_all(jnp.broadcast_to(sent, (nd,) + sent.shape[1:]), 'dp', 0, 0...]
    all_to_all x0 -> x1, starting transfers between devices: none -> 11.4 us  [share_act(): lax.all_to_all(jnp.broadcast_to(sent, (nd,) + sent.shape[1:]), 'dp', 0, 0...]
    ppermute x7, waiting for transfers between devices: 6 us -> 14.6 us  [swap(): return lax.ppermute(value, 'fsdp', [(0, 1), (1, 0)])]
    all_to_all x3, starting transfers between devices: 10.2 us -> 14.4 us  [exchange(): return lax.all_to_all(pieces, BOTH, 0, 0, tiled=True)]
    ppermute x1, starting transfers between devices: 3.48 us -> 7.28 us  [own_columns(): other = lax.ppermute(part, BOTH, [(i, o ^ 1) for i, o in order])]
    unnamed x56 -> x36, local copies, waits for them, and re-layouts: 4.85 us -> 1.06 us
  transfers between devices with their start and end apart: 33 -> 35, of which waited for: 6 -> 11; matrix products, arithmetic and copies ran while one was open for 10% -> 11% of each run, Pallas kernels for 31% -> 32%
where the time goes in v6:
time: 354 us; the launch traced here: 353 us
  Pallas kernels  182 us (51%)
  starting transfers between devices  67.6 us (19%)
  waiting for transfers between devices  42.6 us (12%)
  other arithmetic  26 us (7%)
  local copies, waits for them, and re-layouts  15.7 us (4%)
  between operations  15.5 us (4%)
  matrix products  3.83 us (1%)
    pallas_call x1, Pallas kernels, feed(): pl.pallas_call(feed_kernel, grid=(FF // CHUNK,), in_specs=[SMEM_SPEC, who...  69 us
    pallas_call x1, Pallas kernels, attend(): pl.pallas_call(attend_kernel, grid=(4,), in_specs=[SMEM_SPEC, group_spec(...  33.1 us
    pallas_call x2, Pallas kernels, attend_back(): pl.pallas_call(attend_back_kernel, grid=(count,), in_specs=[SMEM_SPEC, pi...  32.8 us
    pallas_call x1, Pallas kernels, conv_back(): pl.pallas_call(conv_back_kernel, grid=(8 // PAIRS,), in_specs=[SMEM_SPEC,...  16.3 us
    ppermute x7, waiting for transfers between devices, swap(): return lax.ppermute(value, 'fsdp', [(0, 1), (1, 0)])  14.6 us
    all_to_all x3, starting transfers between devices, exchange(): return lax.all_to_all(pieces, BOTH, 0, 0, tiled=True)  14.4 us
    all_to_all x3, waiting for transfers between devices, exchange(): return lax.all_to_all(pieces, BOTH, 0, 0, tiled=True)  12.6 us
    all_to_all x1, waiting for transfers between devices, share_act(): lax.all_to_all(jnp.broadcast_to(sent, (nd,) + sent.shape[1:]), 'dp', 0, 0...  12.4 us
  transfers between devices with their start and end apart: 35, of which 11 were waited for; matrix products, arithmetic and copies ran while one was open for 11% of the time, Pallas kernels for 32%

profile of v6, /device:TPU:0, one launch (start us, length us, event | category | flops | bytes accessed | tf_op | source)
XLA Modules:
  0.0 352.8 jit_solution(16340959462702591874)
XLA Ops:
  7.3 1.0 copy.176
  8.3 1.7 pad_maximum_fusion.7
  10.0 5.1 %collective-permute-start.1 = (bf16[4,48,384]{2,1,0:T(8,128)(2,1)S(1)}, bf16[4,48,384]{2,1,0:T(8,128)(2,1)S(1)}, u32[]{:S(2)}, u32[]{:S(2)}) collective-permute-start(bf16[4,48,384]{2,1,0:T(8,128)(2,1)S(1)} %pad_maximum_fusion.8), channel_id=1, source_target_pairs={{0,24},{2,26},{4,28},{6,30},{8,0},{10,2},{12,4},{14,6},{16,8},{18,... | collective-permute-start | bytes 442376 | tf_op jit(solution)/shard_map/ppermute | solution.py:841
  15.1 1.0 collective-permute-start.3
  16.8 5.1 %all-to-all-start = ((s32[32,1,8]{2,1,0:T(1,128)}), s32[32,1,8]{2,1,0:T(1,128)S(1)}, u32[]{:S(2)}, u32[]{:S(2)}) async-start(s32[32,1,8]{2,1,0:T(1,128)} %broadcast_in_dim.18), calls=%async_computation | async-start | bytes 32768 | tf_op jit(solution)/shard_map/all_to_all | solution.py:811
  21.9 6.0 %prepare.1 = (bf16[4,256,768]{2,1,0:T(8,128)(2,1)}, bf16[4,256,768]{2,1,0:T(8,128)(2,1)}, f32[4,256,768]{2,1,0:T(8,128)}, f32[4,256,1]{2,1,0:T(8,128)}) custom-call(bf16[1024,768]{1,0:T(8,128)(2,1)} %latents.1, bf16[1024,768]{1,0:T(8,128)(2,1)} %cotangent.1), custom_call_target="tpu_custom_call" | custom-call | flops 600000000 | bytes 4194304 | tf_op jit(solution)/shard_map/prepare/pallas_call | solution.py:89
  27.9 4.2 %all-to-all-done = s32[32,1,8]{2,1,0:T(1,128)S(1)} async-done(((s32[32,1,8]{2,1,0:T(1,128)}), s32[32,1,8]{2,1,0:T(1,128)S(1)}, u32[]{:S(2)}, u32[]{:S(2)}) %all-to-all-start) | async-done | bytes 1056 | tf_op jit(solution)/shard_map/all_to_all | solution.py:811
  34.7 1.4 collective-permute-start
  36.3 6.0 %collective-permute-done = f32[128,48]{0,1:T(8,128)S(1)} collective-permute-done((f32[128,48]{0,1:T(8,128)S(1)}, f32[128,48]{0,1:T(8,128)S(1)}, u32[]{:S(2)}, u32[]{:S(2)}) %collective-permute-start) | collective-permute-done | bytes 24608 | tf_op jit(solution)/shard_map/ppermute | solution.py:865
  43.0 0.9 fusion.48
  44.8 11.4 %all-to-all-start.1 = ((bf16[16,173,48]{1,2,0:T(8,128)(2,1)}), bf16[16,173,48]{1,2,0:T(8,128)(2,1)S(1)}, u32[]{:S(2)}, u32[]{:S(2)}) async-start(bf16[16,173,48]{1,2,0:T(8,128)(2,1)} %broadcast_in_dim.32), calls=%async_computation.1 | async-start | bytes 786432 | tf_op jit(solution)/shard_map/all_to_all | solution.py:929
  57.0 12.4 %all-to-all-done.1 = bf16[16,173,48]{1,2,0:T(8,128)(2,1)S(1)} async-done(((bf16[16,173,48]{1,2,0:T(8,128)(2,1)}), bf16[16,173,48]{1,2,0:T(8,128)(2,1)S(1)}, u32[]{:S(2)}, u32[]{:S(2)}) %all-to-all-start.1) | async-done | bytes 265760 | tf_op jit(solution)/shard_map/all_to_all | solution.py:929
  69.5 1.3 pad_maximum_fusion.1.own_b
  70.8 4.2 %collective-permute-done.6 = bf16[2,4,2,48,384]{4,3,2,1,0:T(8,128)(2,1)} collective-permute-done((bf16[2,4,2,48,384]{4,3,2,1,0:T(8,128)(2,1)}, bf16[2,4,2,48,384]{4,3,2,1,0:T(8,128)(2,1)}, u32[]{:S(2)}, u32[]{:S(2)}) %collective-permute-start.6) | collective-permute-done | bytes 589856 | tf_op jit(solution)/shard_map/ppermute | solution.py:865
  75.0 2.2 pad_maximum_fusion.own_a
  78.8 0.9 reshape.217
  79.7 5.4 %all-to-all-start.2 = ((f32[32,1,1152]{2,1,0:T(1,128)}), f32[32,1,1152]{2,1,0:T(1,128)S(1)}, u32[]{:S(2)}, u32[]{:S(2)}) async-start(f32[32,1,1152]{2,1,0:T(1,128)} %reshape.217), calls=%async_computation.2 | async-start | bytes 294912 | tf_op jit(solution)/shard_map/all_to_all | solution.py:811
  86.6 0.8 reshape.197.kernel
  87.4 7.7 %all-to-all-done.2 = f32[32,1,1152]{2,1,0:T(1,128)S(1)} async-done(((f32[32,1,1152]{2,1,0:T(1,128)}), f32[32,1,1152]{2,1,0:T(1,128)S(1)}, u32[]{:S(2)}, u32[]{:S(2)}) %all-to-all-start.2) | async-done | bytes 147488 | tf_op jit(solution)/shard_map/all_to_all | solution.py:811
  96.0 0.9 broadcast_in_dim.36.mods
  96.9 6.1 %first_conv.1.conv_in = bf16[4,256,768]{2,1,0:T(8,128)(2,1)} custom-call(s32[1]{0:T(128)S(6)} %copy.177.tag_ref, f32[4,256,768]{2,1,0:T(8,128)} %get-tuple-element.69.norm, f32[6,4,8,768]{3,2,1,0:T(8,128)} %broadcast_in_dim.36.mods, f32[9,768]{1,0:T(8,128)} %reshape.193.kernel), custom_call_target="tpu_custom_call" | custom-call | flops 600000000 | bytes 4194304 | tf_op jit(solution)/shard_map/first_conv/pallas_call | solution.py:225
  103.1 33.1 %attend.1 = (bf16[4,2304,256]{2,1,0:T(8,128)(2,1)}, bf16[4,256,768]{2,1,0:T(8,128)(2,1)}, bf16[4,256,768]{2,1,0:T(8,128)(2,1)}, f32[4,256,768]{2,1,0:T(8,128)}, ...) custom-call(s32[5]{0:T(128)} %stack.85.where.tag_ref, ...), custom_call_target="tpu_custom_call" | custom-call | flops 3800000000 | bytes 4194304 | tf_op jit(solution)/shard_map/attend/pallas_call | solution.py:340
  136.2 69.0 %feed.1 = (f32[4,256,768]{2,1,0:T(8,128)}, f32[4,256,768]{2,1,0:T(8,128)}, bf16[8,2,4,48,384]{4,3,2,1,0:T(8,128)(2,1)}, bf16[8,2,4,48,384]{4,3,2,1,0:T(8,128)(2,...) custom-call(s32[5]{0:T(128)} %stack.85.where.tag_ref, ...), custom_call_target="tpu_custom_call" | custom-call | flops 3800000000 | bytes 4194304 | tf_op jit(solution)/shard_map/feed/pallas_call | solution.py:455
  205.8 9.7 %attend_back_0.1 = (bf16[1,256,768]{2,1,0:T(8,128)(2,1)}, f32[1,256,768]{2,1,0:T(8,128)}, bf16[2304,256]{1,0:T(8,128)(2,1)}, bf16[768,256]{1,0:T(8,128)(2,1)}, f32[4,4,768]{2,1,0:T(4,128)}) custom-call(s32[5]{0:T(128)} %stack.85.where.tag_ref, f32[4,256,768]{2,1,0:T(8,128)} %get-tuple-element.75.resid, f32[4,256,768]{2,1,0:T(8,128)} %get-tuple-element.78.shrunk, ...), custom_call_target="tpu_custom_call" | custom-call | flops 900000000 | bytes 4194304 | tf_op jit(solution)/shard_map/attend_back_0/pallas_call | solution.py:576
  215.6 3.3 dynamic-slice_add_fusion
  219.4 2.1 dynamic-slice_add_fusion.1
  221.5 1.4 collective-permute-start.12
  222.9 23.1 %attend_back_1.1 = (bf16[3,256,768]{2,1,0:T(8,128)(2,1)}, f32[3,256,768]{2,1,0:T(8,128)}, bf16[2304,768]{1,0:T(8,128)(2,1)}, bf16[768,768]{1,0:T(8,128)(2,1)}, f32[4,4,768]{2,1,0:T(4,128)}) custom-call(s32[5]{0:T(128)} %stack.85.where.tag_ref, f32[4,256,768]{2,1,0:T(8,128)} %get-tuple-element.75.resid, f32[4,256,768]{2,1,0:T(8,128)} %get-tuple-element.78.shrunk, ...), custom_call_target="tpu_custom_call" | custom-call | flops 2700000000 | bytes 4194304 | tf_op jit(solution)/shard_map/attend_back_1/pallas_call | solution.py:576
  246.0 1.0 collective-permute-done.13
  247.0 2.2 collective-permute-done.12
  249.2 0.9 bitcast_add_fusion.1
  250.2 1.5 collective-permute-start.16
  251.7 0.9 bitcast_add_fusion
  252.6 1.1 collective-permute-start.17
  253.7 9.8 %project_grads.1 = (bf16[8,2,2,48,384]{4,3,2,1,0:T(8,128)(2,1)}, bf16[8,2,2,48,384]{4,3,2,1,0:T(8,128)(2,1)}, bf16[8,2,2,48,384]{4,3,2,1,0:T(8,128)(2,1)}, bf16[8,2,2,48,384]{4,3,2,1,0:T(8,128)(2,1)}) custom-call(s32[5]{0:T(128)} %stack.85.where.tag_ref, bf16[2304,256]{1,0:T(8,128)(2,1)} %get-tuple-element.84.d_qkv0, ...), custom_call_target="tpu_custom_call" | custom-call | flops 800000000 | bytes 4194304 | tf_op jit(solution)/shard_map/project_grads/pallas_call | solution.py:646
  264.5 2.3 collective-permute-done.17
  266.8 1.2 constant_dynamic-slice_fusion.2
  268.0 1.3 constant_dynamic-slice_fusion
  269.7 1.1 pad_maximum_fusion.4
  271.7 0.9 fusion
  273.4 0.9 fusion.1
  274.3 1.6 collective-permute-start.18
  276.1 16.3 %conv_back.1 = (f32[4,256,768]{2,1,0:T(8,128)}, bf16[32,16,288]{2,1,0:T(8,128)(2,1)}) custom-call(s32[5]{0:T(128)} %stack.85.where.tag_ref, bf16[2304,256]{1,0:T(8,128)(2,1)} %get-tuple-element.84.d_qkv0, bf16[2304,768]{1,0:T(8,128)(2,1)} %get-tuple-element.92.d_qkv1, bf16[2304,768]{1,0:T(8,128)(2,1)} %get-tuple-element.106.weight, ...), custom_call_target="tpu_custom_call" | custom-call | flops 1500000000 | bytes 4194304 | tf_op jit(solution)/shard_map/conv_back/pallas_call | solution.py:731
  292.4 3.9 %all-to-all-start.3 = ((bf16[32,16,288]{2,1,0:T(8,128)(2,1)}), bf16[32,16,288]{2,1,0:T(8,128)(2,1)S(1)}, u32[]{:S(2)}, u32[]{:S(2)}) async-start(bf16[32,16,288]{2,1,0:T(8,128)(2,1)} %get-tuple-element.114), calls=%async_computation.3 | async-start | bytes 786432 | tf_op jit(solution)/shard_map/all_to_all | solution.py:811
  296.5 1.9 fusion.16
  298.4 2.7 collective-permute-start.28
  301.1 1.0 fusion.23
  302.1 1.5 collective-permute-start.24
  303.6 1.0 fusion.24
  304.6 1.6 collective-permute-start.23
  306.2 8.4 %finish.1 = (bf16[1024,768]{1,0:T(8,128)(2,1)}, f32[1024,768]{1,0:T(8,128)}) custom-call(f32[4,256,768]{2,1,0:T(8,128)} %get-tuple-element.115.d_first, f32[4,256,768]{2,1,0:T(8,128)} %get-tuple-element.69.norm, f32[4,256,1]{2,1,0:T(8,128)} %get-tuple-element.116.factor, f32[1,256,768]{2,1,0:T(8,128)} %get-tuple-element.117.d_resid0, ...), custom_call_target="tpu_custom_call" | custom-call | flops 800000000 | bytes 4194304 | tf_op jit(solution)/shard_map/finish/pallas_call | solution.py:789
  315.4 1.0 fusion.41
  318.0 0.8 copy.133
  318.8 3.6 %all-to-all-start.4 = ((f32[16,24,128]{2,1,0:T(8,128)}), f32[16,24,128]{2,1,0:T(8,128)S(1)}, u32[]{:S(2)}, u32[]{:S(2)}) async-start(f32[16,24,128]{2,1,0:T(8,128)} %bitcast.74), calls=%async_computation.4 | async-start | bytes 393216 | tf_op jit(solution)/shard_map/all_to_all | solution.py:940
  322.4 1.1 bitcast_add_fusion.4
  323.5 1.1 bitcast_add_fusion.6
  324.7 2.0 collective-permute-start.25
  326.7 2.4 collective-permute-start.26
  329.1 1.5 collective-permute-start.27
  330.5 1.3 all-to-all-done.4
  332.6 7.3 %collective-permute-start.22 = (f32[24,128]{1,0:T(8,128)S(1)}, f32[24,128]{1,0:T(8,128)S(1)}, u32[]{:S(2)}, u32[]{:S(2)}) collective-permute-start(f32[24,128]{1,0:T(8,128)S(1)} %reduce_sum.28), channel_id=1, source_target_pairs={{0,1},{1,17},{2,0},{3,16},{4,3},{5,19},{6,2},{7,18},{8,5},{9,21},{... | collective-permute-start | bytes 36872 | tf_op jit(solution)/shard_map/ppermute | solution.py:955
  339.8 1.3 convert_add_fusion
  342.7 0.9 fusion.4
  343.6 0.9 fusion.7
  (142 shorter events, 19.6 us)
Async XLA Ops:
  7.2 71.3 %copy-start = (bf16[384,288]{0,1:T(8,128)(2,1)S(1)}, bf16[384,288]{0,1:T(8,128)(2,1)}, u32[]{:S(2)}) copy-start(bf16[384,288]{0,1:T(8,128)(2,1)} %param.20) | copy-start | bytes 663556
  7.2 2.8 copy-start.10
  7.2 2.8 copy-start.9
  7.2 8.9 %copy-start.16 = (s32[1,4]{1,0:T(1,128)S(1)}, s32[1,4]{1,0:T(1,128)}, u32[]{:S(2)}) copy-start(s32[1,4]{1,0:T(1,128)} %param.16) | copy-start | bytes 52
  7.2 8.9 %copy-start.15 = (s32[1,4]{1,0:T(1,128)S(1)}, s32[1,4]{1,0:T(1,128)}, u32[]{:S(2)}) copy-start(s32[1,4]{1,0:T(1,128)} %param.17) | copy-start | bytes 52
  7.2 129.0 %all-gather.2.cloned.1.call-start = ((), (), s32[]{:S(2)}) async-start(), calls=%async_computation.5 | async-start | bytes 9732096 | tf_op jit(solution)/shard_map/all_gather | solution.py:825
  10.0 22.7 %collective-permute-start.1 = (bf16[4,48,384]{2,1,0:T(8,128)(2,1)S(1)}, bf16[4,48,384]{2,1,0:T(8,128)(2,1)S(1)}, u32[]{:S(2)}, u32[]{:S(2)}) collective-permute-start(bf16[4,48,384]{2,1,0:T(8,128)(2,1)S(1)} %pad_maximum_fusion.8), channel_id=1, source_target_pairs={{0,24},{2,26},{4,28},{6,30},{8,0},{10,2},{12,4},{14,6},{16,8},{18,... | collective-permute-start | bytes 442376 | tf_op jit(solution)/shard_map/ppermute | solution.py:841
  15.1 17.7 %collective-permute-start.2 = (bf16[4,48,384]{2,1,0:T(8,128)(2,1)S(1)}, bf16[4,48,384]{2,1,0:T(8,128)(2,1)S(1)}, u32[]{:S(2)}, u32[]{:S(2)}) collective-permute-start(bf16[4,48,384]{2,1,0:T(8,128)(2,1)S(1)} %pad_maximum_fusion.8), channel_id=1, source_target_pairs={{0,16},{2,18},{4,20},{6,22},{8,24},{10,26},{12,28},{14,30},{16,0},... | collective-permute-start | bytes 442376 | tf_op jit(solution)/shard_map/ppermute | solution.py:841
  15.1 17.7 %collective-permute-start.3 = (bf16[4,48,384]{2,1,0:T(8,128)(2,1)S(1)}, bf16[4,48,384]{2,1,0:T(8,128)(2,1)S(1)}, u32[]{:S(2)}, u32[]{:S(2)}) collective-permute-start(bf16[4,48,384]{2,1,0:T(8,128)(2,1)S(1)} %pad_maximum_fusion.8), channel_id=1, source_target_pairs={{0,8},{2,10},{4,12},{6,14},{8,16},{10,18},{12,20},{14,22},{16,24},... | collective-permute-start | bytes 442376 | tf_op jit(solution)/shard_map/ppermute | solution.py:841
  16.8 15.3 %all-to-all-start = ((s32[32,1,8]{2,1,0:T(1,128)}), s32[32,1,8]{2,1,0:T(1,128)S(1)}, u32[]{:S(2)}, u32[]{:S(2)}) async-start(s32[32,1,8]{2,1,0:T(1,128)} %broadcast_in_dim.18), calls=%async_computation | async-start | bytes 32768 | tf_op jit(solution)/shard_map/all_to_all | solution.py:811
  21.9 10.5 %copy-start.13 = (bf16[500,48]{0,1:T(8,128)(2,1)S(1)}, bf16[500,48]{0,1:T(8,128)(2,1)}, u32[]{:S(2)}) copy-start(bf16[500,48]{0,1:T(8,128)(2,1)} %param.18) | copy-start | bytes 144004
  32.7 1.7 copy-start.14
  32.8 3.3 copy-start.11
  32.8 3.3 copy-start.12
  32.9 9.4 %collective-permute-start.5 = (bf16[4,2,48,384]{3,2,1,0:T(8,128)(2,1)S(1)}, bf16[4,2,48,384]{3,2,1,0:T(8,128)(2,1)S(1)}, u32[]{:S(2)}, u32[]{:S(2)}) collective-permute-start(bf16[4,2,48,384]{3,2,1,0:T(8,128)(2,1)S(1)} %get-tuple-element.159), channel_id=1, source_target_pairs={{0,1},{1,0},{2,3},{3,2},{4,5},{5,4},{6,7},{7,6},{8,9},{9,8},{10,11... | collective-permute-start | bytes 884744 | tf_op jit(solution)/shard_map/ppermute | solution.py:865
  33.6 9.4 %collective-permute-start.4 = (bf16[4,2,48,384]{3,2,1,0:T(8,128)(2,1)S(1)}, bf16[4,2,48,384]{3,2,1,0:T(8,128)(2,1)S(1)}, u32[]{:S(2)}, u32[]{:S(2)}) collective-permute-start(bf16[4,2,48,384]{3,2,1,0:T(8,128)(2,1)S(1)} %get-tuple-element.161), channel_id=1, source_target_pairs={{0,4},{2,6},{4,0},{6,2},{8,12},{10,14},{12,8},{14,10},{16,20},{18,... | collective-permute-start | bytes 884744 | tf_op jit(solution)/shard_map/ppermute | solution.py:866
  34.7 7.6 %collective-permute-start = (f32[128,48]{0,1:T(8,128)S(1)}, f32[128,48]{0,1:T(8,128)S(1)}, u32[]{:S(2)}, u32[]{:S(2)}) collective-permute-start(f32[128,48]{0,1:T(8,128)S(1)} %convolution_add_fusion), channel_id=1, source_target_pairs={{0,1},{1,0},{2,3},{3,2},{4,5},{5,4},{6,7},{7,6},{8,9},{9,8},{10,11... | collective-permute-start | bytes 73736 | tf_op jit(solution)/shard_map/ppermute | solution.py:865
  42.4 27.0 %collective-permute-start.7 = (bf16[2,4,2,48,384]{4,3,2,1,0:T(8,128)(2,1)S(1)}, bf16[2,4,2,48,384]{4,3,2,1,0:T(8,128)(2,1)}, u32[]{:S(2)}, u32[]{:S(2)}) collective-permute-start(bf16[2,4,2,48,384]{4,3,2,1,0:T(8,128)(2,1)S(1)} %get-tuple-element.155), channel_id=1, source_target_pairs={{0,4},{2,6},{4,0},{6,2},{8,12},{10,14},{12,8},{14,10},{16,20},{18,... | collective-permute-start | bytes 1769480 | tf_op jit(solution)/shard_map/ppermute | solution.py:866
  44.8 24.6 %all-to-all-start.1 = ((bf16[16,173,48]{1,2,0:T(8,128)(2,1)}), bf16[16,173,48]{1,2,0:T(8,128)(2,1)S(1)}, u32[]{:S(2)}, u32[]{:S(2)}) async-start(bf16[16,173,48]{1,2,0:T(8,128)(2,1)} %broadcast_in_dim.32), calls=%async_computation.1 | async-start | bytes 786432 | tf_op jit(solution)/shard_map/all_to_all | solution.py:929
  56.2 18.8 %collective-permute-start.6 = (bf16[2,4,2,48,384]{4,3,2,1,0:T(8,128)(2,1)}, bf16[2,4,2,48,384]{4,3,2,1,0:T(8,128)(2,1)}, u32[]{:S(2)}, u32[]{:S(2)}) collective-permute-start(bf16[2,4,2,48,384]{4,3,2,1,0:T(8,128)(2,1)} %get-tuple-element.157), channel_id=1, source_target_pairs={{0,1},{1,0},{2,3},{3,2},{4,5},{5,4},{6,7},{7,6},{8,9},{9,8},{10,11... | collective-permute-start | bytes 1769480 | tf_op jit(solution)/shard_map/ppermute | solution.py:865
  69.4 9.0 %copy-start.6 = (bf16[16,128,48]{1,2,0:T(8,128)(2,1)}, bf16[16,128,48]{1,2,0:T(8,128)(2,1)S(1)}, u32[]{:S(2)}) copy-start(bf16[16,128,48]{1,2,0:T(8,128)(2,1)S(1)} %slice.101) | copy-start | bytes 589828
  70.7 6.5 %copy-start.5 = (bf16[2,2,4,2,48,384]{5,4,3,2,1,0:T(8,128)(2,1)}, bf16[2,2,4,2,48,384]{5,4,3,2,1,0:T(8,128)(2,1)S(1)}, u32[]{:S(2)}) copy-start(bf16[2,2,4,2,48,384]{5,4,3,2,1,0:T(8,128)(2,1)S(1)} %pad_maximum_fusion.1.own_b) | copy-start | bytes 3538948
  70.8 32.3 %collective-permute-start.9 = (bf16[2,2,4,2,48,384]{5,4,3,2,1,0:T(8,128)(2,1)S(1)}, bf16[2,2,4,2,48,384]{5,4,3,2,1,0:T(8,128)(2,1)}, u32[]{:S(2)}, u32[]{:S(2)}) collective-permute-start(bf16[2,2,4,2,48,384]{5,4,3,2,1,0:T(8,128)(2,1)S(1)} %pad_maximum_fusion.1.own_b), channel_id=1, source_target_pairs={{0,2},{2,0},{4,6},{6,4},{8,10},{10,8},{12,14},{14,12},{16,18},{18,... | collective-permute-start | bytes 3538952 | tf_op jit(solution)/shard_map/ppermute | solution.py:866
  77.2 25.8 %collective-permute-start.8 = (bf16[2,2,4,2,48,384]{5,4,3,2,1,0:T(8,128)(2,1)}, bf16[2,2,4,2,48,384]{5,4,3,2,1,0:T(8,128)(2,1)}, u32[]{:S(2)}, u32[]{:S(2)}) collective-permute-start(bf16[2,2,4,2,48,384]{5,4,3,2,1,0:T(8,128)(2,1)} %pad_maximum_fusion.own_a), channel_id=1, source_target_pairs={{0,2},{2,0},{4,6},{6,4},{8,10},{10,8},{12,14},{14,12},{16,18},{18,... | collective-permute-start | bytes 3538952 | tf_op jit(solution)/shard_map/ppermute | solution.py:866
  79.7 15.4 %all-to-all-start.2 = ((f32[32,1,1152]{2,1,0:T(1,128)}), f32[32,1,1152]{2,1,0:T(1,128)S(1)}, u32[]{:S(2)}, u32[]{:S(2)}) async-start(f32[32,1,1152]{2,1,0:T(1,128)} %reshape.217), calls=%async_computation.2 | async-start | bytes 294912 | tf_op jit(solution)/shard_map/all_to_all | solution.py:811
  205.2 10.3 %collective-permute-start.11 = (bf16[8,2,4,48,384]{4,3,2,1,0:T(8,128)(2,1)}, bf16[8,2,4,48,384]{4,3,2,1,0:T(8,128)(2,1)}, u32[]{:S(2)}, u32[]{:S(2)}) collective-permute-start(bf16[8,2,4,48,384]{4,3,2,1,0:T(8,128)(2,1)} %get-tuple-element.89), channel_id=1, source_target_pairs={{0,2},{2,0},{4,6},{6,4},{8,10},{10,8},{12,14},{14,12},{16,18},{18,... | collective-permute-start | bytes 7077896 | tf_op jit(solution)/shard_map/ppermute | solution.py:866
  205.3 10.3 %collective-permute-start.10 = (bf16[8,2,4,48,384]{4,3,2,1,0:T(8,128)(2,1)}, bf16[8,2,4,48,384]{4,3,2,1,0:T(8,128)(2,1)}, u32[]{:S(2)}, u32[]{:S(2)}) collective-permute-start(bf16[8,2,4,48,384]{4,3,2,1,0:T(8,128)(2,1)} %get-tuple-element.86), channel_id=1, source_target_pairs={{0,2},{2,0},{4,6},{6,4},{8,10},{10,8},{12,14},{14,12},{16,18},{18,... | collective-permute-start | bytes 7077896 | tf_op jit(solution)/shard_map/ppermute | solution.py:866
  205.8 9.8 %copy-start.2 = (bf16[8,2,4,48,384]{4,3,2,1,0:T(8,128)(2,1)S(1)}, bf16[8,2,4,48,384]{4,3,2,1,0:T(8,128)(2,1)}, u32[]{:S(2)}) copy-start(bf16[8,2,4,48,384]{4,3,2,1,0:T(8,128)(2,1)} %get-tuple-element.88) | copy-start | bytes 7077892
  215.6 3.8 %copy-start.1 = (bf16[8,2,4,48,384]{4,3,2,1,0:T(8,128)(2,1)S(1)}, bf16[8,2,4,48,384]{4,3,2,1,0:T(8,128)(2,1)}, u32[]{:S(2)}) copy-start(bf16[8,2,4,48,384]{4,3,2,1,0:T(8,128)(2,1)} %get-tuple-element.85) | copy-start | bytes 7077892
  218.9 28.2 %collective-permute-start.13 = (bf16[4,2,4,48,384]{4,3,2,1,0:T(8,128)(2,1)}, bf16[4,2,4,48,384]{4,3,2,1,0:T(8,128)(2,1)S(1)}, u32[]{:S(2)}, u32[]{:S(2)}) collective-permute-start(bf16[4,2,4,48,384]{4,3,2,1,0:T(8,128)(2,1)} %get-tuple-element.128), channel_id=1, source_target_pairs={{0,4},{2,6},{4,0},{6,2},{8,12},{10,14},{12,8},{14,10},{16,20},{18,... | collective-permute-start | bytes 3538952 | tf_op jit(solution)/shard_map/ppermute | solution.py:866
  221.5 27.7 %collective-permute-start.12 = (bf16[4,2,4,48,384]{4,3,2,1,0:T(8,128)(2,1)S(1)}, bf16[4,2,4,48,384]{4,3,2,1,0:T(8,128)(2,1)S(1)}, u32[]{:S(2)}, u32[]{:S(2)}) collective-permute-start(bf16[4,2,4,48,384]{4,3,2,1,0:T(8,128)(2,1)S(1)} %get-tuple-element.130), channel_id=1, source_target_pairs={{0,1},{1,0},{2,3},{3,2},{4,5},{5,4},{6,7},{7,6},{8,9},{9,8},{10,11... | collective-permute-start | bytes 3538952 | tf_op jit(solution)/shard_map/ppermute | solution.py:865
  250.2 14.4 %collective-permute-start.16 = (bf16[4,4,48,384]{3,2,1,0:T(8,128)(2,1)}, bf16[4,4,48,384]{3,2,1,0:T(8,128)(2,1)S(1)}, u32[]{:S(2)}, u32[]{:S(2)}) collective-permute-start(bf16[4,4,48,384]{3,2,1,0:T(8,128)(2,1)} %get-tuple-element.132), channel_id=1, source_target_pairs={{0,4},{2,6},{4,0},{6,2},{8,12},{10,14},{12,8},{14,10},{16,20},{18,... | collective-permute-start | bytes 1769480 | tf_op jit(solution)/shard_map/ppermute | solution.py:866
  252.6 14.2 %collective-permute-start.17 = (bf16[4,4,48,384]{3,2,1,0:T(8,128)(2,1)}, bf16[4,4,48,384]{3,2,1,0:T(8,128)(2,1)}, u32[]{:S(2)}, u32[]{:S(2)}) collective-permute-start(bf16[4,4,48,384]{3,2,1,0:T(8,128)(2,1)} %get-tuple-element.134), channel_id=1, source_target_pairs={{0,1},{1,0},{2,3},{3,2},{4,5},{5,4},{6,7},{7,6},{8,9},{9,8},{10,11... | collective-permute-start | bytes 1769480 | tf_op jit(solution)/shard_map/ppermute | solution.py:865
  263.5 7.9 %collective-permute-start.15 = (bf16[8,2,2,48,384]{4,3,2,1,0:T(8,128)(2,1)}, bf16[8,2,2,48,384]{4,3,2,1,0:T(8,128)(2,1)S(1)}, u32[]{:S(2)}, u32[]{:S(2)}) collective-permute-start(bf16[8,2,2,48,384]{4,3,2,1,0:T(8,128)(2,1)} %get-tuple-element.103), channel_id=1, source_target_pairs={{0,2},{2,0},{4,6},{6,4},{8,10},{10,8},{12,14},{14,12},{16,18},{18,... | collective-permute-start | bytes 3538952 | tf_op jit(solution)/shard_map/ppermute | solution.py:866
  263.7 9.5 %collective-permute-start.14 = (bf16[8,2,2,48,384]{4,3,2,1,0:T(8,128)(2,1)}, bf16[8,2,2,48,384]{4,3,2,1,0:T(8,128)(2,1)S(1)}, u32[]{:S(2)}, u32[]{:S(2)}) collective-permute-start(bf16[8,2,2,48,384]{4,3,2,1,0:T(8,128)(2,1)} %get-tuple-element.101), channel_id=1, source_target_pairs={{0,2},{2,0},{4,6},{6,4},{8,10},{10,8},{12,14},{14,12},{16,18},{18,... | collective-permute-start | bytes 3538952 | tf_op jit(solution)/shard_map/ppermute | solution.py:866
  264.5 2.3 copy-start.8
  269.5 1.9 copy-start.4
  270.9 25.6 %collective-permute-start.20 = (bf16[2,8,48,384]{3,1,2,0:T(8,128)(2,1)}, bf16[2,8,48,384]{3,1,2,0:T(8,128)(2,1)}, u32[]{:S(2)}, u32[]{:S(2)}) collective-permute-start(bf16[2,8,48,384]{3,1,2,0:T(8,128)(2,1)} %pad_maximum_fusion.4), channel_id=1, source_target_pairs={{0,8},{2,10},{4,12},{6,14},{8,0},{10,2},{12,4},{14,6},{16,24},{18,... | collective-permute-start | bytes 1769480 | tf_op jit(solution)/shard_map/ppermute | solution.py:866
  271.7 1.5 copy-start.3
  272.6 28.5 %collective-permute-start.19 = (bf16[4,2,2,48,384]{4,3,2,0,1:T(8,128)(2,1)}, bf16[4,2,2,48,384]{4,3,2,0,1:T(8,128)(2,1)}, u32[]{:S(2)}, u32[]{:S(2)}) collective-permute-start(bf16[4,2,2,48,384]{4,3,2,0,1:T(8,128)(2,1)} %fusion), channel_id=1, source_target_pairs={{0,4},{2,6},{4,0},{6,2},{8,12},{10,14},{12,8},{14,10},{16,20},{18,... | collective-permute-start | bytes 1769480 | tf_op jit(solution)/shard_map/ppermute | solution.py:866
  274.3 26.8 %collective-permute-start.18 = (bf16[4,2,2,48,384]{4,3,2,0,1:T(8,128)(2,1)}, bf16[4,2,2,48,384]{4,3,2,0,1:T(8,128)(2,1)}, u32[]{:S(2)}, u32[]{:S(2)}) collective-permute-start(bf16[4,2,2,48,384]{4,3,2,0,1:T(8,128)(2,1)} %fusion.1), channel_id=1, source_target_pairs={{0,1},{1,0},{2,3},{3,2},{4,5},{5,4},{6,7},{7,6},{8,9},{9,8},{10,11... | collective-permute-start | bytes 1769480 | tf_op jit(solution)/shard_map/ppermute | solution.py:865
  292.4 22.9 %all-to-all-start.3 = ((bf16[32,16,288]{2,1,0:T(8,128)(2,1)}), bf16[32,16,288]{2,1,0:T(8,128)(2,1)S(1)}, u32[]{:S(2)}, u32[]{:S(2)}) async-start(bf16[32,16,288]{2,1,0:T(8,128)(2,1)} %get-tuple-element.114), calls=%async_computation.3 | async-start | bytes 786432 | tf_op jit(solution)/shard_map/all_to_all | solution.py:811
  298.4 34.2 %collective-permute-start.28 = (bf16[8,48,384]{2,0,1:T(8,128)(2,1)}, bf16[8,48,384]{2,0,1:T(8,128)(2,1)}, u32[]{:S(2)}, u32[]{:S(2)}) collective-permute-start(bf16[8,48,384]{2,0,1:T(8,128)(2,1)} %fusion.16), channel_id=1, source_target_pairs={{0,16},{2,18},{4,20},{6,22},{8,24},{10,26},{12,28},{14,30},{16,0},... | collective-permute-start | bytes 884744 | tf_op jit(solution)/shard_map/ppermute | solution.py:866
  302.1 20.3 %collective-permute-start.24 = (bf16[4,2,48,384]{3,2,1,0:T(8,128)(2,1)S(1)}, bf16[4,2,48,384]{3,2,1,0:T(8,128)(2,1)}, u32[]{:S(2)}, u32[]{:S(2)}) collective-permute-start(bf16[4,2,48,384]{3,2,1,0:T(8,128)(2,1)S(1)} %fusion.23), channel_id=1, source_target_pairs={{0,1},{1,0},{2,3},{3,2},{4,5},{5,4},{6,7},{7,6},{8,9},{9,8},{10,11... | collective-permute-start | bytes 884744 | tf_op jit(solution)/shard_map/ppermute | solution.py:865
  304.6 18.9 %collective-permute-start.23 = (bf16[4,2,48,384]{3,2,1,0:T(8,128)(2,1)S(1)}, bf16[4,2,48,384]{3,2,1,0:T(8,128)(2,1)}, u32[]{:S(2)}, u32[]{:S(2)}) collective-permute-start(bf16[4,2,48,384]{3,2,1,0:T(8,128)(2,1)S(1)} %fusion.24), channel_id=1, source_target_pairs={{0,4},{2,6},{4,0},{6,2},{8,12},{10,14},{12,8},{14,10},{16,20},{18,... | collective-permute-start | bytes 884744 | tf_op jit(solution)/shard_map/ppermute | solution.py:866
  306.2 9.2 %copy-start.7 = (bf16[16,128,48]{1,2,0:T(8,128)(2,1)S(1)}, bf16[16,128,48]{1,2,0:T(8,128)(2,1)}, u32[]{:S(2)}) copy-start(bf16[16,128,48]{1,2,0:T(8,128)(2,1)} %copy-done.6) | copy-start | bytes 589828
  318.8 13.1 %all-to-all-start.4 = ((f32[16,24,128]{2,1,0:T(8,128)}), f32[16,24,128]{2,1,0:T(8,128)S(1)}, u32[]{:S(2)}, u32[]{:S(2)}) async-start(f32[16,24,128]{2,1,0:T(8,128)} %bitcast.74), calls=%async_computation.4 | async-start | bytes 393216 | tf_op jit(solution)/shard_map/all_to_all | solution.py:940
  324.7 19.8 %collective-permute-start.25 = (bf16[4,48,384]{2,1,0:T(8,128)(2,1)S(1)}, bf16[4,48,384]{2,1,0:T(8,128)(2,1)S(1)}, u32[]{:S(2)}, u32[]{:S(2)}) collective-permute-start(bf16[4,48,384]{2,1,0:T(8,128)(2,1)S(1)} %get-tuple-element.143), channel_id=1, source_target_pairs={{0,8},{2,10},{4,12},{6,14},{8,16},{10,18},{12,20},{14,22},{16,24},... | collective-permute-start | bytes 442376 | tf_op jit(solution)/shard_map/ppermute | solution.py:882
  326.7 17.8 %collective-permute-start.26 = (bf16[4,48,384]{2,1,0:T(8,128)(2,1)S(1)}, bf16[4,48,384]{2,1,0:T(8,128)(2,1)S(1)}, u32[]{:S(2)}, u32[]{:S(2)}) collective-permute-start(bf16[4,48,384]{2,1,0:T(8,128)(2,1)S(1)} %get-tuple-element.144), channel_id=1, source_target_pairs={{0,16},{2,18},{4,20},{6,22},{8,24},{10,26},{12,28},{14,30},{16,0},... | collective-permute-start | bytes 442376 | tf_op jit(solution)/shard_map/ppermute | solution.py:882
  329.1 15.5 %collective-permute-start.27 = (bf16[4,48,384]{2,1,0:T(8,128)(2,1)S(1)}, bf16[4,48,384]{2,1,0:T(8,128)(2,1)S(1)}, u32[]{:S(2)}, u32[]{:S(2)}) collective-permute-start(bf16[4,48,384]{2,1,0:T(8,128)(2,1)S(1)} %get-tuple-element.145), channel_id=1, source_target_pairs={{0,24},{2,26},{4,28},{6,30},{8,0},{10,2},{12,4},{14,6},{16,8},{18,... | collective-permute-start | bytes 442376 | tf_op jit(solution)/shard_map/ppermute | solution.py:882
  331.9 10.8 %collective-permute-start.21 = (f32[24,128]{1,0:T(8,128)S(1)}, f32[24,128]{1,0:T(8,128)S(1)}, u32[]{:S(2)}, u32[]{:S(2)}) collective-permute-start(f32[24,128]{1,0:T(8,128)S(1)} %reduce_sum.28), channel_id=1, source_target_pairs={{0,0},{1,16},{2,1},{3,17},{4,2},{5,18},{6,3},{7,19},{8,4},{9,20},{... | collective-permute-start | bytes 36872 | tf_op jit(solution)/shard_map/ppermute | solution.py:954
  332.6 10.1 %collective-permute-start.22 = (f32[24,128]{1,0:T(8,128)S(1)}, f32[24,128]{1,0:T(8,128)S(1)}, u32[]{:S(2)}, u32[]{:S(2)}) collective-permute-start(f32[24,128]{1,0:T(8,128)S(1)} %reduce_sum.28), channel_id=1, source_target_pairs={{0,1},{1,17},{2,0},{3,16},{4,3},{5,19},{6,2},{7,18},{8,5},{9,21},{... | collective-permute-start | bytes 36872 | tf_op jit(solution)/shard_map/ppermute | solution.py:955
Sparse Core Ops, SparseCore 0:
  11.6 92.7 all-gather.1

commit v7 on v6

--- a/solution.py
+++ b/solution.py
@@ -918,17 +918,20 @@
     own = first_row + jnp.arange(step_table.shape[0], dtype=jnp.int32)
     step_hot = (ids[:, :4].reshape(-1, 1) == own[None, :]).astype(BF)
     class_hot = (ids[:, 4:].reshape(-1, 1) == own[None, :]).astype(BF)
-    return step_hot, class_hot, dot(step_hot, step_table, 1, 0) + dot(class_hot, class_table, 1, 0)
+    return step_hot, class_hot, dot(step_table, step_hot, 0, 1) + dot(class_table, class_hot, 0, 1)
 
 
 def share_act(nd, cond, attn_kernel, ffn_kernel):
-    items, width = cond.shape
+    width, items = cond.shape
     act = jax.nn.silu(cond).astype(BF)
-    filters = jnp.concatenate([attn_kernel, ffn_kernel], axis=1).reshape(-1, width)
+    filters = jnp.concatenate([attn_kernel, ffn_kernel], axis=1).reshape(-1)
+    size = filters.shape[0]
+    filters = jnp.pad(filters, (0, -size % items)).reshape(-1, items)
     sent = jnp.concatenate([act, filters], axis=0)[None]
     sent = lax.all_to_all(jnp.broadcast_to(sent, (nd,) + sent.shape[1:]), "dp", 0, 0, tiled=True)
-    act_all = sent[:, :items].transpose(1, 0, 2).reshape(items, nd * width)
-    filters = sent[:, items:].reshape(nd, 9, -1).astype(F32)
+    act_all = sent[:, :width].reshape(nd * width, items)
+    filters = sent[:, width:].reshape(nd, -1)[:, :size]
+    filters = filters.reshape(nd, 9, -1).astype(F32)
     attn_full = filters[:, :, : attn_kernel.shape[1]].transpose(1, 0, 2).reshape(9, -1)
     ffn_full = filters[:, :, attn_kernel.shape[1] :].transpose(1, 0, 2).reshape(9, -1)
     return act_all, attn_full, ffn_full
@@ -997,9 +1000,9 @@
         next_a, next_b = after(next_a, act_all), after(next_b, act_all)
     height, width = modulation_weight.shape
     act_rows = lax.dynamic_slice_in_dim(
-        act_all, lax.axis_index("fsdp") * height, height, axis=1
-    )
-    terms = dot(act_rows, modulation_weight, 1, 0)
+        act_all, lax.axis_index("fsdp") * height, height, axis=0
+    )
+    terms = dot(act_rows, modulation_weight, 0, 0)
     terms = exchange(terms.reshape(slots, 1, 4 * width)).reshape(nd, nf, 4, width)
     if square:
         a, b = jnp.stack([a, next_a]), jnp.stack([b, next_b])
@@ -1100,10 +1103,10 @@
     ]
     cut = attn_kernel.shape[1]
     filters = got[:, 4:13, : cut + ffn_kernel.shape[1]].astype(F32).sum(axis=0)
-    modulation_grad = dot(act_rows, d_mod_all, 0, 0)
+    modulation_grad = dot(act_rows, d_mod_all, 1, 0)
     gate = jax.nn.sigmoid(cond)
     d_cond = own_columns(nd, nf, own_act)
-    d_cond = d_cond * (gate * (1.0 + cond * (1.0 - gate))).T
+    d_cond = d_cond * (gate * (1.0 + cond * (1.0 - gate)))
 
     def table_grad(hot):
         return lax.dot_general(

time: 354 us -> 344 us (0.972)
  waiting for transfers between devices: 42.6 us -> 32.7 us
    all_to_all x3, waiting for transfers between devices: 12.6 us -> 6.43 us  [exchange(): return lax.all_to_all(pieces, BOTH, 0, 0, tiled=True)]
    ppermute x7, waiting for transfers between devices: 14.6 us -> 10.5 us  [swap(): return lax.ppermute(value, 'fsdp', [(0, 1), (1, 0)])]
    ppermute x14, waiting for transfers between devices: 1.56 us -> 5.39 us  [swap(): return lax.ppermute(value, 'dp', [(i, i ^ bit) for i in range(NJ)])]
  transfers between devices with their start and end apart: 35 -> 35, of which waited for: 11 -> 11; matrix products, arithmetic and copies ran while one was open for 11% -> 11% of each run, Pallas kernels for 32% -> 33%
where the time goes in v7:
time: 344 us; the launch traced here: 342 us
  Pallas kernels  182 us (53%)
  starting transfers between devices  65.9 us (19%)
  waiting for transfers between devices  32.7 us (10%)
  other arithmetic  25.5 us (7%)
  local copies, waits for them, and re-layouts  17.3 us (5%)
  between operations  15.6 us (5%)
  matrix products  3.82 us (1%)
    pallas_call x1, Pallas kernels, feed(): pl.pallas_call(feed_kernel, grid=(FF // CHUNK,), in_specs=[SMEM_SPEC, who...  69 us
    pallas_call x1, Pallas kernels, attend(): pl.pallas_call(attend_kernel, grid=(4,), in_specs=[SMEM_SPEC, group_spec(...  33.3 us
    pallas_call x2, Pallas kernels, attend_back(): pl.pallas_call(attend_back_kernel, grid=(count,), in_specs=[SMEM_SPEC, pi...  32.8 us
    pallas_call x1, Pallas kernels, conv_back(): pl.pallas_call(conv_back_kernel, grid=(8 // PAIRS,), in_specs=[SMEM_SPEC,...  16.3 us
    ppermute x14, starting transfers between devices, swap(): return lax.ppermute(value, 'dp', [(i, i ^ bit) for i in range(NJ)])  12.4 us
    all_to_all x1, starting transfers between devices, share_act(): lax.all_to_all(jnp.broadcast_to(sent, (nd,) + sent.shape[1:]), 'dp', 0, 0...  11.3 us
    all_to_all x3, starting transfers between devices, exchange(): return lax.all_to_all(pieces, BOTH, 0, 0, tiled=True)  11.1 us
    ppermute x7, waiting for transfers between devices, swap(): return lax.ppermute(value, 'fsdp', [(0, 1), (1, 0)])  10.5 us
  transfers between devices with their start and end apart: 35, of which 11 were waited for; matrix products, arithmetic and copies ran while one was open for 11% of the time, Pallas kernels for 33%

profile of v7, /device:TPU:0, one launch (start us, length us, event | category | flops | bytes accessed | tf_op | source)
XLA Modules:
  0.0 342.3 jit_solution(13144683090334170684)
XLA Ops:
  7.3 1.0 copy.123
  8.3 1.7 pad_maximum_fusion.7
  10.0 5.1 %collective-permute-start.1 = (bf16[4,48,384]{2,1,0:T(8,128)(2,1)S(1)}, bf16[4,48,384]{2,1,0:T(8,128)(2,1)S(1)}, u32[]{:S(2)}, u32[]{:S(2)}) collective-permute-start(bf16[4,48,384]{2,1,0:T(8,128)(2,1)S(1)} %pad_maximum_fusion.8), channel_id=1, source_target_pairs={{0,24},{2,26},{4,28},{6,30},{8,0},{10,2},{12,4},{14,6},{16,8},{18,... | collective-permute-start | bytes 442376 | tf_op jit(solution)/shard_map/ppermute | solution.py:841
  15.1 1.0 collective-permute-start.3
  16.8 5.1 %all-to-all-start = ((s32[32,1,8]{2,1,0:T(1,128)}), s32[32,1,8]{2,1,0:T(1,128)S(1)}, u32[]{:S(2)}, u32[]{:S(2)}) async-start(s32[32,1,8]{2,1,0:T(1,128)} %broadcast_in_dim.18), calls=%async_computation | async-start | bytes 32768 | tf_op jit(solution)/shard_map/all_to_all | solution.py:811
  22.1 6.0 %prepare.1 = (bf16[4,256,768]{2,1,0:T(8,128)(2,1)}, bf16[4,256,768]{2,1,0:T(8,128)(2,1)}, f32[4,256,768]{2,1,0:T(8,128)}, f32[4,256,1]{2,1,0:T(8,128)}) custom-call(bf16[1024,768]{1,0:T(8,128)(2,1)} %latents.1, bf16[1024,768]{1,0:T(8,128)(2,1)} %cotangent.1), custom_call_target="tpu_custom_call" | custom-call | flops 600000000 | bytes 4194304 | tf_op jit(solution)/shard_map/prepare/pallas_call | solution.py:89
  28.2 4.0 %all-to-all-done = s32[32,1,8]{2,1,0:T(1,128)S(1)} async-done(((s32[32,1,8]{2,1,0:T(1,128)}), s32[32,1,8]{2,1,0:T(1,128)S(1)}, u32[]{:S(2)}, u32[]{:S(2)}) %all-to-all-start) | async-done | bytes 1056 | tf_op jit(solution)/shard_map/all_to_all | solution.py:811
  34.7 1.4 collective-permute-start
  36.1 6.2 %collective-permute-done = f32[48,128]{1,0:T(8,128)S(1)} collective-permute-done((f32[48,128]{1,0:T(8,128)S(1)}, f32[48,128]{1,0:T(8,128)S(1)}, u32[]{:S(2)}, u32[]{:S(2)}) %collective-permute-start) | collective-permute-done | bytes 24608 | tf_op jit(solution)/shard_map/ppermute | solution.py:865
  43.4 11.3 %all-to-all-start.1 = ((bf16[16,65,128]{2,1,0:T(8,128)(2,1)}), bf16[16,65,128]{2,1,0:T(8,128)(2,1)S(1)}, u32[]{:S(2)}, u32[]{:S(2)}) async-start(bf16[16,65,128]{2,1,0:T(8,128)(2,1)} %broadcast_in_dim.32), calls=%async_computation.1 | async-start | bytes 589824 | tf_op jit(solution)/shard_map/all_to_all | solution.py:931
  54.7 1.9 collective-permute-start.7
  58.7 9.0 %all-to-all-done.1 = bf16[16,65,128]{2,1,0:T(8,128)(2,1)S(1)} async-done(((bf16[16,65,128]{2,1,0:T(8,128)(2,1)}), bf16[16,65,128]{2,1,0:T(8,128)(2,1)S(1)}, u32[]{:S(2)}, u32[]{:S(2)}) %all-to-all-start.1) | async-done | bytes 266272 | tf_op jit(solution)/shard_map/all_to_all | solution.py:931
  68.7 0.9 reshape.225
  69.6 2.7 all-to-all-start.2
  72.4 3.7 %collective-permute-done.7 = bf16[2,4,2,48,384]{4,3,2,1,0:T(8,128)(2,1)} collective-permute-done((bf16[2,4,2,48,384]{4,3,2,1,0:T(8,128)(2,1)S(1)}, bf16[2,4,2,48,384]{4,3,2,1,0:T(8,128)(2,1)}, u32[]{:S(2)}, u32[]{:S(2)}) %collective-permute-start.7) | collective-permute-done | bytes 589856 | tf_op jit(solution)/shard_map/ppermute | solution.py:866
  76.1 1.2 pad_maximum_fusion.1.own_b
  77.4 2.6 pad_maximum_fusion.own_a
  82.1 1.7 all-to-all-done.2
  84.7 0.9 broadcast_in_dim.36.mods
  85.6 6.0 %first_conv.1.conv_in = bf16[4,256,768]{2,1,0:T(8,128)(2,1)} custom-call(s32[1]{0:T(128)S(6)} %copy.125.tag_ref, f32[4,256,768]{2,1,0:T(8,128)} %get-tuple-element.69.norm, f32[6,4,8,768]{3,2,1,0:T(8,128)} %broadcast_in_dim.36.mods, f32[9,768]{1,0:T(8,128)} %reshape.201.kernel), custom_call_target="tpu_custom_call" | custom-call | flops 600000000 | bytes 4194304 | tf_op jit(solution)/shard_map/first_conv/pallas_call | solution.py:225
  91.6 1.1 copy-done.13
  92.7 33.3 %attend.1 = (bf16[4,2304,256]{2,1,0:T(8,128)(2,1)}, bf16[4,256,768]{2,1,0:T(8,128)(2,1)}, bf16[4,256,768]{2,1,0:T(8,128)(2,1)}, f32[4,256,768]{2,1,0:T(8,128)}, ...) custom-call(s32[5]{0:T(128)} %stack.85.where.tag_ref, ...), custom_call_target="tpu_custom_call" | custom-call | flops 3800000000 | bytes 4194304 | tf_op jit(solution)/shard_map/attend/pallas_call | solution.py:340
  126.0 69.0 %feed.1 = (f32[4,256,768]{2,1,0:T(8,128)}, f32[4,256,768]{2,1,0:T(8,128)}, bf16[8,2,4,48,384]{4,3,2,1,0:T(8,128)(2,1)}, bf16[8,2,4,48,384]{4,3,2,1,0:T(8,128)(2,...) custom-call(s32[5]{0:T(128)} %stack.85.where.tag_ref, ...), custom_call_target="tpu_custom_call" | custom-call | flops 3800000000 | bytes 4194304 | tf_op jit(solution)/shard_map/feed/pallas_call | solution.py:455
  195.6 9.7 %attend_back_0.1 = (bf16[1,256,768]{2,1,0:T(8,128)(2,1)}, f32[1,256,768]{2,1,0:T(8,128)}, bf16[2304,256]{1,0:T(8,128)(2,1)}, bf16[768,256]{1,0:T(8,128)(2,1)}, f32[4,4,768]{2,1,0:T(4,128)}) custom-call(s32[5]{0:T(128)} %stack.85.where.tag_ref, f32[4,256,768]{2,1,0:T(8,128)} %get-tuple-element.75.resid, f32[4,256,768]{2,1,0:T(8,128)} %get-tuple-element.78.shrunk, ...), custom_call_target="tpu_custom_call" | custom-call | flops 900000000 | bytes 4194304 | tf_op jit(solution)/shard_map/attend_back_0/pallas_call | solution.py:576
  205.4 3.3 dynamic-slice_add_fusion
  208.6 1.3 collective-permute-start.13
  210.0 2.1 dynamic-slice_add_fusion.1
  212.0 1.5 collective-permute-start.12
  213.5 23.1 %attend_back_1.1 = (bf16[3,256,768]{2,1,0:T(8,128)(2,1)}, f32[3,256,768]{2,1,0:T(8,128)}, bf16[2304,768]{1,0:T(8,128)(2,1)}, bf16[768,768]{1,0:T(8,128)(2,1)}, f32[4,4,768]{2,1,0:T(4,128)}) custom-call(s32[5]{0:T(128)} %stack.85.where.tag_ref, f32[4,256,768]{2,1,0:T(8,128)} %get-tuple-element.75.resid, f32[4,256,768]{2,1,0:T(8,128)} %get-tuple-element.78.shrunk, ...), custom_call_target="tpu_custom_call" | custom-call | flops 2700000000 | bytes 4194304 | tf_op jit(solution)/shard_map/attend_back_1/pallas_call | solution.py:576
  236.8 3.2 collective-permute-done.12
  240.0 0.9 bitcast_add_fusion.1
  241.4 1.0 bitcast_add_fusion
  242.4 1.3 collective-permute-start.17
  243.7 9.8 %project_grads.1 = (bf16[8,2,2,48,384]{4,3,2,1,0:T(8,128)(2,1)}, bf16[8,2,2,48,384]{4,3,2,1,0:T(8,128)(2,1)}, bf16[8,2,2,48,384]{4,3,2,1,0:T(8,128)(2,1)}, bf16[8,2,2,48,384]{4,3,2,1,0:T(8,128)(2,1)}) custom-call(s32[5]{0:T(128)} %stack.85.where.tag_ref, bf16[2304,256]{1,0:T(8,128)(2,1)} %get-tuple-element.84.d_qkv0, ...), custom_call_target="tpu_custom_call" | custom-call | flops 800000000 | bytes 4194304 | tf_op jit(solution)/shard_map/project_grads/pallas_call | solution.py:646
  254.0 1.5 collective-permute-done.16
  255.5 1.1 collective-permute-done.17
  256.6 1.2 constant_dynamic-slice_fusion.2
  257.8 1.3 constant_dynamic-slice_fusion
  259.5 1.1 pad_maximum_fusion.4
  260.7 2.0 collective-permute-start.20
  262.9 0.9 fusion.1
  264.6 0.9 fusion.2
  266.1 16.3 %conv_back.1 = (f32[4,256,768]{2,1,0:T(8,128)}, bf16[32,16,288]{2,1,0:T(8,128)(2,1)}) custom-call(s32[5]{0:T(128)} %stack.85.where.tag_ref, bf16[2304,256]{1,0:T(8,128)(2,1)} %get-tuple-element.84.d_qkv0, bf16[2304,768]{1,0:T(8,128)(2,1)} %get-tuple-element.92.d_qkv1, bf16[2304,768]{1,0:T(8,128)(2,1)} %get-tuple-element.106.weight, ...), custom_call_target="tpu_custom_call" | custom-call | flops 1500000000 | bytes 4194304 | tf_op jit(solution)/shard_map/conv_back/pallas_call | solution.py:731
  282.4 3.4 all-to-all-start.3
  286.0 1.9 fusion.17
  287.9 2.7 collective-permute-start.28
  290.5 1.0 fusion.24
  291.6 1.5 collective-permute-start.24
  293.1 1.0 fusion.25
  294.1 1.6 collective-permute-start.23
  295.6 8.4 %finish.1 = (bf16[1024,768]{1,0:T(8,128)(2,1)}, f32[1024,768]{1,0:T(8,128)}) custom-call(f32[4,256,768]{2,1,0:T(8,128)} %get-tuple-element.115.d_first, f32[4,256,768]{2,1,0:T(8,128)} %get-tuple-element.69.norm, f32[4,256,1]{2,1,0:T(8,128)} %get-tuple-element.116.factor, f32[1,256,768]{2,1,0:T(8,128)} %get-tuple-element.117.d_resid0, ...), custom_call_target="tpu_custom_call" | custom-call | flops 800000000 | bytes 4194304 | tf_op jit(solution)/shard_map/finish/pallas_call | solution.py:789
  304.8 1.0 fusion.42
  307.5 0.8 copy.79
  308.3 3.6 %all-to-all-start.4 = ((f32[16,24,128]{2,1,0:T(8,128)}), f32[16,24,128]{2,1,0:T(8,128)S(1)}, u32[]{:S(2)}, u32[]{:S(2)}) async-start(f32[16,24,128]{2,1,0:T(8,128)} %bitcast.74), calls=%async_computation.4 | async-start | bytes 393216 | tf_op jit(solution)/shard_map/all_to_all | solution.py:943
  311.9 1.1 bitcast_add_fusion.4
  313.0 1.1 bitcast_add_fusion.6
  314.2 2.0 collective-permute-start.25
  316.2 2.4 collective-permute-start.26
  318.5 1.5 collective-permute-start.27
  320.0 1.3 all-to-all-done.4
  322.0 7.3 %collective-permute-start.22 = (f32[24,128]{1,0:T(8,128)S(1)}, f32[24,128]{1,0:T(8,128)S(1)}, u32[]{:S(2)}, u32[]{:S(2)}) collective-permute-start(f32[24,128]{1,0:T(8,128)S(1)} %reduce_sum.28), channel_id=1, source_target_pairs={{0,1},{1,17},{2,0},{3,16},{4,3},{5,19},{6,2},{7,18},{8,5},{9,21},{... | collective-permute-start | bytes 36872 | tf_op jit(solution)/shard_map/ppermute | solution.py:958
  329.3 1.3 convert_add_fusion
  332.2 0.9 fusion.5
  333.1 0.9 fusion.8
  (144 shorter events, 19.9 us)
Async XLA Ops:
  7.2 61.2 %copy-start = (bf16[384,288]{0,1:T(8,128)(2,1)S(1)}, bf16[384,288]{0,1:T(8,128)(2,1)}, u32[]{:S(2)}) copy-start(bf16[384,288]{0,1:T(8,128)(2,1)} %param.20) | copy-start | bytes 663556
  7.2 2.8 copy-start.9
  7.2 2.8 copy-start.10
  7.2 8.9 %copy-start.17 = (s32[1,4]{1,0:T(1,128)S(1)}, s32[1,4]{1,0:T(1,128)}, u32[]{:S(2)}) copy-start(s32[1,4]{1,0:T(1,128)} %param.16) | copy-start | bytes 52
  7.2 8.9 %copy-start.16 = (s32[1,4]{1,0:T(1,128)S(1)}, s32[1,4]{1,0:T(1,128)}, u32[]{:S(2)}) copy-start(s32[1,4]{1,0:T(1,128)} %param.17) | copy-start | bytes 52
  7.2 14.7 %copy-start.12 = (bf16[9,48]{1,0:T(8,128)(2,1)S(1)}, bf16[9,48]{1,0:T(8,128)(2,1)}, u32[]{:S(2)}) copy-start(bf16[9,48]{1,0:T(8,128)(2,1)} %param.21) | copy-start | bytes 2596
  7.2 14.7 %copy-start.11 = (bf16[9,192]{1,0:T(8,128)(2,1)S(1)}, bf16[9,192]{1,0:T(8,128)(2,1)}, u32[]{:S(2)}) copy-start(bf16[9,192]{1,0:T(8,128)(2,1)} %param.25) | copy-start | bytes 10372
  7.3 118.8 %all-gather.2.cloned.1.call-start = ((), (), s32[]{:S(2)}) async-start(), calls=%async_computation.5 | async-start | bytes 9732096 | tf_op jit(solution)/shard_map/all_gather | solution.py:825
  10.0 22.7 %collective-permute-start.1 = (bf16[4,48,384]{2,1,0:T(8,128)(2,1)S(1)}, bf16[4,48,384]{2,1,0:T(8,128)(2,1)S(1)}, u32[]{:S(2)}, u32[]{:S(2)}) collective-permute-start(bf16[4,48,384]{2,1,0:T(8,128)(2,1)S(1)} %pad_maximum_fusion.8), channel_id=1, source_target_pairs={{0,24},{2,26},{4,28},{6,30},{8,0},{10,2},{12,4},{14,6},{16,8},{18,... | collective-permute-start | bytes 442376 | tf_op jit(solution)/shard_map/ppermute | solution.py:841
  15.1 17.7 %collective-permute-start.2 = (bf16[4,48,384]{2,1,0:T(8,128)(2,1)S(1)}, bf16[4,48,384]{2,1,0:T(8,128)(2,1)S(1)}, u32[]{:S(2)}, u32[]{:S(2)}) collective-permute-start(bf16[4,48,384]{2,1,0:T(8,128)(2,1)S(1)} %pad_maximum_fusion.8), channel_id=1, source_target_pairs={{0,16},{2,18},{4,20},{6,22},{8,24},{10,26},{12,28},{14,30},{16,0},... | collective-permute-start | bytes 442376 | tf_op jit(solution)/shard_map/ppermute | solution.py:841
  15.1 17.7 %collective-permute-start.3 = (bf16[4,48,384]{2,1,0:T(8,128)(2,1)S(1)}, bf16[4,48,384]{2,1,0:T(8,128)(2,1)S(1)}, u32[]{:S(2)}, u32[]{:S(2)}) collective-permute-start(bf16[4,48,384]{2,1,0:T(8,128)(2,1)S(1)} %pad_maximum_fusion.8), channel_id=1, source_target_pairs={{0,8},{2,10},{4,12},{6,14},{8,16},{10,18},{12,20},{14,22},{16,24},... | collective-permute-start | bytes 442376 | tf_op jit(solution)/shard_map/ppermute | solution.py:841
  16.8 15.3 %all-to-all-start = ((s32[32,1,8]{2,1,0:T(1,128)}), s32[32,1,8]{2,1,0:T(1,128)S(1)}, u32[]{:S(2)}, u32[]{:S(2)}) async-start(s32[32,1,8]{2,1,0:T(1,128)} %broadcast_in_dim.18), calls=%async_computation | async-start | bytes 32768 | tf_op jit(solution)/shard_map/all_to_all | solution.py:811
  22.1 10.4 %copy-start.14 = (bf16[500,48]{0,1:T(8,128)(2,1)S(1)}, bf16[500,48]{0,1:T(8,128)(2,1)}, u32[]{:S(2)}) copy-start(bf16[500,48]{0,1:T(8,128)(2,1)} %param.18) | copy-start | bytes 144004
  32.8 1.7 copy-start.15
  32.9 9.4 %collective-permute-start.5 = (bf16[4,2,48,384]{3,2,1,0:T(8,128)(2,1)S(1)}, bf16[4,2,48,384]{3,2,1,0:T(8,128)(2,1)S(1)}, u32[]{:S(2)}, u32[]{:S(2)}) collective-permute-start(bf16[4,2,48,384]{3,2,1,0:T(8,128)(2,1)S(1)} %get-tuple-element.159), channel_id=1, source_target_pairs={{0,1},{1,0},{2,3},{3,2},{4,5},{5,4},{6,7},{7,6},{8,9},{9,8},{10,11... | collective-permute-start | bytes 884744 | tf_op jit(solution)/shard_map/ppermute | solution.py:865
  33.6 8.8 %collective-permute-start.4 = (bf16[4,2,48,384]{3,2,1,0:T(8,128)(2,1)S(1)}, bf16[4,2,48,384]{3,2,1,0:T(8,128)(2,1)S(1)}, u32[]{:S(2)}, u32[]{:S(2)}) collective-permute-start(bf16[4,2,48,384]{3,2,1,0:T(8,128)(2,1)S(1)} %get-tuple-element.161), channel_id=1, source_target_pairs={{0,4},{2,6},{4,0},{6,2},{8,12},{10,14},{12,8},{14,10},{16,20},{18,... | collective-permute-start | bytes 884744 | tf_op jit(solution)/shard_map/ppermute | solution.py:866
  34.7 7.6 %collective-permute-start = (f32[48,128]{1,0:T(8,128)S(1)}, f32[48,128]{1,0:T(8,128)S(1)}, u32[]{:S(2)}, u32[]{:S(2)}) collective-permute-start(f32[48,128]{1,0:T(8,128)S(1)} %fusion), channel_id=1, source_target_pairs={{0,1},{1,0},{2,3},{3,2},{4,5},{5,4},{6,7},{7,6},{8,9},{9,8},{10,11... | collective-permute-start | bytes 73736 | tf_op jit(solution)/shard_map/ppermute | solution.py:865
  43.4 24.3 %all-to-all-start.1 = ((bf16[16,65,128]{2,1,0:T(8,128)(2,1)}), bf16[16,65,128]{2,1,0:T(8,128)(2,1)S(1)}, u32[]{:S(2)}, u32[]{:S(2)}) async-start(bf16[16,65,128]{2,1,0:T(8,128)(2,1)} %broadcast_in_dim.32), calls=%async_computation.1 | async-start | bytes 589824 | tf_op jit(solution)/shard_map/all_to_all | solution.py:931
  54.7 21.3 %collective-permute-start.7 = (bf16[2,4,2,48,384]{4,3,2,1,0:T(8,128)(2,1)S(1)}, bf16[2,4,2,48,384]{4,3,2,1,0:T(8,128)(2,1)}, u32[]{:S(2)}, u32[]{:S(2)}) collective-permute-start(bf16[2,4,2,48,384]{4,3,2,1,0:T(8,128)(2,1)S(1)} %get-tuple-element.155), channel_id=1, source_target_pairs={{0,4},{2,6},{4,0},{6,2},{8,12},{10,14},{12,8},{14,10},{16,20},{18,... | collective-permute-start | bytes 1769480 | tf_op jit(solution)/shard_map/ppermute | solution.py:866
  56.6 20.7 %collective-permute-start.6 = (bf16[2,4,2,48,384]{4,3,2,1,0:T(8,128)(2,1)S(1)}, bf16[2,4,2,48,384]{4,3,2,1,0:T(8,128)(2,1)}, u32[]{:S(2)}, u32[]{:S(2)}) collective-permute-start(bf16[2,4,2,48,384]{4,3,2,1,0:T(8,128)(2,1)S(1)} %get-tuple-element.157), channel_id=1, source_target_pairs={{0,1},{1,0},{2,3},{3,2},{4,5},{5,4},{6,7},{7,6},{8,9},{9,8},{10,11... | collective-permute-start | bytes 1769480 | tf_op jit(solution)/shard_map/ppermute | solution.py:865
  67.7 0.7 copy-start.6
  69.6 14.2 %all-to-all-start.2 = ((f32[32,1,1152]{2,1,0:T(1,128)}), f32[32,1,1152]{2,1,0:T(1,128)S(1)}, u32[]{:S(2)}, u32[]{:S(2)}) async-start(f32[32,1,1152]{2,1,0:T(1,128)} %reshape.225), calls=%async_computation.2 | async-start | bytes 294912 | tf_op jit(solution)/shard_map/all_to_all | solution.py:811
  77.3 2.7 copy-start.5
  77.3 14.4 %collective-permute-start.9 = (bf16[2,2,4,2,48,384]{5,4,3,2,1,0:T(8,128)(2,1)S(1)}, bf16[2,2,4,2,48,384]{5,4,3,2,1,0:T(8,128)(2,1)}, u32[]{:S(2)}, u32[]{:S(2)}) collective-permute-start(bf16[2,2,4,2,48,384]{5,4,3,2,1,0:T(8,128)(2,1)S(1)} %pad_maximum_fusion.1.own_b), channel_id=1, source_target_pairs={{0,2},{2,0},{4,6},{6,4},{8,10},{10,8},{12,14},{14,12},{16,18},{18,... | collective-permute-start | bytes 3538952 | tf_op jit(solution)/shard_map/ppermute | solution.py:866
  79.9 11.7 %collective-permute-start.8 = (bf16[2,2,4,2,48,384]{5,4,3,2,1,0:T(8,128)(2,1)}, bf16[2,2,4,2,48,384]{5,4,3,2,1,0:T(8,128)(2,1)S(1)}, u32[]{:S(2)}, u32[]{:S(2)}) collective-permute-start(bf16[2,2,4,2,48,384]{5,4,3,2,1,0:T(8,128)(2,1)} %pad_maximum_fusion.own_a), channel_id=1, source_target_pairs={{0,2},{2,0},{4,6},{6,4},{8,10},{10,8},{12,14},{14,12},{16,18},{18,... | collective-permute-start | bytes 3538952 | tf_op jit(solution)/shard_map/ppermute | solution.py:866
  91.6 1.1 copy-start.13
  195.0 10.3 %collective-permute-start.11 = (bf16[8,2,4,48,384]{4,3,2,1,0:T(8,128)(2,1)}, bf16[8,2,4,48,384]{4,3,2,1,0:T(8,128)(2,1)}, u32[]{:S(2)}, u32[]{:S(2)}) collective-permute-start(bf16[8,2,4,48,384]{4,3,2,1,0:T(8,128)(2,1)} %get-tuple-element.89), channel_id=1, source_target_pairs={{0,2},{2,0},{4,6},{6,4},{8,10},{10,8},{12,14},{14,12},{16,18},{18,... | collective-permute-start | bytes 7077896 | tf_op jit(solution)/shard_map/ppermute | solution.py:866
  195.2 10.2 %collective-permute-start.10 = (bf16[8,2,4,48,384]{4,3,2,1,0:T(8,128)(2,1)}, bf16[8,2,4,48,384]{4,3,2,1,0:T(8,128)(2,1)}, u32[]{:S(2)}, u32[]{:S(2)}) collective-permute-start(bf16[8,2,4,48,384]{4,3,2,1,0:T(8,128)(2,1)} %get-tuple-element.86), channel_id=1, source_target_pairs={{0,2},{2,0},{4,6},{6,4},{8,10},{10,8},{12,14},{14,12},{16,18},{18,... | collective-permute-start | bytes 7077896 | tf_op jit(solution)/shard_map/ppermute | solution.py:866
  195.6 9.8 %copy-start.2 = (bf16[8,2,4,48,384]{4,3,2,1,0:T(8,128)(2,1)S(1)}, bf16[8,2,4,48,384]{4,3,2,1,0:T(8,128)(2,1)}, u32[]{:S(2)}) copy-start(bf16[8,2,4,48,384]{4,3,2,1,0:T(8,128)(2,1)} %get-tuple-element.88) | copy-start | bytes 7077892
  205.4 4.6 %copy-start.1 = (bf16[8,2,4,48,384]{4,3,2,1,0:T(8,128)(2,1)S(1)}, bf16[8,2,4,48,384]{4,3,2,1,0:T(8,128)(2,1)}, u32[]{:S(2)}) copy-start(bf16[8,2,4,48,384]{4,3,2,1,0:T(8,128)(2,1)} %get-tuple-element.85) | copy-start | bytes 7077892
  208.6 28.2 %collective-permute-start.13 = (bf16[4,2,4,48,384]{4,3,2,1,0:T(8,128)(2,1)}, bf16[4,2,4,48,384]{4,3,2,1,0:T(8,128)(2,1)S(1)}, u32[]{:S(2)}, u32[]{:S(2)}) collective-permute-start(bf16[4,2,4,48,384]{4,3,2,1,0:T(8,128)(2,1)} %get-tuple-element.128), channel_id=1, source_target_pairs={{0,4},{2,6},{4,0},{6,2},{8,12},{10,14},{12,8},{14,10},{16,20},{18,... | collective-permute-start | bytes 3538952 | tf_op jit(solution)/shard_map/ppermute | solution.py:866
  212.0 27.9 %collective-permute-start.12 = (bf16[4,2,4,48,384]{4,3,2,1,0:T(8,128)(2,1)S(1)}, bf16[4,2,4,48,384]{4,3,2,1,0:T(8,128)(2,1)S(1)}, u32[]{:S(2)}, u32[]{:S(2)}) collective-permute-start(bf16[4,2,4,48,384]{4,3,2,1,0:T(8,128)(2,1)S(1)} %get-tuple-element.130), channel_id=1, source_target_pairs={{0,1},{1,0},{2,3},{3,2},{4,5},{5,4},{6,7},{7,6},{8,9},{9,8},{10,11... | collective-permute-start | bytes 3538952 | tf_op jit(solution)/shard_map/ppermute | solution.py:865
  240.9 14.6 %collective-permute-start.16 = (bf16[4,4,48,384]{3,2,1,0:T(8,128)(2,1)}, bf16[4,4,48,384]{3,2,1,0:T(8,128)(2,1)S(1)}, u32[]{:S(2)}, u32[]{:S(2)}) collective-permute-start(bf16[4,4,48,384]{3,2,1,0:T(8,128)(2,1)} %get-tuple-element.132), channel_id=1, source_target_pairs={{0,4},{2,6},{4,0},{6,2},{8,12},{10,14},{12,8},{14,10},{16,20},{18,... | collective-permute-start | bytes 1769480 | tf_op jit(solution)/shard_map/ppermute | solution.py:866
  242.4 14.2 %collective-permute-start.17 = (bf16[4,4,48,384]{3,2,1,0:T(8,128)(2,1)}, bf16[4,4,48,384]{3,2,1,0:T(8,128)(2,1)}, u32[]{:S(2)}, u32[]{:S(2)}) collective-permute-start(bf16[4,4,48,384]{3,2,1,0:T(8,128)(2,1)} %get-tuple-element.134), channel_id=1, source_target_pairs={{0,1},{1,0},{2,3},{3,2},{4,5},{5,4},{6,7},{7,6},{8,9},{9,8},{10,11... | collective-permute-start | bytes 1769480 | tf_op jit(solution)/shard_map/ppermute | solution.py:865
  253.5 9.2 %collective-permute-start.15 = (bf16[8,2,2,48,384]{4,3,2,1,0:T(8,128)(2,1)}, bf16[8,2,2,48,384]{4,3,2,1,0:T(8,128)(2,1)S(1)}, u32[]{:S(2)}, u32[]{:S(2)}) collective-permute-start(bf16[8,2,2,48,384]{4,3,2,1,0:T(8,128)(2,1)} %get-tuple-element.103), channel_id=1, source_target_pairs={{0,2},{2,0},{4,6},{6,4},{8,10},{10,8},{12,14},{14,12},{16,18},{18,... | collective-permute-start | bytes 3538952 | tf_op jit(solution)/shard_map/ppermute | solution.py:866
  253.7 10.5 %collective-permute-start.14 = (bf16[8,2,2,48,384]{4,3,2,1,0:T(8,128)(2,1)}, bf16[8,2,2,48,384]{4,3,2,1,0:T(8,128)(2,1)S(1)}, u32[]{:S(2)}, u32[]{:S(2)}) collective-permute-start(bf16[8,2,2,48,384]{4,3,2,1,0:T(8,128)(2,1)} %get-tuple-element.101), channel_id=1, source_target_pairs={{0,2},{2,0},{4,6},{6,4},{8,10},{10,8},{12,14},{14,12},{16,18},{18,... | collective-permute-start | bytes 3538952 | tf_op jit(solution)/shard_map/ppermute | solution.py:866
  255.5 1.1 copy-start.8
  259.3 3.4 copy-start.4
  260.7 25.3 %collective-permute-start.20 = (bf16[2,8,48,384]{3,1,2,0:T(8,128)(2,1)}, bf16[2,8,48,384]{3,1,2,0:T(8,128)(2,1)}, u32[]{:S(2)}, u32[]{:S(2)}) collective-permute-start(bf16[2,8,48,384]{3,1,2,0:T(8,128)(2,1)} %pad_maximum_fusion.4), channel_id=1, source_target_pairs={{0,8},{2,10},{4,12},{6,14},{8,0},{10,2},{12,4},{14,6},{16,24},{18,... | collective-permute-start | bytes 1769480 | tf_op jit(solution)/shard_map/ppermute | solution.py:866
  262.9 1.5 copy-start.3
  263.8 26.7 %collective-permute-start.19 = (bf16[4,2,2,48,384]{4,3,2,0,1:T(8,128)(2,1)}, bf16[4,2,2,48,384]{4,3,2,0,1:T(8,128)(2,1)}, u32[]{:S(2)}, u32[]{:S(2)}) collective-permute-start(bf16[4,2,2,48,384]{4,3,2,0,1:T(8,128)(2,1)} %fusion.1), channel_id=1, source_target_pairs={{0,4},{2,6},{4,0},{6,2},{8,12},{10,14},{12,8},{14,10},{16,20},{18,... | collective-permute-start | bytes 1769480 | tf_op jit(solution)/shard_map/ppermute | solution.py:866
  265.5 25.1 %collective-permute-start.18 = (bf16[4,2,2,48,384]{4,3,2,0,1:T(8,128)(2,1)}, bf16[4,2,2,48,384]{4,3,2,0,1:T(8,128)(2,1)}, u32[]{:S(2)}, u32[]{:S(2)}) collective-permute-start(bf16[4,2,2,48,384]{4,3,2,0,1:T(8,128)(2,1)} %fusion.2), channel_id=1, source_target_pairs={{0,1},{1,0},{2,3},{3,2},{4,5},{5,4},{6,7},{7,6},{8,9},{9,8},{10,11... | collective-permute-start | bytes 1769480 | tf_op jit(solution)/shard_map/ppermute | solution.py:865
  282.4 22.3 %all-to-all-start.3 = ((bf16[32,16,288]{2,1,0:T(8,128)(2,1)}), bf16[32,16,288]{2,1,0:T(8,128)(2,1)S(1)}, u32[]{:S(2)}, u32[]{:S(2)}) async-start(bf16[32,16,288]{2,1,0:T(8,128)(2,1)} %get-tuple-element.114), calls=%async_computation.3 | async-start | bytes 786432 | tf_op jit(solution)/shard_map/all_to_all | solution.py:811
  287.9 34.2 %collective-permute-start.28 = (bf16[8,48,384]{2,0,1:T(8,128)(2,1)}, bf16[8,48,384]{2,0,1:T(8,128)(2,1)}, u32[]{:S(2)}, u32[]{:S(2)}) collective-permute-start(bf16[8,48,384]{2,0,1:T(8,128)(2,1)} %fusion.17), channel_id=1, source_target_pairs={{0,16},{2,18},{4,20},{6,22},{8,24},{10,26},{12,28},{14,30},{16,0},... | collective-permute-start | bytes 884744 | tf_op jit(solution)/shard_map/ppermute | solution.py:866
  291.6 20.3 %collective-permute-start.24 = (bf16[4,2,48,384]{3,2,1,0:T(8,128)(2,1)S(1)}, bf16[4,2,48,384]{3,2,1,0:T(8,128)(2,1)}, u32[]{:S(2)}, u32[]{:S(2)}) collective-permute-start(bf16[4,2,48,384]{3,2,1,0:T(8,128)(2,1)S(1)} %fusion.24), channel_id=1, source_target_pairs={{0,1},{1,0},{2,3},{3,2},{4,5},{5,4},{6,7},{7,6},{8,9},{9,8},{10,11... | collective-permute-start | bytes 884744 | tf_op jit(solution)/shard_map/ppermute | solution.py:865
  294.1 18.9 %collective-permute-start.23 = (bf16[4,2,48,384]{3,2,1,0:T(8,128)(2,1)S(1)}, bf16[4,2,48,384]{3,2,1,0:T(8,128)(2,1)}, u32[]{:S(2)}, u32[]{:S(2)}) collective-permute-start(bf16[4,2,48,384]{3,2,1,0:T(8,128)(2,1)S(1)} %fusion.25), channel_id=1, source_target_pairs={{0,4},{2,6},{4,0},{6,2},{8,12},{10,14},{12,8},{14,10},{16,20},{18,... | collective-permute-start | bytes 884744 | tf_op jit(solution)/shard_map/ppermute | solution.py:866
  295.6 9.2 %copy-start.7 = (bf16[16,48,128]{2,1,0:T(8,128)(2,1)S(1)}, bf16[16,48,128]{2,1,0:T(8,128)(2,1)}, u32[]{:S(2)}) copy-start(bf16[16,48,128]{2,1,0:T(8,128)(2,1)} %copy-done.6) | copy-start | bytes 589828
  308.3 13.1 %all-to-all-start.4 = ((f32[16,24,128]{2,1,0:T(8,128)}), f32[16,24,128]{2,1,0:T(8,128)S(1)}, u32[]{:S(2)}, u32[]{:S(2)}) async-start(f32[16,24,128]{2,1,0:T(8,128)} %bitcast.74), calls=%async_computation.4 | async-start | bytes 393216 | tf_op jit(solution)/shard_map/all_to_all | solution.py:943
  314.2 19.8 %collective-permute-start.25 = (bf16[4,48,384]{2,1,0:T(8,128)(2,1)S(1)}, bf16[4,48,384]{2,1,0:T(8,128)(2,1)S(1)}, u32[]{:S(2)}, u32[]{:S(2)}) collective-permute-start(bf16[4,48,384]{2,1,0:T(8,128)(2,1)S(1)} %get-tuple-element.143), channel_id=1, source_target_pairs={{0,8},{2,10},{4,12},{6,14},{8,16},{10,18},{12,20},{14,22},{16,24},... | collective-permute-start | bytes 442376 | tf_op jit(solution)/shard_map/ppermute | solution.py:882
  316.2 17.9 %collective-permute-start.26 = (bf16[4,48,384]{2,1,0:T(8,128)(2,1)S(1)}, bf16[4,48,384]{2,1,0:T(8,128)(2,1)S(1)}, u32[]{:S(2)}, u32[]{:S(2)}) collective-permute-start(bf16[4,48,384]{2,1,0:T(8,128)(2,1)S(1)} %get-tuple-element.144), channel_id=1, source_target_pairs={{0,16},{2,18},{4,20},{6,22},{8,24},{10,26},{12,28},{14,30},{16,0},... | collective-permute-start | bytes 442376 | tf_op jit(solution)/shard_map/ppermute | solution.py:882
  318.5 15.5 %collective-permute-start.27 = (bf16[4,48,384]{2,1,0:T(8,128)(2,1)S(1)}, bf16[4,48,384]{2,1,0:T(8,128)(2,1)S(1)}, u32[]{:S(2)}, u32[]{:S(2)}) collective-permute-start(bf16[4,48,384]{2,1,0:T(8,128)(2,1)S(1)} %get-tuple-element.145), channel_id=1, source_target_pairs={{0,24},{2,26},{4,28},{6,30},{8,0},{10,2},{12,4},{14,6},{16,8},{18,... | collective-permute-start | bytes 442376 | tf_op jit(solution)/shard_map/ppermute | solution.py:882
  321.4 10.8 %collective-permute-start.21 = (f32[24,128]{1,0:T(8,128)S(1)}, f32[24,128]{1,0:T(8,128)S(1)}, u32[]{:S(2)}, u32[]{:S(2)}) collective-permute-start(f32[24,128]{1,0:T(8,128)S(1)} %reduce_sum.28), channel_id=1, source_target_pairs={{0,0},{1,16},{2,1},{3,17},{4,2},{5,18},{6,3},{7,19},{8,4},{9,20},{... | collective-permute-start | bytes 36872 | tf_op jit(solution)/shard_map/ppermute | solution.py:957
  322.0 10.1 %collective-permute-start.22 = (f32[24,128]{1,0:T(8,128)S(1)}, f32[24,128]{1,0:T(8,128)S(1)}, u32[]{:S(2)}, u32[]{:S(2)}) collective-permute-start(f32[24,128]{1,0:T(8,128)S(1)} %reduce_sum.28), channel_id=1, source_target_pairs={{0,1},{1,17},{2,0},{3,16},{4,3},{5,19},{6,2},{7,18},{8,5},{9,21},{... | collective-permute-start | bytes 36872 | tf_op jit(solution)/shard_map/ppermute | solution.py:958
Sparse Core Ops, SparseCore 0:
  11.6 94.6 all-gather.1

commit v8 on v7

--- a/solution.py
+++ b/solution.py
@@ -921,7 +921,7 @@
     return step_hot, class_hot, dot(step_table, step_hot, 0, 1) + dot(class_table, class_hot, 0, 1)
 
 
-def share_act(nd, cond, attn_kernel, ffn_kernel):
+def share_act(nd, cond, attn_kernel, ffn_kernel, beside):
     width, items = cond.shape
     act = jax.nn.silu(cond).astype(BF)
     filters = jnp.concatenate([attn_kernel, ffn_kernel], axis=1).reshape(-1)
@@ -929,6 +929,7 @@
     filters = jnp.pad(filters, (0, -size % items)).reshape(-1, items)
     sent = jnp.concatenate([act, filters], axis=0)[None]
     sent = lax.all_to_all(jnp.broadcast_to(sent, (nd,) + sent.shape[1:]), "dp", 0, 0, tiled=True)
+    sent = after(sent, *beside)
     act_all = sent[:, :width].reshape(nd * width, items)
     filters = sent[:, width:].reshape(nd, -1)[:, :size]
     filters = filters.reshape(nd, 9, -1).astype(F32)
@@ -988,15 +989,18 @@
     step_hot, class_hot, part = look_up(ids, step_table, class_table)
     if square:
         cond = part + swap(part, None)
+        own, *turns = (after(x, cond) for x in (own, *turns))
         a = jnp.stack([own[:2]] + [turn[:2] for turn in turns])
         b = jnp.stack([own[2:]] + [turn[2:] for turn in turns])
-        a, b = widen(a, b, 2, None)
-        cond = after(cond, a, b)
+        next_a, next_b = swap(a, 2), swap(b, None)
+        a, b = jnp.stack([a, next_a]), jnp.stack([b, next_b])
+        beside = (a, b)
+    else:
+        beside = ()
+        cond = lax.psum(part, "fsdp")
+    act_all, attn_full, ffn_full = share_act(nd, cond, attn_kernel, ffn_kernel, beside)
+    if square:
         next_a, next_b = swap(a, None), swap(b, 2)
-    else:
-        cond = lax.psum(part, "fsdp")
-    act_all, attn_full, ffn_full = share_act(nd, cond, attn_kernel, ffn_kernel)
-    if square:
         next_a, next_b = after(next_a, act_all), after(next_b, act_all)
     height, width = modulation_weight.shape
     act_rows = lax.dynamic_slice_in_dim(

time: 344 us -> 335 us (0.974)
  waiting for transfers between devices: 32.7 us -> 24.5 us
    ppermute x7, waiting for transfers between devices: 10.5 us -> 5.16 us  [swap(): return lax.ppermute(value, 'fsdp', [(0, 1), (1, 0)])]
    ppermute x14, waiting for transfers between devices: 5.39 us -> 1.04 us  [swap(): return lax.ppermute(value, 'dp', [(i, i ^ bit) for i in range(NJ)])]
    all_to_all x3, starting transfers between devices: 11.1 us -> 15.1 us  [exchange(): return lax.all_to_all(pieces, BOTH, 0, 0, tiled=True)]
  transfers between devices with their start and end apart: 35 -> 35, of which waited for: 11 -> 9; matrix products, arithmetic and copies ran while one was open for 11% -> 11% of each run, Pallas kernels for 33% -> 34%
where the time goes in v8:
time: 335 us; the launch traced here: 334 us
  Pallas kernels  181 us (54%)
  starting transfers between devices  68.2 us (20%)
  other arithmetic  25.8 us (8%)
  waiting for transfers between devices  24.5 us (7%)
  between operations  15.5 us (5%)
  local copies, waits for them, and re-layouts  15.1 us (5%)
  matrix products  3.83 us (1%)
    pallas_call x1, Pallas kernels, feed(): pl.pallas_call(feed_kernel, grid=(FF // CHUNK,), in_specs=[SMEM_SPEC, who...  69 us
    pallas_call x1, Pallas kernels, attend(): pl.pallas_call(attend_kernel, grid=(4,), in_specs=[SMEM_SPEC, group_spec(...  33.1 us
    pallas_call x2, Pallas kernels, attend_back(): pl.pallas_call(attend_back_kernel, grid=(count,), in_specs=[SMEM_SPEC, pi...  32.7 us
    pallas_call x1, Pallas kernels, conv_back(): pl.pallas_call(conv_back_kernel, grid=(8 // PAIRS,), in_specs=[SMEM_SPEC,...  16.3 us
    all_to_all x3, starting transfers between devices, exchange(): return lax.all_to_all(pieces, BOTH, 0, 0, tiled=True)  15.1 us
    ppermute x14, starting transfers between devices, swap(): return lax.ppermute(value, 'dp', [(i, i ^ bit) for i in range(NJ)])  13.6 us
    pallas_call x1, Pallas kernels, project_grads(): pl.pallas_call(project_grads_kernel, grid=(8 // PAIRS,), in_specs=[SMEM_S...  9.75 us
    all_to_all x3, waiting for transfers between devices, exchange(): return lax.all_to_all(pieces, BOTH, 0, 0, tiled=True)  9.02 us
  transfers between devices with their start and end apart: 35, of which 9 were waited for; matrix products, arithmetic and copies ran while one was open for 11% of the time, Pallas kernels for 34%

profile of v8, /device:TPU:0, one launch (start us, length us, event | category | flops | bytes accessed | tf_op | source)
XLA Modules:
  0.0 334.1 jit_solution(11792201328337955055)
XLA Ops:
  7.3 1.0 copy.123
  8.3 1.7 pad_maximum_fusion.7
  10.0 5.1 %collective-permute-start.1 = (bf16[4,48,384]{2,1,0:T(8,128)(2,1)S(1)}, bf16[4,48,384]{2,1,0:T(8,128)(2,1)S(1)}, u32[]{:S(2)}, u32[]{:S(2)}) collective-permute-start(bf16[4,48,384]{2,1,0:T(8,128)(2,1)S(1)} %pad_maximum_fusion.8), channel_id=1, source_target_pairs={{0,24},{2,26},{4,28},{6,30},{8,0},{10,2},{12,4},{14,6},{16,8},{18,... | collective-permute-start | bytes 442376 | tf_op jit(solution)/shard_map/ppermute | solution.py:841
  15.1 1.0 collective-permute-start.3
  16.8 5.1 %all-to-all-start = ((s32[32,1,8]{2,1,0:T(1,128)}), s32[32,1,8]{2,1,0:T(1,128)S(1)}, u32[]{:S(2)}, u32[]{:S(2)}) async-start(s32[32,1,8]{2,1,0:T(1,128)} %broadcast_in_dim.18), calls=%async_computation | async-start | bytes 32768 | tf_op jit(solution)/shard_map/all_to_all | solution.py:811
  21.9 6.0 %prepare.1 = (bf16[4,256,768]{2,1,0:T(8,128)(2,1)}, bf16[4,256,768]{2,1,0:T(8,128)(2,1)}, f32[4,256,768]{2,1,0:T(8,128)}, f32[4,256,1]{2,1,0:T(8,128)}) custom-call(bf16[1024,768]{1,0:T(8,128)(2,1)} %latents.1, bf16[1024,768]{1,0:T(8,128)(2,1)} %cotangent.1), custom_call_target="tpu_custom_call" | custom-call | flops 600000000 | bytes 4194304 | tf_op jit(solution)/shard_map/prepare/pallas_call | solution.py:89
  28.0 4.2 %all-to-all-done = s32[32,1,8]{2,1,0:T(1,128)S(1)} async-done(((s32[32,1,8]{2,1,0:T(1,128)}), s32[32,1,8]{2,1,0:T(1,128)S(1)}, u32[]{:S(2)}, u32[]{:S(2)}) %all-to-all-start) | async-done | bytes 1056 | tf_op jit(solution)/shard_map/all_to_all | solution.py:811
  33.8 3.1 collective-permute-done
  39.3 8.8 %all-to-all-start.1 = ((bf16[16,65,128]{2,1,0:T(8,128)(2,1)}), bf16[16,65,128]{2,1,0:T(8,128)(2,1)S(1)}, u32[]{:S(2)}, u32[]{:S(2)}) async-start(bf16[16,65,128]{2,1,0:T(8,128)(2,1)} %broadcast_in_dim.32), calls=%async_computation.1 | async-start | bytes 589824 | tf_op jit(solution)/shard_map/all_to_all | solution.py:931
  48.2 2.0 collective-permute-start.7
  50.3 1.3 collective-permute-start.6
  52.9 7.9 %all-to-all-done.1 = bf16[16,65,128]{2,1,0:T(8,128)(2,1)S(1)} async-done(((bf16[16,65,128]{2,1,0:T(8,128)(2,1)}), bf16[16,65,128]{2,1,0:T(8,128)(2,1)S(1)}, u32[]{:S(2)}, u32[]{:S(2)}) %all-to-all-start.1) | async-done | bytes 266272 | tf_op jit(solution)/shard_map/all_to_all | solution.py:931
  61.1 0.9 reshape.225
  62.1 7.2 %all-to-all-start.2 = ((f32[32,1,1152]{2,1,0:T(1,128)}), f32[32,1,1152]{2,1,0:T(1,128)S(1)}, u32[]{:S(2)}, u32[]{:S(2)}) async-start(f32[32,1,1152]{2,1,0:T(1,128)} %reshape.225), calls=%async_computation.2 | async-start | bytes 294912 | tf_op jit(solution)/shard_map/all_to_all | solution.py:811
  69.3 1.4 pad_maximum_fusion.1.own_b
  71.0 2.3 pad_maximum_fusion.own_a
  75.6 4.7 %all-to-all-done.2 = f32[32,1,1152]{2,1,0:T(1,128)S(1)} async-done(((f32[32,1,1152]{2,1,0:T(1,128)}), f32[32,1,1152]{2,1,0:T(1,128)S(1)}, u32[]{:S(2)}, u32[]{:S(2)}) %all-to-all-start.2) | async-done | bytes 147488 | tf_op jit(solution)/shard_map/all_to_all | solution.py:811
  81.2 0.9 broadcast_in_dim.36.mods
  82.1 6.1 %first_conv.1.conv_in = bf16[4,256,768]{2,1,0:T(8,128)(2,1)} custom-call(s32[1]{0:T(128)S(6)} %copy.125.tag_ref, f32[4,256,768]{2,1,0:T(8,128)} %get-tuple-element.73.norm, f32[6,4,8,768]{3,2,1,0:T(8,128)} %broadcast_in_dim.36.mods, f32[9,768]{1,0:T(8,128)} %reshape.201.kernel), custom_call_target="tpu_custom_call" | custom-call | flops 600000000 | bytes 4194304 | tf_op jit(solution)/shard_map/first_conv/pallas_call | solution.py:225
  88.2 33.1 %attend.1 = (bf16[4,2304,256]{2,1,0:T(8,128)(2,1)}, bf16[4,256,768]{2,1,0:T(8,128)(2,1)}, bf16[4,256,768]{2,1,0:T(8,128)(2,1)}, f32[4,256,768]{2,1,0:T(8,128)}, ...) custom-call(s32[5]{0:T(128)} %stack.85.where.tag_ref, ...), custom_call_target="tpu_custom_call" | custom-call | flops 3800000000 | bytes 4194304 | tf_op jit(solution)/shard_map/attend/pallas_call | solution.py:340
  121.3 69.0 %feed.1 = (f32[4,256,768]{2,1,0:T(8,128)}, f32[4,256,768]{2,1,0:T(8,128)}, bf16[8,2,4,48,384]{4,3,2,1,0:T(8,128)(2,1)}, bf16[8,2,4,48,384]{4,3,2,1,0:T(8,128)(2,...) custom-call(s32[5]{0:T(128)} %stack.85.where.tag_ref, ...), custom_call_target="tpu_custom_call" | custom-call | flops 3800000000 | bytes 4194304 | tf_op jit(solution)/shard_map/feed/pallas_call | solution.py:455
  190.9 9.7 %attend_back_0.1 = (bf16[1,256,768]{2,1,0:T(8,128)(2,1)}, f32[1,256,768]{2,1,0:T(8,128)}, bf16[2304,256]{1,0:T(8,128)(2,1)}, bf16[768,256]{1,0:T(8,128)(2,1)}, f32[4,4,768]{2,1,0:T(4,128)}) custom-call(s32[5]{0:T(128)} %stack.85.where.tag_ref, f32[4,256,768]{2,1,0:T(8,128)} %get-tuple-element.83.resid, f32[4,256,768]{2,1,0:T(8,128)} %get-tuple-element.86.shrunk, ...), custom_call_target="tpu_custom_call" | custom-call | flops 900000000 | bytes 4194304 | tf_op jit(solution)/shard_map/attend_back_0/pallas_call | solution.py:576
  200.6 3.1 dynamic-slice_add_fusion.1
  203.7 1.0 collective-permute-start.12
  204.7 1.9 dynamic-slice_add_fusion
  206.5 1.6 collective-permute-start.13
  208.1 23.0 %attend_back_1.1 = (bf16[3,256,768]{2,1,0:T(8,128)(2,1)}, f32[3,256,768]{2,1,0:T(8,128)}, bf16[2304,768]{1,0:T(8,128)(2,1)}, bf16[768,768]{1,0:T(8,128)(2,1)}, f32[4,4,768]{2,1,0:T(4,128)}) custom-call(s32[5]{0:T(128)} %stack.85.where.tag_ref, f32[4,256,768]{2,1,0:T(8,128)} %get-tuple-element.83.resid, f32[4,256,768]{2,1,0:T(8,128)} %get-tuple-element.86.shrunk, ...), custom_call_target="tpu_custom_call" | custom-call | flops 2700000000 | bytes 4194304 | tf_op jit(solution)/shard_map/attend_back_1/pallas_call | solution.py:576
  231.8 1.0 bitcast_add_fusion.1
  232.8 1.4 collective-permute-start.16
  234.3 0.9 bitcast_add_fusion
  235.2 1.1 collective-permute-start.17
  236.3 9.8 %project_grads.1 = (bf16[8,2,2,48,384]{4,3,2,1,0:T(8,128)(2,1)}, bf16[8,2,2,48,384]{4,3,2,1,0:T(8,128)(2,1)}, bf16[8,2,2,48,384]{4,3,2,1,0:T(8,128)(2,1)}, bf16[8,2,2,48,384]{4,3,2,1,0:T(8,128)(2,1)}) custom-call(s32[5]{0:T(128)} %stack.85.where.tag_ref, bf16[2304,256]{1,0:T(8,128)(2,1)} %get-tuple-element.92.d_qkv0, ...), custom_call_target="tpu_custom_call" | custom-call | flops 800000000 | bytes 4194304 | tf_op jit(solution)/shard_map/project_grads/pallas_call | solution.py:646
  246.7 1.0 collective-permute-done.16
  247.7 1.1 constant_dynamic-slice_fusion.2
  248.8 1.3 collective-permute-done.17
  250.1 1.1 constant_dynamic-slice_fusion
  251.7 1.1 pad_maximum_fusion.4
  252.8 0.8 collective-permute-start.20
  253.9 0.9 fusion.1
  254.8 1.2 collective-permute-start.19
  256.2 0.9 fusion.2
  257.1 1.0 collective-permute-start.18
  258.4 16.3 %conv_back.1 = (f32[4,256,768]{2,1,0:T(8,128)}, bf16[32,16,288]{2,1,0:T(8,128)(2,1)}) custom-call(s32[5]{0:T(128)} %stack.85.where.tag_ref, bf16[2304,256]{1,0:T(8,128)(2,1)} %get-tuple-element.92.d_qkv0, bf16[2304,768]{1,0:T(8,128)(2,1)} %get-tuple-element.100.d_qkv1, bf16[2304,768]{1,0:T(8,128)(2,1)} %get-tuple-element.114.weight, ...), custom_call_target="tpu_custom_call" | custom-call | flops 1500000000 | bytes 4194304 | tf_op jit(solution)/shard_map/conv_back/pallas_call | solution.py:731
  274.6 2.9 all-to-all-start.3
  277.8 1.9 fusion.17
  279.7 2.7 collective-permute-start.28
  282.3 1.7 fusion.24
  284.0 1.5 collective-permute-start.24
  285.5 1.0 fusion.25
  286.5 1.6 collective-permute-start.23
  288.1 8.4 %finish.1 = (bf16[1024,768]{1,0:T(8,128)(2,1)}, f32[1024,768]{1,0:T(8,128)}) custom-call(f32[4,256,768]{2,1,0:T(8,128)} %get-tuple-element.123.d_first, f32[4,256,768]{2,1,0:T(8,128)} %get-tuple-element.73.norm, f32[4,256,1]{2,1,0:T(8,128)} %get-tuple-element.124.factor, f32[1,256,768]{2,1,0:T(8,128)} %get-tuple-element.125.d_resid0, ...), custom_call_target="tpu_custom_call" | custom-call | flops 800000000 | bytes 4194304 | tf_op jit(solution)/shard_map/finish/pallas_call | solution.py:789
  296.6 1.0 fusion.42
  299.2 0.8 copy.79
  300.0 3.6 %all-to-all-start.4 = ((f32[16,24,128]{2,1,0:T(8,128)}), f32[16,24,128]{2,1,0:T(8,128)S(1)}, u32[]{:S(2)}, u32[]{:S(2)}) async-start(f32[16,24,128]{2,1,0:T(8,128)} %bitcast.74), calls=%async_computation.4 | async-start | bytes 393216 | tf_op jit(solution)/shard_map/all_to_all | solution.py:944
  303.6 1.1 bitcast_add_fusion.4
  304.8 1.1 bitcast_add_fusion.6
  306.0 2.0 collective-permute-start.25
  308.0 2.4 collective-permute-start.26
  310.3 1.5 collective-permute-start.27
  311.8 1.3 all-to-all-done.4
  313.8 7.3 %collective-permute-start.22 = (f32[24,128]{1,0:T(8,128)S(1)}, f32[24,128]{1,0:T(8,128)S(1)}, u32[]{:S(2)}, u32[]{:S(2)}) collective-permute-start(f32[24,128]{1,0:T(8,128)S(1)} %reduce_sum.28), channel_id=1, source_target_pairs={{0,1},{1,17},{2,0},{3,16},{4,3},{5,19},{6,2},{7,18},{8,5},{9,21},{... | collective-permute-start | bytes 36872 | tf_op jit(solution)/shard_map/ppermute | solution.py:959
  321.1 1.3 convert_add_fusion
  323.9 0.9 fusion.5
  324.9 0.9 fusion.8
  (135 shorter events, 18.1 us)
Async XLA Ops:
  7.2 53.7 %copy-start = (bf16[384,288]{0,1:T(8,128)(2,1)S(1)}, bf16[384,288]{0,1:T(8,128)(2,1)}, u32[]{:S(2)}) copy-start(bf16[384,288]{0,1:T(8,128)(2,1)} %param.20) | copy-start | bytes 663556
  7.2 2.8 copy-start.6
  7.2 2.8 copy-start.7
  7.2 8.9 %copy-start.13 = (s32[1,4]{1,0:T(1,128)S(1)}, s32[1,4]{1,0:T(1,128)}, u32[]{:S(2)}) copy-start(s32[1,4]{1,0:T(1,128)} %param.16) | copy-start | bytes 52
  7.2 8.9 %copy-start.12 = (s32[1,4]{1,0:T(1,128)S(1)}, s32[1,4]{1,0:T(1,128)}, u32[]{:S(2)}) copy-start(s32[1,4]{1,0:T(1,128)} %param.17) | copy-start | bytes 52
  7.2 114.1 %all-gather.2.cloned.1.call-start = ((), (), s32[]{:S(2)}) async-start(), calls=%async_computation.5 | async-start | bytes 9732096 | tf_op jit(solution)/shard_map/all_gather | solution.py:825
  10.0 26.9 %collective-permute-start.1 = (bf16[4,48,384]{2,1,0:T(8,128)(2,1)S(1)}, bf16[4,48,384]{2,1,0:T(8,128)(2,1)S(1)}, u32[]{:S(2)}, u32[]{:S(2)}) collective-permute-start(bf16[4,48,384]{2,1,0:T(8,128)(2,1)S(1)} %pad_maximum_fusion.8), channel_id=1, source_target_pairs={{0,24},{2,26},{4,28},{6,30},{8,0},{10,2},{12,4},{14,6},{16,8},{18,... | collective-permute-start | bytes 442376 | tf_op jit(solution)/shard_map/ppermute | solution.py:841
  15.1 21.8 %collective-permute-start.2 = (bf16[4,48,384]{2,1,0:T(8,128)(2,1)S(1)}, bf16[4,48,384]{2,1,0:T(8,128)(2,1)S(1)}, u32[]{:S(2)}, u32[]{:S(2)}) collective-permute-start(bf16[4,48,384]{2,1,0:T(8,128)(2,1)S(1)} %pad_maximum_fusion.8), channel_id=1, source_target_pairs={{0,16},{2,18},{4,20},{6,22},{8,24},{10,26},{12,28},{14,30},{16,0},... | collective-permute-start | bytes 442376 | tf_op jit(solution)/shard_map/ppermute | solution.py:841
  15.1 21.8 %collective-permute-start.3 = (bf16[4,48,384]{2,1,0:T(8,128)(2,1)S(1)}, bf16[4,48,384]{2,1,0:T(8,128)(2,1)S(1)}, u32[]{:S(2)}, u32[]{:S(2)}) collective-permute-start(bf16[4,48,384]{2,1,0:T(8,128)(2,1)S(1)} %pad_maximum_fusion.8), channel_id=1, source_target_pairs={{0,8},{2,10},{4,12},{6,14},{8,16},{10,18},{12,20},{14,22},{16,24},... | collective-permute-start | bytes 442376 | tf_op jit(solution)/shard_map/ppermute | solution.py:841
  16.8 15.3 %all-to-all-start = ((s32[32,1,8]{2,1,0:T(1,128)}), s32[32,1,8]{2,1,0:T(1,128)S(1)}, u32[]{:S(2)}, u32[]{:S(2)}) async-start(s32[32,1,8]{2,1,0:T(1,128)} %broadcast_in_dim.18), calls=%async_computation | async-start | bytes 32768 | tf_op jit(solution)/shard_map/all_to_all | solution.py:811
  21.9 10.5 %copy-start.10 = (bf16[500,48]{0,1:T(8,128)(2,1)S(1)}, bf16[500,48]{0,1:T(8,128)(2,1)}, u32[]{:S(2)}) copy-start(bf16[500,48]{0,1:T(8,128)(2,1)} %param.18) | copy-start | bytes 144004
  21.9 10.8 %copy-start.11 = (bf16[500,48]{0,1:T(8,128)(2,1)S(1)}, bf16[500,48]{0,1:T(8,128)(2,1)}, u32[]{:S(2)}) copy-start(bf16[500,48]{0,1:T(8,128)(2,1)} %param.19) | copy-start | bytes 144004
  21.9 11.7 %copy-start.8 = (bf16[9,192]{1,0:T(8,128)(2,1)S(1)}, bf16[9,192]{1,0:T(8,128)(2,1)}, u32[]{:S(2)}) copy-start(bf16[9,192]{1,0:T(8,128)(2,1)} %param.25) | copy-start | bytes 10372
  21.9 11.7 %copy-start.9 = (bf16[9,48]{1,0:T(8,128)(2,1)S(1)}, bf16[9,48]{1,0:T(8,128)(2,1)}, u32[]{:S(2)}) copy-start(bf16[9,48]{1,0:T(8,128)(2,1)} %param.21) | copy-start | bytes 2596
  33.0 3.9 %collective-permute-start = (f32[48,128]{1,0:T(8,128)S(1)}, f32[48,128]{1,0:T(8,128)S(1)}, u32[]{:S(2)}, u32[]{:S(2)}) collective-permute-start(f32[48,128]{1,0:T(8,128)S(1)} %fusion), channel_id=1, source_target_pairs={{0,1},{1,0},{2,3},{3,2},{4,5},{5,4},{6,7},{7,6},{8,9},{9,8},{10,11... | collective-permute-start | bytes 73736 | tf_op jit(solution)/shard_map/ppermute | solution.py:865
  37.1 11.0 %collective-permute-start.5 = (bf16[4,2,48,384]{3,2,1,0:T(8,128)(2,1)S(1)}, bf16[4,2,48,384]{3,2,1,0:T(8,128)(2,1)S(1)}, u32[]{:S(2)}, u32[]{:S(2)}) collective-permute-start(bf16[4,2,48,384]{3,2,1,0:T(8,128)(2,1)S(1)} %get-tuple-element.169), channel_id=1, source_target_pairs={{0,1},{1,0},{2,3},{3,2},{4,5},{5,4},{6,7},{7,6},{8,9},{9,8},{10,11... | collective-permute-start | bytes 884744 | tf_op jit(solution)/shard_map/ppermute | solution.py:865
  37.8 12.4 %collective-permute-start.4 = (bf16[4,2,48,384]{3,2,1,0:T(8,128)(2,1)S(1)}, bf16[4,2,48,384]{3,2,1,0:T(8,128)(2,1)S(1)}, u32[]{:S(2)}, u32[]{:S(2)}) collective-permute-start(bf16[4,2,48,384]{3,2,1,0:T(8,128)(2,1)S(1)} %get-tuple-element.171), channel_id=1, source_target_pairs={{0,4},{2,6},{4,0},{6,2},{8,12},{10,14},{12,8},{14,10},{16,20},{18,... | collective-permute-start | bytes 884744 | tf_op jit(solution)/shard_map/ppermute | solution.py:866
  39.3 21.5 %all-to-all-start.1 = ((bf16[16,65,128]{2,1,0:T(8,128)(2,1)}), bf16[16,65,128]{2,1,0:T(8,128)(2,1)S(1)}, u32[]{:S(2)}, u32[]{:S(2)}) async-start(bf16[16,65,128]{2,1,0:T(8,128)(2,1)} %broadcast_in_dim.32), calls=%async_computation.1 | async-start | bytes 589824 | tf_op jit(solution)/shard_map/all_to_all | solution.py:931
  48.2 21.0 %collective-permute-start.7 = (bf16[2,4,2,48,384]{4,3,2,1,0:T(8,128)(2,1)S(1)}, bf16[2,4,2,48,384]{4,3,2,1,0:T(8,128)(2,1)}, u32[]{:S(2)}, u32[]{:S(2)}) collective-permute-start(bf16[2,4,2,48,384]{4,3,2,1,0:T(8,128)(2,1)S(1)} %get-tuple-element.165), channel_id=1, source_target_pairs={{0,4},{2,6},{4,0},{6,2},{8,12},{10,14},{12,8},{14,10},{16,20},{18,... | collective-permute-start | bytes 1769480 | tf_op jit(solution)/shard_map/ppermute | solution.py:866
  50.3 20.6 %collective-permute-start.6 = (bf16[2,4,2,48,384]{4,3,2,1,0:T(8,128)(2,1)S(1)}, bf16[2,4,2,48,384]{4,3,2,1,0:T(8,128)(2,1)}, u32[]{:S(2)}, u32[]{:S(2)}) collective-permute-start(bf16[2,4,2,48,384]{4,3,2,1,0:T(8,128)(2,1)S(1)} %get-tuple-element.167), channel_id=1, source_target_pairs={{0,1},{1,0},{2,3},{3,2},{4,5},{5,4},{6,7},{7,6},{8,9},{9,8},{10,11... | collective-permute-start | bytes 1769480 | tf_op jit(solution)/shard_map/ppermute | solution.py:865
  62.1 18.2 %all-to-all-start.2 = ((f32[32,1,1152]{2,1,0:T(1,128)}), f32[32,1,1152]{2,1,0:T(1,128)S(1)}, u32[]{:S(2)}, u32[]{:S(2)}) async-start(f32[32,1,1152]{2,1,0:T(1,128)} %reshape.225), calls=%async_computation.2 | async-start | bytes 294912 | tf_op jit(solution)/shard_map/all_to_all | solution.py:811
  70.6 2.7 copy-start.5
  70.6 17.5 %collective-permute-start.9 = (bf16[2,2,4,2,48,384]{5,4,3,2,1,0:T(8,128)(2,1)S(1)}, bf16[2,2,4,2,48,384]{5,4,3,2,1,0:T(8,128)(2,1)}, u32[]{:S(2)}, u32[]{:S(2)}) collective-permute-start(bf16[2,2,4,2,48,384]{5,4,3,2,1,0:T(8,128)(2,1)S(1)} %pad_maximum_fusion.1.own_b), channel_id=1, source_target_pairs={{0,2},{2,0},{4,6},{6,4},{8,10},{10,8},{12,14},{14,12},{16,18},{18,... | collective-permute-start | bytes 3538952 | tf_op jit(solution)/shard_map/ppermute | solution.py:866
  73.3 14.9 %collective-permute-start.8 = (bf16[2,2,4,2,48,384]{5,4,3,2,1,0:T(8,128)(2,1)}, bf16[2,2,4,2,48,384]{5,4,3,2,1,0:T(8,128)(2,1)}, u32[]{:S(2)}, u32[]{:S(2)}) collective-permute-start(bf16[2,2,4,2,48,384]{5,4,3,2,1,0:T(8,128)(2,1)} %pad_maximum_fusion.own_a), channel_id=1, source_target_pairs={{0,2},{2,0},{4,6},{6,4},{8,10},{10,8},{12,14},{14,12},{16,18},{18,... | collective-permute-start | bytes 3538952 | tf_op jit(solution)/shard_map/ppermute | solution.py:866
  190.3 10.3 %collective-permute-start.11 = (bf16[8,2,4,48,384]{4,3,2,1,0:T(8,128)(2,1)}, bf16[8,2,4,48,384]{4,3,2,1,0:T(8,128)(2,1)}, u32[]{:S(2)}, u32[]{:S(2)}) collective-permute-start(bf16[8,2,4,48,384]{4,3,2,1,0:T(8,128)(2,1)} %get-tuple-element.97), channel_id=1, source_target_pairs={{0,2},{2,0},{4,6},{6,4},{8,10},{10,8},{12,14},{14,12},{16,18},{18,... | collective-permute-start | bytes 7077896 | tf_op jit(solution)/shard_map/ppermute | solution.py:866
  190.4 10.2 %collective-permute-start.10 = (bf16[8,2,4,48,384]{4,3,2,1,0:T(8,128)(2,1)}, bf16[8,2,4,48,384]{4,3,2,1,0:T(8,128)(2,1)}, u32[]{:S(2)}, u32[]{:S(2)}) collective-permute-start(bf16[8,2,4,48,384]{4,3,2,1,0:T(8,128)(2,1)} %get-tuple-element.94), channel_id=1, source_target_pairs={{0,2},{2,0},{4,6},{6,4},{8,10},{10,8},{12,14},{14,12},{16,18},{18,... | collective-permute-start | bytes 7077896 | tf_op jit(solution)/shard_map/ppermute | solution.py:866
  190.9 9.7 %copy-start.2 = (bf16[8,2,4,48,384]{4,3,2,1,0:T(8,128)(2,1)S(1)}, bf16[8,2,4,48,384]{4,3,2,1,0:T(8,128)(2,1)}, u32[]{:S(2)}) copy-start(bf16[8,2,4,48,384]{4,3,2,1,0:T(8,128)(2,1)} %get-tuple-element.93) | copy-start | bytes 7077892
  200.6 4.1 %copy-start.1 = (bf16[8,2,4,48,384]{4,3,2,1,0:T(8,128)(2,1)S(1)}, bf16[8,2,4,48,384]{4,3,2,1,0:T(8,128)(2,1)}, u32[]{:S(2)}) copy-start(bf16[8,2,4,48,384]{4,3,2,1,0:T(8,128)(2,1)} %get-tuple-element.96) | copy-start | bytes 7077892
  203.7 28.2 %collective-permute-start.12 = (bf16[4,2,4,48,384]{4,3,2,1,0:T(8,128)(2,1)}, bf16[4,2,4,48,384]{4,3,2,1,0:T(8,128)(2,1)S(1)}, u32[]{:S(2)}, u32[]{:S(2)}) collective-permute-start(bf16[4,2,4,48,384]{4,3,2,1,0:T(8,128)(2,1)} %get-tuple-element.140), channel_id=1, source_target_pairs={{0,1},{1,0},{2,3},{3,2},{4,5},{5,4},{6,7},{7,6},{8,9},{9,8},{10,11... | collective-permute-start | bytes 3538952 | tf_op jit(solution)/shard_map/ppermute | solution.py:865
  206.5 27.7 %collective-permute-start.13 = (bf16[4,2,4,48,384]{4,3,2,1,0:T(8,128)(2,1)S(1)}, bf16[4,2,4,48,384]{4,3,2,1,0:T(8,128)(2,1)S(1)}, u32[]{:S(2)}, u32[]{:S(2)}) collective-permute-start(bf16[4,2,4,48,384]{4,3,2,1,0:T(8,128)(2,1)S(1)} %get-tuple-element.138), channel_id=1, source_target_pairs={{0,4},{2,6},{4,0},{6,2},{8,12},{10,14},{12,8},{14,10},{16,20},{18,... | collective-permute-start | bytes 3538952 | tf_op jit(solution)/shard_map/ppermute | solution.py:866
  232.8 14.9 %collective-permute-start.16 = (bf16[4,4,48,384]{3,2,1,0:T(8,128)(2,1)}, bf16[4,4,48,384]{3,2,1,0:T(8,128)(2,1)}, u32[]{:S(2)}, u32[]{:S(2)}) collective-permute-start(bf16[4,4,48,384]{3,2,1,0:T(8,128)(2,1)} %get-tuple-element.142), channel_id=1, source_target_pairs={{0,4},{2,6},{4,0},{6,2},{8,12},{10,14},{12,8},{14,10},{16,20},{18,... | collective-permute-start | bytes 1769480 | tf_op jit(solution)/shard_map/ppermute | solution.py:866
  235.2 14.9 %collective-permute-start.17 = (bf16[4,4,48,384]{3,2,1,0:T(8,128)(2,1)}, bf16[4,4,48,384]{3,2,1,0:T(8,128)(2,1)}, u32[]{:S(2)}, u32[]{:S(2)}) collective-permute-start(bf16[4,4,48,384]{3,2,1,0:T(8,128)(2,1)} %get-tuple-element.144), channel_id=1, source_target_pairs={{0,1},{1,0},{2,3},{3,2},{4,5},{5,4},{6,7},{7,6},{8,9},{9,8},{10,11... | collective-permute-start | bytes 1769480 | tf_op jit(solution)/shard_map/ppermute | solution.py:865
  246.0 7.6 %collective-permute-start.15 = (bf16[8,2,2,48,384]{4,3,2,1,0:T(8,128)(2,1)}, bf16[8,2,2,48,384]{4,3,2,1,0:T(8,128)(2,1)S(1)}, u32[]{:S(2)}, u32[]{:S(2)}) collective-permute-start(bf16[8,2,2,48,384]{4,3,2,1,0:T(8,128)(2,1)} %get-tuple-element.111), channel_id=1, source_target_pairs={{0,2},{2,0},{4,6},{6,4},{8,10},{10,8},{12,14},{14,12},{16,18},{18,... | collective-permute-start | bytes 3538952 | tf_op jit(solution)/shard_map/ppermute | solution.py:866
  246.2 9.8 %collective-permute-start.14 = (bf16[8,2,2,48,384]{4,3,2,1,0:T(8,128)(2,1)}, bf16[8,2,2,48,384]{4,3,2,1,0:T(8,128)(2,1)S(1)}, u32[]{:S(2)}, u32[]{:S(2)}) collective-permute-start(bf16[8,2,2,48,384]{4,3,2,1,0:T(8,128)(2,1)} %get-tuple-element.109), channel_id=1, source_target_pairs={{0,2},{2,0},{4,6},{6,4},{8,10},{10,8},{12,14},{14,12},{16,18},{18,... | collective-permute-start | bytes 3538952 | tf_op jit(solution)/shard_map/ppermute | solution.py:866
  251.5 2.2 copy-start.4
  252.8 25.0 %collective-permute-start.20 = (bf16[2,8,48,384]{3,1,2,0:T(8,128)(2,1)}, bf16[2,8,48,384]{3,1,2,0:T(8,128)(2,1)}, u32[]{:S(2)}, u32[]{:S(2)}) collective-permute-start(bf16[2,8,48,384]{3,1,2,0:T(8,128)(2,1)} %pad_maximum_fusion.4), channel_id=1, source_target_pairs={{0,8},{2,10},{4,12},{6,14},{8,0},{10,2},{12,4},{14,6},{16,24},{18,... | collective-permute-start | bytes 1769480 | tf_op jit(solution)/shard_map/ppermute | solution.py:866
  253.9 2.2 copy-start.3
  254.8 27.6 %collective-permute-start.19 = (bf16[4,2,2,48,384]{4,3,2,0,1:T(8,128)(2,1)}, bf16[4,2,2,48,384]{4,3,2,0,1:T(8,128)(2,1)}, u32[]{:S(2)}, u32[]{:S(2)}) collective-permute-start(bf16[4,2,2,48,384]{4,3,2,0,1:T(8,128)(2,1)} %fusion.1), channel_id=1, source_target_pairs={{0,4},{2,6},{4,0},{6,2},{8,12},{10,14},{12,8},{14,10},{16,20},{18,... | collective-permute-start | bytes 1769480 | tf_op jit(solution)/shard_map/ppermute | solution.py:866
  257.1 25.2 %collective-permute-start.18 = (bf16[4,2,2,48,384]{4,3,2,0,1:T(8,128)(2,1)}, bf16[4,2,2,48,384]{4,3,2,0,1:T(8,128)(2,1)}, u32[]{:S(2)}, u32[]{:S(2)}) collective-permute-start(bf16[4,2,2,48,384]{4,3,2,0,1:T(8,128)(2,1)} %fusion.2), channel_id=1, source_target_pairs={{0,1},{1,0},{2,3},{3,2},{4,5},{5,4},{6,7},{7,6},{8,9},{9,8},{10,11... | collective-permute-start | bytes 1769480 | tf_op jit(solution)/shard_map/ppermute | solution.py:865
  274.6 21.9 %all-to-all-start.3 = ((bf16[32,16,288]{2,1,0:T(8,128)(2,1)}), bf16[32,16,288]{2,1,0:T(8,128)(2,1)S(1)}, u32[]{:S(2)}, u32[]{:S(2)}) async-start(bf16[32,16,288]{2,1,0:T(8,128)(2,1)} %get-tuple-element.122), calls=%async_computation.3 | async-start | bytes 786432 | tf_op jit(solution)/shard_map/all_to_all | solution.py:811
  279.7 34.1 %collective-permute-start.28 = (bf16[8,48,384]{2,0,1:T(8,128)(2,1)}, bf16[8,48,384]{2,0,1:T(8,128)(2,1)}, u32[]{:S(2)}, u32[]{:S(2)}) collective-permute-start(bf16[8,48,384]{2,0,1:T(8,128)(2,1)} %fusion.17), channel_id=1, source_target_pairs={{0,16},{2,18},{4,20},{6,22},{8,24},{10,26},{12,28},{14,30},{16,0},... | collective-permute-start | bytes 884744 | tf_op jit(solution)/shard_map/ppermute | solution.py:866
  284.0 19.6 %collective-permute-start.24 = (bf16[4,2,48,384]{3,2,1,0:T(8,128)(2,1)}, bf16[4,2,48,384]{3,2,1,0:T(8,128)(2,1)}, u32[]{:S(2)}, u32[]{:S(2)}) collective-permute-start(bf16[4,2,48,384]{3,2,1,0:T(8,128)(2,1)} %fusion.24), channel_id=1, source_target_pairs={{0,1},{1,0},{2,3},{3,2},{4,5},{5,4},{6,7},{7,6},{8,9},{9,8},{10,11... | collective-permute-start | bytes 884744 | tf_op jit(solution)/shard_map/ppermute | solution.py:865
  286.5 18.3 %collective-permute-start.23 = (bf16[4,2,48,384]{3,2,1,0:T(8,128)(2,1)S(1)}, bf16[4,2,48,384]{3,2,1,0:T(8,128)(2,1)}, u32[]{:S(2)}, u32[]{:S(2)}) collective-permute-start(bf16[4,2,48,384]{3,2,1,0:T(8,128)(2,1)S(1)} %fusion.25), channel_id=1, source_target_pairs={{0,4},{2,6},{4,0},{6,2},{8,12},{10,14},{12,8},{14,10},{16,20},{18,... | collective-permute-start | bytes 884744 | tf_op jit(solution)/shard_map/ppermute | solution.py:866
  300.0 13.1 %all-to-all-start.4 = ((f32[16,24,128]{2,1,0:T(8,128)}), f32[16,24,128]{2,1,0:T(8,128)S(1)}, u32[]{:S(2)}, u32[]{:S(2)}) async-start(f32[16,24,128]{2,1,0:T(8,128)} %bitcast.74), calls=%async_computation.4 | async-start | bytes 393216 | tf_op jit(solution)/shard_map/all_to_all | solution.py:944
  306.0 19.8 %collective-permute-start.25 = (bf16[4,48,384]{2,1,0:T(8,128)(2,1)S(1)}, bf16[4,48,384]{2,1,0:T(8,128)(2,1)S(1)}, u32[]{:S(2)}, u32[]{:S(2)}) collective-permute-start(bf16[4,48,384]{2,1,0:T(8,128)(2,1)S(1)} %get-tuple-element.153), channel_id=1, source_target_pairs={{0,8},{2,10},{4,12},{6,14},{8,16},{10,18},{12,20},{14,22},{16,24},... | collective-permute-start | bytes 442376 | tf_op jit(solution)/shard_map/ppermute | solution.py:882
  308.0 17.8 %collective-permute-start.26 = (bf16[4,48,384]{2,1,0:T(8,128)(2,1)S(1)}, bf16[4,48,384]{2,1,0:T(8,128)(2,1)S(1)}, u32[]{:S(2)}, u32[]{:S(2)}) collective-permute-start(bf16[4,48,384]{2,1,0:T(8,128)(2,1)S(1)} %get-tuple-element.154), channel_id=1, source_target_pairs={{0,16},{2,18},{4,20},{6,22},{8,24},{10,26},{12,28},{14,30},{16,0},... | collective-permute-start | bytes 442376 | tf_op jit(solution)/shard_map/ppermute | solution.py:882
  310.3 15.5 %collective-permute-start.27 = (bf16[4,48,384]{2,1,0:T(8,128)(2,1)S(1)}, bf16[4,48,384]{2,1,0:T(8,128)(2,1)S(1)}, u32[]{:S(2)}, u32[]{:S(2)}) collective-permute-start(bf16[4,48,384]{2,1,0:T(8,128)(2,1)S(1)} %get-tuple-element.155), channel_id=1, source_target_pairs={{0,24},{2,26},{4,28},{6,30},{8,0},{10,2},{12,4},{14,6},{16,8},{18,... | collective-permute-start | bytes 442376 | tf_op jit(solution)/shard_map/ppermute | solution.py:882
  313.1 10.8 %collective-permute-start.21 = (f32[24,128]{1,0:T(8,128)S(1)}, f32[24,128]{1,0:T(8,128)S(1)}, u32[]{:S(2)}, u32[]{:S(2)}) collective-permute-start(f32[24,128]{1,0:T(8,128)S(1)} %reduce_sum.28), channel_id=1, source_target_pairs={{0,0},{1,16},{2,1},{3,17},{4,2},{5,18},{6,3},{7,19},{8,4},{9,20},{... | collective-permute-start | bytes 36872 | tf_op jit(solution)/shard_map/ppermute | solution.py:958
  313.8 10.1 %collective-permute-start.22 = (f32[24,128]{1,0:T(8,128)S(1)}, f32[24,128]{1,0:T(8,128)S(1)}, u32[]{:S(2)}, u32[]{:S(2)}) collective-permute-start(f32[24,128]{1,0:T(8,128)S(1)} %reduce_sum.28), channel_id=1, source_target_pairs={{0,1},{1,17},{2,0},{3,16},{4,3},{5,19},{6,2},{7,18},{8,5},{9,21},{... | collective-permute-start | bytes 36872 | tf_op jit(solution)/shard_map/ppermute | solution.py:959
Sparse Core Ops, SparseCore 0:
  11.6 93.0 all-gather.1

commit v9 on v8

--- a/solution.py
+++ b/solution.py
@@ -381,7 +381,7 @@
 def feed_kernel(
     tag_ref, second, gradient, mods, w_expand, w_shrink, kernel,
     shrunk, d_second, keep_expand, send_expand, keep_shrink, send_shrink, g_kernel,
-    d_shrunk, d_shrunk_t, expand, shrink, field, slope, hidden, d_field,
+    d_shrunk, d_shrunk_t, expand, shrink, field, slope, hidden, d_field, shrunk_sum, second_sum,
 ):
     step = pl.program_id(0)
     tag, core = tag_ref[0], tag_ref[1]
@@ -392,8 +392,8 @@
         value = gradient[...].astype(F32).reshape(4, 2, 8, 2, 8, D) * gate
         d_shrunk[...] = value.reshape(TOK, D).astype(BF)
         d_shrunk_t[...] = d_shrunk[...].T
-        shrunk[...] = jnp.zeros_like(shrunk)
-        d_second[...] = jnp.zeros_like(d_second)
+        shrunk_sum[...] = jnp.zeros_like(shrunk_sum)
+        second_sum[...] = jnp.zeros_like(second_sum)
 
     join_rows(w_expand, expand)
     for q in range(2):
@@ -440,8 +440,13 @@
         keep_shrink[:, 0, q] = jnp.where(core == 0, part[:, 0], part[:, 1])
         send_shrink[:, 0, q] = jnp.where(core == 0, part[:, 1], part[:, 0])
     share_out(dot(d_fld, second[...].reshape(TOK, D), 0, 0), core, (0, 4), keep_expand, send_expand)
-    shrunk[...] += dot(hid, shrink[...], 1, 1).reshape(4, GROUP, D)
-    d_second[...] += dot(d_fld, expand[...], 1, 0).reshape(4, GROUP, D)
+    shrunk_sum[...] += dot(hid, shrink[...], 1, 1).reshape(4, GROUP, D)
+    second_sum[...] += dot(d_fld, expand[...], 1, 0).reshape(4, GROUP, D)
+
+    @pl.when(step == pl.num_programs(0) - 1)
+    def _():
+        shrunk[...] = shrunk_sum[...].astype(BF)
+        d_second[...] = second_sum[...].astype(BF)
 
 
 def packed_half(units):
@@ -474,8 +479,8 @@
             pl.BlockSpec((9, CHUNK), lambda c: (0, c)),
         ],
         out_shape=[
-            jax.ShapeDtypeStruct((4, GROUP, D), F32),
-            jax.ShapeDtypeStruct((4, GROUP, D), F32),
+            jax.ShapeDtypeStruct((4, GROUP, D), BF),
+            jax.ShapeDtypeStruct((4, GROUP, D), BF),
             packed_half(4),
             packed_half(4),
             packed_half(4),
@@ -491,6 +496,8 @@
             pltpu.VMEM((4, GROUP, CHUNK), F32),
             pltpu.VMEM((4, GROUP, CHUNK), BF),
             pltpu.VMEM((4, GROUP, CHUNK), BF),
+            pltpu.VMEM((4, GROUP, D), F32),
+            pltpu.VMEM((4, GROUP, D), F32),
         ],
         compiler_params=params(60),
         cost_estimate=cost(38),
@@ -513,9 +520,9 @@
         half = i // 2
         base = resid[0, rows, :]
         normal, factor = norm_stats(base)
-        shrunk_rows = shrunk[0, rows, :]
+        shrunk_rows = shrunk[0, rows, :].astype(F32)
         outward = gradient[0, rows, :].astype(F32)
-        d_sec = d_second[0, rows, :]
+        d_sec = d_second[0, rows, :].astype(F32)
 
         def by_item(value):
             return value.reshape(4, 2, 8, D)
@@ -940,25 +947,24 @@
 
 def exchange_columns(nd, nf, d_act):
     rows, items = d_act.shape
+    half = lax.axis_index("fsdp")
     if (nd, nf) == (NJ, NK):
-        return lax.all_to_all(d_act.reshape(nd, rows // nd, items), "dp", 0, 0, tiled=True)
-    spread = lax.dynamic_update_slice_in_dim(
-        jnp.zeros((rows * nf, items), F32), d_act, lax.axis_index("fsdp") * rows, axis=0
-    )
+        spread = jnp.zeros((nd, 2 * rows // nd, items), BF)
+        own = d_act.astype(BF).reshape(nd // 2, 2 * rows // nd, items)
+        spread = lax.dynamic_update_slice_in_dim(spread, own, half * (nd // 2), axis=0)
+        return lax.all_to_all(spread, "dp", 0, 0, tiled=True)
+    spread = jnp.zeros((rows * nf, items), F32)
+    spread = lax.dynamic_update_slice_in_dim(spread, d_act, half * rows, axis=0)
     spread = spread.reshape(nd, 1, -1, items)
     spread = jnp.broadcast_to(spread, (nd, nf) + spread.shape[2:])
     return exchange(spread.reshape((nd * nf,) + spread.shape[2:]))
 
 
 def own_columns(nd, nf, terms):
-    part = terms.sum(axis=0)
+    part = terms.astype(F32).sum(axis=0)
     if (nd, nf) != (NJ, NK):
         return part
-    order = [(j * NK + k, k * NJ + j) for j in range(NJ) for k in range(NK)]
-    own = lax.ppermute(part, BOTH, order)
-    other = lax.ppermute(part, BOTH, [(i, o ^ 1) for i, o in order])
-    first = lax.axis_index("fsdp") == 0
-    return jnp.concatenate([jnp.where(first, own, other), jnp.where(first, other, own)])
+    return part + swap(part, None)
 
 
 def body(

time: 335 us -> 332 us (level)
  starting transfers between devices: 68.2 us -> 61.7 us
    ppermute x2 -> x0, starting transfers between devices: 7.94 us -> none  [the longest x1 7.28 us: own_columns(): other = lax.ppermute(part, BOTH, [(i, o ^ 1) for i, o in order])]
    ppermute x7 -> x8, starting transfers between devices: 7.14 us -> 8.68 us  [swap(): return lax.ppermute(value, 'fsdp', [(0, 1), (1, 0)])]
  transfers between devices with their start and end apart: 35 -> 34, of which waited for: 9 -> 11; matrix products, arithmetic and copies ran while one was open for 11% -> 12% of each run, Pallas kernels for 34% -> 34%
where the time goes in v9:
time: 332 us; the launch traced here: 331 us
  Pallas kernels  181 us (55%)
  starting transfers between devices  61.7 us (19%)
  waiting for transfers between devices  27.4 us (8%)
  other arithmetic  25.8 us (8%)
  local copies, waits for them, and re-layouts  15.8 us (5%)
  between operations  15.5 us (5%)
  matrix products  3.83 us (1%)
    pallas_call x1, Pallas kernels, feed(): pl.pallas_call(feed_kernel, grid=(FF // CHUNK,), in_specs=[SMEM_SPEC, who...  69.1 us
    pallas_call x1, Pallas kernels, attend(): pl.pallas_call(attend_kernel, grid=(4,), in_specs=[SMEM_SPEC, group_spec(...  33.1 us
    pallas_call x2, Pallas kernels, attend_back(): pl.pallas_call(attend_back_kernel, grid=(count,), in_specs=[SMEM_SPEC, pi...  31.9 us
    pallas_call x1, Pallas kernels, conv_back(): pl.pallas_call(conv_back_kernel, grid=(8 // PAIRS,), in_specs=[SMEM_SPEC,...  16.3 us
    all_to_all x3, starting transfers between devices, exchange(): return lax.all_to_all(pieces, BOTH, 0, 0, tiled=True)  15.1 us
    ppermute x14, starting transfers between devices, swap(): return lax.ppermute(value, 'dp', [(i, i ^ bit) for i in range(NJ)])  13.6 us
    pallas_call x1, Pallas kernels, project_grads(): pl.pallas_call(project_grads_kernel, grid=(8 // PAIRS,), in_specs=[SMEM_S...  9.76 us
    all_to_all x3, waiting for transfers between devices, exchange(): return lax.all_to_all(pieces, BOTH, 0, 0, tiled=True)  9.07 us
  transfers between devices with their start and end apart: 34, of which 11 were waited for; matrix products, arithmetic and copies ran while one was open for 12% of the time, Pallas kernels for 34%

profile of v9, /device:TPU:0, one launch (start us, length us, event | category | flops | bytes accessed | tf_op | source)
XLA Modules:
  0.0 330.5 jit_solution(17732822783934553742)
XLA Ops:
  7.3 1.0 copy.123
  8.3 1.7 pad_maximum_fusion.7
  10.0 5.1 %collective-permute-start.1 = (bf16[4,48,384]{2,1,0:T(8,128)(2,1)S(1)}, bf16[4,48,384]{2,1,0:T(8,128)(2,1)S(1)}, u32[]{:S(2)}, u32[]{:S(2)}) collective-permute-start(bf16[4,48,384]{2,1,0:T(8,128)(2,1)S(1)} %pad_maximum_fusion.8), channel_id=1, source_target_pairs={{0,24},{2,26},{4,28},{6,30},{8,0},{10,2},{12,4},{14,6},{16,8},{18,... | collective-permute-start | bytes 442376 | tf_op jit(solution)/shard_map/ppermute | solution.py:848
  15.1 1.0 collective-permute-start.3
  16.8 5.1 %all-to-all-start = ((s32[32,1,8]{2,1,0:T(1,128)}), s32[32,1,8]{2,1,0:T(1,128)S(1)}, u32[]{:S(2)}, u32[]{:S(2)}) async-start(s32[32,1,8]{2,1,0:T(1,128)} %broadcast_in_dim.34), calls=%async_computation | async-start | bytes 32768 | tf_op jit(solution)/shard_map/all_to_all | solution.py:818
  21.9 6.0 %prepare.1 = (bf16[4,256,768]{2,1,0:T(8,128)(2,1)}, bf16[4,256,768]{2,1,0:T(8,128)(2,1)}, f32[4,256,768]{2,1,0:T(8,128)}, f32[4,256,1]{2,1,0:T(8,128)}) custom-call(bf16[1024,768]{1,0:T(8,128)(2,1)} %latents.1, bf16[1024,768]{1,0:T(8,128)(2,1)} %cotangent.1), custom_call_target="tpu_custom_call" | custom-call | flops 600000000 | bytes 4194304 | tf_op jit(solution)/shard_map/prepare/pallas_call | solution.py:89
  28.0 4.2 %all-to-all-done = s32[32,1,8]{2,1,0:T(1,128)S(1)} async-done(((s32[32,1,8]{2,1,0:T(1,128)}), s32[32,1,8]{2,1,0:T(1,128)S(1)}, u32[]{:S(2)}, u32[]{:S(2)}) %all-to-all-start) | async-done | bytes 1056 | tf_op jit(solution)/shard_map/all_to_all | solution.py:818
  33.8 3.1 collective-permute-done
  39.3 8.8 %all-to-all-start.1 = ((bf16[16,65,128]{2,1,0:T(8,128)(2,1)}), bf16[16,65,128]{2,1,0:T(8,128)(2,1)S(1)}, u32[]{:S(2)}, u32[]{:S(2)}) async-start(bf16[16,65,128]{2,1,0:T(8,128)(2,1)} %broadcast_in_dim.35), calls=%async_computation.1 | async-start | bytes 589824 | tf_op jit(solution)/shard_map/all_to_all | solution.py:938
  48.2 2.0 collective-permute-start.7
  50.3 1.3 collective-permute-start.6
  52.9 7.9 %all-to-all-done.1 = bf16[16,65,128]{2,1,0:T(8,128)(2,1)S(1)} async-done(((bf16[16,65,128]{2,1,0:T(8,128)(2,1)}), bf16[16,65,128]{2,1,0:T(8,128)(2,1)S(1)}, u32[]{:S(2)}, u32[]{:S(2)}) %all-to-all-start.1) | async-done | bytes 266272 | tf_op jit(solution)/shard_map/all_to_all | solution.py:938
  61.1 0.9 reshape.225
  62.1 7.2 %all-to-all-start.2 = ((f32[32,1,1152]{2,1,0:T(1,128)}), f32[32,1,1152]{2,1,0:T(1,128)S(1)}, u32[]{:S(2)}, u32[]{:S(2)}) async-start(f32[32,1,1152]{2,1,0:T(1,128)} %reshape.225), calls=%async_computation.2 | async-start | bytes 294912 | tf_op jit(solution)/shard_map/all_to_all | solution.py:818
  69.3 1.4 pad_maximum_fusion.1.own_b
  71.0 2.3 pad_maximum_fusion.own_a
  75.5 4.8 %all-to-all-done.2 = f32[32,1,1152]{2,1,0:T(1,128)S(1)} async-done(((f32[32,1,1152]{2,1,0:T(1,128)}), f32[32,1,1152]{2,1,0:T(1,128)S(1)}, u32[]{:S(2)}, u32[]{:S(2)}) %all-to-all-start.2) | async-done | bytes 147488 | tf_op jit(solution)/shard_map/all_to_all | solution.py:818
  81.2 0.9 broadcast_in_dim.39.mods
  82.1 6.1 %first_conv.1.conv_in = bf16[4,256,768]{2,1,0:T(8,128)(2,1)} custom-call(s32[1]{0:T(128)S(6)} %copy.126.tag_ref, f32[4,256,768]{2,1,0:T(8,128)} %get-tuple-element.73.norm, f32[6,4,8,768]{3,2,1,0:T(8,128)} %broadcast_in_dim.39.mods, f32[9,768]{1,0:T(8,128)} %reshape.201.kernel), custom_call_target="tpu_custom_call" | custom-call | flops 600000000 | bytes 4194304 | tf_op jit(solution)/shard_map/first_conv/pallas_call | solution.py:225
  88.2 33.1 %attend.1 = (bf16[4,2304,256]{2,1,0:T(8,128)(2,1)}, bf16[4,256,768]{2,1,0:T(8,128)(2,1)}, bf16[4,256,768]{2,1,0:T(8,128)(2,1)}, f32[4,256,768]{2,1,0:T(8,128)}, ...) custom-call(s32[5]{0:T(128)} %stack.85.where.tag_ref, ...), custom_call_target="tpu_custom_call" | custom-call | flops 3800000000 | bytes 4194304 | tf_op jit(solution)/shard_map/attend/pallas_call | solution.py:340
  121.3 69.1 %feed.1 = (bf16[4,256,768]{2,1,0:T(8,128)(2,1)}, bf16[4,256,768]{2,1,0:T(8,128)(2,1)}, bf16[8,2,4,48,384]{4,3,2,1,0:T(8,128)(2,1)}, bf16[8,2,4,48,384]{4,3,2,1,0...) custom-call(s32[5]{0:T(128)} %stack.85.where.tag_ref, ...), custom_call_target="tpu_custom_call" | custom-call | flops 3800000000 | bytes 4194304 | tf_op jit(solution)/shard_map/feed/pallas_call | solution.py:460
  190.9 9.5 %attend_back_0.1 = (bf16[1,256,768]{2,1,0:T(8,128)(2,1)}, f32[1,256,768]{2,1,0:T(8,128)}, bf16[2304,256]{1,0:T(8,128)(2,1)}, bf16[768,256]{1,0:T(8,128)(2,1)}, f32[4,4,768]{2,1,0:T(4,128)}) custom-call(s32[5]{0:T(128)} %stack.85.where.tag_ref, f32[4,256,768]{2,1,0:T(8,128)} %get-tuple-element.83.resid, bf16[4,256,768]{2,1,0:T(8,128)(2,1)} %get-tuple-element.86.shrunk, ...), custom_call_target="tpu_custom_call" | custom-call | flops 900000000 | bytes 4194304 | tf_op jit(solution)/shard_map/attend_back_0/pallas_call | solution.py:583
  200.5 3.1 dynamic-slice_add_fusion.1
  203.5 1.0 collective-permute-start.12
  204.5 1.9 dynamic-slice_add_fusion
  206.4 1.5 collective-permute-start.13
  208.0 22.4 %attend_back_1.1 = (bf16[3,256,768]{2,1,0:T(8,128)(2,1)}, f32[3,256,768]{2,1,0:T(8,128)}, bf16[2304,768]{1,0:T(8,128)(2,1)}, bf16[768,768]{1,0:T(8,128)(2,1)}, f32[4,4,768]{2,1,0:T(4,128)}) custom-call(s32[5]{0:T(128)} %stack.85.where.tag_ref, f32[4,256,768]{2,1,0:T(8,128)} %get-tuple-element.83.resid, bf16[4,256,768]{2,1,0:T(8,128)(2,1)} %get-tuple-element.86.shrunk, ...), custom_call_target="tpu_custom_call" | custom-call | flops 2700000000 | bytes 4194304 | tf_op jit(solution)/shard_map/attend_back_1/pallas_call | solution.py:583
  230.4 1.3 collective-permute-done.12
  231.7 0.9 bitcast_add_fusion.1
  232.7 1.5 collective-permute-start.16
  234.2 1.0 bitcast_add_fusion
  235.1 1.0 collective-permute-start.17
  236.2 9.8 %project_grads.1 = (bf16[8,2,2,48,384]{4,3,2,1,0:T(8,128)(2,1)}, bf16[8,2,2,48,384]{4,3,2,1,0:T(8,128)(2,1)}, bf16[8,2,2,48,384]{4,3,2,1,0:T(8,128)(2,1)}, bf16[8,2,2,48,384]{4,3,2,1,0:T(8,128)(2,1)}) custom-call(s32[5]{0:T(128)} %stack.85.where.tag_ref, bf16[2304,256]{1,0:T(8,128)(2,1)} %get-tuple-element.92.d_qkv0, ...), custom_call_target="tpu_custom_call" | custom-call | flops 800000000 | bytes 4194304 | tf_op jit(solution)/shard_map/project_grads/pallas_call | solution.py:653
  246.6 1.0 collective-permute-done.16
  247.6 1.1 constant_dynamic-slice_fusion.2
  248.7 1.3 collective-permute-done.17
  250.0 1.1 constant_dynamic-slice_fusion
  251.6 1.1 pad_maximum_fusion.4
  253.8 0.9 fusion.1
  254.7 1.3 collective-permute-start.19
  256.1 0.9 fusion.2
  257.0 1.0 collective-permute-start.18
  258.3 16.3 %conv_back.1 = (f32[4,256,768]{2,1,0:T(8,128)}, bf16[32,16,288]{2,1,0:T(8,128)(2,1)}) custom-call(s32[5]{0:T(128)} %stack.85.where.tag_ref, bf16[2304,256]{1,0:T(8,128)(2,1)} %get-tuple-element.92.d_qkv0, bf16[2304,768]{1,0:T(8,128)(2,1)} %get-tuple-element.100.d_qkv1, bf16[2304,768]{1,0:T(8,128)(2,1)} %get-tuple-element.114.weight, ...), custom_call_target="tpu_custom_call" | custom-call | flops 1500000000 | bytes 4194304 | tf_op jit(solution)/shard_map/conv_back/pallas_call | solution.py:738
  274.6 2.9 all-to-all-start.3
  277.7 1.9 fusion.17
  279.6 2.7 collective-permute-start.27
  282.2 1.7 fusion.24
  284.0 1.5 collective-permute-start.23
  285.4 1.0 fusion.25
  286.4 1.6 collective-permute-start.22
  288.0 8.4 %finish.1 = (bf16[1024,768]{1,0:T(8,128)(2,1)}, f32[1024,768]{1,0:T(8,128)}) custom-call(f32[4,256,768]{2,1,0:T(8,128)} %get-tuple-element.123.d_first, f32[4,256,768]{2,1,0:T(8,128)} %get-tuple-element.73.norm, f32[4,256,1]{2,1,0:T(8,128)} %get-tuple-element.124.factor, f32[1,256,768]{2,1,0:T(8,128)} %get-tuple-element.125.d_resid0, ...), custom_call_target="tpu_custom_call" | custom-call | flops 800000000 | bytes 4194304 | tf_op jit(solution)/shard_map/finish/pallas_call | solution.py:796
  296.5 1.0 fusion.42
  300.6 3.6 %all-to-all-start.4 = ((bf16[16,48,128]{2,1,0:T(8,128)(2,1)}), bf16[16,48,128]{2,1,0:T(8,128)(2,1)S(1)}, u32[]{:S(2)}, u32[]{:S(2)}) async-start(bf16[16,48,128]{2,1,0:T(8,128)(2,1)} %constant_dynamic-update-slice_fusion), calls=%async_computation.4 | async-start | bytes 393216 | tf_op jit(solution)/shard_map/all_to_all | solution.py:955
  304.2 1.1 bitcast_add_fusion.4
  305.4 1.1 bitcast_add_fusion.6
  306.6 2.0 collective-permute-start.24
  308.5 2.4 collective-permute-start.25
  310.9 1.5 collective-permute-start.26
  312.4 1.3 all-to-all-done.4
  313.7 1.5 collective-permute-start.21
  315.3 1.3 convert_add_fusion
  318.1 0.9 fusion.5
  319.0 0.9 fusion.8
  320.0 2.3 collective-permute-done.25
  (134 shorter events, 19.0 us)
Async XLA Ops:
  7.2 53.7 %copy-start = (bf16[384,288]{0,1:T(8,128)(2,1)S(1)}, bf16[384,288]{0,1:T(8,128)(2,1)}, u32[]{:S(2)}) copy-start(bf16[384,288]{0,1:T(8,128)(2,1)} %param.20) | copy-start | bytes 663556
  7.2 2.8 copy-start.6
  7.2 2.8 copy-start.7
  7.2 8.9 %copy-start.13 = (s32[1,4]{1,0:T(1,128)S(1)}, s32[1,4]{1,0:T(1,128)}, u32[]{:S(2)}) copy-start(s32[1,4]{1,0:T(1,128)} %param.16) | copy-start | bytes 52
  7.2 8.9 %copy-start.12 = (s32[1,4]{1,0:T(1,128)S(1)}, s32[1,4]{1,0:T(1,128)}, u32[]{:S(2)}) copy-start(s32[1,4]{1,0:T(1,128)} %param.17) | copy-start | bytes 52
  7.2 114.0 %all-gather.2.cloned.1.call-start = ((), (), s32[]{:S(2)}) async-start(), calls=%async_computation.5 | async-start | bytes 9732096 | tf_op jit(solution)/shard_map/all_gather | solution.py:832
  10.0 26.9 %collective-permute-start.1 = (bf16[4,48,384]{2,1,0:T(8,128)(2,1)S(1)}, bf16[4,48,384]{2,1,0:T(8,128)(2,1)S(1)}, u32[]{:S(2)}, u32[]{:S(2)}) collective-permute-start(bf16[4,48,384]{2,1,0:T(8,128)(2,1)S(1)} %pad_maximum_fusion.8), channel_id=1, source_target_pairs={{0,24},{2,26},{4,28},{6,30},{8,0},{10,2},{12,4},{14,6},{16,8},{18,... | collective-permute-start | bytes 442376 | tf_op jit(solution)/shard_map/ppermute | solution.py:848
  15.1 21.8 %collective-permute-start.2 = (bf16[4,48,384]{2,1,0:T(8,128)(2,1)S(1)}, bf16[4,48,384]{2,1,0:T(8,128)(2,1)S(1)}, u32[]{:S(2)}, u32[]{:S(2)}) collective-permute-start(bf16[4,48,384]{2,1,0:T(8,128)(2,1)S(1)} %pad_maximum_fusion.8), channel_id=1, source_target_pairs={{0,16},{2,18},{4,20},{6,22},{8,24},{10,26},{12,28},{14,30},{16,0},... | collective-permute-start | bytes 442376 | tf_op jit(solution)/shard_map/ppermute | solution.py:848
  15.1 21.8 %collective-permute-start.3 = (bf16[4,48,384]{2,1,0:T(8,128)(2,1)S(1)}, bf16[4,48,384]{2,1,0:T(8,128)(2,1)S(1)}, u32[]{:S(2)}, u32[]{:S(2)}) collective-permute-start(bf16[4,48,384]{2,1,0:T(8,128)(2,1)S(1)} %pad_maximum_fusion.8), channel_id=1, source_target_pairs={{0,8},{2,10},{4,12},{6,14},{8,16},{10,18},{12,20},{14,22},{16,24},... | collective-permute-start | bytes 442376 | tf_op jit(solution)/shard_map/ppermute | solution.py:848
  16.8 15.3 %all-to-all-start = ((s32[32,1,8]{2,1,0:T(1,128)}), s32[32,1,8]{2,1,0:T(1,128)S(1)}, u32[]{:S(2)}, u32[]{:S(2)}) async-start(s32[32,1,8]{2,1,0:T(1,128)} %broadcast_in_dim.34), calls=%async_computation | async-start | bytes 32768 | tf_op jit(solution)/shard_map/all_to_all | solution.py:818
  21.9 10.5 %copy-start.10 = (bf16[500,48]{0,1:T(8,128)(2,1)S(1)}, bf16[500,48]{0,1:T(8,128)(2,1)}, u32[]{:S(2)}) copy-start(bf16[500,48]{0,1:T(8,128)(2,1)} %param.18) | copy-start | bytes 144004
  21.9 10.8 %copy-start.11 = (bf16[500,48]{0,1:T(8,128)(2,1)S(1)}, bf16[500,48]{0,1:T(8,128)(2,1)}, u32[]{:S(2)}) copy-start(bf16[500,48]{0,1:T(8,128)(2,1)} %param.19) | copy-start | bytes 144004
  21.9 11.7 %copy-start.8 = (bf16[9,192]{1,0:T(8,128)(2,1)S(1)}, bf16[9,192]{1,0:T(8,128)(2,1)}, u32[]{:S(2)}) copy-start(bf16[9,192]{1,0:T(8,128)(2,1)} %param.25) | copy-start | bytes 10372
  21.9 11.7 %copy-start.9 = (bf16[9,48]{1,0:T(8,128)(2,1)S(1)}, bf16[9,48]{1,0:T(8,128)(2,1)}, u32[]{:S(2)}) copy-start(bf16[9,48]{1,0:T(8,128)(2,1)} %param.21) | copy-start | bytes 2596
  33.0 3.9 %collective-permute-start = (f32[48,128]{1,0:T(8,128)S(1)}, f32[48,128]{1,0:T(8,128)S(1)}, u32[]{:S(2)}, u32[]{:S(2)}) collective-permute-start(f32[48,128]{1,0:T(8,128)S(1)} %fusion), channel_id=1, source_target_pairs={{0,1},{1,0},{2,3},{3,2},{4,5},{5,4},{6,7},{7,6},{8,9},{9,8},{10,11... | collective-permute-start | bytes 73736 | tf_op jit(solution)/shard_map/ppermute | solution.py:872
  37.1 11.0 %collective-permute-start.5 = (bf16[4,2,48,384]{3,2,1,0:T(8,128)(2,1)S(1)}, bf16[4,2,48,384]{3,2,1,0:T(8,128)(2,1)S(1)}, u32[]{:S(2)}, u32[]{:S(2)}) collective-permute-start(bf16[4,2,48,384]{3,2,1,0:T(8,128)(2,1)S(1)} %get-tuple-element.169), channel_id=1, source_target_pairs={{0,1},{1,0},{2,3},{3,2},{4,5},{5,4},{6,7},{7,6},{8,9},{9,8},{10,11... | collective-permute-start | bytes 884744 | tf_op jit(solution)/shard_map/ppermute | solution.py:872
  37.8 12.4 %collective-permute-start.4 = (bf16[4,2,48,384]{3,2,1,0:T(8,128)(2,1)S(1)}, bf16[4,2,48,384]{3,2,1,0:T(8,128)(2,1)S(1)}, u32[]{:S(2)}, u32[]{:S(2)}) collective-permute-start(bf16[4,2,48,384]{3,2,1,0:T(8,128)(2,1)S(1)} %get-tuple-element.171), channel_id=1, source_target_pairs={{0,4},{2,6},{4,0},{6,2},{8,12},{10,14},{12,8},{14,10},{16,20},{18,... | collective-permute-start | bytes 884744 | tf_op jit(solution)/shard_map/ppermute | solution.py:873
  39.3 21.5 %all-to-all-start.1 = ((bf16[16,65,128]{2,1,0:T(8,128)(2,1)}), bf16[16,65,128]{2,1,0:T(8,128)(2,1)S(1)}, u32[]{:S(2)}, u32[]{:S(2)}) async-start(bf16[16,65,128]{2,1,0:T(8,128)(2,1)} %broadcast_in_dim.35), calls=%async_computation.1 | async-start | bytes 589824 | tf_op jit(solution)/shard_map/all_to_all | solution.py:938
  48.2 21.0 %collective-permute-start.7 = (bf16[2,4,2,48,384]{4,3,2,1,0:T(8,128)(2,1)S(1)}, bf16[2,4,2,48,384]{4,3,2,1,0:T(8,128)(2,1)}, u32[]{:S(2)}, u32[]{:S(2)}) collective-permute-start(bf16[2,4,2,48,384]{4,3,2,1,0:T(8,128)(2,1)S(1)} %get-tuple-element.165), channel_id=1, source_target_pairs={{0,4},{2,6},{4,0},{6,2},{8,12},{10,14},{12,8},{14,10},{16,20},{18,... | collective-permute-start | bytes 1769480 | tf_op jit(solution)/shard_map/ppermute | solution.py:873
  50.3 20.6 %collective-permute-start.6 = (bf16[2,4,2,48,384]{4,3,2,1,0:T(8,128)(2,1)S(1)}, bf16[2,4,2,48,384]{4,3,2,1,0:T(8,128)(2,1)}, u32[]{:S(2)}, u32[]{:S(2)}) collective-permute-start(bf16[2,4,2,48,384]{4,3,2,1,0:T(8,128)(2,1)S(1)} %get-tuple-element.167), channel_id=1, source_target_pairs={{0,1},{1,0},{2,3},{3,2},{4,5},{5,4},{6,7},{7,6},{8,9},{9,8},{10,11... | collective-permute-start | bytes 1769480 | tf_op jit(solution)/shard_map/ppermute | solution.py:872
  62.1 18.2 %all-to-all-start.2 = ((f32[32,1,1152]{2,1,0:T(1,128)}), f32[32,1,1152]{2,1,0:T(1,128)S(1)}, u32[]{:S(2)}, u32[]{:S(2)}) async-start(f32[32,1,1152]{2,1,0:T(1,128)} %reshape.225), calls=%async_computation.2 | async-start | bytes 294912 | tf_op jit(solution)/shard_map/all_to_all | solution.py:818
  70.6 2.6 copy-start.5
  70.6 17.5 %collective-permute-start.9 = (bf16[2,2,4,2,48,384]{5,4,3,2,1,0:T(8,128)(2,1)S(1)}, bf16[2,2,4,2,48,384]{5,4,3,2,1,0:T(8,128)(2,1)}, u32[]{:S(2)}, u32[]{:S(2)}) collective-permute-start(bf16[2,2,4,2,48,384]{5,4,3,2,1,0:T(8,128)(2,1)S(1)} %pad_maximum_fusion.1.own_b), channel_id=1, source_target_pairs={{0,2},{2,0},{4,6},{6,4},{8,10},{10,8},{12,14},{14,12},{16,18},{18,... | collective-permute-start | bytes 3538952 | tf_op jit(solution)/shard_map/ppermute | solution.py:873
  73.3 14.9 %collective-permute-start.8 = (bf16[2,2,4,2,48,384]{5,4,3,2,1,0:T(8,128)(2,1)}, bf16[2,2,4,2,48,384]{5,4,3,2,1,0:T(8,128)(2,1)}, u32[]{:S(2)}, u32[]{:S(2)}) collective-permute-start(bf16[2,2,4,2,48,384]{5,4,3,2,1,0:T(8,128)(2,1)} %pad_maximum_fusion.own_a), channel_id=1, source_target_pairs={{0,2},{2,0},{4,6},{6,4},{8,10},{10,8},{12,14},{14,12},{16,18},{18,... | collective-permute-start | bytes 3538952 | tf_op jit(solution)/shard_map/ppermute | solution.py:873
  190.3 10.1 %collective-permute-start.11 = (bf16[8,2,4,48,384]{4,3,2,1,0:T(8,128)(2,1)}, bf16[8,2,4,48,384]{4,3,2,1,0:T(8,128)(2,1)}, u32[]{:S(2)}, u32[]{:S(2)}) collective-permute-start(bf16[8,2,4,48,384]{4,3,2,1,0:T(8,128)(2,1)} %get-tuple-element.97), channel_id=1, source_target_pairs={{0,2},{2,0},{4,6},{6,4},{8,10},{10,8},{12,14},{14,12},{16,18},{18,... | collective-permute-start | bytes 7077896 | tf_op jit(solution)/shard_map/ppermute | solution.py:873
  190.4 10.0 %collective-permute-start.10 = (bf16[8,2,4,48,384]{4,3,2,1,0:T(8,128)(2,1)}, bf16[8,2,4,48,384]{4,3,2,1,0:T(8,128)(2,1)}, u32[]{:S(2)}, u32[]{:S(2)}) collective-permute-start(bf16[8,2,4,48,384]{4,3,2,1,0:T(8,128)(2,1)} %get-tuple-element.94), channel_id=1, source_target_pairs={{0,2},{2,0},{4,6},{6,4},{8,10},{10,8},{12,14},{14,12},{16,18},{18,... | collective-permute-start | bytes 7077896 | tf_op jit(solution)/shard_map/ppermute | solution.py:873
  190.9 9.5 %copy-start.2 = (bf16[8,2,4,48,384]{4,3,2,1,0:T(8,128)(2,1)S(1)}, bf16[8,2,4,48,384]{4,3,2,1,0:T(8,128)(2,1)}, u32[]{:S(2)}) copy-start(bf16[8,2,4,48,384]{4,3,2,1,0:T(8,128)(2,1)} %get-tuple-element.93) | copy-start | bytes 7077892
  200.4 4.1 %copy-start.1 = (bf16[8,2,4,48,384]{4,3,2,1,0:T(8,128)(2,1)S(1)}, bf16[8,2,4,48,384]{4,3,2,1,0:T(8,128)(2,1)}, u32[]{:S(2)}) copy-start(bf16[8,2,4,48,384]{4,3,2,1,0:T(8,128)(2,1)} %get-tuple-element.96) | copy-start | bytes 7077892
  203.5 28.2 %collective-permute-start.12 = (bf16[4,2,4,48,384]{4,3,2,1,0:T(8,128)(2,1)}, bf16[4,2,4,48,384]{4,3,2,1,0:T(8,128)(2,1)S(1)}, u32[]{:S(2)}, u32[]{:S(2)}) collective-permute-start(bf16[4,2,4,48,384]{4,3,2,1,0:T(8,128)(2,1)} %get-tuple-element.140), channel_id=1, source_target_pairs={{0,1},{1,0},{2,3},{3,2},{4,5},{5,4},{6,7},{7,6},{8,9},{9,8},{10,11... | collective-permute-start | bytes 3538952 | tf_op jit(solution)/shard_map/ppermute | solution.py:872
  206.4 27.7 %collective-permute-start.13 = (bf16[4,2,4,48,384]{4,3,2,1,0:T(8,128)(2,1)S(1)}, bf16[4,2,4,48,384]{4,3,2,1,0:T(8,128)(2,1)S(1)}, u32[]{:S(2)}, u32[]{:S(2)}) collective-permute-start(bf16[4,2,4,48,384]{4,3,2,1,0:T(8,128)(2,1)S(1)} %get-tuple-element.138), channel_id=1, source_target_pairs={{0,4},{2,6},{4,0},{6,2},{8,12},{10,14},{12,8},{14,10},{16,20},{18,... | collective-permute-start | bytes 3538952 | tf_op jit(solution)/shard_map/ppermute | solution.py:873
  232.7 14.9 %collective-permute-start.16 = (bf16[4,4,48,384]{3,2,1,0:T(8,128)(2,1)}, bf16[4,4,48,384]{3,2,1,0:T(8,128)(2,1)}, u32[]{:S(2)}, u32[]{:S(2)}) collective-permute-start(bf16[4,4,48,384]{3,2,1,0:T(8,128)(2,1)} %get-tuple-element.142), channel_id=1, source_target_pairs={{0,4},{2,6},{4,0},{6,2},{8,12},{10,14},{12,8},{14,10},{16,20},{18,... | collective-permute-start | bytes 1769480 | tf_op jit(solution)/shard_map/ppermute | solution.py:873
  235.1 14.9 %collective-permute-start.17 = (bf16[4,4,48,384]{3,2,1,0:T(8,128)(2,1)}, bf16[4,4,48,384]{3,2,1,0:T(8,128)(2,1)}, u32[]{:S(2)}, u32[]{:S(2)}) collective-permute-start(bf16[4,4,48,384]{3,2,1,0:T(8,128)(2,1)} %get-tuple-element.144), channel_id=1, source_target_pairs={{0,1},{1,0},{2,3},{3,2},{4,5},{5,4},{6,7},{7,6},{8,9},{9,8},{10,11... | collective-permute-start | bytes 1769480 | tf_op jit(solution)/shard_map/ppermute | solution.py:872
  245.9 7.6 %collective-permute-start.15 = (bf16[8,2,2,48,384]{4,3,2,1,0:T(8,128)(2,1)}, bf16[8,2,2,48,384]{4,3,2,1,0:T(8,128)(2,1)S(1)}, u32[]{:S(2)}, u32[]{:S(2)}) collective-permute-start(bf16[8,2,2,48,384]{4,3,2,1,0:T(8,128)(2,1)} %get-tuple-element.111), channel_id=1, source_target_pairs={{0,2},{2,0},{4,6},{6,4},{8,10},{10,8},{12,14},{14,12},{16,18},{18,... | collective-permute-start | bytes 3538952 | tf_op jit(solution)/shard_map/ppermute | solution.py:873
  246.1 9.8 %collective-permute-start.14 = (bf16[8,2,2,48,384]{4,3,2,1,0:T(8,128)(2,1)}, bf16[8,2,2,48,384]{4,3,2,1,0:T(8,128)(2,1)S(1)}, u32[]{:S(2)}, u32[]{:S(2)}) collective-permute-start(bf16[8,2,2,48,384]{4,3,2,1,0:T(8,128)(2,1)} %get-tuple-element.109), channel_id=1, source_target_pairs={{0,2},{2,0},{4,6},{6,4},{8,10},{10,8},{12,14},{14,12},{16,18},{18,... | collective-permute-start | bytes 3538952 | tf_op jit(solution)/shard_map/ppermute | solution.py:873
  251.3 2.2 copy-start.4
  252.7 25.0 %collective-permute-start.20 = (bf16[2,8,48,384]{3,1,2,0:T(8,128)(2,1)}, bf16[2,8,48,384]{3,1,2,0:T(8,128)(2,1)}, u32[]{:S(2)}, u32[]{:S(2)}) collective-permute-start(bf16[2,8,48,384]{3,1,2,0:T(8,128)(2,1)} %pad_maximum_fusion.4), channel_id=1, source_target_pairs={{0,8},{2,10},{4,12},{6,14},{8,0},{10,2},{12,4},{14,6},{16,24},{18,... | collective-permute-start | bytes 1769480 | tf_op jit(solution)/shard_map/ppermute | solution.py:873
  253.8 2.2 copy-start.3
  254.7 27.6 %collective-permute-start.19 = (bf16[4,2,2,48,384]{4,3,2,0,1:T(8,128)(2,1)}, bf16[4,2,2,48,384]{4,3,2,0,1:T(8,128)(2,1)}, u32[]{:S(2)}, u32[]{:S(2)}) collective-permute-start(bf16[4,2,2,48,384]{4,3,2,0,1:T(8,128)(2,1)} %fusion.1), channel_id=1, source_target_pairs={{0,4},{2,6},{4,0},{6,2},{8,12},{10,14},{12,8},{14,10},{16,20},{18,... | collective-permute-start | bytes 1769480 | tf_op jit(solution)/shard_map/ppermute | solution.py:873
  257.0 25.2 %collective-permute-start.18 = (bf16[4,2,2,48,384]{4,3,2,0,1:T(8,128)(2,1)}, bf16[4,2,2,48,384]{4,3,2,0,1:T(8,128)(2,1)}, u32[]{:S(2)}, u32[]{:S(2)}) collective-permute-start(bf16[4,2,2,48,384]{4,3,2,0,1:T(8,128)(2,1)} %fusion.2), channel_id=1, source_target_pairs={{0,1},{1,0},{2,3},{3,2},{4,5},{5,4},{6,7},{7,6},{8,9},{9,8},{10,11... | collective-permute-start | bytes 1769480 | tf_op jit(solution)/shard_map/ppermute | solution.py:872
  274.6 21.9 %all-to-all-start.3 = ((bf16[32,16,288]{2,1,0:T(8,128)(2,1)}), bf16[32,16,288]{2,1,0:T(8,128)(2,1)S(1)}, u32[]{:S(2)}, u32[]{:S(2)}) async-start(bf16[32,16,288]{2,1,0:T(8,128)(2,1)} %get-tuple-element.122), calls=%async_computation.3 | async-start | bytes 786432 | tf_op jit(solution)/shard_map/all_to_all | solution.py:818
  279.6 32.8 %collective-permute-start.27 = (bf16[8,48,384]{2,0,1:T(8,128)(2,1)}, bf16[8,48,384]{2,0,1:T(8,128)(2,1)}, u32[]{:S(2)}, u32[]{:S(2)}) collective-permute-start(bf16[8,48,384]{2,0,1:T(8,128)(2,1)} %fusion.17), channel_id=1, source_target_pairs={{0,16},{2,18},{4,20},{6,22},{8,24},{10,26},{12,28},{14,30},{16,0},... | collective-permute-start | bytes 884744 | tf_op jit(solution)/shard_map/ppermute | solution.py:873
  284.0 20.3 %collective-permute-start.23 = (bf16[4,2,48,384]{3,2,1,0:T(8,128)(2,1)}, bf16[4,2,48,384]{3,2,1,0:T(8,128)(2,1)}, u32[]{:S(2)}, u32[]{:S(2)}) collective-permute-start(bf16[4,2,48,384]{3,2,1,0:T(8,128)(2,1)} %fusion.24), channel_id=1, source_target_pairs={{0,1},{1,0},{2,3},{3,2},{4,5},{5,4},{6,7},{7,6},{8,9},{9,8},{10,11... | collective-permute-start | bytes 884744 | tf_op jit(solution)/shard_map/ppermute | solution.py:872
  286.4 18.9 %collective-permute-start.22 = (bf16[4,2,48,384]{3,2,1,0:T(8,128)(2,1)S(1)}, bf16[4,2,48,384]{3,2,1,0:T(8,128)(2,1)}, u32[]{:S(2)}, u32[]{:S(2)}) collective-permute-start(bf16[4,2,48,384]{3,2,1,0:T(8,128)(2,1)S(1)} %fusion.25), channel_id=1, source_target_pairs={{0,4},{2,6},{4,0},{6,2},{8,12},{10,14},{12,8},{14,10},{16,20},{18,... | collective-permute-start | bytes 884744 | tf_op jit(solution)/shard_map/ppermute | solution.py:873
  300.6 13.1 %all-to-all-start.4 = ((bf16[16,48,128]{2,1,0:T(8,128)(2,1)}), bf16[16,48,128]{2,1,0:T(8,128)(2,1)S(1)}, u32[]{:S(2)}, u32[]{:S(2)}) async-start(bf16[16,48,128]{2,1,0:T(8,128)(2,1)} %constant_dynamic-update-slice_fusion), calls=%async_computation.4 | async-start | bytes 393216 | tf_op jit(solution)/shard_map/all_to_all | solution.py:955
  306.6 13.4 %collective-permute-start.24 = (bf16[4,48,384]{2,1,0:T(8,128)(2,1)S(1)}, bf16[4,48,384]{2,1,0:T(8,128)(2,1)S(1)}, u32[]{:S(2)}, u32[]{:S(2)}) collective-permute-start(bf16[4,48,384]{2,1,0:T(8,128)(2,1)S(1)} %get-tuple-element.153), channel_id=1, source_target_pairs={{0,8},{2,10},{4,12},{6,14},{8,16},{10,18},{12,20},{14,22},{16,24},... | collective-permute-start | bytes 442376 | tf_op jit(solution)/shard_map/ppermute | solution.py:889
  308.5 13.7 %collective-permute-start.25 = (bf16[4,48,384]{2,1,0:T(8,128)(2,1)S(1)}, bf16[4,48,384]{2,1,0:T(8,128)(2,1)S(1)}, u32[]{:S(2)}, u32[]{:S(2)}) collective-permute-start(bf16[4,48,384]{2,1,0:T(8,128)(2,1)S(1)} %get-tuple-element.154), channel_id=1, source_target_pairs={{0,16},{2,18},{4,20},{6,22},{8,24},{10,26},{12,28},{14,30},{16,0},... | collective-permute-start | bytes 442376 | tf_op jit(solution)/shard_map/ppermute | solution.py:889
  310.9 11.4 %collective-permute-start.26 = (bf16[4,48,384]{2,1,0:T(8,128)(2,1)S(1)}, bf16[4,48,384]{2,1,0:T(8,128)(2,1)S(1)}, u32[]{:S(2)}, u32[]{:S(2)}) collective-permute-start(bf16[4,48,384]{2,1,0:T(8,128)(2,1)S(1)} %get-tuple-element.155), channel_id=1, source_target_pairs={{0,24},{2,26},{4,28},{6,30},{8,0},{10,2},{12,4},{14,6},{16,8},{18,... | collective-permute-start | bytes 442376 | tf_op jit(solution)/shard_map/ppermute | solution.py:889
  313.7 4.4 %collective-permute-start.21 = (f32[48,128]{1,0:T(8,128)S(1)}, f32[48,128]{1,0:T(8,128)S(1)}, u32[]{:S(2)}, u32[]{:S(2)}) collective-permute-start(f32[48,128]{1,0:T(8,128)S(1)} %convert_reduce_fusion.1), channel_id=1, source_target_pairs={{0,1},{1,0},{2,3},{3,2},{4,5},{5,4},{6,7},{7,6},{8,9},{9,8},{10,11... | collective-permute-start | bytes 73736 | tf_op jit(solution)/shard_map/ppermute | solution.py:872
Sparse Core Ops, SparseCore 0:
  11.6 93.0 all-gather.1

commit v10 on v9

--- a/solution.py
+++ b/solution.py
@@ -207,31 +207,38 @@
     tag = tag_ref[0]
     left, right = edge_columns(tag)
     keep = 1.0 - tag.astype(F32)
-    taps = [jnp.broadcast_to(kernel[i : i + 1, :], (16, 128)) for i in range(9)]
-
-    def load(g, p):
-        q = 2 * (p // 8)
-        shift = mods[0, q : q + 2].reshape(16, 128)
-        scale = mods[1, q : q + 2].reshape(16, 128)
-        return norm[g, p * 16 : p * 16 + 16, :] * (1.0 + scale) + shift
-
-    def emit(g, p, value):
-        out[g, p * 16 : p * 16 + 16, :] = value.astype(BF)
-
-    conv_rows(load, taps, left, right, keep, emit)
+
+    def lanes(i, _):
+        cols = pl.ds(pl.multiple_of(i * 128, 128), 128)
+        taps = [jnp.broadcast_to(kernel[t : t + 1, cols], (16, 128)) for t in range(9)]
+
+        def load(g, p):
+            q = 2 * (p // 8)
+            shift = mods[0, q : q + 2, :, cols].reshape(16, 128)
+            scale = mods[1, q : q + 2, :, cols].reshape(16, 128)
+            return norm[g, p * 16 : p * 16 + 16, cols] * (1.0 + scale) + shift
+
+        def emit(g, p, value):
+            out[g, p * 16 : p * 16 + 16, cols] = value.astype(BF)
+
+        conv_rows(load, taps, left, right, keep, emit)
+        return 0
+
+    lax.fori_loop(0, 2, lanes, 0)
 
 
 def first_conv(tag, norm, mods, kernel):
+    lanes = pl.BlockSpec((4, GROUP, 256), lambda i: (0, 0, i))
     return pl.pallas_call(
         first_conv_kernel,
-        grid=(D // 128,),
+        grid=(D // 256,),
         in_specs=[
             SMEM_SPEC,
-            pl.BlockSpec((4, GROUP, 128), lambda i: (0, 0, i)),
-            pl.BlockSpec((6, 4, 8, 128), lambda i: (0, 0, 0, i)),
-            pl.BlockSpec((9, 128), lambda i: (0, i)),
-        ],
-        out_specs=pl.BlockSpec((4, GROUP, 128), lambda i: (0, 0, i)),
+            lanes,
+            pl.BlockSpec((2, 4, 8, 256), lambda i: (0, 0, 0, i)),
+            pl.BlockSpec((9, 256), lambda i: (0, i)),
+        ],
+        out_specs=lanes,
         out_shape=jax.ShapeDtypeStruct((4, GROUP, D), BF),
         compiler_params=params(),
         cost_estimate=cost(6),
@@ -539,7 +546,7 @@
         mean = jnp.mean(inner, axis=-1, keepdims=True)
         along = jnp.mean(inner * normal, axis=-1, keepdims=True)
         back = outward + (inner - mean - normal * along) * factor
-        d_resid[0, rows, :] = back
+        d_resid[0, rows, :] = back.astype(BF)
         add(0, back * attn[0, rows, :].astype(F32))
         gated = (by_item(back) * quadrant_rows(mods, 2, half)).reshape(64, D)
         d_attn[rows, :] = gated.astype(BF)
@@ -604,7 +611,7 @@
         ],
         out_shape=[
             jax.ShapeDtypeStruct((count, GROUP, D), BF),
-            jax.ShapeDtypeStruct((count, GROUP, D), F32),
+            jax.ShapeDtypeStruct((count, GROUP, D), BF),
             jax.ShapeDtypeStruct((3 * D, count * GROUP), BF),
             jax.ShapeDtypeStruct((D, count * GROUP), BF),
             jax.ShapeDtypeStruct((4, 4, D), F32),
@@ -697,7 +704,7 @@
 
             def emit(g, p, value):
                 rows = slice(p * 16, p * 16 + 16)
-                d_first[g, rows, cols] = value
+                d_first[g, rows, cols] = value.astype(BF)
                 sums[0][p // 8] += value
                 sums[1][p // 8] += value * norm[g, rows, cols]
 
@@ -743,7 +750,7 @@
             *column_specs(ROWS),
             pl.BlockSpec((ROWS, D), lambda i: (i, 0)),
             whole((4, GROUP, D)),
-            whole((6, 4, 8, D)),
+            whole((2, 4, 8, D)),
             whole((9, D)),
             whole((4, 4, D)),
             whole((4, 4, D)),
@@ -751,7 +758,7 @@
         ],
         out_specs=[whole((4, GROUP, D)), whole((slots, 16, width))],
         out_shape=[
-            jax.ShapeDtypeStruct((4, GROUP, D), F32),
+            jax.ShapeDtypeStruct((4, GROUP, D), BF),
             jax.ShapeDtypeStruct((slots, 16, width), BF),
         ],
         scratch_shapes=[
@@ -772,8 +779,8 @@
     half = pl.program_id(0) // 2
 
     for g in range(4):
-        base = d_resid1[g - 1] if g else d_resid0[0]
-        value = d_first[g]
+        base = (d_resid1[g - 1] if g else d_resid0[0]).astype(F32)
+        value = d_first[g].astype(F32)
         normal = norm[g]
         inner = (value.reshape(4, 2, 8, D) * (1.0 + quadrant_rows(mods, 1, half))).reshape(64, D)
         mean = jnp.mean(inner, axis=-1, keepdims=True)
@@ -798,7 +805,7 @@
         grid=(4,),
         in_specs=[split(4, D), split(4, D), split(4, 1)]
         + [split(count, D) for _, count in PARTS] * 2
-        + [whole((6, 4, 8, D))],
+        + [whole((2, 4, 8, D))],
         out_specs=[flat, flat],
         out_shape=[
             jax.ShapeDtypeStruct((TOK, D), BF),

time: 332 us -> 331 us (level)
  transfers between devices with their start and end apart: 34 -> 34, of which waited for: 11 -> 10; matrix products, arithmetic and copies ran while one was open for 12% -> 12% of each run, Pallas kernels for 34% -> 33%
where the time goes in v10:
time: 331 us; the launch traced here: 329 us
  Pallas kernels  178 us (54%)
  starting transfers between devices  61.8 us (19%)
  waiting for transfers between devices  28.2 us (9%)
  other arithmetic  25.7 us (8%)
  local copies, waits for them, and re-layouts  15.9 us (5%)
  between operations  15.5 us (5%)
  matrix products  3.83 us (1%)
    pallas_call x1, Pallas kernels, feed(): pl.pallas_call(feed_kernel, grid=(FF // CHUNK,), in_specs=[SMEM_SPEC, who...  69.1 us
    pallas_call x1, Pallas kernels, attend(): pl.pallas_call(attend_kernel, grid=(4,), in_specs=[SMEM_SPEC, group_spec(...  33.1 us
    pallas_call x2, Pallas kernels, attend_back(): pl.pallas_call(attend_back_kernel, grid=(count,), in_specs=[SMEM_SPEC, pi...  31.9 us
    pallas_call x1, Pallas kernels, conv_back(): pl.pallas_call(conv_back_kernel, grid=(8 // PAIRS,), in_specs=[SMEM_SPEC,...  15.9 us
    all_to_all x3, starting transfers between devices, exchange(): return lax.all_to_all(pieces, BOTH, 0, 0, tiled=True)  15.1 us
    ppermute x14, starting transfers between devices, swap(): return lax.ppermute(value, 'dp', [(i, i ^ bit) for i in range(NJ)])  13.7 us
    all_to_all x3, waiting for transfers between devices, exchange(): return lax.all_to_all(pieces, BOTH, 0, 0, tiled=True)  9.85 us
    pallas_call x1, Pallas kernels, project_grads(): pl.pallas_call(project_grads_kernel, grid=(8 // PAIRS,), in_specs=[SMEM_S...  9.75 us
  transfers between devices with their start and end apart: 34, of which 10 were waited for; matrix products, arithmetic and copies ran while one was open for 12% of the time, Pallas kernels for 33%

profile of v10, /device:TPU:0, one launch (start us, length us, event | category | flops | bytes accessed | tf_op | source)
XLA Modules:
  0.0 329.3 jit_solution(3683064242560686014)
XLA Ops:
  7.3 1.0 copy.123
  8.3 1.7 pad_maximum_fusion.7
  10.0 5.1 %collective-permute-start.1 = (bf16[4,48,384]{2,1,0:T(8,128)(2,1)S(1)}, bf16[4,48,384]{2,1,0:T(8,128)(2,1)S(1)}, u32[]{:S(2)}, u32[]{:S(2)}) collective-permute-start(bf16[4,48,384]{2,1,0:T(8,128)(2,1)S(1)} %pad_maximum_fusion.8), channel_id=1, source_target_pairs={{0,24},{2,26},{4,28},{6,30},{8,0},{10,2},{12,4},{14,6},{16,8},{18,... | collective-permute-start | bytes 442376 | tf_op jit(solution)/shard_map/ppermute | solution.py:855
  15.1 1.0 collective-permute-start.3
  16.8 5.1 %all-to-all-start = ((s32[32,1,8]{2,1,0:T(1,128)}), s32[32,1,8]{2,1,0:T(1,128)S(1)}, u32[]{:S(2)}, u32[]{:S(2)}) async-start(s32[32,1,8]{2,1,0:T(1,128)} %broadcast_in_dim.34), calls=%async_computation | async-start | bytes 32768 | tf_op jit(solution)/shard_map/all_to_all | solution.py:825
  21.9 6.0 %prepare.1 = (bf16[4,256,768]{2,1,0:T(8,128)(2,1)}, bf16[4,256,768]{2,1,0:T(8,128)(2,1)}, f32[4,256,768]{2,1,0:T(8,128)}, f32[4,256,1]{2,1,0:T(8,128)}) custom-call(bf16[1024,768]{1,0:T(8,128)(2,1)} %latents.1, bf16[1024,768]{1,0:T(8,128)(2,1)} %cotangent.1), custom_call_target="tpu_custom_call" | custom-call | flops 600000000 | bytes 4194304 | tf_op jit(solution)/shard_map/prepare/pallas_call | solution.py:89
  28.0 4.2 %all-to-all-done = s32[32,1,8]{2,1,0:T(1,128)S(1)} async-done(((s32[32,1,8]{2,1,0:T(1,128)}), s32[32,1,8]{2,1,0:T(1,128)S(1)}, u32[]{:S(2)}, u32[]{:S(2)}) %all-to-all-start) | async-done | bytes 1056 | tf_op jit(solution)/shard_map/all_to_all | solution.py:825
  33.8 3.1 collective-permute-done
  39.3 8.8 %all-to-all-start.1 = ((bf16[16,65,128]{2,1,0:T(8,128)(2,1)}), bf16[16,65,128]{2,1,0:T(8,128)(2,1)S(1)}, u32[]{:S(2)}, u32[]{:S(2)}) async-start(bf16[16,65,128]{2,1,0:T(8,128)(2,1)} %broadcast_in_dim.35), calls=%async_computation.1 | async-start | bytes 589824 | tf_op jit(solution)/shard_map/all_to_all | solution.py:945
  48.2 2.0 collective-permute-start.7
  50.3 1.3 collective-permute-start.6
  53.0 7.8 %all-to-all-done.1 = bf16[16,65,128]{2,1,0:T(8,128)(2,1)S(1)} async-done(((bf16[16,65,128]{2,1,0:T(8,128)(2,1)}), bf16[16,65,128]{2,1,0:T(8,128)(2,1)S(1)}, u32[]{:S(2)}, u32[]{:S(2)}) %all-to-all-start.1) | async-done | bytes 266272 | tf_op jit(solution)/shard_map/all_to_all | solution.py:945
  61.1 0.9 reshape.225
  62.1 7.2 %all-to-all-start.2 = ((f32[32,1,1152]{2,1,0:T(1,128)}), f32[32,1,1152]{2,1,0:T(1,128)S(1)}, u32[]{:S(2)}, u32[]{:S(2)}) async-start(f32[32,1,1152]{2,1,0:T(1,128)} %reshape.225), calls=%async_computation.2 | async-start | bytes 294912 | tf_op jit(solution)/shard_map/all_to_all | solution.py:825
  69.3 1.4 pad_maximum_fusion.1.own_b
  71.0 2.3 pad_maximum_fusion.own_a
  75.5 4.8 %all-to-all-done.2 = f32[32,1,1152]{2,1,0:T(1,128)S(1)} async-done(((f32[32,1,1152]{2,1,0:T(1,128)}), f32[32,1,1152]{2,1,0:T(1,128)S(1)}, u32[]{:S(2)}, u32[]{:S(2)}) %all-to-all-start.2) | async-done | bytes 147488 | tf_op jit(solution)/shard_map/all_to_all | solution.py:825
  81.2 0.9 broadcast_in_dim.39.mods
  82.1 5.2 %first_conv.1.conv_in = bf16[4,256,768]{2,1,0:T(8,128)(2,1)} custom-call(s32[1]{0:T(128)S(6)} %copy.126.tag_ref, f32[4,256,768]{2,1,0:T(8,128)} %get-tuple-element.73.norm, f32[6,4,8,768]{3,2,1,0:T(8,128)} %broadcast_in_dim.39.mods, f32[9,768]{1,0:T(8,128)} %reshape.201.kernel), custom_call_target="tpu_custom_call" | custom-call | flops 600000000 | bytes 4194304 | tf_op jit(solution)/shard_map/first_conv/pallas_call | solution.py:232
  87.3 33.1 %attend.1 = (bf16[4,2304,256]{2,1,0:T(8,128)(2,1)}, bf16[4,256,768]{2,1,0:T(8,128)(2,1)}, bf16[4,256,768]{2,1,0:T(8,128)(2,1)}, f32[4,256,768]{2,1,0:T(8,128)}, ...) custom-call(s32[5]{0:T(128)} %stack.85.where.tag_ref, ...), custom_call_target="tpu_custom_call" | custom-call | flops 3800000000 | bytes 4194304 | tf_op jit(solution)/shard_map/attend/pallas_call | solution.py:347
  120.4 69.1 %feed.1 = (bf16[4,256,768]{2,1,0:T(8,128)(2,1)}, bf16[4,256,768]{2,1,0:T(8,128)(2,1)}, bf16[8,2,4,48,384]{4,3,2,1,0:T(8,128)(2,1)}, bf16[8,2,4,48,384]{4,3,2,1,0...) custom-call(s32[5]{0:T(128)} %stack.85.where.tag_ref, ...), custom_call_target="tpu_custom_call" | custom-call | flops 3800000000 | bytes 4194304 | tf_op jit(solution)/shard_map/feed/pallas_call | solution.py:467
  190.0 9.5 %attend_back_0.1 = (bf16[1,256,768]{2,1,0:T(8,128)(2,1)}, bf16[1,256,768]{2,1,0:T(8,128)(2,1)}, bf16[2304,256]{1,0:T(8,128)(2,1)}, bf16[768,256]{1,0:T(8,128)(2,1)}, f32[4,4,768]{2,1,0:T(4,128)}) custom-call(s32[5]{0:T(128)} %stack.85.where.tag_ref, f32[4,256,768]{2,1,0:T(8,128)} %get-tuple-element.83.resid, bf16[4,256,768]{2,1,0:T(8,128)(2,1)} %get-tuple-element.86.shrunk, ...), custom_call_target="tpu_custom_call" | custom-call | flops 900000000 | bytes 4194304 | tf_op jit(solution)/shard_map/attend_back_0/pallas_call | solution.py:590
  199.6 3.1 dynamic-slice_add_fusion.1
  202.7 1.0 collective-permute-start.12
  203.7 1.9 dynamic-slice_add_fusion
  205.6 1.5 collective-permute-start.13
  207.1 22.4 %attend_back_1.1 = (bf16[3,256,768]{2,1,0:T(8,128)(2,1)}, bf16[3,256,768]{2,1,0:T(8,128)(2,1)}, bf16[2304,768]{1,0:T(8,128)(2,1)}, bf16[768,768]{1,0:T(8,128)(2,1)}, f32[4,4,768]{2,1,0:T(4,128)}) custom-call(s32[5]{0:T(128)} %stack.85.where.tag_ref, f32[4,256,768]{2,1,0:T(8,128)} %get-tuple-element.83.resid, bf16[4,256,768]{2,1,0:T(8,128)(2,1)} %get-tuple-element.86.shrunk, ...), custom_call_target="tpu_custom_call" | custom-call | flops 2700000000 | bytes 4194304 | tf_op jit(solution)/shard_map/attend_back_1/pallas_call | solution.py:590
  229.5 1.4 collective-permute-done.12
  230.8 1.0 bitcast_add_fusion.1
  231.8 1.5 collective-permute-start.16
  233.3 1.0 bitcast_add_fusion
  234.3 1.0 collective-permute-start.17
  235.3 9.7 %project_grads.1 = (bf16[8,2,2,48,384]{4,3,2,1,0:T(8,128)(2,1)}, bf16[8,2,2,48,384]{4,3,2,1,0:T(8,128)(2,1)}, bf16[8,2,2,48,384]{4,3,2,1,0:T(8,128)(2,1)}, bf16[8,2,2,48,384]{4,3,2,1,0:T(8,128)(2,1)}) custom-call(s32[5]{0:T(128)} %stack.85.where.tag_ref, bf16[2304,256]{1,0:T(8,128)(2,1)} %get-tuple-element.92.d_qkv0, ...), custom_call_target="tpu_custom_call" | custom-call | flops 800000000 | bytes 4194304 | tf_op jit(solution)/shard_map/project_grads/pallas_call | solution.py:660
  245.7 1.0 collective-permute-done.16
  246.7 1.1 constant_dynamic-slice_fusion.2
  247.8 1.3 collective-permute-done.17
  249.2 1.1 constant_dynamic-slice_fusion
  250.7 1.1 pad_maximum_fusion.4
  252.9 0.9 fusion.1
  253.8 1.2 collective-permute-start.19
  256.2 1.0 collective-permute-start.18
  257.4 15.9 %conv_back.1 = (bf16[4,256,768]{2,1,0:T(8,128)(2,1)}, bf16[32,16,288]{2,1,0:T(8,128)(2,1)}) custom-call(s32[5]{0:T(128)} %stack.85.where.tag_ref, bf16[2304,256]{1,0:T(8,128)(2,1)} %get-tuple-element.92.d_qkv0, bf16[2304,768]{1,0:T(8,128)(2,1)} %get-tuple-element.100.d_qkv1, bf16[2304,768]{1,0:T(8,128)(2,1)} %get-tuple-element.114.weight, ...), custom_call_target="tpu_custom_call" | custom-call | flops 1500000000 | bytes 4194304 | tf_op jit(solution)/shard_map/conv_back/pallas_call | solution.py:745
  273.3 2.9 all-to-all-start.3
  276.5 1.9 fusion.17
  278.3 2.7 collective-permute-start.27
  281.0 1.7 fusion.24
  282.7 1.5 collective-permute-start.23
  284.2 1.0 fusion.25
  285.2 1.6 collective-permute-start.22
  286.8 7.6 %finish.1 = (bf16[1024,768]{1,0:T(8,128)(2,1)}, f32[1024,768]{1,0:T(8,128)}) custom-call(bf16[4,256,768]{2,1,0:T(8,128)(2,1)} %get-tuple-element.123.d_first, f32[4,256,768]{2,1,0:T(8,128)} %get-tuple-element.73.norm, f32[4,256,1]{2,1,0:T(8,128)} %get-tuple-element.124.factor, bf16[1,256,768]{2,1,0:T(8,128)(2,1)} %get-tuple-element.125.d_resid0, ...), custom_call_target="tpu_custom_call" | custom-call | flops 800000000 | bytes 4194304 | tf_op jit(solution)/shard_map/finish/pallas_call | solution.py:803
  294.3 0.9 all-to-all-done.3
  295.3 1.0 fusion.42
  299.4 3.6 %all-to-all-start.4 = ((bf16[16,48,128]{2,1,0:T(8,128)(2,1)}), bf16[16,48,128]{2,1,0:T(8,128)(2,1)S(1)}, u32[]{:S(2)}, u32[]{:S(2)}) async-start(bf16[16,48,128]{2,1,0:T(8,128)(2,1)} %constant_dynamic-update-slice_fusion), calls=%async_computation.4 | async-start | bytes 393216 | tf_op jit(solution)/shard_map/all_to_all | solution.py:962
  303.0 1.1 bitcast_add_fusion.4
  304.1 1.1 bitcast_add_fusion.6
  305.3 2.0 collective-permute-start.24
  307.3 2.4 collective-permute-start.25
  309.7 1.5 collective-permute-start.26
  311.1 1.3 all-to-all-done.4
  312.5 1.5 collective-permute-start.21
  314.0 1.3 convert_add_fusion
  316.9 0.9 fusion.5
  317.8 0.9 fusion.8
  318.7 2.3 collective-permute-done.25
  (134 shorter events, 19.9 us)
Async XLA Ops:
  7.2 53.7 %copy-start = (bf16[384,288]{0,1:T(8,128)(2,1)S(1)}, bf16[384,288]{0,1:T(8,128)(2,1)}, u32[]{:S(2)}) copy-start(bf16[384,288]{0,1:T(8,128)(2,1)} %param.20) | copy-start | bytes 663556
  7.2 2.8 copy-start.6
  7.2 2.8 copy-start.7
  7.2 8.9 %copy-start.13 = (s32[1,4]{1,0:T(1,128)S(1)}, s32[1,4]{1,0:T(1,128)}, u32[]{:S(2)}) copy-start(s32[1,4]{1,0:T(1,128)} %param.16) | copy-start | bytes 52
  7.2 8.9 %copy-start.12 = (s32[1,4]{1,0:T(1,128)S(1)}, s32[1,4]{1,0:T(1,128)}, u32[]{:S(2)}) copy-start(s32[1,4]{1,0:T(1,128)} %param.17) | copy-start | bytes 52
  7.2 113.2 %all-gather.2.cloned.1.call-start = ((), (), s32[]{:S(2)}) async-start(), calls=%async_computation.5 | async-start | bytes 9732096 | tf_op jit(solution)/shard_map/all_gather | solution.py:839
  10.0 26.9 %collective-permute-start.1 = (bf16[4,48,384]{2,1,0:T(8,128)(2,1)S(1)}, bf16[4,48,384]{2,1,0:T(8,128)(2,1)S(1)}, u32[]{:S(2)}, u32[]{:S(2)}) collective-permute-start(bf16[4,48,384]{2,1,0:T(8,128)(2,1)S(1)} %pad_maximum_fusion.8), channel_id=1, source_target_pairs={{0,24},{2,26},{4,28},{6,30},{8,0},{10,2},{12,4},{14,6},{16,8},{18,... | collective-permute-start | bytes 442376 | tf_op jit(solution)/shard_map/ppermute | solution.py:855
  15.1 21.8 %collective-permute-start.2 = (bf16[4,48,384]{2,1,0:T(8,128)(2,1)S(1)}, bf16[4,48,384]{2,1,0:T(8,128)(2,1)S(1)}, u32[]{:S(2)}, u32[]{:S(2)}) collective-permute-start(bf16[4,48,384]{2,1,0:T(8,128)(2,1)S(1)} %pad_maximum_fusion.8), channel_id=1, source_target_pairs={{0,16},{2,18},{4,20},{6,22},{8,24},{10,26},{12,28},{14,30},{16,0},... | collective-permute-start | bytes 442376 | tf_op jit(solution)/shard_map/ppermute | solution.py:855
  15.1 21.8 %collective-permute-start.3 = (bf16[4,48,384]{2,1,0:T(8,128)(2,1)S(1)}, bf16[4,48,384]{2,1,0:T(8,128)(2,1)S(1)}, u32[]{:S(2)}, u32[]{:S(2)}) collective-permute-start(bf16[4,48,384]{2,1,0:T(8,128)(2,1)S(1)} %pad_maximum_fusion.8), channel_id=1, source_target_pairs={{0,8},{2,10},{4,12},{6,14},{8,16},{10,18},{12,20},{14,22},{16,24},... | collective-permute-start | bytes 442376 | tf_op jit(solution)/shard_map/ppermute | solution.py:855
  16.8 15.3 %all-to-all-start = ((s32[32,1,8]{2,1,0:T(1,128)}), s32[32,1,8]{2,1,0:T(1,128)S(1)}, u32[]{:S(2)}, u32[]{:S(2)}) async-start(s32[32,1,8]{2,1,0:T(1,128)} %broadcast_in_dim.34), calls=%async_computation | async-start | bytes 32768 | tf_op jit(solution)/shard_map/all_to_all | solution.py:825
  21.9 10.5 %copy-start.10 = (bf16[500,48]{0,1:T(8,128)(2,1)S(1)}, bf16[500,48]{0,1:T(8,128)(2,1)}, u32[]{:S(2)}) copy-start(bf16[500,48]{0,1:T(8,128)(2,1)} %param.18) | copy-start | bytes 144004
  21.9 10.8 %copy-start.11 = (bf16[500,48]{0,1:T(8,128)(2,1)S(1)}, bf16[500,48]{0,1:T(8,128)(2,1)}, u32[]{:S(2)}) copy-start(bf16[500,48]{0,1:T(8,128)(2,1)} %param.19) | copy-start | bytes 144004
  21.9 11.7 %copy-start.8 = (bf16[9,192]{1,0:T(8,128)(2,1)S(1)}, bf16[9,192]{1,0:T(8,128)(2,1)}, u32[]{:S(2)}) copy-start(bf16[9,192]{1,0:T(8,128)(2,1)} %param.25) | copy-start | bytes 10372
  21.9 11.7 %copy-start.9 = (bf16[9,48]{1,0:T(8,128)(2,1)S(1)}, bf16[9,48]{1,0:T(8,128)(2,1)}, u32[]{:S(2)}) copy-start(bf16[9,48]{1,0:T(8,128)(2,1)} %param.21) | copy-start | bytes 2596
  33.0 3.9 %collective-permute-start = (f32[48,128]{1,0:T(8,128)S(1)}, f32[48,128]{1,0:T(8,128)S(1)}, u32[]{:S(2)}, u32[]{:S(2)}) collective-permute-start(f32[48,128]{1,0:T(8,128)S(1)} %fusion), channel_id=1, source_target_pairs={{0,1},{1,0},{2,3},{3,2},{4,5},{5,4},{6,7},{7,6},{8,9},{9,8},{10,11... | collective-permute-start | bytes 73736 | tf_op jit(solution)/shard_map/ppermute | solution.py:879
  37.1 11.0 %collective-permute-start.5 = (bf16[4,2,48,384]{3,2,1,0:T(8,128)(2,1)S(1)}, bf16[4,2,48,384]{3,2,1,0:T(8,128)(2,1)S(1)}, u32[]{:S(2)}, u32[]{:S(2)}) collective-permute-start(bf16[4,2,48,384]{3,2,1,0:T(8,128)(2,1)S(1)} %get-tuple-element.169), channel_id=1, source_target_pairs={{0,1},{1,0},{2,3},{3,2},{4,5},{5,4},{6,7},{7,6},{8,9},{9,8},{10,11... | collective-permute-start | bytes 884744 | tf_op jit(solution)/shard_map/ppermute | solution.py:879
  37.8 12.4 %collective-permute-start.4 = (bf16[4,2,48,384]{3,2,1,0:T(8,128)(2,1)S(1)}, bf16[4,2,48,384]{3,2,1,0:T(8,128)(2,1)S(1)}, u32[]{:S(2)}, u32[]{:S(2)}) collective-permute-start(bf16[4,2,48,384]{3,2,1,0:T(8,128)(2,1)S(1)} %get-tuple-element.171), channel_id=1, source_target_pairs={{0,4},{2,6},{4,0},{6,2},{8,12},{10,14},{12,8},{14,10},{16,20},{18,... | collective-permute-start | bytes 884744 | tf_op jit(solution)/shard_map/ppermute | solution.py:880
  39.3 21.5 %all-to-all-start.1 = ((bf16[16,65,128]{2,1,0:T(8,128)(2,1)}), bf16[16,65,128]{2,1,0:T(8,128)(2,1)S(1)}, u32[]{:S(2)}, u32[]{:S(2)}) async-start(bf16[16,65,128]{2,1,0:T(8,128)(2,1)} %broadcast_in_dim.35), calls=%async_computation.1 | async-start | bytes 589824 | tf_op jit(solution)/shard_map/all_to_all | solution.py:945
  48.2 21.0 %collective-permute-start.7 = (bf16[2,4,2,48,384]{4,3,2,1,0:T(8,128)(2,1)S(1)}, bf16[2,4,2,48,384]{4,3,2,1,0:T(8,128)(2,1)}, u32[]{:S(2)}, u32[]{:S(2)}) collective-permute-start(bf16[2,4,2,48,384]{4,3,2,1,0:T(8,128)(2,1)S(1)} %get-tuple-element.165), channel_id=1, source_target_pairs={{0,4},{2,6},{4,0},{6,2},{8,12},{10,14},{12,8},{14,10},{16,20},{18,... | collective-permute-start | bytes 1769480 | tf_op jit(solution)/shard_map/ppermute | solution.py:880
  50.3 20.6 %collective-permute-start.6 = (bf16[2,4,2,48,384]{4,3,2,1,0:T(8,128)(2,1)S(1)}, bf16[2,4,2,48,384]{4,3,2,1,0:T(8,128)(2,1)}, u32[]{:S(2)}, u32[]{:S(2)}) collective-permute-start(bf16[2,4,2,48,384]{4,3,2,1,0:T(8,128)(2,1)S(1)} %get-tuple-element.167), channel_id=1, source_target_pairs={{0,1},{1,0},{2,3},{3,2},{4,5},{5,4},{6,7},{7,6},{8,9},{9,8},{10,11... | collective-permute-start | bytes 1769480 | tf_op jit(solution)/shard_map/ppermute | solution.py:879
  62.1 18.2 %all-to-all-start.2 = ((f32[32,1,1152]{2,1,0:T(1,128)}), f32[32,1,1152]{2,1,0:T(1,128)S(1)}, u32[]{:S(2)}, u32[]{:S(2)}) async-start(f32[32,1,1152]{2,1,0:T(1,128)} %reshape.225), calls=%async_computation.2 | async-start | bytes 294912 | tf_op jit(solution)/shard_map/all_to_all | solution.py:825
  70.6 2.6 copy-start.5
  70.6 16.7 %collective-permute-start.9 = (bf16[2,2,4,2,48,384]{5,4,3,2,1,0:T(8,128)(2,1)S(1)}, bf16[2,2,4,2,48,384]{5,4,3,2,1,0:T(8,128)(2,1)}, u32[]{:S(2)}, u32[]{:S(2)}) collective-permute-start(bf16[2,2,4,2,48,384]{5,4,3,2,1,0:T(8,128)(2,1)S(1)} %pad_maximum_fusion.1.own_b), channel_id=1, source_target_pairs={{0,2},{2,0},{4,6},{6,4},{8,10},{10,8},{12,14},{14,12},{16,18},{18,... | collective-permute-start | bytes 3538952 | tf_op jit(solution)/shard_map/ppermute | solution.py:880
  73.3 14.1 %collective-permute-start.8 = (bf16[2,2,4,2,48,384]{5,4,3,2,1,0:T(8,128)(2,1)}, bf16[2,2,4,2,48,384]{5,4,3,2,1,0:T(8,128)(2,1)}, u32[]{:S(2)}, u32[]{:S(2)}) collective-permute-start(bf16[2,2,4,2,48,384]{5,4,3,2,1,0:T(8,128)(2,1)} %pad_maximum_fusion.own_a), channel_id=1, source_target_pairs={{0,2},{2,0},{4,6},{6,4},{8,10},{10,8},{12,14},{14,12},{16,18},{18,... | collective-permute-start | bytes 3538952 | tf_op jit(solution)/shard_map/ppermute | solution.py:880
  189.5 10.1 %collective-permute-start.11 = (bf16[8,2,4,48,384]{4,3,2,1,0:T(8,128)(2,1)}, bf16[8,2,4,48,384]{4,3,2,1,0:T(8,128)(2,1)}, u32[]{:S(2)}, u32[]{:S(2)}) collective-permute-start(bf16[8,2,4,48,384]{4,3,2,1,0:T(8,128)(2,1)} %get-tuple-element.97), channel_id=1, source_target_pairs={{0,2},{2,0},{4,6},{6,4},{8,10},{10,8},{12,14},{14,12},{16,18},{18,... | collective-permute-start | bytes 7077896 | tf_op jit(solution)/shard_map/ppermute | solution.py:880
  189.6 10.0 %collective-permute-start.10 = (bf16[8,2,4,48,384]{4,3,2,1,0:T(8,128)(2,1)}, bf16[8,2,4,48,384]{4,3,2,1,0:T(8,128)(2,1)}, u32[]{:S(2)}, u32[]{:S(2)}) collective-permute-start(bf16[8,2,4,48,384]{4,3,2,1,0:T(8,128)(2,1)} %get-tuple-element.94), channel_id=1, source_target_pairs={{0,2},{2,0},{4,6},{6,4},{8,10},{10,8},{12,14},{14,12},{16,18},{18,... | collective-permute-start | bytes 7077896 | tf_op jit(solution)/shard_map/ppermute | solution.py:880
  190.0 9.5 %copy-start.2 = (bf16[8,2,4,48,384]{4,3,2,1,0:T(8,128)(2,1)S(1)}, bf16[8,2,4,48,384]{4,3,2,1,0:T(8,128)(2,1)}, u32[]{:S(2)}) copy-start(bf16[8,2,4,48,384]{4,3,2,1,0:T(8,128)(2,1)} %get-tuple-element.93) | copy-start | bytes 7077892
  199.6 4.1 %copy-start.1 = (bf16[8,2,4,48,384]{4,3,2,1,0:T(8,128)(2,1)S(1)}, bf16[8,2,4,48,384]{4,3,2,1,0:T(8,128)(2,1)}, u32[]{:S(2)}) copy-start(bf16[8,2,4,48,384]{4,3,2,1,0:T(8,128)(2,1)} %get-tuple-element.96) | copy-start | bytes 7077892
  202.7 28.2 %collective-permute-start.12 = (bf16[4,2,4,48,384]{4,3,2,1,0:T(8,128)(2,1)}, bf16[4,2,4,48,384]{4,3,2,1,0:T(8,128)(2,1)S(1)}, u32[]{:S(2)}, u32[]{:S(2)}) collective-permute-start(bf16[4,2,4,48,384]{4,3,2,1,0:T(8,128)(2,1)} %get-tuple-element.140), channel_id=1, source_target_pairs={{0,1},{1,0},{2,3},{3,2},{4,5},{5,4},{6,7},{7,6},{8,9},{9,8},{10,11... | collective-permute-start | bytes 3538952 | tf_op jit(solution)/shard_map/ppermute | solution.py:879
  205.6 27.7 %collective-permute-start.13 = (bf16[4,2,4,48,384]{4,3,2,1,0:T(8,128)(2,1)S(1)}, bf16[4,2,4,48,384]{4,3,2,1,0:T(8,128)(2,1)S(1)}, u32[]{:S(2)}, u32[]{:S(2)}) collective-permute-start(bf16[4,2,4,48,384]{4,3,2,1,0:T(8,128)(2,1)S(1)} %get-tuple-element.138), channel_id=1, source_target_pairs={{0,4},{2,6},{4,0},{6,2},{8,12},{10,14},{12,8},{14,10},{16,20},{18,... | collective-permute-start | bytes 3538952 | tf_op jit(solution)/shard_map/ppermute | solution.py:880
  231.8 14.9 %collective-permute-start.16 = (bf16[4,4,48,384]{3,2,1,0:T(8,128)(2,1)}, bf16[4,4,48,384]{3,2,1,0:T(8,128)(2,1)}, u32[]{:S(2)}, u32[]{:S(2)}) collective-permute-start(bf16[4,4,48,384]{3,2,1,0:T(8,128)(2,1)} %get-tuple-element.142), channel_id=1, source_target_pairs={{0,4},{2,6},{4,0},{6,2},{8,12},{10,14},{12,8},{14,10},{16,20},{18,... | collective-permute-start | bytes 1769480 | tf_op jit(solution)/shard_map/ppermute | solution.py:880
  234.3 14.9 %collective-permute-start.17 = (bf16[4,4,48,384]{3,2,1,0:T(8,128)(2,1)}, bf16[4,4,48,384]{3,2,1,0:T(8,128)(2,1)}, u32[]{:S(2)}, u32[]{:S(2)}) collective-permute-start(bf16[4,4,48,384]{3,2,1,0:T(8,128)(2,1)} %get-tuple-element.144), channel_id=1, source_target_pairs={{0,1},{1,0},{2,3},{3,2},{4,5},{5,4},{6,7},{7,6},{8,9},{9,8},{10,11... | collective-permute-start | bytes 1769480 | tf_op jit(solution)/shard_map/ppermute | solution.py:879
  245.0 7.7 %collective-permute-start.15 = (bf16[8,2,2,48,384]{4,3,2,1,0:T(8,128)(2,1)}, bf16[8,2,2,48,384]{4,3,2,1,0:T(8,128)(2,1)S(1)}, u32[]{:S(2)}, u32[]{:S(2)}) collective-permute-start(bf16[8,2,2,48,384]{4,3,2,1,0:T(8,128)(2,1)} %get-tuple-element.111), channel_id=1, source_target_pairs={{0,2},{2,0},{4,6},{6,4},{8,10},{10,8},{12,14},{14,12},{16,18},{18,... | collective-permute-start | bytes 3538952 | tf_op jit(solution)/shard_map/ppermute | solution.py:880
  245.2 9.8 %collective-permute-start.14 = (bf16[8,2,2,48,384]{4,3,2,1,0:T(8,128)(2,1)}, bf16[8,2,2,48,384]{4,3,2,1,0:T(8,128)(2,1)S(1)}, u32[]{:S(2)}, u32[]{:S(2)}) collective-permute-start(bf16[8,2,2,48,384]{4,3,2,1,0:T(8,128)(2,1)} %get-tuple-element.109), channel_id=1, source_target_pairs={{0,2},{2,0},{4,6},{6,4},{8,10},{10,8},{12,14},{14,12},{16,18},{18,... | collective-permute-start | bytes 3538952 | tf_op jit(solution)/shard_map/ppermute | solution.py:880
  250.5 2.2 copy-start.4
  251.9 24.6 %collective-permute-start.20 = (bf16[2,8,48,384]{3,1,2,0:T(8,128)(2,1)}, bf16[2,8,48,384]{3,1,2,0:T(8,128)(2,1)}, u32[]{:S(2)}, u32[]{:S(2)}) collective-permute-start(bf16[2,8,48,384]{3,1,2,0:T(8,128)(2,1)} %pad_maximum_fusion.4), channel_id=1, source_target_pairs={{0,8},{2,10},{4,12},{6,14},{8,0},{10,2},{12,4},{14,6},{16,24},{18,... | collective-permute-start | bytes 1769480 | tf_op jit(solution)/shard_map/ppermute | solution.py:880
  252.9 2.1 copy-start.3
  253.8 27.2 %collective-permute-start.19 = (bf16[4,2,2,48,384]{4,3,2,0,1:T(8,128)(2,1)}, bf16[4,2,2,48,384]{4,3,2,0,1:T(8,128)(2,1)}, u32[]{:S(2)}, u32[]{:S(2)}) collective-permute-start(bf16[4,2,2,48,384]{4,3,2,0,1:T(8,128)(2,1)} %fusion.1), channel_id=1, source_target_pairs={{0,4},{2,6},{4,0},{6,2},{8,12},{10,14},{12,8},{14,10},{16,20},{18,... | collective-permute-start | bytes 1769480 | tf_op jit(solution)/shard_map/ppermute | solution.py:880
  256.2 24.9 %collective-permute-start.18 = (bf16[4,2,2,48,384]{4,3,2,0,1:T(8,128)(2,1)}, bf16[4,2,2,48,384]{4,3,2,0,1:T(8,128)(2,1)}, u32[]{:S(2)}, u32[]{:S(2)}) collective-permute-start(bf16[4,2,2,48,384]{4,3,2,0,1:T(8,128)(2,1)} %fusion.2), channel_id=1, source_target_pairs={{0,1},{1,0},{2,3},{3,2},{4,5},{5,4},{6,7},{7,6},{8,9},{9,8},{10,11... | collective-permute-start | bytes 1769480 | tf_op jit(solution)/shard_map/ppermute | solution.py:879
  273.3 21.9 %all-to-all-start.3 = ((bf16[32,16,288]{2,1,0:T(8,128)(2,1)}), bf16[32,16,288]{2,1,0:T(8,128)(2,1)S(1)}, u32[]{:S(2)}, u32[]{:S(2)}) async-start(bf16[32,16,288]{2,1,0:T(8,128)(2,1)} %get-tuple-element.122), calls=%async_computation.3 | async-start | bytes 786432 | tf_op jit(solution)/shard_map/all_to_all | solution.py:825
  278.3 32.8 %collective-permute-start.27 = (bf16[8,48,384]{2,0,1:T(8,128)(2,1)}, bf16[8,48,384]{2,0,1:T(8,128)(2,1)}, u32[]{:S(2)}, u32[]{:S(2)}) collective-permute-start(bf16[8,48,384]{2,0,1:T(8,128)(2,1)} %fusion.17), channel_id=1, source_target_pairs={{0,16},{2,18},{4,20},{6,22},{8,24},{10,26},{12,28},{14,30},{16,0},... | collective-permute-start | bytes 884744 | tf_op jit(solution)/shard_map/ppermute | solution.py:880
  282.7 20.3 %collective-permute-start.23 = (bf16[4,2,48,384]{3,2,1,0:T(8,128)(2,1)}, bf16[4,2,48,384]{3,2,1,0:T(8,128)(2,1)}, u32[]{:S(2)}, u32[]{:S(2)}) collective-permute-start(bf16[4,2,48,384]{3,2,1,0:T(8,128)(2,1)} %fusion.24), channel_id=1, source_target_pairs={{0,1},{1,0},{2,3},{3,2},{4,5},{5,4},{6,7},{7,6},{8,9},{9,8},{10,11... | collective-permute-start | bytes 884744 | tf_op jit(solution)/shard_map/ppermute | solution.py:879
  285.2 18.9 %collective-permute-start.22 = (bf16[4,2,48,384]{3,2,1,0:T(8,128)(2,1)S(1)}, bf16[4,2,48,384]{3,2,1,0:T(8,128)(2,1)}, u32[]{:S(2)}, u32[]{:S(2)}) collective-permute-start(bf16[4,2,48,384]{3,2,1,0:T(8,128)(2,1)S(1)} %fusion.25), channel_id=1, source_target_pairs={{0,4},{2,6},{4,0},{6,2},{8,12},{10,14},{12,8},{14,10},{16,20},{18,... | collective-permute-start | bytes 884744 | tf_op jit(solution)/shard_map/ppermute | solution.py:880
  299.4 13.1 %all-to-all-start.4 = ((bf16[16,48,128]{2,1,0:T(8,128)(2,1)}), bf16[16,48,128]{2,1,0:T(8,128)(2,1)S(1)}, u32[]{:S(2)}, u32[]{:S(2)}) async-start(bf16[16,48,128]{2,1,0:T(8,128)(2,1)} %constant_dynamic-update-slice_fusion), calls=%async_computation.4 | async-start | bytes 393216 | tf_op jit(solution)/shard_map/all_to_all | solution.py:962
  305.3 13.4 %collective-permute-start.24 = (bf16[4,48,384]{2,1,0:T(8,128)(2,1)S(1)}, bf16[4,48,384]{2,1,0:T(8,128)(2,1)S(1)}, u32[]{:S(2)}, u32[]{:S(2)}) collective-permute-start(bf16[4,48,384]{2,1,0:T(8,128)(2,1)S(1)} %get-tuple-element.153), channel_id=1, source_target_pairs={{0,8},{2,10},{4,12},{6,14},{8,16},{10,18},{12,20},{14,22},{16,24},... | collective-permute-start | bytes 442376 | tf_op jit(solution)/shard_map/ppermute | solution.py:896
  307.3 13.7 %collective-permute-start.25 = (bf16[4,48,384]{2,1,0:T(8,128)(2,1)S(1)}, bf16[4,48,384]{2,1,0:T(8,128)(2,1)S(1)}, u32[]{:S(2)}, u32[]{:S(2)}) collective-permute-start(bf16[4,48,384]{2,1,0:T(8,128)(2,1)S(1)} %get-tuple-element.154), channel_id=1, source_target_pairs={{0,16},{2,18},{4,20},{6,22},{8,24},{10,26},{12,28},{14,30},{16,0},... | collective-permute-start | bytes 442376 | tf_op jit(solution)/shard_map/ppermute | solution.py:896
  309.7 11.4 %collective-permute-start.26 = (bf16[4,48,384]{2,1,0:T(8,128)(2,1)S(1)}, bf16[4,48,384]{2,1,0:T(8,128)(2,1)S(1)}, u32[]{:S(2)}, u32[]{:S(2)}) collective-permute-start(bf16[4,48,384]{2,1,0:T(8,128)(2,1)S(1)} %get-tuple-element.155), channel_id=1, source_target_pairs={{0,24},{2,26},{4,28},{6,30},{8,0},{10,2},{12,4},{14,6},{16,8},{18,... | collective-permute-start | bytes 442376 | tf_op jit(solution)/shard_map/ppermute | solution.py:896
  312.5 4.4 %collective-permute-start.21 = (f32[48,128]{1,0:T(8,128)S(1)}, f32[48,128]{1,0:T(8,128)S(1)}, u32[]{:S(2)}, u32[]{:S(2)}) collective-permute-start(f32[48,128]{1,0:T(8,128)S(1)} %convert_reduce_fusion.1), channel_id=1, source_target_pairs={{0,1},{1,0},{2,3},{3,2},{4,5},{5,4},{6,7},{7,6},{8,9},{9,8},{10,11... | collective-permute-start | bytes 73736 | tf_op jit(solution)/shard_map/ppermute | solution.py:879
Sparse Core Ops, SparseCore 0:
  11.6 93.0 all-gather.1

commit v11 on v10

--- a/solution.py
+++ b/solution.py
@@ -628,7 +628,7 @@
     )(tag, resid, shrunk, d_second, gradient, attn, mods, qkv, lse, proj_t)
 
 
-PAIRS = 2
+PAIRS = 4
 ROWS = 288 * PAIRS
 
 

time: 331 us -> 331 us (level)
  no operation moved by 1% of the time
where the time goes in v11:
time: 331 us; the launch traced here: 329 us
  Pallas kernels  178 us (54%)
  starting transfers between devices  61.8 us (19%)
  waiting for transfers between devices  27.9 us (8%)
  other arithmetic  25.7 us (8%)
  local copies, waits for them, and re-layouts  15.9 us (5%)
  between operations  15.5 us (5%)
  matrix products  3.83 us (1%)
    pallas_call x1, Pallas kernels, feed(): pl.pallas_call(feed_kernel, grid=(FF // CHUNK,), in_specs=[SMEM_SPEC, who...  69.1 us
    pallas_call x1, Pallas kernels, attend(): pl.pallas_call(attend_kernel, grid=(4,), in_specs=[SMEM_SPEC, group_spec(...  33.1 us
    pallas_call x2, Pallas kernels, attend_back(): pl.pallas_call(attend_back_kernel, grid=(count,), in_specs=[SMEM_SPEC, pi...  31.9 us
    pallas_call x1, Pallas kernels, conv_back(): pl.pallas_call(conv_back_kernel, grid=(8 // PAIRS,), in_specs=[SMEM_SPEC,...  15.5 us
    all_to_all x3, starting transfers between devices, exchange(): return lax.all_to_all(pieces, BOTH, 0, 0, tiled=True)  15.4 us
    ppermute x14, starting transfers between devices, swap(): return lax.ppermute(value, 'dp', [(i, i ^ bit) for i in range(NJ)])  13.4 us
    pallas_call x1, Pallas kernels, project_grads(): pl.pallas_call(project_grads_kernel, grid=(8 // PAIRS,), in_specs=[SMEM_S...  10.1 us
    all_to_all x3, waiting for transfers between devices, exchange(): return lax.all_to_all(pieces, BOTH, 0, 0, tiled=True)  9.85 us
  transfers between devices with their start and end apart: 34, of which 10 were waited for; matrix products, arithmetic and copies ran while one was open for 12% of the time, Pallas kernels for 33%

profile of v11, /device:TPU:0, one launch (start us, length us, event | category | flops | bytes accessed | tf_op | source)
XLA Modules:
  0.0 328.9 jit_solution(6831312887986970597)
XLA Ops:
  7.3 1.0 copy.123
  8.3 1.7 pad_maximum_fusion.7
  10.0 5.1 %collective-permute-start.1 = (bf16[4,48,384]{2,1,0:T(8,128)(2,1)S(1)}, bf16[4,48,384]{2,1,0:T(8,128)(2,1)S(1)}, u32[]{:S(2)}, u32[]{:S(2)}) collective-permute-start(bf16[4,48,384]{2,1,0:T(8,128)(2,1)S(1)} %pad_maximum_fusion.8), channel_id=1, source_target_pairs={{0,24},{2,26},{4,28},{6,30},{8,0},{10,2},{12,4},{14,6},{16,8},{18,... | collective-permute-start | bytes 442376 | tf_op jit(solution)/shard_map/ppermute | solution.py:855
  15.1 1.0 collective-permute-start.3
  16.8 5.1 %all-to-all-start = ((s32[32,1,8]{2,1,0:T(1,128)}), s32[32,1,8]{2,1,0:T(1,128)S(1)}, u32[]{:S(2)}, u32[]{:S(2)}) async-start(s32[32,1,8]{2,1,0:T(1,128)} %broadcast_in_dim.34), calls=%async_computation | async-start | bytes 32768 | tf_op jit(solution)/shard_map/all_to_all | solution.py:825
  21.9 6.0 %prepare.1 = (bf16[4,256,768]{2,1,0:T(8,128)(2,1)}, bf16[4,256,768]{2,1,0:T(8,128)(2,1)}, f32[4,256,768]{2,1,0:T(8,128)}, f32[4,256,1]{2,1,0:T(8,128)}) custom-call(bf16[1024,768]{1,0:T(8,128)(2,1)} %latents.1, bf16[1024,768]{1,0:T(8,128)(2,1)} %cotangent.1), custom_call_target="tpu_custom_call" | custom-call | flops 600000000 | bytes 4194304 | tf_op jit(solution)/shard_map/prepare/pallas_call | solution.py:89
  28.0 4.2 %all-to-all-done = s32[32,1,8]{2,1,0:T(1,128)S(1)} async-done(((s32[32,1,8]{2,1,0:T(1,128)}), s32[32,1,8]{2,1,0:T(1,128)S(1)}, u32[]{:S(2)}, u32[]{:S(2)}) %all-to-all-start) | async-done | bytes 1056 | tf_op jit(solution)/shard_map/all_to_all | solution.py:825
  33.8 3.1 collective-permute-done
  39.3 8.8 %all-to-all-start.1 = ((bf16[16,65,128]{2,1,0:T(8,128)(2,1)}), bf16[16,65,128]{2,1,0:T(8,128)(2,1)S(1)}, u32[]{:S(2)}, u32[]{:S(2)}) async-start(bf16[16,65,128]{2,1,0:T(8,128)(2,1)} %broadcast_in_dim.35), calls=%async_computation.1 | async-start | bytes 589824 | tf_op jit(solution)/shard_map/all_to_all | solution.py:945
  48.2 2.0 collective-permute-start.7
  50.3 1.3 collective-permute-start.6
  53.0 7.8 %all-to-all-done.1 = bf16[16,65,128]{2,1,0:T(8,128)(2,1)S(1)} async-done(((bf16[16,65,128]{2,1,0:T(8,128)(2,1)}), bf16[16,65,128]{2,1,0:T(8,128)(2,1)S(1)}, u32[]{:S(2)}, u32[]{:S(2)}) %all-to-all-start.1) | async-done | bytes 266272 | tf_op jit(solution)/shard_map/all_to_all | solution.py:945
  61.1 0.9 reshape.225
  62.1 7.2 %all-to-all-start.2 = ((f32[32,1,1152]{2,1,0:T(1,128)}), f32[32,1,1152]{2,1,0:T(1,128)S(1)}, u32[]{:S(2)}, u32[]{:S(2)}) async-start(f32[32,1,1152]{2,1,0:T(1,128)} %reshape.225), calls=%async_computation.2 | async-start | bytes 294912 | tf_op jit(solution)/shard_map/all_to_all | solution.py:825
  69.3 1.4 pad_maximum_fusion.1.own_b
  71.0 2.3 pad_maximum_fusion.own_a
  75.5 4.8 %all-to-all-done.2 = f32[32,1,1152]{2,1,0:T(1,128)S(1)} async-done(((f32[32,1,1152]{2,1,0:T(1,128)}), f32[32,1,1152]{2,1,0:T(1,128)S(1)}, u32[]{:S(2)}, u32[]{:S(2)}) %all-to-all-start.2) | async-done | bytes 147488 | tf_op jit(solution)/shard_map/all_to_all | solution.py:825
  81.2 0.9 broadcast_in_dim.39.mods
  82.1 5.2 %first_conv.1.conv_in = bf16[4,256,768]{2,1,0:T(8,128)(2,1)} custom-call(s32[1]{0:T(128)S(6)} %copy.126.tag_ref, f32[4,256,768]{2,1,0:T(8,128)} %get-tuple-element.73.norm, f32[6,4,8,768]{3,2,1,0:T(8,128)} %broadcast_in_dim.39.mods, f32[9,768]{1,0:T(8,128)} %reshape.201.kernel), custom_call_target="tpu_custom_call" | custom-call | flops 600000000 | bytes 4194304 | tf_op jit(solution)/shard_map/first_conv/pallas_call | solution.py:232
  87.3 33.1 %attend.1 = (bf16[4,2304,256]{2,1,0:T(8,128)(2,1)}, bf16[4,256,768]{2,1,0:T(8,128)(2,1)}, bf16[4,256,768]{2,1,0:T(8,128)(2,1)}, f32[4,256,768]{2,1,0:T(8,128)}, ...) custom-call(s32[5]{0:T(128)} %stack.85.where.tag_ref, ...), custom_call_target="tpu_custom_call" | custom-call | flops 3800000000 | bytes 4194304 | tf_op jit(solution)/shard_map/attend/pallas_call | solution.py:347
  120.4 69.1 %feed.1 = (bf16[4,256,768]{2,1,0:T(8,128)(2,1)}, bf16[4,256,768]{2,1,0:T(8,128)(2,1)}, bf16[8,2,4,48,384]{4,3,2,1,0:T(8,128)(2,1)}, bf16[8,2,4,48,384]{4,3,2,1,0...) custom-call(s32[5]{0:T(128)} %stack.85.where.tag_ref, ...), custom_call_target="tpu_custom_call" | custom-call | flops 3800000000 | bytes 4194304 | tf_op jit(solution)/shard_map/feed/pallas_call | solution.py:467
  190.0 9.5 %attend_back_0.1 = (bf16[1,256,768]{2,1,0:T(8,128)(2,1)}, bf16[1,256,768]{2,1,0:T(8,128)(2,1)}, bf16[2304,256]{1,0:T(8,128)(2,1)}, bf16[768,256]{1,0:T(8,128)(2,1)}, f32[4,4,768]{2,1,0:T(4,128)}) custom-call(s32[5]{0:T(128)} %stack.85.where.tag_ref, f32[4,256,768]{2,1,0:T(8,128)} %get-tuple-element.83.resid, bf16[4,256,768]{2,1,0:T(8,128)(2,1)} %get-tuple-element.86.shrunk, ...), custom_call_target="tpu_custom_call" | custom-call | flops 900000000 | bytes 4194304 | tf_op jit(solution)/shard_map/attend_back_0/pallas_call | solution.py:590
  199.6 3.1 dynamic-slice_add_fusion.1
  202.7 1.0 collective-permute-start.12
  203.7 1.9 dynamic-slice_add_fusion
  205.6 1.5 collective-permute-start.13
  207.1 22.4 %attend_back_1.1 = (bf16[3,256,768]{2,1,0:T(8,128)(2,1)}, bf16[3,256,768]{2,1,0:T(8,128)(2,1)}, bf16[2304,768]{1,0:T(8,128)(2,1)}, bf16[768,768]{1,0:T(8,128)(2,1)}, f32[4,4,768]{2,1,0:T(4,128)}) custom-call(s32[5]{0:T(128)} %stack.85.where.tag_ref, f32[4,256,768]{2,1,0:T(8,128)} %get-tuple-element.83.resid, bf16[4,256,768]{2,1,0:T(8,128)(2,1)} %get-tuple-element.86.shrunk, ...), custom_call_target="tpu_custom_call" | custom-call | flops 2700000000 | bytes 4194304 | tf_op jit(solution)/shard_map/attend_back_1/pallas_call | solution.py:590
  229.5 1.4 collective-permute-done.12
  230.8 1.0 bitcast_add_fusion.1
  231.8 1.5 collective-permute-start.16
  233.3 1.0 bitcast_add_fusion
  234.3 1.0 collective-permute-start.17
  235.3 10.1 %project_grads.1 = (bf16[8,2,2,48,384]{4,3,2,1,0:T(8,128)(2,1)}, bf16[8,2,2,48,384]{4,3,2,1,0:T(8,128)(2,1)}, bf16[8,2,2,48,384]{4,3,2,1,0:T(8,128)(2,1)}, bf16[8,2,2,48,384]{4,3,2,1,0:T(8,128)(2,1)}) custom-call(s32[5]{0:T(128)} %stack.85.where.tag_ref, bf16[2304,256]{1,0:T(8,128)(2,1)} %get-tuple-element.92.d_qkv0, ...), custom_call_target="tpu_custom_call" | custom-call | flops 800000000 | bytes 4194304 | tf_op jit(solution)/shard_map/project_grads/pallas_call | solution.py:660
  246.7 1.1 constant_dynamic-slice_fusion.2
  247.8 1.3 collective-permute-done.17
  249.2 1.1 constant_dynamic-slice_fusion
  250.7 1.1 pad_maximum_fusion.4
  252.9 0.9 fusion.1
  253.8 1.2 collective-permute-start.19
  255.3 0.9 fusion.2
  256.2 1.0 collective-permute-start.18
  257.4 15.5 %conv_back.1 = (bf16[4,256,768]{2,1,0:T(8,128)(2,1)}, bf16[32,16,288]{2,1,0:T(8,128)(2,1)}) custom-call(s32[5]{0:T(128)} %stack.85.where.tag_ref, bf16[2304,256]{1,0:T(8,128)(2,1)} %get-tuple-element.92.d_qkv0, bf16[2304,768]{1,0:T(8,128)(2,1)} %get-tuple-element.100.d_qkv1, bf16[2304,768]{1,0:T(8,128)(2,1)} %get-tuple-element.114.weight, ...), custom_call_target="tpu_custom_call" | custom-call | flops 1500000000 | bytes 4194304 | tf_op jit(solution)/shard_map/conv_back/pallas_call | solution.py:745
  272.9 3.2 all-to-all-start.3
  276.3 1.9 fusion.17
  278.2 2.4 collective-permute-start.27
  280.6 1.7 fusion.24
  282.3 1.5 collective-permute-start.23
  283.8 1.0 fusion.25
  284.8 1.6 collective-permute-start.22
  286.3 7.6 %finish.1 = (bf16[1024,768]{1,0:T(8,128)(2,1)}, f32[1024,768]{1,0:T(8,128)}) custom-call(bf16[4,256,768]{2,1,0:T(8,128)(2,1)} %get-tuple-element.123.d_first, f32[4,256,768]{2,1,0:T(8,128)} %get-tuple-element.73.norm, f32[4,256,1]{2,1,0:T(8,128)} %get-tuple-element.124.factor, bf16[1,256,768]{2,1,0:T(8,128)(2,1)} %get-tuple-element.125.d_resid0, ...), custom_call_target="tpu_custom_call" | custom-call | flops 800000000 | bytes 4194304 | tf_op jit(solution)/shard_map/finish/pallas_call | solution.py:803
  293.9 0.9 all-to-all-done.3
  294.9 1.0 fusion.42
  299.0 3.6 %all-to-all-start.4 = ((bf16[16,48,128]{2,1,0:T(8,128)(2,1)}), bf16[16,48,128]{2,1,0:T(8,128)(2,1)S(1)}, u32[]{:S(2)}, u32[]{:S(2)}) async-start(bf16[16,48,128]{2,1,0:T(8,128)(2,1)} %constant_dynamic-update-slice_fusion), calls=%async_computation.4 | async-start | bytes 393216 | tf_op jit(solution)/shard_map/all_to_all | solution.py:962
  302.6 1.1 bitcast_add_fusion.4
  303.7 1.1 bitcast_add_fusion.6
  304.9 2.0 collective-permute-start.24
  306.9 2.4 collective-permute-start.25
  309.2 1.5 collective-permute-start.26
  310.7 1.3 all-to-all-done.4
  312.1 1.5 collective-permute-start.21
  313.6 1.3 convert_add_fusion
  316.5 0.9 fusion.5
  317.4 0.9 fusion.8
  318.3 2.3 collective-permute-done.25
  (134 shorter events, 19.7 us)
Async XLA Ops:
  7.2 53.7 %copy-start = (bf16[384,288]{0,1:T(8,128)(2,1)S(1)}, bf16[384,288]{0,1:T(8,128)(2,1)}, u32[]{:S(2)}) copy-start(bf16[384,288]{0,1:T(8,128)(2,1)} %param.20) | copy-start | bytes 663556
  7.2 2.8 copy-start.6
  7.2 2.8 copy-start.7
  7.2 8.9 %copy-start.13 = (s32[1,4]{1,0:T(1,128)S(1)}, s32[1,4]{1,0:T(1,128)}, u32[]{:S(2)}) copy-start(s32[1,4]{1,0:T(1,128)} %param.16) | copy-start | bytes 52
  7.2 8.9 %copy-start.12 = (s32[1,4]{1,0:T(1,128)S(1)}, s32[1,4]{1,0:T(1,128)}, u32[]{:S(2)}) copy-start(s32[1,4]{1,0:T(1,128)} %param.17) | copy-start | bytes 52
  7.2 113.2 %all-gather.2.cloned.1.call-start = ((), (), s32[]{:S(2)}) async-start(), calls=%async_computation.5 | async-start | bytes 9732096 | tf_op jit(solution)/shard_map/all_gather | solution.py:839
  10.0 26.9 %collective-permute-start.1 = (bf16[4,48,384]{2,1,0:T(8,128)(2,1)S(1)}, bf16[4,48,384]{2,1,0:T(8,128)(2,1)S(1)}, u32[]{:S(2)}, u32[]{:S(2)}) collective-permute-start(bf16[4,48,384]{2,1,0:T(8,128)(2,1)S(1)} %pad_maximum_fusion.8), channel_id=1, source_target_pairs={{0,24},{2,26},{4,28},{6,30},{8,0},{10,2},{12,4},{14,6},{16,8},{18,... | collective-permute-start | bytes 442376 | tf_op jit(solution)/shard_map/ppermute | solution.py:855
  15.1 21.8 %collective-permute-start.2 = (bf16[4,48,384]{2,1,0:T(8,128)(2,1)S(1)}, bf16[4,48,384]{2,1,0:T(8,128)(2,1)S(1)}, u32[]{:S(2)}, u32[]{:S(2)}) collective-permute-start(bf16[4,48,384]{2,1,0:T(8,128)(2,1)S(1)} %pad_maximum_fusion.8), channel_id=1, source_target_pairs={{0,16},{2,18},{4,20},{6,22},{8,24},{10,26},{12,28},{14,30},{16,0},... | collective-permute-start | bytes 442376 | tf_op jit(solution)/shard_map/ppermute | solution.py:855
  15.1 21.8 %collective-permute-start.3 = (bf16[4,48,384]{2,1,0:T(8,128)(2,1)S(1)}, bf16[4,48,384]{2,1,0:T(8,128)(2,1)S(1)}, u32[]{:S(2)}, u32[]{:S(2)}) collective-permute-start(bf16[4,48,384]{2,1,0:T(8,128)(2,1)S(1)} %pad_maximum_fusion.8), channel_id=1, source_target_pairs={{0,8},{2,10},{4,12},{6,14},{8,16},{10,18},{12,20},{14,22},{16,24},... | collective-permute-start | bytes 442376 | tf_op jit(solution)/shard_map/ppermute | solution.py:855
  16.8 15.3 %all-to-all-start = ((s32[32,1,8]{2,1,0:T(1,128)}), s32[32,1,8]{2,1,0:T(1,128)S(1)}, u32[]{:S(2)}, u32[]{:S(2)}) async-start(s32[32,1,8]{2,1,0:T(1,128)} %broadcast_in_dim.34), calls=%async_computation | async-start | bytes 32768 | tf_op jit(solution)/shard_map/all_to_all | solution.py:825
  21.9 10.5 %copy-start.10 = (bf16[500,48]{0,1:T(8,128)(2,1)S(1)}, bf16[500,48]{0,1:T(8,128)(2,1)}, u32[]{:S(2)}) copy-start(bf16[500,48]{0,1:T(8,128)(2,1)} %param.18) | copy-start | bytes 144004
  21.9 10.8 %copy-start.11 = (bf16[500,48]{0,1:T(8,128)(2,1)S(1)}, bf16[500,48]{0,1:T(8,128)(2,1)}, u32[]{:S(2)}) copy-start(bf16[500,48]{0,1:T(8,128)(2,1)} %param.19) | copy-start | bytes 144004
  21.9 11.7 %copy-start.8 = (bf16[9,192]{1,0:T(8,128)(2,1)S(1)}, bf16[9,192]{1,0:T(8,128)(2,1)}, u32[]{:S(2)}) copy-start(bf16[9,192]{1,0:T(8,128)(2,1)} %param.25) | copy-start | bytes 10372
  21.9 11.7 %copy-start.9 = (bf16[9,48]{1,0:T(8,128)(2,1)S(1)}, bf16[9,48]{1,0:T(8,128)(2,1)}, u32[]{:S(2)}) copy-start(bf16[9,48]{1,0:T(8,128)(2,1)} %param.21) | copy-start | bytes 2596
  33.0 3.9 %collective-permute-start = (f32[48,128]{1,0:T(8,128)S(1)}, f32[48,128]{1,0:T(8,128)S(1)}, u32[]{:S(2)}, u32[]{:S(2)}) collective-permute-start(f32[48,128]{1,0:T(8,128)S(1)} %fusion), channel_id=1, source_target_pairs={{0,1},{1,0},{2,3},{3,2},{4,5},{5,4},{6,7},{7,6},{8,9},{9,8},{10,11... | collective-permute-start | bytes 73736 | tf_op jit(solution)/shard_map/ppermute | solution.py:879
  37.1 11.0 %collective-permute-start.5 = (bf16[4,2,48,384]{3,2,1,0:T(8,128)(2,1)S(1)}, bf16[4,2,48,384]{3,2,1,0:T(8,128)(2,1)S(1)}, u32[]{:S(2)}, u32[]{:S(2)}) collective-permute-start(bf16[4,2,48,384]{3,2,1,0:T(8,128)(2,1)S(1)} %get-tuple-element.169), channel_id=1, source_target_pairs={{0,1},{1,0},{2,3},{3,2},{4,5},{5,4},{6,7},{7,6},{8,9},{9,8},{10,11... | collective-permute-start | bytes 884744 | tf_op jit(solution)/shard_map/ppermute | solution.py:879
  37.8 12.4 %collective-permute-start.4 = (bf16[4,2,48,384]{3,2,1,0:T(8,128)(2,1)S(1)}, bf16[4,2,48,384]{3,2,1,0:T(8,128)(2,1)S(1)}, u32[]{:S(2)}, u32[]{:S(2)}) collective-permute-start(bf16[4,2,48,384]{3,2,1,0:T(8,128)(2,1)S(1)} %get-tuple-element.171), channel_id=1, source_target_pairs={{0,4},{2,6},{4,0},{6,2},{8,12},{10,14},{12,8},{14,10},{16,20},{18,... | collective-permute-start | bytes 884744 | tf_op jit(solution)/shard_map/ppermute | solution.py:880
  39.3 21.5 %all-to-all-start.1 = ((bf16[16,65,128]{2,1,0:T(8,128)(2,1)}), bf16[16,65,128]{2,1,0:T(8,128)(2,1)S(1)}, u32[]{:S(2)}, u32[]{:S(2)}) async-start(bf16[16,65,128]{2,1,0:T(8,128)(2,1)} %broadcast_in_dim.35), calls=%async_computation.1 | async-start | bytes 589824 | tf_op jit(solution)/shard_map/all_to_all | solution.py:945
  48.2 21.0 %collective-permute-start.7 = (bf16[2,4,2,48,384]{4,3,2,1,0:T(8,128)(2,1)S(1)}, bf16[2,4,2,48,384]{4,3,2,1,0:T(8,128)(2,1)}, u32[]{:S(2)}, u32[]{:S(2)}) collective-permute-start(bf16[2,4,2,48,384]{4,3,2,1,0:T(8,128)(2,1)S(1)} %get-tuple-element.165), channel_id=1, source_target_pairs={{0,4},{2,6},{4,0},{6,2},{8,12},{10,14},{12,8},{14,10},{16,20},{18,... | collective-permute-start | bytes 1769480 | tf_op jit(solution)/shard_map/ppermute | solution.py:880
  50.3 20.6 %collective-permute-start.6 = (bf16[2,4,2,48,384]{4,3,2,1,0:T(8,128)(2,1)S(1)}, bf16[2,4,2,48,384]{4,3,2,1,0:T(8,128)(2,1)}, u32[]{:S(2)}, u32[]{:S(2)}) collective-permute-start(bf16[2,4,2,48,384]{4,3,2,1,0:T(8,128)(2,1)S(1)} %get-tuple-element.167), channel_id=1, source_target_pairs={{0,1},{1,0},{2,3},{3,2},{4,5},{5,4},{6,7},{7,6},{8,9},{9,8},{10,11... | collective-permute-start | bytes 1769480 | tf_op jit(solution)/shard_map/ppermute | solution.py:879
  62.1 18.2 %all-to-all-start.2 = ((f32[32,1,1152]{2,1,0:T(1,128)}), f32[32,1,1152]{2,1,0:T(1,128)S(1)}, u32[]{:S(2)}, u32[]{:S(2)}) async-start(f32[32,1,1152]{2,1,0:T(1,128)} %reshape.225), calls=%async_computation.2 | async-start | bytes 294912 | tf_op jit(solution)/shard_map/all_to_all | solution.py:825
  70.6 2.6 copy-start.5
  70.6 16.7 %collective-permute-start.9 = (bf16[2,2,4,2,48,384]{5,4,3,2,1,0:T(8,128)(2,1)S(1)}, bf16[2,2,4,2,48,384]{5,4,3,2,1,0:T(8,128)(2,1)}, u32[]{:S(2)}, u32[]{:S(2)}) collective-permute-start(bf16[2,2,4,2,48,384]{5,4,3,2,1,0:T(8,128)(2,1)S(1)} %pad_maximum_fusion.1.own_b), channel_id=1, source_target_pairs={{0,2},{2,0},{4,6},{6,4},{8,10},{10,8},{12,14},{14,12},{16,18},{18,... | collective-permute-start | bytes 3538952 | tf_op jit(solution)/shard_map/ppermute | solution.py:880
  73.3 14.1 %collective-permute-start.8 = (bf16[2,2,4,2,48,384]{5,4,3,2,1,0:T(8,128)(2,1)}, bf16[2,2,4,2,48,384]{5,4,3,2,1,0:T(8,128)(2,1)}, u32[]{:S(2)}, u32[]{:S(2)}) collective-permute-start(bf16[2,2,4,2,48,384]{5,4,3,2,1,0:T(8,128)(2,1)} %pad_maximum_fusion.own_a), channel_id=1, source_target_pairs={{0,2},{2,0},{4,6},{6,4},{8,10},{10,8},{12,14},{14,12},{16,18},{18,... | collective-permute-start | bytes 3538952 | tf_op jit(solution)/shard_map/ppermute | solution.py:880
  189.5 10.1 %collective-permute-start.11 = (bf16[8,2,4,48,384]{4,3,2,1,0:T(8,128)(2,1)}, bf16[8,2,4,48,384]{4,3,2,1,0:T(8,128)(2,1)}, u32[]{:S(2)}, u32[]{:S(2)}) collective-permute-start(bf16[8,2,4,48,384]{4,3,2,1,0:T(8,128)(2,1)} %get-tuple-element.97), channel_id=1, source_target_pairs={{0,2},{2,0},{4,6},{6,4},{8,10},{10,8},{12,14},{14,12},{16,18},{18,... | collective-permute-start | bytes 7077896 | tf_op jit(solution)/shard_map/ppermute | solution.py:880
  189.6 10.0 %collective-permute-start.10 = (bf16[8,2,4,48,384]{4,3,2,1,0:T(8,128)(2,1)}, bf16[8,2,4,48,384]{4,3,2,1,0:T(8,128)(2,1)}, u32[]{:S(2)}, u32[]{:S(2)}) collective-permute-start(bf16[8,2,4,48,384]{4,3,2,1,0:T(8,128)(2,1)} %get-tuple-element.94), channel_id=1, source_target_pairs={{0,2},{2,0},{4,6},{6,4},{8,10},{10,8},{12,14},{14,12},{16,18},{18,... | collective-permute-start | bytes 7077896 | tf_op jit(solution)/shard_map/ppermute | solution.py:880
  190.0 9.5 %copy-start.2 = (bf16[8,2,4,48,384]{4,3,2,1,0:T(8,128)(2,1)S(1)}, bf16[8,2,4,48,384]{4,3,2,1,0:T(8,128)(2,1)}, u32[]{:S(2)}) copy-start(bf16[8,2,4,48,384]{4,3,2,1,0:T(8,128)(2,1)} %get-tuple-element.93) | copy-start | bytes 7077892
  199.6 4.1 %copy-start.1 = (bf16[8,2,4,48,384]{4,3,2,1,0:T(8,128)(2,1)S(1)}, bf16[8,2,4,48,384]{4,3,2,1,0:T(8,128)(2,1)}, u32[]{:S(2)}) copy-start(bf16[8,2,4,48,384]{4,3,2,1,0:T(8,128)(2,1)} %get-tuple-element.96) | copy-start | bytes 7077892
  202.7 28.2 %collective-permute-start.12 = (bf16[4,2,4,48,384]{4,3,2,1,0:T(8,128)(2,1)}, bf16[4,2,4,48,384]{4,3,2,1,0:T(8,128)(2,1)S(1)}, u32[]{:S(2)}, u32[]{:S(2)}) collective-permute-start(bf16[4,2,4,48,384]{4,3,2,1,0:T(8,128)(2,1)} %get-tuple-element.140), channel_id=1, source_target_pairs={{0,1},{1,0},{2,3},{3,2},{4,5},{5,4},{6,7},{7,6},{8,9},{9,8},{10,11... | collective-permute-start | bytes 3538952 | tf_op jit(solution)/shard_map/ppermute | solution.py:879
  205.6 27.7 %collective-permute-start.13 = (bf16[4,2,4,48,384]{4,3,2,1,0:T(8,128)(2,1)S(1)}, bf16[4,2,4,48,384]{4,3,2,1,0:T(8,128)(2,1)S(1)}, u32[]{:S(2)}, u32[]{:S(2)}) collective-permute-start(bf16[4,2,4,48,384]{4,3,2,1,0:T(8,128)(2,1)S(1)} %get-tuple-element.138), channel_id=1, source_target_pairs={{0,4},{2,6},{4,0},{6,2},{8,12},{10,14},{12,8},{14,10},{16,20},{18,... | collective-permute-start | bytes 3538952 | tf_op jit(solution)/shard_map/ppermute | solution.py:880
  231.8 14.9 %collective-permute-start.16 = (bf16[4,4,48,384]{3,2,1,0:T(8,128)(2,1)}, bf16[4,4,48,384]{3,2,1,0:T(8,128)(2,1)}, u32[]{:S(2)}, u32[]{:S(2)}) collective-permute-start(bf16[4,4,48,384]{3,2,1,0:T(8,128)(2,1)} %get-tuple-element.142), channel_id=1, source_target_pairs={{0,4},{2,6},{4,0},{6,2},{8,12},{10,14},{12,8},{14,10},{16,20},{18,... | collective-permute-start | bytes 1769480 | tf_op jit(solution)/shard_map/ppermute | solution.py:880
  234.3 14.9 %collective-permute-start.17 = (bf16[4,4,48,384]{3,2,1,0:T(8,128)(2,1)}, bf16[4,4,48,384]{3,2,1,0:T(8,128)(2,1)}, u32[]{:S(2)}, u32[]{:S(2)}) collective-permute-start(bf16[4,4,48,384]{3,2,1,0:T(8,128)(2,1)} %get-tuple-element.144), channel_id=1, source_target_pairs={{0,1},{1,0},{2,3},{3,2},{4,5},{5,4},{6,7},{7,6},{8,9},{9,8},{10,11... | collective-permute-start | bytes 1769480 | tf_op jit(solution)/shard_map/ppermute | solution.py:879
  245.3 7.4 %collective-permute-start.15 = (bf16[8,2,2,48,384]{4,3,2,1,0:T(8,128)(2,1)}, bf16[8,2,2,48,384]{4,3,2,1,0:T(8,128)(2,1)S(1)}, u32[]{:S(2)}, u32[]{:S(2)}) collective-permute-start(bf16[8,2,2,48,384]{4,3,2,1,0:T(8,128)(2,1)} %get-tuple-element.111), channel_id=1, source_target_pairs={{0,2},{2,0},{4,6},{6,4},{8,10},{10,8},{12,14},{14,12},{16,18},{18,... | collective-permute-start | bytes 3538952 | tf_op jit(solution)/shard_map/ppermute | solution.py:880
  245.5 9.6 %collective-permute-start.14 = (bf16[8,2,2,48,384]{4,3,2,1,0:T(8,128)(2,1)}, bf16[8,2,2,48,384]{4,3,2,1,0:T(8,128)(2,1)S(1)}, u32[]{:S(2)}, u32[]{:S(2)}) collective-permute-start(bf16[8,2,2,48,384]{4,3,2,1,0:T(8,128)(2,1)} %get-tuple-element.109), channel_id=1, source_target_pairs={{0,2},{2,0},{4,6},{6,4},{8,10},{10,8},{12,14},{14,12},{16,18},{18,... | collective-permute-start | bytes 3538952 | tf_op jit(solution)/shard_map/ppermute | solution.py:880
  250.5 2.2 copy-start.4
  251.9 24.4 %collective-permute-start.20 = (bf16[2,8,48,384]{3,1,2,0:T(8,128)(2,1)}, bf16[2,8,48,384]{3,1,2,0:T(8,128)(2,1)}, u32[]{:S(2)}, u32[]{:S(2)}) collective-permute-start(bf16[2,8,48,384]{3,1,2,0:T(8,128)(2,1)} %pad_maximum_fusion.4), channel_id=1, source_target_pairs={{0,8},{2,10},{4,12},{6,14},{8,0},{10,2},{12,4},{14,6},{16,24},{18,... | collective-permute-start | bytes 1769480 | tf_op jit(solution)/shard_map/ppermute | solution.py:880
  252.9 2.1 copy-start.3
  253.8 26.7 %collective-permute-start.19 = (bf16[4,2,2,48,384]{4,3,2,0,1:T(8,128)(2,1)}, bf16[4,2,2,48,384]{4,3,2,0,1:T(8,128)(2,1)}, u32[]{:S(2)}, u32[]{:S(2)}) collective-permute-start(bf16[4,2,2,48,384]{4,3,2,0,1:T(8,128)(2,1)} %fusion.1), channel_id=1, source_target_pairs={{0,4},{2,6},{4,0},{6,2},{8,12},{10,14},{12,8},{14,10},{16,20},{18,... | collective-permute-start | bytes 1769480 | tf_op jit(solution)/shard_map/ppermute | solution.py:880
  256.2 24.4 %collective-permute-start.18 = (bf16[4,2,2,48,384]{4,3,2,0,1:T(8,128)(2,1)}, bf16[4,2,2,48,384]{4,3,2,0,1:T(8,128)(2,1)}, u32[]{:S(2)}, u32[]{:S(2)}) collective-permute-start(bf16[4,2,2,48,384]{4,3,2,0,1:T(8,128)(2,1)} %fusion.2), channel_id=1, source_target_pairs={{0,1},{1,0},{2,3},{3,2},{4,5},{5,4},{6,7},{7,6},{8,9},{9,8},{10,11... | collective-permute-start | bytes 1769480 | tf_op jit(solution)/shard_map/ppermute | solution.py:879
  272.9 21.9 %all-to-all-start.3 = ((bf16[32,16,288]{2,1,0:T(8,128)(2,1)}), bf16[32,16,288]{2,1,0:T(8,128)(2,1)S(1)}, u32[]{:S(2)}, u32[]{:S(2)}) async-start(bf16[32,16,288]{2,1,0:T(8,128)(2,1)} %get-tuple-element.122), calls=%async_computation.3 | async-start | bytes 786432 | tf_op jit(solution)/shard_map/all_to_all | solution.py:825
  278.2 32.5 %collective-permute-start.27 = (bf16[8,48,384]{2,0,1:T(8,128)(2,1)}, bf16[8,48,384]{2,0,1:T(8,128)(2,1)}, u32[]{:S(2)}, u32[]{:S(2)}) collective-permute-start(bf16[8,48,384]{2,0,1:T(8,128)(2,1)} %fusion.17), channel_id=1, source_target_pairs={{0,16},{2,18},{4,20},{6,22},{8,24},{10,26},{12,28},{14,30},{16,0},... | collective-permute-start | bytes 884744 | tf_op jit(solution)/shard_map/ppermute | solution.py:880
  282.3 20.3 %collective-permute-start.23 = (bf16[4,2,48,384]{3,2,1,0:T(8,128)(2,1)}, bf16[4,2,48,384]{3,2,1,0:T(8,128)(2,1)}, u32[]{:S(2)}, u32[]{:S(2)}) collective-permute-start(bf16[4,2,48,384]{3,2,1,0:T(8,128)(2,1)} %fusion.24), channel_id=1, source_target_pairs={{0,1},{1,0},{2,3},{3,2},{4,5},{5,4},{6,7},{7,6},{8,9},{9,8},{10,11... | collective-permute-start | bytes 884744 | tf_op jit(solution)/shard_map/ppermute | solution.py:879
  284.8 18.9 %collective-permute-start.22 = (bf16[4,2,48,384]{3,2,1,0:T(8,128)(2,1)S(1)}, bf16[4,2,48,384]{3,2,1,0:T(8,128)(2,1)}, u32[]{:S(2)}, u32[]{:S(2)}) collective-permute-start(bf16[4,2,48,384]{3,2,1,0:T(8,128)(2,1)S(1)} %fusion.25), channel_id=1, source_target_pairs={{0,4},{2,6},{4,0},{6,2},{8,12},{10,14},{12,8},{14,10},{16,20},{18,... | collective-permute-start | bytes 884744 | tf_op jit(solution)/shard_map/ppermute | solution.py:880
  299.0 13.1 %all-to-all-start.4 = ((bf16[16,48,128]{2,1,0:T(8,128)(2,1)}), bf16[16,48,128]{2,1,0:T(8,128)(2,1)S(1)}, u32[]{:S(2)}, u32[]{:S(2)}) async-start(bf16[16,48,128]{2,1,0:T(8,128)(2,1)} %constant_dynamic-update-slice_fusion), calls=%async_computation.4 | async-start | bytes 393216 | tf_op jit(solution)/shard_map/all_to_all | solution.py:962
  304.9 13.4 %collective-permute-start.24 = (bf16[4,48,384]{2,1,0:T(8,128)(2,1)S(1)}, bf16[4,48,384]{2,1,0:T(8,128)(2,1)S(1)}, u32[]{:S(2)}, u32[]{:S(2)}) collective-permute-start(bf16[4,48,384]{2,1,0:T(8,128)(2,1)S(1)} %get-tuple-element.153), channel_id=1, source_target_pairs={{0,8},{2,10},{4,12},{6,14},{8,16},{10,18},{12,20},{14,22},{16,24},... | collective-permute-start | bytes 442376 | tf_op jit(solution)/shard_map/ppermute | solution.py:896
  306.9 13.7 %collective-permute-start.25 = (bf16[4,48,384]{2,1,0:T(8,128)(2,1)S(1)}, bf16[4,48,384]{2,1,0:T(8,128)(2,1)S(1)}, u32[]{:S(2)}, u32[]{:S(2)}) collective-permute-start(bf16[4,48,384]{2,1,0:T(8,128)(2,1)S(1)} %get-tuple-element.154), channel_id=1, source_target_pairs={{0,16},{2,18},{4,20},{6,22},{8,24},{10,26},{12,28},{14,30},{16,0},... | collective-permute-start | bytes 442376 | tf_op jit(solution)/shard_map/ppermute | solution.py:896
  309.2 11.4 %collective-permute-start.26 = (bf16[4,48,384]{2,1,0:T(8,128)(2,1)S(1)}, bf16[4,48,384]{2,1,0:T(8,128)(2,1)S(1)}, u32[]{:S(2)}, u32[]{:S(2)}) collective-permute-start(bf16[4,48,384]{2,1,0:T(8,128)(2,1)S(1)} %get-tuple-element.155), channel_id=1, source_target_pairs={{0,24},{2,26},{4,28},{6,30},{8,0},{10,2},{12,4},{14,6},{16,8},{18,... | collective-permute-start | bytes 442376 | tf_op jit(solution)/shard_map/ppermute | solution.py:896
  312.1 4.4 %collective-permute-start.21 = (f32[48,128]{1,0:T(8,128)S(1)}, f32[48,128]{1,0:T(8,128)S(1)}, u32[]{:S(2)}, u32[]{:S(2)}) collective-permute-start(f32[48,128]{1,0:T(8,128)S(1)} %convert_reduce_fusion.1), channel_id=1, source_target_pairs={{0,1},{1,0},{2,3},{3,2},{4,5},{5,4},{6,7},{7,6},{8,9},{9,8},{10,11... | collective-permute-start | bytes 73736 | tf_op jit(solution)/shard_map/ppermute | solution.py:879
Sparse Core Ops, SparseCore 0:
  11.6 93.0 all-gather.1
